TPU v7x, 32 devices: a whole 2x2x4 slice. The times are simulated.
32 devices in a mesh: dom: 8 (over z, y), rep: 4 (over x, core).
Axes of the slice: x: 2, y: 2, z: 4, core: 2. Of those that a mesh axis runs over, the one named last changes fastest.
Arguments:
- features: bfloat16 [16384, 768], P(('dom', 'rep')), may hold values from -13 to 13
- sketch_matrix: bfloat16 [768, 256], replicated, may hold values from -0.21875 to 0.21875
- tiles: bfloat16 [8, 20, 256, 256], P('dom'), may hold values from 0 to 2, as said below
- tile_dst: int32 [8, 20], P('dom'), may hold values from -1 to 7, as said below
- tile_src: int32 [8, 20], P('dom'), may hold values from 0 to 11, as said below
- halo_index: int32 [8, 1024], P('dom'), may hold values from 0 to 2047
- send_order: int32 [8, 2048], P('dom'), may hold values from 0 to 2047, each once within a row
- arrival_place: int32 [8, 2048], P('dom'), may hold values from 0 to 2047, each once within a row
Outputs:
- signals: bfloat16 [3, 256, 16384], P(None, 'rep', 'dom')
Inputs may be any that keep to these rules, and one draw needn't show every extreme that they name: `tiles`: entries are zero or positive; in slot t < 8 of every partition the tile's diagonal is positive. `tile_dst`: in every partition slot t < 8 holds t, the live slots come first and the others hold -1; some partition uses every slot and some only the first 12. `tile_src`: slot t < 12 holds t in every partition; empty slots hold 0. `halo_index`: A row may be listed for several peers and more than once. `send_order`: each row is a permutation. `arrival_place`: each row is a permutation.
All inputs are finite; a program needn't handle non-finite values.
Results may differ from a plain program's by a relative error of at most 0.0034.
Values may be sent and summed in bfloat16 or wider, within the bound.
No kernel may reach another device: no remote copies, remote signals or barrier semaphores. Data moves between devices by JAX's collectives and lax.ppermute only.
A program may use at most 64 MiB of HBM per device.

v0:
```python
import jax
import jax.numpy as jnp
from jax import lax
from jax.sharding import PartitionSpec as P


def on_device(
    features, sketch_matrix, tiles, tile_dst, tile_src, halo_index, send_order, arrival_place
):
    sketched = lax.dot_general(
        sketch_matrix, features, (((0,), (1,)), ((), ())), preferred_element_type=jnp.float32
    ).astype(jnp.bfloat16)
    hop0 = lax.all_to_all(sketched, "rep", split_axis=0, concat_axis=1, tiled=True)
    tile_set = tiles[0]
    targets = tile_dst[0]
    sources = tile_src[0]
    halo_rows = halo_index[0]
    order = send_order[0]
    place = arrival_place[0]
    channels, node_count = hop0.shape
    tile_size = tile_set.shape[-1]
    block_count = node_count // tile_size
    onehot = (targets[:, None] == jnp.arange(block_count, dtype=jnp.int32)[None, :]).astype(
        jnp.float32
    )
    row_sums = jnp.sum(tile_set, axis=2, dtype=jnp.float32)
    degree = jnp.einsum("ti,tb->bi", row_sums, onehot, precision=lax.Precision.HIGHEST).reshape(
        node_count
    )

    def combine(layer, received):
        columns = jnp.concatenate([layer, received], 1)
        blocks = columns.reshape(channels, -1, tile_size)[:, sources, :]
        products = jnp.einsum("ctj,tij->cti", blocks, tile_set, preferred_element_type=jnp.float32)
        summed = jnp.einsum("cti,tb->cbi", products, onehot, precision=lax.Precision.HIGHEST)
        summed = summed.reshape(channels, node_count)
        return (summed / degree[None, :]).astype(jnp.bfloat16)

    hop1 = combine(
        hop0, lax.all_to_all(hop0[:, halo_rows], "dom", split_axis=1, concat_axis=1, tiled=True)
    )
    hop2 = combine(
        hop1, lax.all_to_all(hop1[:, halo_rows], "dom", split_axis=1, concat_axis=1, tiled=True)
    )
    stacked = jnp.concatenate([hop0, hop1, hop2], 0)[:, order]
    arrived = lax.all_to_all(stacked, "dom", split_axis=1, concat_axis=1, tiled=True)
    placed = jnp.zeros_like(arrived).at[:, place].set(arrived)
    return placed.reshape(3, channels, node_count)


def solution(mesh):
    in_specs = (
        P(("dom", "rep"), None),
        P(),
        P("dom", None, None, None),
        P("dom", None),
        P("dom", None),
        P("dom", None),
        P("dom", None),
        P("dom", None),
    )
    out_specs = P(None, "rep", "dom")
    return jax.shard_map(
        on_device, mesh=mesh, in_specs=in_specs, out_specs=out_specs, check_vma=False
    )
```

profile of v0, /device:TPU:0, one launch (start us, length us, event | category | flops | bytes accessed | tf_op | source)
XLA Modules:
  0.0 109.8 jit_solution(15514057003822116897)
XLA Ops:
  0.0 0.0 copy-start
  0.0 1.1 %copy-done = bf16[512,768]{1,0:T(8,128)(2,1)S(1)} copy-done((bf16[512,768]{1,0:T(8,128)(2,1)S(1)}, bf16[512,768]{1,0:T(8,128)(2,1)}, u32[]{:S(2)}) %copy-start) | copy-done | bytes 786456
  1.1 2.1 %convolution_convert_fusion = bf16[256,512]{1,0:T(8,128)(2,1)} fusion(bf16[768,256]{1,0:T(8,128)(2,1)} %param.9, bf16[512,768]{1,0:T(8,128)(2,1)S(1)} %copy-done), kind=kOutput, calls=%fused_computation.17 | convolution fusion | flops 201457664 | bytes 1441792 | tf_op jit(solution)/shard_map/dot_general | solution.py:10
  3.3 4.4 %all-to-all-start = ((bf16[4,64,512]{2,1,0:T(8,128)(2,1)}), bf16[4,64,512]{2,1,0:T(8,128)(2,1)S(1)}, u32[]{:S(2)}, u32[]{:S(2)}) async-start(bf16[4,64,512]{2,1,0:T(8,128)(2,1)} %bitcast.2), calls=%async_computation | async-start | bytes 524288 | tf_op jit(solution)/shard_map/all_to_all | solution.py:13
  7.6 0.0 copy-done.10
  7.6 2.5 %convert_reduce_fusion = f32[20,256]{1,0:T(8,128)S(1)} fusion(bf16[1,20,256,256]{3,2,1,0:T(8,128)(2,1)} %param.10), kind=kLoop, calls=%fused_computation.6 | loop fusion | flops 2616320 | bytes 2641920 | tf_op jit(solution)/shard_map/reduce_sum | solution.py:26
  10.1 0.0 copy-done.8
  10.1 0.1 convolution_bitcast_fusion
  10.3 3.3 %all-to-all-done = bf16[4,64,512]{2,1,0:T(8,128)(2,1)S(1)} async-done(((bf16[4,64,512]{2,1,0:T(8,128)(2,1)}), bf16[4,64,512]{2,1,0:T(8,128)(2,1)S(1)}, u32[]{:S(2)}, u32[]{:S(2)}) %all-to-all-start) | async-done | bytes 262176 | tf_op jit(solution)/shard_map/all_to_all | solution.py:13
  13.7 0.3 copy.76
  13.9 3.2 %gather_fusion = bf16[1024,64]{1,0:T(8,128)(2,1)S(1)} fusion(bf16[64,2048]{0,1:T(8,128)(2,1)S(1)} %copy.76, s32[1024]{0:T(1024)S(1)} %broadcast_clamp_fusion.1), kind=kCustom, calls=%fused_computation | custom fusion | bytes 266240 | tf_op jit(solution)/shard_map/gather | solution.py:40
  17.2 0.8 copy.77
  17.9 6.5 %all-to-all-start.1 = ((bf16[64,8,128]{2,0,1:T(8,128)(2,1)}), bf16[64,8,128]{2,0,1:T(8,128)(2,1)S(1)}, u32[]{:S(2)}, u32[]{:S(2)}) async-start(bf16[64,8,128]{2,0,1:T(8,128)(2,1)} %copy.77), calls=%async_computation.1 | async-start | bytes 262144 | tf_op jit(solution)/shard_map/all_to_all | solution.py:40
  24.4 7.3 %all-to-all-done.1 = bf16[64,8,128]{2,0,1:T(8,128)(2,1)S(1)} async-done(((bf16[64,8,128]{2,0,1:T(8,128)(2,1)}), bf16[64,8,128]{2,0,1:T(8,128)(2,1)S(1)}, u32[]{:S(2)}, u32[]{:S(2)}) %all-to-all-start.1) | async-done | bytes 131104 | tf_op jit(solution)/shard_map/all_to_all | solution.py:40
  31.8 0.0 copy-start.1
  31.8 1.1 %pad_maximum_fusion.1 = bf16[64,3072]{1,0:T(8,128)(2,1)S(1)} fusion(bf16[64,1024]{1,0:T(8,128)(2,1)S(1)} %copy_bitcast_fusion.3, bf16[64,2048]{1,0:T(8,128)(2,1)} %bitcast.87), kind=kLoop, calls=%fused_computation.28 | loop fusion | flops 786432 | bytes 786432 | tf_op jit(solution)/shard_map/concatenate | solution.py:32
  32.9 0.8 copy.109
  33.7 2.5 %gather_fusion.1 = bf16[20,64,256]{2,1,0:T(8,128)(2,1)} fusion(bf16[64,12,256]{2,0,1:T(8,128)(2,1)} %bitcast.90, s32[1024]{0:T(1024)S(1)} %pad_clamp_fusion), kind=kCustom, calls=%fused_computation.1 | custom fusion | bytes 1310800 | tf_op jit(solution)/shard_map/gather | solution.py:33
  36.1 0.0 copy-done.1
  36.2 2.0 %fusion.8 = f32[64,20,256]{2,0,1:T(8,128)S(1)} fusion(bf16[1,20,256,256]{3,2,1,0:T(8,128)(2,1)S(1)} %copy-done.1, bf16[20,64,256]{2,1,0:T(8,128)(2,1)} %gather_fusion.1), kind=kOutput, calls=%fused_computation.15 | convolution fusion | flops 167772160 | bytes 4587520 | tf_op jit(solution)/shard_map/ctj,tij->cti/dot_general | solution.py:34
  38.1 1.3 %fusion.6 = f32[8,64,256]{2,0,1:T(8,128)S(1)} fusion(f32[64,20,256]{2,0,1:T(8,128)S(1)} %fusion.8, s32[20]{0:T(128)S(1)} %bitcast.109), kind=kOutput, calls=%fused_computation.13 | convolution fusion | flops 31457440 | bytes 1835088 | tf_op jit(solution)/shard_map/cti,tb->cbi/dot_general | solution.py:35
  39.5 0.2 copy.97
  39.6 0.0 copy-start.5
  39.7 0.7 divide_convert_fusion.1
  40.4 2.0 %copy.81 = bf16[64,2048]{0,1:T(8,128)(2,1)} copy(bf16[64,2048]{1,0:T(8,128)(2,1)} %divide_convert_fusion.1) | data formatting | bytes 524288 | tf_op jit(solution)/shard_map/convert_element_type | solution.py:37
  42.3 5.1 %gather_fusion.2 = bf16[1024,64]{1,0:T(8,128)(2,1)} fusion(bf16[64,2048]{0,1:T(8,128)(2,1)} %copy.81, s32[1024]{0:T(1024)S(1)} %broadcast_clamp_fusion.1), kind=kCustom, calls=%fused_computation.2 | custom fusion | bytes 266240 | tf_op jit(solution)/shard_map/gather | solution.py:43
  47.5 1.7 %copy.82 = bf16[64,8,128]{2,0,1:T(8,128)(2,1)} copy(bf16[64,8,128]{0,2,1:T(8,128)(2,1)} %bitcast.101) | data formatting | bytes 262144 | tf_op jit(solution)/shard_map/all_to_all | solution.py:43
  49.2 3.4 %all-to-all-start.2 = ((bf16[64,8,128]{2,0,1:T(8,128)(2,1)}), bf16[64,8,128]{2,0,1:T(8,128)(2,1)S(1)}, u32[]{:S(2)}, u32[]{:S(2)}) async-start(bf16[64,8,128]{2,0,1:T(8,128)(2,1)} %copy.82), calls=%async_computation.2 | async-start | bytes 262144 | tf_op jit(solution)/shard_map/all_to_all | solution.py:43
  52.6 7.2 %all-to-all-done.2 = bf16[64,8,128]{2,0,1:T(8,128)(2,1)S(1)} async-done(((bf16[64,8,128]{2,0,1:T(8,128)(2,1)}), bf16[64,8,128]{2,0,1:T(8,128)(2,1)S(1)}, u32[]{:S(2)}, u32[]{:S(2)}) %all-to-all-start.2) | async-done | bytes 131104 | tf_op jit(solution)/shard_map/all_to_all | solution.py:43
  59.9 1.0 pad_maximum_fusion.2
  60.9 0.8 copy.108
  61.7 2.6 %gather_fusion.3 = bf16[20,64,256]{2,1,0:T(8,128)(2,1)} fusion(bf16[64,12,256]{2,0,1:T(8,128)(2,1)} %bitcast.89, s32[1024]{0:T(1024)} %copy-done.7), kind=kCustom, calls=%fused_computation.3 | custom fusion | bytes 1310800 | tf_op jit(solution)/shard_map/gather | solution.py:33
  64.2 2.0 %fusion.11 = f32[64,20,256]{2,0,1:T(8,128)S(1)} fusion(bf16[1,20,256,256]{3,2,1,0:T(8,128)(2,1)S(1)} %copy-done.1, bf16[20,64,256]{2,1,0:T(8,128)(2,1)} %gather_fusion.3), kind=kOutput, calls=%fused_computation.16 | convolution fusion | flops 167772160 | bytes 4587520 | tf_op jit(solution)/shard_map/ctj,tij->cti/dot_general | solution.py:34
  66.2 0.0 copy-start.2
  66.3 0.0 copy-start.4
  66.3 1.3 %fusion.4 = f32[8,64,256]{2,0,1:T(8,128)S(1)} fusion(f32[64,20,256]{2,0,1:T(8,128)S(1)} %fusion.11, s32[20]{0:T(128)S(1)} %bitcast.110), kind=kOutput, calls=%fused_computation.11 | convolution fusion | flops 31457440 | bytes 1835088 | tf_op jit(solution)/shard_map/cti,tb->cbi/dot_general | solution.py:35
  67.6 0.2 copy.99
  67.8 0.1 pad_maximum_fusion
  67.9 0.5 copy.86
  68.4 7.5 %gather_fusion.4 = bf16[2048,192]{1,0:T(8,128)(2,1)S(1)} fusion(bf16[192,2048]{0,1:T(8,128)(2,1)S(1)} %copy.86, s32[2048]{0:T(1024)S(1)} %broadcast_clamp_fusion), kind=kCustom, calls=%fused_computation.4 | custom fusion | bytes 1581056 | tf_op jit(solution)/shard_map/gather | solution.py:45
  75.9 0.0 copy-start.6
  75.9 1.3 %copy.87 = bf16[192,8,256]{2,0,1:T(8,128)(2,1)} copy(bf16[192,8,256]{0,2,1:T(8,128)(2,1)S(1)} %bitcast.91) | data formatting | bytes 1572864 | tf_op jit(solution)/shard_map/all_to_all | solution.py:46
  77.2 3.5 %all-to-all-start.3 = ((bf16[192,8,256]{2,0,1:T(8,128)(2,1)}), bf16[192,8,256]{2,0,1:T(8,128)(2,1)S(1)}, u32[]{:S(2)}, u32[]{:S(2)}) async-start(bf16[192,8,256]{2,0,1:T(8,128)(2,1)} %copy.87), calls=%async_computation.3 | async-start | bytes 1572864 | tf_op jit(solution)/shard_map/all_to_all | solution.py:46
  80.8 17.5 %all-to-all-done.3 = bf16[192,8,256]{2,0,1:T(8,128)(2,1)S(1)} async-done(((bf16[192,8,256]{2,0,1:T(8,128)(2,1)}), bf16[192,8,256]{2,0,1:T(8,128)(2,1)S(1)}, u32[]{:S(2)}, u32[]{:S(2)}) %all-to-all-start.3) | async-done | bytes 786464 | tf_op jit(solution)/shard_map/all_to_all | solution.py:46
  98.3 0.1 copy.96
  98.4 0.5 copy.89
  98.9 9.6 %scatter_custom_fusion = bf16[192,2048]{0,1:T(8,128)(2,1)S(1)} fusion(s32[2048]{0:T(1024)S(1)} %bitcast.107, bf16[2048,192]{1,0:T(8,128)(2,1)S(1)} %copy.89, bf16[]{:T(256)} %constant.5.clone.1), kind=kCustom, calls=%fused_computation.24 | custom fusion | bytes 786434 | tf_op jit(solution)/shard_map/scatter | solution.py:47
  108.5 1.2 %copy.90 = bf16[192,2048]{1,0:T(8,128)(2,1)} copy(bf16[192,2048]{0,1:T(8,128)(2,1)S(1)} %scatter_custom_fusion) | data formatting | bytes 1572864 | tf_op jit(solution)/shard_map/scatter | solution.py:47
  (26 shorter events, 0.2 us)
Async XLA Ops:
  0.0 1.1 %copy-start = (bf16[512,768]{1,0:T(8,128)(2,1)S(1)}, bf16[512,768]{1,0:T(8,128)(2,1)}, u32[]{:S(2)}) copy-start(bf16[512,768]{1,0:T(8,128)(2,1)} %param.8) | copy-start | bytes 2359300
  0.0 7.6 %copy-start.10 = (s32[1,1024]{1,0:T(1,128)S(1)}, s32[1,1024]{1,0:T(1,128)}, u32[]{:S(2)}) copy-start(s32[1,1024]{1,0:T(1,128)} %param.13) | copy-start | bytes 12292
  3.3 6.9 %copy-start.8 = (s32[1,20]{1,0:T(1,128)S(1)}, s32[1,20]{1,0:T(1,128)}, u32[]{:S(2)}) copy-start(s32[1,20]{1,0:T(1,128)} %param.11) | copy-start | bytes 244
  3.3 10.4 %all-to-all-start = ((bf16[4,64,512]{2,1,0:T(8,128)(2,1)}), bf16[4,64,512]{2,1,0:T(8,128)(2,1)S(1)}, u32[]{:S(2)}, u32[]{:S(2)}) async-start(bf16[4,64,512]{2,1,0:T(8,128)(2,1)} %bitcast.2), calls=%async_computation | async-start | bytes 524288 | tf_op jit(solution)/shard_map/all_to_all | solution.py:13
  13.6 10.8 %copy-start.11 = (s32[1,20]{1,0:T(1,128)S(1)}, s32[1,20]{1,0:T(1,128)}, u32[]{:S(2)}) copy-start(s32[1,20]{1,0:T(1,128)} %param.12) | copy-start | bytes 244
  13.7 18.1 %copy-start.3 = (bf16[4,8,8,512]{3,2,0,1:T(8,128)(2,1)}, bf16[4,8,8,512]{3,2,0,1:T(8,128)(2,1)S(1)}, u32[]{:S(2)}) copy-start(bf16[4,8,8,512]{3,2,0,1:T(8,128)(2,1)S(1)} %copy.93) | copy-start | bytes 786436
  17.9 13.8 %all-to-all-start.1 = ((bf16[64,8,128]{2,0,1:T(8,128)(2,1)}), bf16[64,8,128]{2,0,1:T(8,128)(2,1)S(1)}, u32[]{:S(2)}, u32[]{:S(2)}) async-start(bf16[64,8,128]{2,0,1:T(8,128)(2,1)} %copy.77), calls=%async_computation.1 | async-start | bytes 262144 | tf_op jit(solution)/shard_map/all_to_all | solution.py:40
  24.4 11.7 %copy-start.7 = (s32[1024]{0:T(1024)}, s32[1024]{0:T(1024)S(1)}, u32[]{:S(2)}) copy-start(s32[1024]{0:T(1024)S(1)} %pad_clamp_fusion) | copy-start | bytes 12292
  31.8 4.4 %copy-start.1 = (bf16[1,20,256,256]{3,2,1,0:T(8,128)(2,1)S(1)}, bf16[1,20,256,256]{3,2,1,0:T(8,128)(2,1)}, u32[]{:S(2)}) copy-start(bf16[1,20,256,256]{3,2,1,0:T(8,128)(2,1)} %param.10) | copy-start | bytes 7864324
  39.6 13.0 %copy-start.5 = (s32[1,2048]{1,0:T(1,128)S(1)}, s32[1,2048]{1,0:T(1,128)}, u32[]{:S(2)}) copy-start(s32[1,2048]{1,0:T(1,128)} %param.14) | copy-start | bytes 24580
  49.2 10.7 %all-to-all-start.2 = ((bf16[64,8,128]{2,0,1:T(8,128)(2,1)}), bf16[64,8,128]{2,0,1:T(8,128)(2,1)S(1)}, u32[]{:S(2)}, u32[]{:S(2)}) async-start(bf16[64,8,128]{2,0,1:T(8,128)(2,1)} %copy.82), calls=%async_computation.2 | async-start | bytes 262144 | tf_op jit(solution)/shard_map/all_to_all | solution.py:43
  64.2 2.0 %copy-start.9 = (s32[1,20]{1,0:T(1,128)S(1)}, s32[1,20]{1,0:T(1,128)}, u32[]{:S(2)}) copy-start(s32[1,20]{1,0:T(1,128)} %param.11) | copy-start | bytes 244
  66.2 1.6 %copy-start.2 = (bf16[64,2048]{1,0:T(8,128)(2,1)S(1)}, bf16[64,2048]{1,0:T(8,128)(2,1)}, u32[]{:S(2)}) copy-start(bf16[64,2048]{1,0:T(8,128)(2,1)} %divide_convert_fusion.1) | copy-start | bytes 786436
  66.3 1.6 %copy-start.4 = (bf16[4,8,8,512]{3,2,0,1:T(8,128)(2,1)S(1)}, bf16[4,8,8,512]{3,2,0,1:T(8,128)(2,1)}, u32[]{:S(2)}) copy-start(bf16[4,8,8,512]{3,2,0,1:T(8,128)(2,1)} %copy-done.3) | copy-start | bytes 786436
  75.9 4.8 %copy-start.6 = (s32[1,2048]{1,0:T(1,128)S(1)}, s32[1,2048]{1,0:T(1,128)}, u32[]{:S(2)}) copy-start(s32[1,2048]{1,0:T(1,128)} %param.15) | copy-start | bytes 24580
  77.2 21.1 %all-to-all-start.3 = ((bf16[192,8,256]{2,0,1:T(8,128)(2,1)}), bf16[192,8,256]{2,0,1:T(8,128)(2,1)S(1)}, u32[]{:S(2)}, u32[]{:S(2)}) async-start(bf16[192,8,256]{2,0,1:T(8,128)(2,1)} %copy.87), calls=%async_computation.3 | async-start | bytes 1572864 | tf_op jit(solution)/shard_map/all_to_all | solution.py:46
where the time goes:
time: 111 us; the launch traced here: 110 us
  local copies, waits for them, and re-layouts  41.9 us (38%)
  waiting for transfers between devices  35.4 us (32%)
  starting transfers between devices  17.7 us (16%)
  matrix products  8.87 us (8%)
  other arithmetic  5.49 us (5%)
    all_to_all x1, waiting for transfers between devices, on_device(): lax.all_to_all(stacked, 'dom', split_axis=1, concat_axis=1, tiled=True)  17.5 us
    scatter x2, local copies, waits for them, and re-layouts, on_device(): placed = jnp.zeros_like(arrived).at[:, place].set(arrived)  10.8 us
    gather x1, local copies, waits for them, and re-layouts, on_device(): stacked = jnp.concatenate([hop0, hop1, hop2], 0)[:, order]  7.5 us
    all_to_all x1, waiting for transfers between devices, on_device(): lax.all_to_all(hop0[:, halo_rows], 'dom', split_axis=1, concat_axis=1, ti...  7.3 us
    all_to_all x1, waiting for transfers between devices, on_device(): lax.all_to_all(hop1[:, halo_rows], 'dom', split_axis=1, concat_axis=1, ti...  7.24 us
    all_to_all x1, starting transfers between devices, on_device(): lax.all_to_all(hop0[:, halo_rows], 'dom', split_axis=1, concat_axis=1, ti...  6.45 us
    gather x1, local copies, waits for them, and re-layouts, on_device(): hop1[:, halo_rows]  5.14 us
    gather x2, local copies, waits for them, and re-layouts, combine(): blocks = columns.reshape(channels, -1, tile_size)[:, sources, :]  5.03 us
  transfers between devices with their start and end apart: 4, of which 4 were waited for; matrix products, arithmetic and copies ran while one was open for 2% of the time, Pallas kernels for 0%

commit v1 on v0

v1 whole, which is shorter than its diff:
```python
import functools

import jax
import jax.numpy as jnp
from jax import lax
from jax.experimental import pallas as pl
from jax.experimental.pallas import tpu as pltpu
from jax.sharding import PartitionSpec as P

BF16 = jnp.bfloat16
F32 = jnp.float32
EXTRA = 16
VMEM_LIMIT = 40 * 1024 * 1024


def params():
    return pltpu.CompilerParams(vmem_limit_bytes=VMEM_LIMIT)


def cost(flops, size):
    return pl.CostEstimate(flops=flops, bytes_accessed=size, transcendentals=0)


def whole(count):
    return [pl.BlockSpec(memory_space=pltpu.VMEM)] * count


def table_kernel(index_ref, table_ref):
    rows, columns = table_ref.shape
    step = 256
    index = index_ref[...]

    def body(chunk, carry):
        base = chunk * step
        row = lax.broadcasted_iota(jnp.int32, (step, columns), 0) + base
        table_ref[pl.ds(pl.multiple_of(base, step), step), :] = jnp.where(
            row == index, 1.0, 0.0
        ).astype(BF16)
        return carry

    lax.fori_loop(0, rows // step, body, 0)


def make_table(index, rows):
    columns = index.shape[1]
    return pl.pallas_call(
        table_kernel,
        out_shape=jax.ShapeDtypeStruct((rows, columns), BF16),
        in_specs=whole(1),
        out_specs=pl.BlockSpec(memory_space=pltpu.VMEM),
        compiler_params=params(),
        cost_estimate=cost(4 * rows * columns, 2 * rows * columns),
        name="table",
    )(index)


def store_slots(send_ref, picked):
    if len(send_ref.shape) == 2:
        send_ref[...] = picked
    else:
        slot = send_ref.shape[2]
        for peer in range(send_ref.shape[0]):
            send_ref[peer] = picked[:, peer * slot : (peer + 1) * slot]


def pick_kernel(arrived_ref, table_ref, hop_ref, send_ref):
    parts, _, width = arrived_ref.shape
    for part in range(parts):
        hop_ref[:, part * width : (part + 1) * width] = arrived_ref[part]
    picked = jnp.dot(hop_ref[...], table_ref[...], preferred_element_type=F32)
    store_slots(send_ref, picked.astype(BF16))


def send_shape(channels, peers, slot):
    if slot % 128:
        return jax.ShapeDtypeStruct((channels, peers * slot), BF16)
    return jax.ShapeDtypeStruct((peers, channels, slot), BF16)


def chunk_major(send, peers):
    if send.ndim == 3:
        return send
    channels = send.shape[0]
    return send.reshape(channels, peers, -1).transpose(1, 0, 2)


def exchange(send, peers):
    return lax.all_to_all(chunk_major(send, peers), "dom", 0, 0, tiled=True)


def wide(arrived):
    if arrived.shape[2] % 128 == 0:
        return arrived
    return arrived.transpose(1, 0, 2).reshape(arrived.shape[1], -1)


def load_wide(ref):
    if len(ref.shape) == 2:
        return ref[...]
    return jnp.concatenate([ref[peer] for peer in range(ref.shape[0])], axis=1)


def local_kernel(hop_ref, tiles_ref, total_ref):
    channels, nodes = hop_ref.shape
    side = tiles_ref.shape[1]
    ones = jnp.ones((EXTRA, side), BF16)
    for block in range(nodes // side):
        columns = jnp.concatenate([hop_ref[:, block * side : (block + 1) * side], ones], 0)
        total_ref[block] = lax.dot_general(
            columns, tiles_ref[block], (((1,), (1,)), ((), ())), preferred_element_type=F32
        )


def local_part(hop, tiles):
    channels, nodes = hop.shape
    side = tiles.shape[1]
    blocks = nodes // side
    return pl.pallas_call(
        local_kernel,
        out_shape=jax.ShapeDtypeStruct((blocks, channels + EXTRA, side), F32),
        in_specs=[
            pl.BlockSpec((channels, nodes), lambda i: (0, 0)),
            pl.BlockSpec((blocks, side, side), lambda i: (0, 0, 0)),
        ],
        out_specs=pl.BlockSpec((blocks, channels + EXTRA, side), lambda i: (0, 0, 0)),
        grid=(1,),
        compiler_params=params(),
        cost_estimate=cost(2 * nodes * side * channels, 2 * nodes * side),
        name="local_part",
    )(hop, tiles)


def combine_body(
    dst_ref, src_ref, hop_ref, total_ref, arrived_ref, tiles_ref, columns, sums, result_ref
):
    channels, nodes = hop_ref.shape
    slots, side, _ = tiles_ref.shape
    blocks = nodes // side
    arrived = load_wide(arrived_ref)
    fixed = blocks + arrived.shape[1] // side
    columns[:, channels:, :] = jnp.ones((fixed, EXTRA, side), BF16)
    for block in range(blocks):
        columns[block, :channels, :] = hop_ref[:, block * side : (block + 1) * side]
        sums[block] = total_ref[block]
    for block in range(blocks, fixed):
        start = (block - blocks) * side
        columns[block, :channels, :] = arrived[:, start : start + side]
    for slot in range(blocks, slots):
        target = dst_ref[0, slot]
        target = jnp.where(target < 0, blocks, target)
        source = slot if slot < fixed else src_ref[0, slot]
        product = lax.dot_general(
            columns[source], tiles_ref[slot], (((1,), (1,)), ((), ())), preferred_element_type=F32
        )
        sums[target] = sums[target] + product
    for block in range(blocks):
        block_sums = sums[block]
        result_ref[:, block * side : (block + 1) * side] = (
            block_sums[:channels] / block_sums[channels : channels + 1]
        ).astype(BF16)


def combine_pick_kernel(
    dst_ref, src_ref, hop_ref, total_ref, arrived_ref, tiles_ref, table_ref,
    result_ref, send_ref, columns, sums,
):
    combine_body(
        dst_ref, src_ref, hop_ref, total_ref, arrived_ref, tiles_ref, columns, sums, result_ref
    )
    picked = jnp.dot(result_ref[...], table_ref[...], preferred_element_type=F32)
    store_slots(send_ref, picked.astype(BF16))


def combine_last_kernel(
    dst_ref, src_ref, hop0_ref, hop_ref, total_ref, arrived_ref, tiles_ref, table_ref,
    send_ref, result_ref, columns, sums,
):
    combine_body(
        dst_ref, src_ref, hop_ref, total_ref, arrived_ref, tiles_ref, columns, sums, result_ref
    )
    stacked = jnp.concatenate([hop0_ref[...], hop_ref[...], result_ref[...]], 0)
    picked = jnp.dot(stacked, table_ref[...], preferred_element_type=F32)
    store_slots(send_ref, picked.astype(BF16))


def combine_scratch(channels, nodes, halo, side):
    return [
        pltpu.VMEM(((nodes + halo) // side, channels + EXTRA, side), BF16),
        pltpu.VMEM((nodes // side + 1, channels + EXTRA, side), F32),
    ]


def smem(count):
    return [pl.BlockSpec(memory_space=pltpu.SMEM)] * count


def place_kernel(arrived_ref, table_ref, out_ref):
    hops, channels, nodes = out_ref.shape
    stacked = load_wide(arrived_ref)
    side = 256
    for start in range(0, nodes, side):
        placed = lax.dot_general(
            stacked, table_ref[start : start + side, :], (((1,), (1,)), ((), ())),
            preferred_element_type=F32,
        ).astype(BF16)
        for hop in range(hops):
            out_ref[hop, :, start : start + side] = placed[hop * channels : (hop + 1) * channels]


def on_device(
    features, sketch_matrix, tiles, tile_dst, tile_src, halo_index, send_order, arrival_place
):
    sketched = lax.dot_general(
        sketch_matrix, features, (((0,), (1,)), ((), ())), preferred_element_type=F32
    ).astype(BF16)
    reps = lax.axis_size("rep")
    peers = lax.axis_size("dom")
    channels = sketched.shape[0] // reps
    arrived = lax.all_to_all(
        sketched.reshape(reps, channels, -1), "rep", 0, 0, tiled=True
    )
    nodes = arrived.shape[2] * reps
    halo = halo_index.shape[1]
    tiles = tiles[0]
    side = tiles.shape[-1]
    halo_table = make_table(halo_index, nodes)
    send_table = make_table(send_order, nodes)
    place_table = make_table(arrival_place, nodes)
    hop_shape = jax.ShapeDtypeStruct((channels, nodes), BF16)
    halo_shape = send_shape(channels, peers, halo // peers)
    hop0, send = pl.pallas_call(
        pick_kernel,
        out_shape=(hop_shape, halo_shape),
        in_specs=whole(2),
        out_specs=tuple(whole(2)),
        compiler_params=params(),
        name="pick",
    )(arrived, halo_table)
    halo0 = wide(exchange(send, peers))
    total0 = local_part(hop0, tiles)
    hop1, send = pl.pallas_call(
        combine_pick_kernel,
        out_shape=(hop_shape, halo_shape),
        in_specs=smem(2) + whole(5),
        out_specs=tuple(whole(2)),
        scratch_shapes=combine_scratch(channels, nodes, halo, side),
        compiler_params=params(),
        name="combine_pick",
    )(tile_dst, tile_src, hop0, total0, halo0, tiles, halo_table)
    halo1 = wide(exchange(send, peers))
    total1 = local_part(hop1, tiles)
    send = pl.pallas_call(
        combine_last_kernel,
        out_shape=send_shape(3 * channels, peers, nodes // peers),
        in_specs=smem(2) + whole(6),
        out_specs=whole(1)[0],
        scratch_shapes=[pltpu.VMEM((channels, nodes), BF16)]
        + combine_scratch(channels, nodes, halo, side),
        compiler_params=params(),
        name="combine_last",
    )(tile_dst, tile_src, hop0, hop1, total1, halo1, tiles, send_table)
    last = wide(exchange(send, peers))
    return pl.pallas_call(
        place_kernel,
        out_shape=jax.ShapeDtypeStruct((3, channels, nodes), BF16),
        in_specs=whole(2),
        out_specs=whole(1)[0],
        compiler_params=params(),
        name="place",
    )(last, place_table)


def solution(mesh):
    in_specs = (
        P(("dom", "rep"), None),
        P(),
        P("dom", None, None, None),
        P("dom", None),
        P("dom", None),
        P("dom", None),
        P("dom", None),
        P("dom", None),
    )
    out_specs = P(None, "rep", "dom")
    return jax.shard_map(
        on_device, mesh=mesh, in_specs=in_specs, out_specs=out_specs, check_vma=False
    )
```

time: 111 us -> 92.7 us (0.84)
  Pallas kernels: 0 us -> 15 us
  waiting for transfers between devices: 35.4 us -> 22.9 us
  local copies, waits for them, and re-layouts: 41.9 us -> 32.7 us
  matrix products: 8.87 us -> 2.12 us
  other arithmetic: 5.49 us -> 0 us
  starting transfers between devices: 17.7 us -> 18.9 us
    unnamed x27 -> x56, local copies, waits for them, and re-layouts: 1.52 us -> 32.7 us
    gather x5 -> x0, local copies, waits for them, and re-layouts: 20.9 us -> none  [the longest x1 7.5 us: on_device(): stacked = jnp.concatenate([hop0, hop1, hop2], 0)[:, order]]
    pallas_call x0 -> x9, Pallas kernels: none -> 15 us  [the longest x1 3.75 us: on_device(): pl.pallas_call(place_kernel, out_shape=jax.ShapeDtypeStruct((3, channels,...]
    all_to_all x4, waiting for transfers between devices: 35.4 us -> 22.9 us  [the longest x3 19.8 us: exchange(): return lax.all_to_all(chunk_major(send, peers), 'dom', 0, 0, tiled=True)]
    scatter x2 -> x0, local copies, waits for them, and re-layouts: 10.8 us -> none  [on_device(): placed = jnp.zeros_like(arrived).at[:, place].set(arrived)]
    dot_general x5 -> x0, matrix products: 6.75 us -> none  [the longest x2 3.99 us: combine(): jnp.einsum('ctj,tij->cti', blocks, tile_set, preferred_element_type=jnp.f...]
    all_to_all x9 -> x0, local copies, waits for them, and re-layouts: 4.69 us -> none  [the longest x3 1.85 us: on_device(): lax.all_to_all(stacked, 'dom', split_axis=1, concat_axis=1, tiled=True)]
    reduce_sum x1 -> x0, other arithmetic: 2.49 us -> none  [on_device(): row_sums = jnp.sum(tile_set, axis=2, dtype=jnp.float32)]
  transfers between devices with their start and end apart: 4 -> 4, of which waited for: 4 -> 4; matrix products, arithmetic and copies ran while one was open for 2% -> 0% of each run, Pallas kernels for 0% -> 5%
where the time goes in v1:
time: 92.7 us; the launch traced here: 91.9 us
  local copies, waits for them, and re-layouts  32.7 us (35%)
  waiting for transfers between devices  22.9 us (25%)
  starting transfers between devices  18.9 us (20%)
  Pallas kernels  15 us (16%)
  matrix products  2.12 us (2%)
    unnamed x56, local copies, waits for them, and re-layouts  32.7 us
    all_to_all x3, waiting for transfers between devices, exchange(): return lax.all_to_all(chunk_major(send, peers), 'dom', 0, 0, tiled=True)  19.8 us
    all_to_all x3, starting transfers between devices, exchange(): return lax.all_to_all(chunk_major(send, peers), 'dom', 0, 0, tiled=True)  14.7 us
    all_to_all x1, starting transfers between devices, on_device(): lax.all_to_all(sketched.reshape(reps, channels, -1), 'rep', 0, 0, tiled=T...  4.24 us
    pallas_call x1, Pallas kernels, on_device(): pl.pallas_call(place_kernel, out_shape=jax.ShapeDtypeStruct((3, channels,...  3.75 us
    pallas_call x3, Pallas kernels, make_table(): pl.pallas_call(table_kernel, out_shape=jax.ShapeDtypeStruct((rows, column...  3.69 us
    all_to_all x1, waiting for transfers between devices, on_device(): lax.all_to_all(sketched.reshape(reps, channels, -1), 'rep', 0, 0, tiled=T...  3.1 us
    pallas_call x1, Pallas kernels, on_device(): pl.pallas_call(combine_last_kernel, out_shape=send_shape(3 * channels, pe...  2.88 us
  transfers between devices with their start and end apart: 4, of which 4 were waited for; matrix products, arithmetic and copies ran while one was open for 0% of the time, Pallas kernels for 5%

profile of v1, /device:TPU:0, one launch (start us, length us, event | category | flops | bytes accessed | tf_op | source)
XLA Modules:
  0.0 91.9 jit_solution(15626006159325867315)
XLA Ops:
  0.0 0.0 copy-start
  0.0 1.1 %copy-done = bf16[512,768]{1,0:T(8,128)(2,1)S(1)} copy-done((bf16[512,768]{1,0:T(8,128)(2,1)S(1)}, bf16[512,768]{1,0:T(8,128)(2,1)}, u32[]{:S(2)}) %copy-start) | copy-done | bytes 786456
  1.1 2.1 %convolution_convert_fusion = bf16[256,512]{1,0:T(8,128)(2,1)} fusion(bf16[768,256]{1,0:T(8,128)(2,1)} %param.9, bf16[512,768]{1,0:T(8,128)(2,1)S(1)} %copy-done), kind=kOutput, calls=%fused_computation | convolution fusion | flops 201457664 | bytes 1441792 | tf_op jit(solution)/shard_map/dot_general | solution.py:213
  3.3 4.2 %all-to-all-start = ((bf16[4,64,512]{2,1,0:T(8,128)(2,1)}), bf16[4,64,512]{2,1,0:T(8,128)(2,1)}, u32[]{:S(2)}, u32[]{:S(2)}) async-start(bf16[4,64,512]{2,1,0:T(8,128)(2,1)} %bitcast.8), calls=%async_computation | async-start | bytes 524288 | tf_op jit(solution)/shard_map/all_to_all | solution.py:219
  7.5 0.7 copy-done.25
  8.2 0.8 table.3.table_ref
  9.0 0.0 copy-start.2
  9.0 2.0 %copy-done.2 = bf16[2048,1024]{1,0:T(8,128)(2,1)} copy-done((bf16[2048,1024]{1,0:T(8,128)(2,1)}, bf16[2048,1024]{1,0:T(8,128)(2,1)S(1)}, u32[]{:S(2)}) %copy-start.2) | copy-done | bytes 4194328
  10.9 3.1 %all-to-all-done.arrived_ref = bf16[4,64,512]{2,1,0:T(8,128)(2,1)} async-done(((bf16[4,64,512]{2,1,0:T(8,128)(2,1)}), bf16[4,64,512]{2,1,0:T(8,128)(2,1)}, u32[]{:S(2)}, u32[]{:S(2)}) %all-to-all-start) | async-done | bytes 262176 | tf_op jit(solution)/shard_map/all_to_all | solution.py:219
  14.0 2.2 %copy-done.3 = bf16[2048,1024]{1,0:T(8,128)(2,1)S(1)} copy-done((bf16[2048,1024]{1,0:T(8,128)(2,1)S(1)}, bf16[2048,1024]{1,0:T(8,128)(2,1)}, u32[]{:S(2)}) %copy-start.3) | copy-done | bytes 4194328
  16.2 1.8 %pick.1 = (bf16[64,2048]{1,0:T(8,128)(2,1)S(1)}, bf16[8,64,128]{2,1,0:T(8,128)(2,1)S(1)}) custom-call(bf16[4,64,512]{2,1,0:T(8,128)(2,1)} %all-to-all-done.arrived_ref, bf16[2048,1024]{1,0:T(8,128)(2,1)S(1)} %copy-done.3), custom_call_target="tpu_custom_call" | custom-call | tf_op jit(solution)/shard_map/pick/pallas_call | solution.py:231
  18.0 0.0 copy-start.14
  18.0 0.7 copy-done.14
  18.8 0.6 copy-done.22
  19.4 6.6 %all-to-all-start.1 = ((bf16[8,64,128]{2,1,0:T(8,128)(2,1)}), bf16[8,64,128]{2,1,0:T(8,128)(2,1)S(1)}, u32[]{:S(2)}, u32[]{:S(2)}) async-start(bf16[8,64,128]{2,1,0:T(8,128)(2,1)} %copy-done.22), calls=%async_computation.1 | async-start | bytes 262144 | tf_op jit(solution)/shard_map/all_to_all | solution.py:88
  26.0 0.0 copy-start.15
  26.1 0.9 %copy-done.15 = bf16[64,2048]{1,0:T(8,128)(2,1)S(1)} copy-done((bf16[64,2048]{1,0:T(8,128)(2,1)S(1)}, bf16[64,2048]{1,0:T(8,128)(2,1)}, u32[]{:S(2)}) %copy-start.15) | copy-done | bytes 262168
  27.0 0.4 local_part.2.total_ref
  27.4 0.0 copy-start.10
  27.4 0.8 copy-done.10
  28.3 5.1 %all-to-all-done.1.arrived_ref = bf16[8,64,128]{2,1,0:T(8,128)(2,1)S(1)} async-done(((bf16[8,64,128]{2,1,0:T(8,128)(2,1)}), bf16[8,64,128]{2,1,0:T(8,128)(2,1)S(1)}, u32[]{:S(2)}, u32[]{:S(2)}) %all-to-all-start.1) | async-done | bytes 131104 | tf_op jit(solution)/shard_map/all_to_all | solution.py:88
  33.4 0.0 copy-done.27
  33.4 2.2 %copy-done.4 = bf16[2048,1024]{1,0:T(8,128)(2,1)S(1)} copy-done((bf16[2048,1024]{1,0:T(8,128)(2,1)S(1)}, bf16[2048,1024]{1,0:T(8,128)(2,1)}, u32[]{:S(2)}) %copy-start.4) | copy-done | bytes 4194328
  35.6 1.1 %copy-done.11 = f32[8,80,256]{2,1,0:T(8,128)S(1)} copy-done((f32[8,80,256]{2,1,0:T(8,128)S(1)}, f32[8,80,256]{2,1,0:T(8,128)}, u32[]{:S(2)}) %copy-start.11) | copy-done | bytes 655384
  36.7 0.9 %copy-done.16 = bf16[64,2048]{1,0:T(8,128)(2,1)S(1)} copy-done((bf16[64,2048]{1,0:T(8,128)(2,1)S(1)}, bf16[64,2048]{1,0:T(8,128)(2,1)}, u32[]{:S(2)}) %copy-start.16) | copy-done | bytes 262168
  37.6 2.0 %combine_pick.1 = (bf16[64,2048]{1,0:T(8,128)(2,1)S(1)}, bf16[8,64,128]{2,1,0:T(8,128)(2,1)S(1)}) custom-call(s32[1,20]{1,0:T(1,128)S(1)} %copy-done.26, s32[1,20]{1,0:T(1,128)S(1)} %copy-done.27, bf16[64,2048]{1,0:T(8,128)(2,1)S(1)} %copy-done.16, f32[8,80,256]{2,1,0:T(8,128)S(1)} %copy-done.11, bf16[8,64,128]{2,1,0:T(8,128)(2,1)S(1)} %all-to-all-done.1.arrived_ref, ...), custom_call_target="tpu_custom_call" | custom-call | tf_op jit(solution)/shard_map/combine_pick/pallas_call | solution.py:241
  39.6 0.7 copy-done.18
  40.3 0.6 copy-done.21
  41.0 3.4 %all-to-all-start.2 = ((bf16[8,64,128]{2,1,0:T(8,128)(2,1)}), bf16[8,64,128]{2,1,0:T(8,128)(2,1)S(1)}, u32[]{:S(2)}, u32[]{:S(2)}) async-start(bf16[8,64,128]{2,1,0:T(8,128)(2,1)} %copy-done.21), calls=%async_computation.2 | async-start | bytes 262144 | tf_op jit(solution)/shard_map/all_to_all | solution.py:88
  44.4 1.5 %table.4.table_ref = bf16[2048,2048]{1,0:T(8,128)(2,1)S(1)} custom-call(s32[1,2048]{1,0:T(1,128)S(1)} %copy-done.23), custom_call_target="tpu_custom_call" | custom-call | flops 16777216 | bytes 8388608 | tf_op jit(solution)/shard_map/table/pallas_call | solution.py:46
  45.9 3.3 %copy-done.7 = bf16[2048,2048]{1,0:T(8,128)(2,1)} copy-done((bf16[2048,2048]{1,0:T(8,128)(2,1)}, bf16[2048,2048]{1,0:T(8,128)(2,1)S(1)}, u32[]{:S(2)}) %copy-start.7) | copy-done | bytes 8388632
  49.1 0.4 local_part.3.total_ref
  49.6 0.8 copy-done.12
  50.4 1.2 %all-to-all-done.2.arrived_ref = bf16[8,64,128]{2,1,0:T(8,128)(2,1)S(1)} async-done(((bf16[8,64,128]{2,1,0:T(8,128)(2,1)}), bf16[8,64,128]{2,1,0:T(8,128)(2,1)S(1)}, u32[]{:S(2)}, u32[]{:S(2)}) %all-to-all-start.2) | async-done | bytes 131104 | tf_op jit(solution)/shard_map/all_to_all | solution.py:88
  51.7 3.4 %copy-done.8 = bf16[2048,2048]{1,0:T(8,128)(2,1)S(1)} copy-done((bf16[2048,2048]{1,0:T(8,128)(2,1)S(1)}, bf16[2048,2048]{1,0:T(8,128)(2,1)}, u32[]{:S(2)}) %copy-start.8) | copy-done | bytes 8388632
  55.0 1.1 %copy-done.13 = f32[8,80,256]{2,1,0:T(8,128)S(1)} copy-done((f32[8,80,256]{2,1,0:T(8,128)S(1)}, f32[8,80,256]{2,1,0:T(8,128)}, u32[]{:S(2)}) %copy-start.13) | copy-done | bytes 655384
  56.1 0.9 %copy-done.17 = bf16[64,2048]{1,0:T(8,128)(2,1)S(1)} copy-done((bf16[64,2048]{1,0:T(8,128)(2,1)S(1)}, bf16[64,2048]{1,0:T(8,128)(2,1)}, u32[]{:S(2)}) %copy-start.17) | copy-done | bytes 262168
  57.1 0.9 %copy-done.20 = bf16[64,2048]{1,0:T(8,128)(2,1)S(1)} copy-done((bf16[64,2048]{1,0:T(8,128)(2,1)S(1)}, bf16[64,2048]{1,0:T(8,128)(2,1)}, u32[]{:S(2)}) %copy-start.20) | copy-done | bytes 262168
  58.0 2.9 %combine_last.1 = bf16[8,192,256]{2,1,0:T(8,128)(2,1)S(1)} custom-call(s32[1,20]{1,0:T(1,128)S(1)} %copy-done.26, s32[1,20]{1,0:T(1,128)S(1)} %copy-done.27, bf16[64,2048]{1,0:T(8,128)(2,1)S(1)} %copy-done.17, bf16[64,2048]{1,0:T(8,128)(2,1)S(1)} %copy-done.20, f32[8,80,256]{2,1,0:T(8,128)S(1)} %copy-done.13, ...), custom_call_target="tpu_custom_call" | custom-call | tf_op jit(solution)/shard_map/combine_last/pallas_call | solution.py:252
  60.9 0.0 copy-start.9
  60.9 0.9 copy-done.9
  61.8 4.7 %all-to-all-start.3 = ((bf16[8,192,256]{2,1,0:T(8,128)(2,1)}), bf16[8,192,256]{2,1,0:T(8,128)(2,1)S(1)}, u32[]{:S(2)}, u32[]{:S(2)}) async-start(bf16[8,192,256]{2,1,0:T(8,128)(2,1)} %copy-done.9), calls=%async_computation.3 | async-start | bytes 1572864 | tf_op jit(solution)/shard_map/all_to_all | solution.py:88
  66.5 0.0 copy-done.24
  66.5 1.5 %table.5.table_ref = bf16[2048,2048]{1,0:T(8,128)(2,1)S(1)} custom-call(s32[1,2048]{1,0:T(1,128)S(1)} %copy-done.24), custom_call_target="tpu_custom_call" | custom-call | flops 16777216 | bytes 8388608 | tf_op jit(solution)/shard_map/table/pallas_call | solution.py:46
  68.0 3.3 %copy-done.5 = bf16[2048,2048]{1,0:T(8,128)(2,1)} copy-done((bf16[2048,2048]{1,0:T(8,128)(2,1)}, bf16[2048,2048]{1,0:T(8,128)(2,1)S(1)}, u32[]{:S(2)}) %copy-start.5) | copy-done | bytes 8388632
  71.2 13.5 %all-to-all-done.3.arrived_ref = bf16[8,192,256]{2,1,0:T(8,128)(2,1)S(1)} async-done(((bf16[8,192,256]{2,1,0:T(8,128)(2,1)}), bf16[8,192,256]{2,1,0:T(8,128)(2,1)S(1)}, u32[]{:S(2)}, u32[]{:S(2)}) %all-to-all-start.3) | async-done | bytes 786464 | tf_op jit(solution)/shard_map/all_to_all | solution.py:88
  84.7 3.4 %copy-done.6 = bf16[2048,2048]{1,0:T(8,128)(2,1)S(1)} copy-done((bf16[2048,2048]{1,0:T(8,128)(2,1)S(1)}, bf16[2048,2048]{1,0:T(8,128)(2,1)}, u32[]{:S(2)}) %copy-start.6) | copy-done | bytes 8388632
  88.1 3.8 %place.1 = bf16[3,64,2048]{2,1,0:T(8,128)(2,1)} custom-call(bf16[8,192,256]{2,1,0:T(8,128)(2,1)S(1)} %all-to-all-done.3.arrived_ref, bf16[2048,2048]{1,0:T(8,128)(2,1)S(1)} %copy-done.6), custom_call_target="tpu_custom_call" | custom-call | tf_op jit(solution)/shard_map/place/pallas_call | solution.py:263
  (26 shorter events, 0.0 us)
Async XLA Ops:
  0.0 1.1 %copy-start = (bf16[512,768]{1,0:T(8,128)(2,1)S(1)}, bf16[512,768]{1,0:T(8,128)(2,1)}, u32[]{:S(2)}) copy-start(bf16[512,768]{1,0:T(8,128)(2,1)} %param.8) | copy-start | bytes 2359300
  0.0 26.0 %copy-start.1 = (bf16[1,20,256,256]{3,2,1,0:T(8,128)(2,1)S(1)}, bf16[1,20,256,256]{3,2,1,0:T(8,128)(2,1)}, u32[]{:S(2)}) copy-start(bf16[1,20,256,256]{3,2,1,0:T(8,128)(2,1)} %param.10) | copy-start | bytes 7864324
  3.3 10.8 %all-to-all-start = ((bf16[4,64,512]{2,1,0:T(8,128)(2,1)}), bf16[4,64,512]{2,1,0:T(8,128)(2,1)}, u32[]{:S(2)}, u32[]{:S(2)}) async-start(bf16[4,64,512]{2,1,0:T(8,128)(2,1)} %bitcast.8), calls=%async_computation | async-start | bytes 524288 | tf_op jit(solution)/shard_map/all_to_all | solution.py:219
  7.5 0.7 copy-start.25
  8.2 25.2 %copy-start.26 = (s32[1,20]{1,0:T(1,128)S(1)}, s32[1,20]{1,0:T(1,128)}, u32[]{:S(2)}) copy-start(s32[1,20]{1,0:T(1,128)} %dst_ref.3) | copy-start | bytes 244
  8.2 25.2 %copy-start.27 = (s32[1,20]{1,0:T(1,128)S(1)}, s32[1,20]{1,0:T(1,128)}, u32[]{:S(2)}) copy-start(s32[1,20]{1,0:T(1,128)} %src_ref.3) | copy-start | bytes 244
  9.0 2.0 %copy-start.2 = (bf16[2048,1024]{1,0:T(8,128)(2,1)}, bf16[2048,1024]{1,0:T(8,128)(2,1)S(1)}, u32[]{:S(2)}) copy-start(bf16[2048,1024]{1,0:T(8,128)(2,1)S(1)} %table.3.table_ref) | copy-start | bytes 12582916
  14.0 2.2 %copy-start.3 = (bf16[2048,1024]{1,0:T(8,128)(2,1)S(1)}, bf16[2048,1024]{1,0:T(8,128)(2,1)}, u32[]{:S(2)}) copy-start(bf16[2048,1024]{1,0:T(8,128)(2,1)} %copy-done.2) | copy-start | bytes 12582916
  16.2 28.2 %copy-start.23 = (s32[1,2048]{1,0:T(1,128)S(1)}, s32[1,2048]{1,0:T(1,128)}, u32[]{:S(2)}) copy-start(s32[1,2048]{1,0:T(1,128)} %index_ref.4) | copy-start | bytes 24580
  18.0 0.7 copy-start.14
  18.8 0.6 copy-start.22
  19.4 14.0 %all-to-all-start.1 = ((bf16[8,64,128]{2,1,0:T(8,128)(2,1)}), bf16[8,64,128]{2,1,0:T(8,128)(2,1)S(1)}, u32[]{:S(2)}, u32[]{:S(2)}) async-start(bf16[8,64,128]{2,1,0:T(8,128)(2,1)} %copy-done.22), calls=%async_computation.1 | async-start | bytes 262144 | tf_op jit(solution)/shard_map/all_to_all | solution.py:88
  26.0 1.0 %copy-start.15 = (bf16[64,2048]{1,0:T(8,128)(2,1)S(1)}, bf16[64,2048]{1,0:T(8,128)(2,1)}, u32[]{:S(2)}) copy-start(bf16[64,2048]{1,0:T(8,128)(2,1)} %copy-done.14) | copy-start | bytes 786436
  27.4 0.8 copy-start.10
  33.4 2.2 %copy-start.4 = (bf16[2048,1024]{1,0:T(8,128)(2,1)S(1)}, bf16[2048,1024]{1,0:T(8,128)(2,1)}, u32[]{:S(2)}) copy-start(bf16[2048,1024]{1,0:T(8,128)(2,1)} %copy-done.2) | copy-start | bytes 12582916
  35.6 1.1 %copy-start.11 = (f32[8,80,256]{2,1,0:T(8,128)S(1)}, f32[8,80,256]{2,1,0:T(8,128)}, u32[]{:S(2)}) copy-start(f32[8,80,256]{2,1,0:T(8,128)} %copy-done.10) | copy-start | bytes 1966084
  36.7 0.9 %copy-start.16 = (bf16[64,2048]{1,0:T(8,128)(2,1)S(1)}, bf16[64,2048]{1,0:T(8,128)(2,1)}, u32[]{:S(2)}) copy-start(bf16[64,2048]{1,0:T(8,128)(2,1)} %copy-done.14) | copy-start | bytes 786436
  39.6 0.7 copy-start.18
  40.3 0.7 copy-start.21
  41.0 10.7 %all-to-all-start.2 = ((bf16[8,64,128]{2,1,0:T(8,128)(2,1)}), bf16[8,64,128]{2,1,0:T(8,128)(2,1)S(1)}, u32[]{:S(2)}, u32[]{:S(2)}) async-start(bf16[8,64,128]{2,1,0:T(8,128)(2,1)} %copy-done.21), calls=%async_computation.2 | async-start | bytes 262144 | tf_op jit(solution)/shard_map/all_to_all | solution.py:88
  44.4 4.8 %copy-start.19 = (bf16[64,2048]{1,0:T(8,128)(2,1)S(1)}, bf16[64,2048]{1,0:T(8,128)(2,1)}, u32[]{:S(2)}) copy-start(bf16[64,2048]{1,0:T(8,128)(2,1)} %copy-done.18) | copy-start | bytes 786436
  45.9 3.3 %copy-start.7 = (bf16[2048,2048]{1,0:T(8,128)(2,1)}, bf16[2048,2048]{1,0:T(8,128)(2,1)S(1)}, u32[]{:S(2)}) copy-start(bf16[2048,2048]{1,0:T(8,128)(2,1)S(1)} %table.4.table_ref) | copy-start | bytes 25165828
  49.1 17.3 %copy-start.24 = (s32[1,2048]{1,0:T(1,128)S(1)}, s32[1,2048]{1,0:T(1,128)}, u32[]{:S(2)}) copy-start(s32[1,2048]{1,0:T(1,128)} %index_ref.5) | copy-start | bytes 24580
  49.6 0.8 copy-start.12
  51.7 3.4 %copy-start.8 = (bf16[2048,2048]{1,0:T(8,128)(2,1)S(1)}, bf16[2048,2048]{1,0:T(8,128)(2,1)}, u32[]{:S(2)}) copy-start(bf16[2048,2048]{1,0:T(8,128)(2,1)} %copy-done.7) | copy-start | bytes 25165828
  55.0 1.1 %copy-start.13 = (f32[8,80,256]{2,1,0:T(8,128)S(1)}, f32[8,80,256]{2,1,0:T(8,128)}, u32[]{:S(2)}) copy-start(f32[8,80,256]{2,1,0:T(8,128)} %copy-done.12) | copy-start | bytes 1966084
  56.1 0.9 %copy-start.17 = (bf16[64,2048]{1,0:T(8,128)(2,1)S(1)}, bf16[64,2048]{1,0:T(8,128)(2,1)}, u32[]{:S(2)}) copy-start(bf16[64,2048]{1,0:T(8,128)(2,1)} %copy-done.14) | copy-start | bytes 786436
  57.1 0.9 %copy-start.20 = (bf16[64,2048]{1,0:T(8,128)(2,1)S(1)}, bf16[64,2048]{1,0:T(8,128)(2,1)}, u32[]{:S(2)}) copy-start(bf16[64,2048]{1,0:T(8,128)(2,1)} %copy-done.18) | copy-start | bytes 786436
  60.9 0.9 copy-start.9
  61.8 22.9 %all-to-all-start.3 = ((bf16[8,192,256]{2,1,0:T(8,128)(2,1)}), bf16[8,192,256]{2,1,0:T(8,128)(2,1)S(1)}, u32[]{:S(2)}, u32[]{:S(2)}) async-start(bf16[8,192,256]{2,1,0:T(8,128)(2,1)} %copy-done.9), calls=%async_computation.3 | async-start | bytes 1572864 | tf_op jit(solution)/shard_map/all_to_all | solution.py:88
  68.0 3.3 %copy-start.5 = (bf16[2048,2048]{1,0:T(8,128)(2,1)}, bf16[2048,2048]{1,0:T(8,128)(2,1)S(1)}, u32[]{:S(2)}) copy-start(bf16[2048,2048]{1,0:T(8,128)(2,1)S(1)} %table.5.table_ref) | copy-start | bytes 25165828
  84.7 3.4 %copy-start.6 = (bf16[2048,2048]{1,0:T(8,128)(2,1)S(1)}, bf16[2048,2048]{1,0:T(8,128)(2,1)}, u32[]{:S(2)}) copy-start(bf16[2048,2048]{1,0:T(8,128)(2,1)} %copy-done.5) | copy-start | bytes 25165828

commit v2 on v0

v2 whole, which is shorter than its diff:
```python
import jax
import jax.numpy as jnp
from jax import lax
from jax.experimental import pallas as pl
from jax.experimental.pallas import tpu as pltpu
from jax.sharding import PartitionSpec as P

BF16 = jnp.bfloat16
F32 = jnp.float32
EXTRA = 16
NN = (((1,), (0,)), ((), ()))
NT = (((1,), (1,)), ((), ()))
VMEM = pl.BlockSpec(memory_space=pltpu.VMEM)
SMEM = pl.BlockSpec(memory_space=pltpu.SMEM)
HBM = pl.BlockSpec(memory_space=pltpu.HBM)


def params():
    return pltpu.CompilerParams(vmem_limit_bytes=40 * 1024 * 1024)


def cost(flops, size):
    return pl.CostEstimate(flops=flops, bytes_accessed=size, transcendentals=0)


def dot(left, right, dims=NN):
    return lax.dot_general(left, right, dims, preferred_element_type=F32)


def one_hot(index, base, rows):
    row = lax.broadcasted_iota(jnp.int32, (rows, index.shape[1]), 0) + base
    return jnp.where(row == index, 1.0, 0.0).astype(BF16)


def pick(blocks, index, side, group):
    parts = []
    for start in range(0, index.shape[1], group):
        some = index[:, start : start + group]
        total = None
        for block, columns in enumerate(blocks):
            term = dot(columns, one_hot(some, block * side, side))
            total = term if total is None else total + term
        parts.append(total.astype(BF16))
    return parts


def store_slots(buffer, parts, group):
    if len(buffer.shape) == 2:
        for place, part in enumerate(parts):
            buffer[:, place * group : (place + 1) * group] = part
        return
    slot = buffer.shape[2]
    for place, part in enumerate(parts):
        for start in range(0, group, slot):
            buffer[(place * group + start) // slot] = part[:, start : start + slot]


def send_shape(channels, peers, slot):
    if slot % 128:
        return (channels, peers * slot)
    return (peers, channels, slot)


def exchange(send, peers):
    if send.ndim == 2:
        send = send.reshape(send.shape[0], peers, -1).transpose(1, 0, 2)
    arrived = lax.all_to_all(send, "dom", 0, 0, tiled=True)
    if arrived.shape[2] % 128 == 0:
        return arrived
    return arrived.transpose(1, 0, 2).reshape(arrived.shape[1], -1)


def load_wide(ref):
    if len(ref.shape) == 2:
        return ref[...]
    return jnp.concatenate([ref[peer] for peer in range(ref.shape[0])], axis=1)


def sketch_kernel(count, me_ref, features_ref, sketch_ref, *rest):
    outs, full = rest[:count], rest[count]
    channels = outs[0].shape[0]
    product = dot(features_ref[...], sketch_ref[...])
    product = product.T.astype(BF16)
    for part in range(count):
        full[part] = product[part * channels : (part + 1) * channels]
    me = me_ref[0, 0]
    for step in range(count):
        outs[step][...] = full[partner(me, step, count)]


def partner(me, step, count):
    if count & (count - 1) == 0:
        return me ^ step
    return lax.rem(me + step, count)


def source(me, step, count):
    if count & (count - 1) == 0:
        return me ^ step
    return lax.rem(me + count - step, count)


def pick_kernel(count, group, me_ref, index_ref, *rest):
    arrived, (hop_out, send_out, hop, send, sems) = rest[:count], rest[count:]
    blocks, _, side = hop.shape
    per = blocks // count
    me = me_ref[0, 0]
    for step in range(count):
        first = source(me, step, count) * per
        for part in range(per):
            hop[first + part] = arrived[step][:, part * side : (part + 1) * side]
    hop_copy = pltpu.make_async_copy(hop, hop_out, sems.at[0])
    hop_copy.start()
    parts = pick([hop[block] for block in range(blocks)], index_ref[...], side, group)
    store_slots(send, parts, group)
    send_copy = pltpu.make_async_copy(send, send_out, sems.at[1])
    send_copy.start()
    hop_copy.wait()
    send_copy.wait()


def combine(dst_ref, src_ref, hop_in, arrived_ref, tiles_ref, columns, sums, result, sem):
    blocks, channels, side = result.shape
    slots = tiles_ref.shape[0]
    fixed = columns.shape[0]
    fetch = pltpu.make_async_copy(
        hop_in, columns.at[pl.ds(0, blocks), pl.ds(0, channels), :], sem
    )
    fetch.start()
    columns[:, channels:, :] = jnp.ones((fixed, EXTRA, side), BF16)
    arrived = load_wide(arrived_ref)
    for block in range(blocks, fixed):
        start = (block - blocks) * side
        columns[block, :channels, :] = arrived[:, start : start + side]
    fetch.wait()
    for block in range(blocks):
        sums[block] = dot(columns[block], tiles_ref[block], NT)
    for slot in range(blocks, slots):
        target = dst_ref[0, slot]
        target = jnp.where(target < 0, blocks, target)
        start = slot if slot < fixed else src_ref[0, slot]
        sums[target] = sums[target] + dot(columns[start], tiles_ref[slot], NT)
    for block in range(blocks):
        block_sums = sums[block]
        result[block] = (block_sums[:channels] / block_sums[channels : channels + 1]).astype(BF16)


def combine_pick_kernel(
    group, dst_ref, src_ref, index_ref, hop_in, arrived_ref, tiles_ref, hop_out, send_out,
    columns, sums, result, send, sems,
):
    blocks, _, side = result.shape
    combine(
        dst_ref, src_ref, hop_in, arrived_ref, tiles_ref, columns, sums, result, sems.at[2]
    )
    hop_copy = pltpu.make_async_copy(result, hop_out, sems.at[0])
    hop_copy.start()
    parts = pick([result[block] for block in range(blocks)], index_ref[...], side, group)
    store_slots(send, parts, group)
    send_copy = pltpu.make_async_copy(send, send_out, sems.at[1])
    send_copy.start()
    hop_copy.wait()
    send_copy.wait()


def combine_last_kernel(
    group, dst_ref, src_ref, index_ref, hop0_in, hop_in, arrived_ref, tiles_ref, send_out,
    columns, sums, result, hop0, send, sems,
):
    blocks, channels, side = result.shape
    first = pltpu.make_async_copy(hop0_in, hop0, sems.at[1])
    first.start()
    combine(
        dst_ref, src_ref, hop_in, arrived_ref, tiles_ref, columns, sums, result, sems.at[2]
    )
    first.wait()
    stacks = [
        jnp.concatenate([hop0[block], columns[block, :channels, :], result[block]], 0)
        for block in range(blocks)
    ]
    parts = pick(stacks, index_ref[...], side, group)
    store_slots(send, parts, group)
    send_copy = pltpu.make_async_copy(send, send_out, sems.at[0])
    send_copy.start()
    send_copy.wait()


def place_kernel(index_ref, arrived_ref, out_ref):
    hops, channels, width = out_ref.shape
    stacked = load_wide(arrived_ref)
    table = one_hot(index_ref[...], pl.program_id(0) * width, width)
    placed = dot(stacked, table, NT).astype(BF16)
    for hop in range(hops):
        out_ref[hop] = placed[hop * channels : (hop + 1) * channels]


def on_device(
    features, sketch_matrix, tiles, tile_dst, tile_src, halo_index, send_order, arrival_place
):
    reps = lax.axis_size("rep")
    peers = lax.axis_size("dom")
    width = features.shape[0]
    nodes = width * reps
    channels = sketch_matrix.shape[1] // reps
    halo = halo_index.shape[1]
    tiles = tiles[0]
    slots, side, _ = tiles.shape
    blocks = nodes // side
    fixed = (nodes + halo) // side
    me = lax.axis_index("rep").astype(jnp.int32).reshape(1, 1)
    vmem, dma = pltpu.VMEM, pltpu.SemaphoreType.DMA
    hop_shape = (blocks, channels, side)
    halo_shape = send_shape(channels, peers, halo // peers)
    last_shape = send_shape(3 * channels, peers, nodes // peers)
    group = 256

    def out(shape):
        return jax.ShapeDtypeStruct(shape, BF16)

    own = pl.pallas_call(
        lambda *refs: sketch_kernel(reps, *refs),
        out_shape=(out((channels, width)),) * reps,
        in_specs=[SMEM, VMEM, VMEM],
        out_specs=(VMEM,) * reps,
        scratch_shapes=[vmem((reps, channels, width), BF16)],
        compiler_params=params(),
        name="sketch",
    )(me, features, sketch_matrix)
    arrived = [own[0]]
    for step in range(1, reps):
        pairs = [(rank, int(partner_static(rank, step, reps))) for rank in range(reps)]
        arrived.append(lax.ppermute(own[step], "rep", pairs))
    hop0, send = pl.pallas_call(
        lambda *refs: pick_kernel(reps, group, *refs),
        out_shape=(out(hop_shape), out(halo_shape)),
        in_specs=[SMEM, VMEM] + [VMEM] * reps,
        out_specs=(HBM, HBM),
        scratch_shapes=[vmem(hop_shape, BF16), vmem(halo_shape, BF16), dma((2,))],
        compiler_params=params(),
        name="pick",
    )(me, halo_index, *arrived)
    halo0 = exchange(send, peers)
    work = [
        vmem((fixed, channels + EXTRA, side), BF16),
        vmem((blocks + 1, channels + EXTRA, side), F32),
        vmem(hop_shape, BF16),
    ]
    hop1, send = pl.pallas_call(
        lambda *refs: combine_pick_kernel(group, *refs),
        out_shape=(out(hop_shape), out(halo_shape)),
        in_specs=[SMEM, SMEM, VMEM, HBM, VMEM, VMEM],
        out_specs=(HBM, HBM),
        scratch_shapes=work + [vmem(halo_shape, BF16), dma((3,))],
        compiler_params=params(),
        name="combine_pick",
    )(tile_dst, tile_src, halo_index, hop0, halo0, tiles)
    halo1 = exchange(send, peers)
    send = pl.pallas_call(
        lambda *refs: combine_last_kernel(group, *refs),
        out_shape=out(last_shape),
        in_specs=[SMEM, SMEM, VMEM, HBM, HBM, VMEM, VMEM],
        out_specs=HBM,
        scratch_shapes=work + [vmem(hop_shape, BF16), vmem(last_shape, BF16), dma((3,))],
        compiler_params=params(),
        name="combine_last",
    )(tile_dst, tile_src, send_order, hop0, hop1, halo1, tiles)
    last = exchange(send, peers)
    return pl.pallas_call(
        place_kernel,
        out_shape=out((3, channels, nodes)),
        in_specs=[
            pl.BlockSpec((1, nodes), lambda i: (0, 0)),
            pl.BlockSpec(last.shape, lambda i: (0,) * last.ndim),
        ],
        out_specs=pl.BlockSpec((3, channels, side), lambda i: (0, 0, i)),
        grid=(blocks,),
        compiler_params=params(),
        name="place",
    )(arrival_place, last)


def partner_static(rank, step, count):
    if count & (count - 1) == 0:
        return rank ^ step
    return (rank + step) % count


def solution(mesh):
    in_specs = (
        P(("dom", "rep"), None),
        P(),
        P("dom", None, None, None),
        P("dom", None),
        P("dom", None),
        P("dom", None),
        P("dom", None),
        P("dom", None),
    )
    out_specs = P(None, "rep", "dom")
    return jax.shard_map(
        on_device, mesh=mesh, in_specs=in_specs, out_specs=out_specs, check_vma=False
    )
```

time: 111 us -> 70.4 us (0.63)
  blocking collectives: 0 us -> 44.2 us
  local copies, waits for them, and re-layouts: 41.9 us -> 5.91 us
  waiting for transfers between devices: 35.4 us -> 4.02 us
  starting transfers between devices: 17.7 us -> 3.15 us
  Pallas kernels: 0 us -> 12.7 us
  matrix products: 8.87 us -> 0 us
  other arithmetic: 5.49 us -> 0 us
    all_to_all x0 -> x3, blocking collectives: none -> 44.2 us  [exchange(): arrived = lax.all_to_all(send, 'dom', 0, 0, tiled=True)]
    all_to_all x4 -> x0, waiting for transfers between devices: 35.4 us -> none  [the longest x1 17.5 us: on_device(): lax.all_to_all(stacked, 'dom', split_axis=1, concat_axis=1, tiled=True)]
    gather x5 -> x0, local copies, waits for them, and re-layouts: 20.9 us -> none  [the longest x1 7.5 us: on_device(): stacked = jnp.concatenate([hop0, hop1, hop2], 0)[:, order]]
    all_to_all x4 -> x0, starting transfers between devices: 17.7 us -> none  [the longest x1 6.45 us: on_device(): lax.all_to_all(hop0[:, halo_rows], 'dom', split_axis=1, concat_axis=1, ti...]
    pallas_call x0 -> x5, Pallas kernels: none -> 12.7 us  [the longest x1 5.07 us: on_device(): pl.pallas_call(place_kernel, out_shape=out((3, channels, nodes)), in_spec...]
    scatter x2 -> x0, local copies, waits for them, and re-layouts: 10.8 us -> none  [on_device(): placed = jnp.zeros_like(arrived).at[:, place].set(arrived)]
    dot_general x6 -> x0, matrix products: 8.87 us -> none  [the longest x2 3.99 us: combine(): jnp.einsum('ctj,tij->cti', blocks, tile_set, preferred_element_type=jnp.f...]
    all_to_all x9 -> x0, local copies, waits for them, and re-layouts: 4.69 us -> none  [the longest x3 1.85 us: on_device(): lax.all_to_all(stacked, 'dom', split_axis=1, concat_axis=1, tiled=True)]
  transfers between devices with their start and end apart: 4 -> 3, of which waited for: 4 -> 2; matrix products, arithmetic and copies ran while one was open for 2% -> 0% of each run, Pallas kernels for 0% -> 0%
where the time goes in v2:
time: 70.4 us; the launch traced here: 70 us
  blocking collectives  44.2 us (63%)
  Pallas kernels  12.7 us (18%)
  local copies, waits for them, and re-layouts  5.91 us (8%)
  waiting for transfers between devices  4.02 us (6%)
  starting transfers between devices  3.15 us (4%)
    all_to_all x3, blocking collectives, exchange(): arrived = lax.all_to_all(send, 'dom', 0, 0, tiled=True)  44.2 us
    unnamed x22, local copies, waits for them, and re-layouts  5.91 us
    pallas_call x1, Pallas kernels, on_device(): pl.pallas_call(place_kernel, out_shape=out((3, channels, nodes)), in_spec...  5.07 us
    ppermute x3, waiting for transfers between devices, on_device(): arrived.append(lax.ppermute(own[step], 'rep', pairs))  4.02 us
    pallas_call x1, Pallas kernels, on_device(): pl.pallas_call(lambda *refs: combine_last_kernel(group, *refs), out_shape...  3.46 us
    ppermute x3, starting transfers between devices, on_device(): arrived.append(lax.ppermute(own[step], 'rep', pairs))  3.15 us
    pallas_call x1, Pallas kernels, on_device(): pl.pallas_call(lambda *refs: combine_pick_kernel(group, *refs), out_shape...  2.63 us
  transfers between devices with their start and end apart: 3, of which 2 were waited for; matrix products, arithmetic and copies ran while one was open for 0% of the time, Pallas kernels for 0%

profile of v2, /device:TPU:0, one launch (start us, length us, event | category | flops | bytes accessed | tf_op | source)
XLA Modules:
  0.0 70.0 jit_solution(5952534782251986322)
XLA Ops:
  0.0 0.0 copy-start.10
  0.0 0.0 copy-start.8
  0.0 0.0 copy-start.2
  0.0 1.2 %copy-done.2 = bf16[512,768]{1,0:T(8,128)(2,1)S(1)} copy-done((bf16[512,768]{1,0:T(8,128)(2,1)S(1)}, bf16[512,768]{1,0:T(8,128)(2,1)}, u32[]{:S(2)}) %copy-start.2) | copy-done | bytes 786456
  1.2 0.0 copy-start.3
  1.2 1.0 %copy-done.3 = bf16[768,256]{1,0:T(8,128)(2,1)S(1)} copy-done((bf16[768,256]{1,0:T(8,128)(2,1)S(1)}, bf16[768,256]{1,0:T(8,128)(2,1)}, u32[]{:S(2)}) %copy-start.3) | copy-done | bytes 393240
  2.2 0.0 copy-start.5
  2.2 0.5 sketch.1
  2.6 0.6 collective-permute-start
  3.2 2.6 %collective-permute-start.1 = (bf16[64,512]{1,0:T(8,128)(2,1)S(1)}, bf16[64,512]{1,0:T(8,128)(2,1)S(1)}, u32[]{:S(2)}, u32[]{:S(2)}) collective-permute-start(bf16[64,512]{1,0:T(8,128)(2,1)S(1)} %get-tuple-element.15), channel_id=1, source_target_pairs={{0,2},{1,3},{2,0},{3,1},{4,6},{5,7},{6,4},{7,5},{8,10},{9,11},{10,... | collective-permute-start | bytes 196616 | tf_op jit(solution)/shard_map/ppermute | solution.py:232
  5.7 0.0 collective-permute-start.2
  5.8 0.0 collective-permute-done.refs_3_
  5.8 2.6 %collective-permute-done.1.refs_4_ = bf16[64,512]{1,0:T(8,128)(2,1)S(1)} collective-permute-done((bf16[64,512]{1,0:T(8,128)(2,1)S(1)}, bf16[64,512]{1,0:T(8,128)(2,1)S(1)}, u32[]{:S(2)}, u32[]{:S(2)}) %collective-permute-start.1) | collective-permute-done | bytes 65568 | tf_op jit(solution)/shard_map/ppermute | solution.py:232
  8.4 1.4 %collective-permute-done.2.refs_5_ = bf16[64,512]{1,0:T(8,128)(2,1)S(1)} collective-permute-done((bf16[64,512]{1,0:T(8,128)(2,1)S(1)}, bf16[64,512]{1,0:T(8,128)(2,1)S(1)}, u32[]{:S(2)}, u32[]{:S(2)}) %collective-permute-start.2) | collective-permute-done | bytes 65568 | tf_op jit(solution)/shard_map/ppermute | solution.py:232
  9.8 0.0 copy-start.4
  9.8 0.7 copy-done.4
  10.5 1.1 %pick.1 = (bf16[8,64,256]{2,1,0:T(8,128)(2,1)S(1)}, bf16[8,64,128]{2,1,0:T(8,128)(2,1)S(1)}) custom-call(s32[1,1]{1,0:T(1,128)} %bitcast.refs_0_, s32[1,1024]{1,0:T(1,128)S(1)} %copy-done.4, bf16[64,512]{1,0:T(8,128)(2,1)S(1)} %get-tuple-element.13.refs_2_, bf16[64,512]{1,0:T(8,128)(2,1)S(1)} %collective-permute-done.refs_3_, ...), custom_call_target="tpu_custom_call" | custom-call | tf_op jit(solution)/shard_map/pick/pallas_call | solution.py:233
  11.6 13.0 %all_to_all.15.refs_4_ = bf16[8,64,128]{2,1,0:T(8,128)(2,1)S(1)} all-to-all(bf16[8,64,128]{2,1,0:T(8,128)(2,1)S(1)} %get-tuple-element.18), channel_id=1, replica_groups=mesh['dom'=8,'rep'=4] {'dom'}, dimensions={0} | all-to-all | bytes 262144 | tf_op jit(solution)/shard_map/all_to_all | solution.py:67
  24.5 0.0 copy-start
  24.5 1.7 %copy-done = bf16[1,20,256,256]{3,2,1,0:T(8,128)(2,1)S(1)} copy-done((bf16[1,20,256,256]{3,2,1,0:T(8,128)(2,1)S(1)}, bf16[1,20,256,256]{3,2,1,0:T(8,128)(2,1)}, u32[]{:S(2)}) %copy-start) | copy-done | bytes 2621464
  26.3 0.0 copy-start.7
  26.3 0.7 copy-done.7
  26.9 0.0 copy-start.9
  26.9 0.7 copy-done.9
  27.6 0.0 copy-start.1
  27.6 2.6 %combine_pick.1 = (bf16[8,64,256]{2,1,0:T(8,128)(2,1)S(1)}, bf16[8,64,128]{2,1,0:T(8,128)(2,1)S(1)}) custom-call(s32[1,20]{1,0:T(1,128)S(1)} %copy-done.7, s32[1,20]{1,0:T(1,128)S(1)} %copy-done.9, s32[1,1024]{1,0:T(1,128)S(1)} %copy-done.4, bf16[8,64,256]{2,1,0:T(8,128)(2,1)S(1)} %get-tuple-element.17.refs_3_, bf16[8,64,128]{2,1,0:T(8,128)(2,1)S(1)} %all_to_all.15.refs_4_, ...), custom_call_target="tpu_custom_call" | custom-call | tf_op jit(solution)/shard_map/combine_pick/pallas_call | solution.py:248
  30.2 9.8 %all_to_all.16.refs_5_ = bf16[8,64,128]{2,1,0:T(8,128)(2,1)S(1)} all-to-all(bf16[8,64,128]{2,1,0:T(8,128)(2,1)S(1)} %get-tuple-element.20), channel_id=1, replica_groups=mesh['dom'=8,'rep'=4] {'dom'}, dimensions={0} | all-to-all | bytes 262144 | tf_op jit(solution)/shard_map/all_to_all | solution.py:67
  40.0 0.0 copy-done.10
  40.1 0.0 copy-done.8
  40.1 0.0 copy-done.5
  40.1 0.0 copy-done.1
  40.1 0.0 copy-start.6
  40.1 3.5 %combine_last.1 = bf16[8,192,256]{2,1,0:T(8,128)(2,1)S(1)} custom-call(s32[1,20]{1,0:T(1,128)S(1)} %copy-done.8, s32[1,20]{1,0:T(1,128)S(1)} %copy-done.10, s32[1,2048]{1,0:T(1,128)S(1)} %copy-done.5, bf16[8,64,256]{2,1,0:T(8,128)(2,1)S(1)} %get-tuple-element.17.refs_3_, bf16[8,64,256]{2,1,0:T(8,128)(2,1)S(1)} %get-tuple-element.19.refs_4_, ...), custom_call_target="tpu_custom_call" | custom-call | tf_op jit(solution)/shard_map/combine_last/pallas_call | solution.py:258
  43.6 21.4 %all_to_all.17.arrived_ref = bf16[8,192,256]{2,1,0:T(8,128)(2,1)S(1)} all-to-all(bf16[8,192,256]{2,1,0:T(8,128)(2,1)S(1)} %combine_last.1), channel_id=1, replica_groups=mesh['dom'=8,'rep'=4] {'dom'}, dimensions={0} | all-to-all | bytes 1572864 | tf_op jit(solution)/shard_map/all_to_all | solution.py:67
  65.0 0.0 copy-done.6
  65.0 5.1 %place.1 = bf16[3,64,2048]{2,1,0:T(8,128)(2,1)} custom-call(s32[1,2048]{1,0:T(1,128)S(1)} %copy-done.6, bf16[8,192,256]{2,1,0:T(8,128)(2,1)S(1)} %all_to_all.17.arrived_ref), custom_call_target="tpu_custom_call" | custom-call | tf_op jit(solution)/shard_map/place/pallas_call | solution.py:268
Async XLA Ops:
  0.0 40.0 %copy-start.10 = (s32[1,20]{1,0:T(1,128)S(1)}, s32[1,20]{1,0:T(1,128)}, u32[]{:S(2)}) copy-start(s32[1,20]{1,0:T(1,128)} %refs_1_.7) | copy-start | bytes 244
  0.0 40.0 %copy-start.8 = (s32[1,20]{1,0:T(1,128)S(1)}, s32[1,20]{1,0:T(1,128)}, u32[]{:S(2)}) copy-start(s32[1,20]{1,0:T(1,128)} %refs_0_.3) | copy-start | bytes 244
  0.0 1.2 %copy-start.2 = (bf16[512,768]{1,0:T(8,128)(2,1)S(1)}, bf16[512,768]{1,0:T(8,128)(2,1)}, u32[]{:S(2)}) copy-start(bf16[512,768]{1,0:T(8,128)(2,1)} %refs_1_.4) | copy-start | bytes 2359300
  1.2 1.0 %copy-start.3 = (bf16[768,256]{1,0:T(8,128)(2,1)S(1)}, bf16[768,256]{1,0:T(8,128)(2,1)}, u32[]{:S(2)}) copy-start(bf16[768,256]{1,0:T(8,128)(2,1)} %refs_2_.3) | copy-start | bytes 1179652
  2.2 37.9 %copy-start.5 = (s32[1,2048]{1,0:T(1,128)S(1)}, s32[1,2048]{1,0:T(1,128)}, u32[]{:S(2)}) copy-start(s32[1,2048]{1,0:T(1,128)} %refs_2_.5) | copy-start | bytes 24580
  2.6 3.2 %collective-permute-start = (bf16[64,512]{1,0:T(8,128)(2,1)S(1)}, bf16[64,512]{1,0:T(8,128)(2,1)S(1)}, u32[]{:S(2)}, u32[]{:S(2)}) collective-permute-start(bf16[64,512]{1,0:T(8,128)(2,1)S(1)} %get-tuple-element.14), channel_id=1, source_target_pairs={{0,1},{1,0},{2,3},{3,2},{4,5},{5,4},{6,7},{7,6},{8,9},{9,8},{10,11... | collective-permute-start | bytes 196616 | tf_op jit(solution)/shard_map/ppermute | solution.py:232
  3.2 5.2 %collective-permute-start.1 = (bf16[64,512]{1,0:T(8,128)(2,1)S(1)}, bf16[64,512]{1,0:T(8,128)(2,1)S(1)}, u32[]{:S(2)}, u32[]{:S(2)}) collective-permute-start(bf16[64,512]{1,0:T(8,128)(2,1)S(1)} %get-tuple-element.15), channel_id=1, source_target_pairs={{0,2},{1,3},{2,0},{3,1},{4,6},{5,7},{6,4},{7,5},{8,10},{9,11},{10,... | collective-permute-start | bytes 196616 | tf_op jit(solution)/shard_map/ppermute | solution.py:232
  5.7 4.1 %collective-permute-start.2 = (bf16[64,512]{1,0:T(8,128)(2,1)S(1)}, bf16[64,512]{1,0:T(8,128)(2,1)S(1)}, u32[]{:S(2)}, u32[]{:S(2)}) collective-permute-start(bf16[64,512]{1,0:T(8,128)(2,1)S(1)} %get-tuple-element.16), channel_id=1, source_target_pairs={{0,3},{1,2},{2,1},{3,0},{4,7},{5,6},{6,5},{7,4},{8,11},{9,10},{10,... | collective-permute-start | bytes 196616 | tf_op jit(solution)/shard_map/ppermute | solution.py:232
  9.8 0.7 copy-start.4
  24.5 1.7 %copy-start = (bf16[1,20,256,256]{3,2,1,0:T(8,128)(2,1)S(1)}, bf16[1,20,256,256]{3,2,1,0:T(8,128)(2,1)}, u32[]{:S(2)}) copy-start(bf16[1,20,256,256]{3,2,1,0:T(8,128)(2,1)} %param.10) | copy-start | bytes 7864324
  26.3 0.7 copy-start.7
  26.9 0.7 copy-start.9
  27.6 12.5 %copy-start.1 = (bf16[1,20,256,256]{3,2,1,0:T(8,128)(2,1)S(1)}, bf16[1,20,256,256]{3,2,1,0:T(8,128)(2,1)}, u32[]{:S(2)}) copy-start(bf16[1,20,256,256]{3,2,1,0:T(8,128)(2,1)} %param.10) | copy-start | bytes 7864324
  40.1 24.9 %copy-start.6 = (s32[1,2048]{1,0:T(1,128)S(1)}, s32[1,2048]{1,0:T(1,128)}, u32[]{:S(2)}) copy-start(s32[1,2048]{1,0:T(1,128)} %index_ref.1) | copy-start | bytes 24580

commit v3 on v2

v3 whole, which is shorter than its diff:
```python
import jax
import jax.numpy as jnp
from jax import lax
from jax.experimental import pallas as pl
from jax.experimental.pallas import tpu as pltpu
from jax.sharding import PartitionSpec as P

BF16 = jnp.bfloat16
F32 = jnp.float32
EXTRA = 16
NN = (((1,), (0,)), ((), ()))
NT = (((1,), (1,)), ((), ()))
VMEM = pl.BlockSpec(memory_space=pltpu.VMEM)
SMEM = pl.BlockSpec(memory_space=pltpu.SMEM)
HBM = pl.BlockSpec(memory_space=pltpu.HBM)


def params():
    return pltpu.CompilerParams(vmem_limit_bytes=40 * 1024 * 1024)


def in_hbm(array):
    return pltpu.with_memory_space_constraint(array, pltpu.HBM)


def dot(left, right, dims=NN):
    return lax.dot_general(left, right, dims, preferred_element_type=F32)


def split(index, side, blocks):
    block = jnp.zeros_like(index)
    for edge in range(1, blocks):
        block += (index >= edge * side).astype(jnp.int32)
    return block, index - block * side


def one_hot(index, rows):
    row = lax.broadcasted_iota(jnp.int32, (rows, index.shape[1]), 0)
    return jnp.where(row == index, 1.0, 0.0).astype(BF16)


def pick(stack, blocks, index, side, group):
    rows = stack.shape[0] // blocks
    parts = []
    for start in range(0, index.shape[1], group):
        block, inner = split(index[:, start : start + group], side, blocks)
        every = dot(stack, one_hot(inner, side))
        chosen = every[:rows]
        for other in range(1, blocks):
            chosen = jnp.where(block == other, every[other * rows : (other + 1) * rows], chosen)
        parts.append(chosen.astype(BF16))
    return parts


def store_slots(buffer, parts, group):
    if len(buffer.shape) == 2:
        for place, part in enumerate(parts):
            buffer[:, place * group : (place + 1) * group] = part
        return
    slot = buffer.shape[2]
    for place, part in enumerate(parts):
        for start in range(0, group, slot):
            buffer[(place * group + start) // slot] = part[:, start : start + slot]


def send_shape(channels, peers, slot):
    if slot % 128:
        return (channels, peers * slot)
    return (peers, channels, slot)


def exchange(send, peers):
    if send.ndim == 2:
        send = send.reshape(send.shape[0], peers, -1).transpose(1, 0, 2)
    arrived = lax.all_to_all(send, "dom", 0, 0, tiled=True)
    if arrived.shape[2] % 128 == 0:
        return arrived
    return arrived.transpose(1, 0, 2).reshape(arrived.shape[1], -1)


def load_wide(ref):
    if len(ref.shape) == 2:
        return ref[...]
    return jnp.concatenate([ref[peer] for peer in range(ref.shape[0])], axis=1)


def partner(me, step, count):
    if count & (count - 1) == 0:
        return me ^ step
    return lax.rem(me + step, count)


def source(me, step, count):
    if count & (count - 1) == 0:
        return me ^ step
    return lax.rem(me + count - step, count)


def pairs(step, count):
    if count & (count - 1) == 0:
        return [(rank, rank ^ step) for rank in range(count)]
    return [(rank, (rank + step) % count) for rank in range(count)]


def sketch_kernel(count, chunks, me_ref, features_in, sketch_in, *rest):
    outs, (full, features, sketch, sems) = rest[:count], rest[count:]
    channels, width = outs[0].shape
    step = width // chunks
    copies = [pltpu.make_async_copy(sketch_in, sketch, sems.at[chunks])]
    for chunk in range(chunks):
        rows = pl.ds(chunk * step, step)
        copies.append(
            pltpu.make_async_copy(features_in.at[rows, :], features.at[rows, :], sems.at[chunk])
        )
    for copy in copies:
        copy.start()
    copies[0].wait()
    for chunk in range(chunks):
        copies[chunk + 1].wait()
        rows = slice(chunk * step, (chunk + 1) * step)
        product = dot(features[rows, :], sketch[...]).T.astype(BF16)
        for part in range(count):
            full[part, :, rows] = product[part * channels : (part + 1) * channels]
    me = me_ref[0, 0]
    for part in range(count):
        outs[part][...] = full[partner(me, part, count)]


def pick_kernel(count, group, me_ref, index_in, *rest):
    arrived, (hop, send, index, sem) = rest[:count], rest[count:]
    fetch = pltpu.make_async_copy(index_in, index, sem)
    fetch.start()
    blocks, _, side = hop.shape
    per = blocks // count
    me = me_ref[0, 0]
    for step in range(count):
        first = source(me, step, count) * per
        for part in range(per):
            hop[first + part] = arrived[step][:, part * side : (part + 1) * side]
    stack = jnp.concatenate([hop[block] for block in range(blocks)], 0)
    fetch.wait()
    store_slots(send, pick(stack, blocks, index[...], side, group), group)


def combine(dst_in, src_in, index_in, tiles_in, hop, arrived_ref, scratch, store):
    dst, src, index, tiles, columns, sums, sems = scratch
    blocks, channels, side = hop.shape
    slots = tiles.shape[0]
    fixed = columns.shape[0]
    small = [
        pltpu.make_async_copy(dst_in, dst, sems.at[0]),
        pltpu.make_async_copy(src_in, src, sems.at[1]),
        pltpu.make_async_copy(index_in, index, sems.at[2]),
    ]
    chunk = 4
    large = []
    for start in range(0, slots, chunk):
        rows = pl.ds(start, chunk)
        large.append(
            pltpu.make_async_copy(tiles_in.at[rows], tiles.at[rows], sems.at[3 + start // chunk])
        )
    for copy in large + small:
        copy.start()
    columns[:, channels:, :] = jnp.ones((fixed, EXTRA, side), BF16)
    for block in range(blocks):
        columns[block, :channels, :] = hop[block]
    arrived = load_wide(arrived_ref)
    for block in range(blocks, fixed):
        start = (block - blocks) * side
        columns[block, :channels, :] = arrived[:, start : start + side]
    for slot in range(slots):
        if slot % chunk == 0:
            large[slot // chunk].wait()
        if slot < blocks:
            sums[slot] = dot(columns[slot], tiles[slot], NT)
            continue
        if slot == blocks:
            for copy in small:
                copy.wait()
        target = dst[0, slot]
        target = jnp.where(target < 0, blocks, target)
        start = slot if slot < fixed else src[0, slot]
        sums[target] = sums[target] + dot(columns[start], tiles[slot], NT)
    results = []
    for block in range(blocks):
        total = sums[block]
        result = (total[:channels] / total[channels : channels + 1]).astype(BF16)
        store(block, result)
        results.append(result)
    return results


def combine_pick_kernel(
    group, dst_in, src_in, index_in, tiles_in, hop, arrived_ref, result, send, *scratch
):
    def store(block, value):
        result[block] = value

    results = combine(dst_in, src_in, index_in, tiles_in, hop, arrived_ref, scratch, store)
    blocks, _, side = hop.shape
    index = scratch[2]
    stack = jnp.concatenate(results, 0)
    store_slots(send, pick(stack, blocks, index[...], side, group), group)


def combine_last_kernel(
    group, dst_in, src_in, index_in, tiles_in, hop, arrived_ref, hop0, send, *scratch
):
    results = combine(
        dst_in, src_in, index_in, tiles_in, hop, arrived_ref, scratch, lambda *_: None
    )
    blocks, _, side = hop.shape
    index = scratch[2]
    stack = []
    for block in range(blocks):
        stack += [hop0[block], hop[block], results[block]]
    stack = jnp.concatenate(stack, 0)
    store_slots(send, pick(stack, blocks, index[...], side, group), group)


def place_kernel(side, index_ref, arrived_ref, out_ref):
    hops, channels, nodes = out_ref.shape
    blocks = nodes // side
    stacked = load_wide(arrived_ref)
    rows = hops * channels
    block, inner = split(index_ref[...], side, blocks)
    table = one_hot(inner, side)
    for other in range(blocks):
        mask = jnp.where(block == other, 1.0, 0.0).astype(BF16)
        placed = dot(stacked * mask, table, NT).astype(BF16)
        for hop in range(hops):
            out_ref[hop, :, other * side : (other + 1) * side] = placed[
                hop * channels : (hop + 1) * channels
            ]


def on_device(
    features, sketch_matrix, tiles, tile_dst, tile_src, halo_index, send_order, arrival_place
):
    reps = lax.axis_size("rep")
    peers = lax.axis_size("dom")
    width = features.shape[0]
    nodes = width * reps
    channels = sketch_matrix.shape[1] // reps
    halo = halo_index.shape[1]
    tiles = tiles[0]
    slots, side, _ = tiles.shape
    blocks = nodes // side
    fixed = (nodes + halo) // side
    me = lax.axis_index("rep").astype(jnp.int32).reshape(1, 1)
    vmem, smem, dma = pltpu.VMEM, pltpu.SMEM, pltpu.SemaphoreType.DMA
    hop_shape = (blocks, channels, side)
    halo_shape = send_shape(channels, peers, halo // peers)
    last_shape = send_shape(3 * channels, peers, nodes // peers)
    group = 256
    chunks = 4

    def out(shape):
        return jax.ShapeDtypeStruct(shape, BF16)

    own = pl.pallas_call(
        lambda *refs: sketch_kernel(reps, chunks, *refs),
        out_shape=(out((channels, width)),) * reps,
        in_specs=[SMEM, HBM, HBM],
        out_specs=(VMEM,) * reps,
        scratch_shapes=[
            vmem((reps, channels, width), BF16),
            vmem(features.shape, BF16),
            vmem(sketch_matrix.shape, BF16),
            dma((chunks + 1,)),
        ],
        compiler_params=params(),
        name="sketch",
    )(me, in_hbm(features), in_hbm(sketch_matrix))
    arrived = [own[0]]
    for step in range(1, reps):
        arrived.append(lax.ppermute(own[step], "rep", pairs(step, reps)))
    hop0, send = pl.pallas_call(
        lambda *refs: pick_kernel(reps, group, *refs),
        out_shape=(out(hop_shape), out(halo_shape)),
        in_specs=[SMEM, HBM] + [VMEM] * reps,
        out_specs=(VMEM, VMEM),
        scratch_shapes=[vmem(halo_index.shape, jnp.int32), dma],
        compiler_params=params(),
        name="pick",
    )(me, in_hbm(halo_index), *arrived)
    halo0 = exchange(send, peers)

    def work(index):
        return [
            smem(tile_dst.shape, jnp.int32),
            smem(tile_src.shape, jnp.int32),
            vmem(index.shape, jnp.int32),
            vmem(tiles.shape, BF16),
            vmem((fixed, channels + EXTRA, side), BF16),
            vmem((blocks + 1, channels + EXTRA, side), F32),
            dma((3 + slots // 4,)),
        ]

    hop1, send = pl.pallas_call(
        lambda *refs: combine_pick_kernel(group, *refs),
        out_shape=(out(hop_shape), out(halo_shape)),
        in_specs=[HBM] * 4 + [VMEM] * 2,
        out_specs=(VMEM, VMEM),
        scratch_shapes=work(halo_index),
        compiler_params=params(),
        name="combine_pick",
    )(in_hbm(tile_dst), in_hbm(tile_src), in_hbm(halo_index), in_hbm(tiles), hop0, halo0)
    halo1 = exchange(send, peers)
    send = pl.pallas_call(
        lambda *refs: combine_last_kernel(group, *refs),
        out_shape=out(last_shape),
        in_specs=[HBM] * 4 + [VMEM] * 3,
        out_specs=VMEM,
        scratch_shapes=work(send_order),
        compiler_params=params(),
        name="combine_last",
    )(in_hbm(tile_dst), in_hbm(tile_src), in_hbm(send_order), in_hbm(tiles), hop1, halo1, hop0)
    last = exchange(send, peers)
    return pl.pallas_call(
        lambda *refs: place_kernel(side, *refs),
        out_shape=out((3, channels, nodes)),
        in_specs=[VMEM, VMEM],
        out_specs=VMEM,
        compiler_params=params(),
        name="place",
    )(arrival_place, last)


def solution(mesh):
    in_specs = (
        P(("dom", "rep"), None),
        P(),
        P("dom", None, None, None),
        P("dom", None),
        P("dom", None),
        P("dom", None),
        P("dom", None),
        P("dom", None),
    )
    out_specs = P(None, "rep", "dom")
    return jax.shard_map(
        on_device, mesh=mesh, in_specs=in_specs, out_specs=out_specs, check_vma=False
    )
```

time: 70.4 us -> 66.5 us (0.945)
  local copies, waits for them, and re-layouts: 5.91 us -> 0.01 us
  Pallas kernels: 12.7 us -> 14.7 us
    unnamed x22 -> x2, local copies, waits for them, and re-layouts: 5.91 us -> 0.01 us
    pallas_call x1, Pallas kernels: 3.46 us -> 4.39 us  [on_device(): pl.pallas_call(lambda *refs: combine_last_kernel(group, *refs), out_shape...]
where the time goes in v3:
time: 66.5 us; the launch traced here: 66.2 us
  blocking collectives  44.2 us (66%)
  Pallas kernels  14.7 us (22%)
  waiting for transfers between devices  4.02 us (6%)
  starting transfers between devices  3.15 us (5%)
    all_to_all x3, blocking collectives, exchange(): arrived = lax.all_to_all(send, 'dom', 0, 0, tiled=True)  44.2 us
    pallas_call x1, Pallas kernels, on_device(): pl.pallas_call(lambda *refs: combine_last_kernel(group, *refs), out_shape...  4.39 us
    ppermute x3, waiting for transfers between devices, on_device(): arrived.append(lax.ppermute(own[step], 'rep', pairs(step, reps)))  4.02 us
    pallas_call x1, Pallas kernels, on_device(): pl.pallas_call(lambda *refs: place_kernel(side, *refs), out_shape=out((3,...  3.74 us
    ppermute x3, starting transfers between devices, on_device(): arrived.append(lax.ppermute(own[step], 'rep', pairs(step, reps)))  3.15 us
    pallas_call x1, Pallas kernels, on_device(): pl.pallas_call(lambda *refs: combine_pick_kernel(group, *refs), out_shape...  3.05 us
    pallas_call x1, Pallas kernels, on_device(): pl.pallas_call(lambda *refs: sketch_kernel(reps, chunks, *refs), out_shap...  2.39 us
  transfers between devices with their start and end apart: 3, of which 2 were waited for; matrix products, arithmetic and copies ran while one was open for 0% of the time, Pallas kernels for 0%

profile of v3, /device:TPU:0, one launch (start us, length us, event | category | flops | bytes accessed | tf_op | source)
XLA Modules:
  0.0 66.2 jit_solution(17584129098842605161)
XLA Ops:
  0.0 2.4 %sketch.1 = (bf16[64,512]{1,0:T(8,128)(2,1)S(1)}, bf16[64,512]{1,0:T(8,128)(2,1)S(1)}, bf16[64,512]{1,0:T(8,128)(2,1)S(1)}, bf16[64,512]{1,0:T(8,128)(2,1)S(1)}) custom-call(s32[1,1]{1,0:T(1,128)} %bitcast.1.refs_0_, bf16[512,768]{1,0:T(8,128)(2,1)} %refs_1_.4, bf16[768,256]{1,0:T(8,128)(2,1)} %refs_2_.3), custom_call_target="tpu_custom_call" | custom-call | tf_op jit(solution)/shard_map/sketch/pallas_call | solution.py:261
  2.4 0.6 collective-permute-start
  3.0 2.6 %collective-permute-start.1 = (bf16[64,512]{1,0:T(8,128)(2,1)S(1)}, bf16[64,512]{1,0:T(8,128)(2,1)S(1)}, u32[]{:S(2)}, u32[]{:S(2)}) collective-permute-start(bf16[64,512]{1,0:T(8,128)(2,1)S(1)} %get-tuple-element.15), channel_id=1, source_target_pairs={{0,2},{1,3},{2,0},{3,1},{4,6},{5,7},{6,4},{7,5},{8,10},{9,11},{10,... | collective-permute-start | bytes 196616 | tf_op jit(solution)/shard_map/ppermute | solution.py:277
  5.5 0.0 collective-permute-start.2
  5.6 0.0 collective-permute-done.refs_3_
  5.6 2.6 %collective-permute-done.1.refs_4_ = bf16[64,512]{1,0:T(8,128)(2,1)S(1)} collective-permute-done((bf16[64,512]{1,0:T(8,128)(2,1)S(1)}, bf16[64,512]{1,0:T(8,128)(2,1)S(1)}, u32[]{:S(2)}, u32[]{:S(2)}) %collective-permute-start.1) | collective-permute-done | bytes 65568 | tf_op jit(solution)/shard_map/ppermute | solution.py:277
  8.2 1.4 %collective-permute-done.2.refs_5_ = bf16[64,512]{1,0:T(8,128)(2,1)S(1)} collective-permute-done((bf16[64,512]{1,0:T(8,128)(2,1)S(1)}, bf16[64,512]{1,0:T(8,128)(2,1)S(1)}, u32[]{:S(2)}, u32[]{:S(2)}) %collective-permute-start.2) | collective-permute-done | bytes 65568 | tf_op jit(solution)/shard_map/ppermute | solution.py:277
  9.6 1.2 %pick.1 = (bf16[8,64,256]{2,1,0:T(8,128)(2,1)S(1)}, bf16[8,64,128]{2,1,0:T(8,128)(2,1)S(1)}) custom-call(s32[1,1]{1,0:T(1,128)} %bitcast.1.refs_0_, s32[1,1024]{1,0:T(1,128)} %refs_2_.4, bf16[64,512]{1,0:T(8,128)(2,1)S(1)} %get-tuple-element.13.refs_2_, bf16[64,512]{1,0:T(8,128)(2,1)S(1)} %collective-permute-done.refs_3_, ...), custom_call_target="tpu_custom_call" | custom-call | tf_op jit(solution)/shard_map/pick/pallas_call | solution.py:278
  10.7 13.0 %all_to_all.15.refs_5_ = bf16[8,64,128]{2,1,0:T(8,128)(2,1)S(1)} all-to-all(bf16[8,64,128]{2,1,0:T(8,128)(2,1)S(1)} %get-tuple-element.18), channel_id=1, replica_groups=mesh['dom'=8,'rep'=4] {'dom'}, dimensions={0} | all-to-all | bytes 262144 | tf_op jit(solution)/shard_map/all_to_all | solution.py:75
  23.7 3.1 %combine_pick.1 = (bf16[8,64,256]{2,1,0:T(8,128)(2,1)S(1)}, bf16[8,64,128]{2,1,0:T(8,128)(2,1)S(1)}) custom-call(s32[1,20]{1,0:T(1,128)} %refs_0_.4, s32[1,20]{1,0:T(1,128)} %refs_1_.7, s32[1,1024]{1,0:T(1,128)} %refs_2_.4, bf16[20,256,256]{2,1,0:T(8,128)(2,1)} %bitcast.2, bf16[8,64,256]{2,1,0:T(8,128)(2,1)S(1)} %get-tuple-element.17.refs_4_.refs_6_, ...), custom_call_target="tpu_custom_call" | custom-call | tf_op jit(solution)/shard_map/combine_pick/pallas_call | solution.py:300
  26.8 9.8 %all_to_all.16.refs_5_ = bf16[8,64,128]{2,1,0:T(8,128)(2,1)S(1)} all-to-all(bf16[8,64,128]{2,1,0:T(8,128)(2,1)S(1)} %get-tuple-element.20), channel_id=1, replica_groups=mesh['dom'=8,'rep'=4] {'dom'}, dimensions={0} | all-to-all | bytes 262144 | tf_op jit(solution)/shard_map/all_to_all | solution.py:75
  36.6 0.0 copy-start
  36.6 4.4 %combine_last.1 = bf16[8,192,256]{2,1,0:T(8,128)(2,1)S(1)} custom-call(s32[1,20]{1,0:T(1,128)} %refs_0_.4, s32[1,20]{1,0:T(1,128)} %refs_1_.7, s32[1,2048]{1,0:T(1,128)} %refs_2_.5, bf16[20,256,256]{2,1,0:T(8,128)(2,1)} %bitcast.3, bf16[8,64,256]{2,1,0:T(8,128)(2,1)S(1)} %get-tuple-element.19.refs_4_, bf16[8,64,128]{2,1,0:T(8,128)(2,1)S(1)} %all_to_all.16.refs_5_, ...), custom_call_target="tpu_custom_call" | custom-call | tf_op jit(solution)/shard_map/combine_last/pallas_call | solution.py:310
  41.0 21.4 %all_to_all.17.refs_1_ = bf16[8,192,256]{2,1,0:T(8,128)(2,1)S(1)} all-to-all(bf16[8,192,256]{2,1,0:T(8,128)(2,1)S(1)} %combine_last.1), channel_id=1, replica_groups=mesh['dom'=8,'rep'=4] {'dom'}, dimensions={0} | all-to-all | bytes 1572864 | tf_op jit(solution)/shard_map/all_to_all | solution.py:75
  62.4 0.0 copy-done
  62.4 3.7 %place.1 = bf16[3,64,2048]{2,1,0:T(8,128)(2,1)} custom-call(s32[1,2048]{1,0:T(1,128)S(1)} %copy-done, bf16[8,192,256]{2,1,0:T(8,128)(2,1)S(1)} %all_to_all.17.refs_1_), custom_call_target="tpu_custom_call" | custom-call | tf_op jit(solution)/shard_map/place/pallas_call | solution.py:320
Async XLA Ops:
  2.4 3.2 %collective-permute-start = (bf16[64,512]{1,0:T(8,128)(2,1)S(1)}, bf16[64,512]{1,0:T(8,128)(2,1)S(1)}, u32[]{:S(2)}, u32[]{:S(2)}) collective-permute-start(bf16[64,512]{1,0:T(8,128)(2,1)S(1)} %get-tuple-element.14), channel_id=1, source_target_pairs={{0,1},{1,0},{2,3},{3,2},{4,5},{5,4},{6,7},{7,6},{8,9},{9,8},{10,11... | collective-permute-start | bytes 196616 | tf_op jit(solution)/shard_map/ppermute | solution.py:277
  3.0 5.2 %collective-permute-start.1 = (bf16[64,512]{1,0:T(8,128)(2,1)S(1)}, bf16[64,512]{1,0:T(8,128)(2,1)S(1)}, u32[]{:S(2)}, u32[]{:S(2)}) collective-permute-start(bf16[64,512]{1,0:T(8,128)(2,1)S(1)} %get-tuple-element.15), channel_id=1, source_target_pairs={{0,2},{1,3},{2,0},{3,1},{4,6},{5,7},{6,4},{7,5},{8,10},{9,11},{10,... | collective-permute-start | bytes 196616 | tf_op jit(solution)/shard_map/ppermute | solution.py:277
  5.5 4.1 %collective-permute-start.2 = (bf16[64,512]{1,0:T(8,128)(2,1)S(1)}, bf16[64,512]{1,0:T(8,128)(2,1)S(1)}, u32[]{:S(2)}, u32[]{:S(2)}) collective-permute-start(bf16[64,512]{1,0:T(8,128)(2,1)S(1)} %get-tuple-element.16), channel_id=1, source_target_pairs={{0,3},{1,2},{2,1},{3,0},{4,7},{5,6},{6,5},{7,4},{8,11},{9,10},{10,... | collective-permute-start | bytes 196616 | tf_op jit(solution)/shard_map/ppermute | solution.py:277
  36.6 25.8 %copy-start = (s32[1,2048]{1,0:T(1,128)S(1)}, s32[1,2048]{1,0:T(1,128)}, u32[]{:S(2)}) copy-start(s32[1,2048]{1,0:T(1,128)} %refs_0_.5) | copy-start | bytes 24580

commit v4 on v3

--- a/solution.py
+++ b/solution.py
@@ -17,6 +17,10 @@
 
 def params():
     return pltpu.CompilerParams(vmem_limit_bytes=40 * 1024 * 1024)
+
+
+def cost(flops, size):
+    return pl.CostEstimate(flops=flops, bytes_accessed=size, transcendentals=0)
 
 
 def in_hbm(array):
@@ -203,6 +207,47 @@
     store_slots(send, pick(stack, blocks, index[...], side, group), group)
 
 
+def early_kernel(me_ref, index_in, hop0, hop1, *rest):
+    peers = len(rest) - 3
+    outs, (full, index, sem) = rest[:peers], rest[peers:]
+    fetch = pltpu.make_async_copy(index_in, index, sem)
+    fetch.start()
+    blocks, _, side = hop0.shape
+    stack = []
+    for block in range(blocks):
+        stack += [hop0[block], hop1[block]]
+    stack = jnp.concatenate(stack, 0)
+    fetch.wait()
+    slot = full.shape[2]
+    for peer, part in enumerate(pick(stack, blocks, index[...], side, slot)):
+        full[peer] = part
+    me = me_ref[0, 0]
+    for step in range(peers):
+        outs[step][...] = full[partner(me, step, peers)]
+
+
+def late_kernel(
+    peers, near, me_ref, dst_in, src_in, index_in, tiles_in, hop, arrived_ref, *rest
+):
+    early, outs, full = rest[:near], rest[near : near + peers], rest[near + peers]
+    scratch = rest[near + peers + 1 :]
+    results = combine(
+        dst_in, src_in, index_in, tiles_in, hop, arrived_ref, scratch, lambda *_: None
+    )
+    blocks, channels, side = hop.shape
+    index = scratch[2]
+    stack = jnp.concatenate(results, 0)
+    for peer, part in enumerate(pick(stack, blocks, index[...], side, full.shape[2])):
+        full[peer] = part
+    me = me_ref[0, 0]
+    for step in range(near):
+        rows = early[step].shape[0]
+        outs[step][:rows] = early[step][...]
+        outs[step][rows:] = full[partner(me, step, peers)]
+    for step in range(near, peers):
+        outs[step][...] = full[partner(me, step, peers)]
+
+
 def combine_last_kernel(
     group, dst_in, src_in, index_in, tiles_in, hop, arrived_ref, hop0, send, *scratch
 ):
@@ -216,6 +261,44 @@
         stack += [hop0[block], hop[block], results[block]]
     stack = jnp.concatenate(stack, 0)
     store_slots(send, pick(stack, blocks, index[...], side, group), group)
+
+
+def place_steps_kernel(peers, near, side, me_ref, index_ref, *rest):
+    whole, early, late = rest[:near], rest[near:peers], rest[peers : 2 * peers - near]
+    out_ref, out, sems = rest[2 * peers - near :]
+    hops, channels, nodes = out.shape
+    blocks = nodes // side
+    slot = nodes // peers
+    me = me_ref[0, 0]
+    parts, indexes = [], []
+    for step in range(peers):
+        start = pl.multiple_of(source(me, step, peers) * slot, slot)
+        indexes.append(index_ref[:, pl.ds(start, slot)])
+        if step < near:
+            parts.append(whole[step][...])
+        else:
+            parts.append(
+                jnp.concatenate([early[step - near][...], late[step - near][...]], 0)
+            )
+    block, inner = split(jnp.concatenate(indexes, 1), side, blocks)
+    table = one_hot(inner, side)
+    stacked = jnp.concatenate(parts, 1)
+    copies = []
+    for other in range(blocks):
+        mask = jnp.where(block == other, 1.0, 0.0).astype(BF16)
+        placed = dot(stacked * mask, table, NT).astype(BF16)
+        columns = slice(other * side, (other + 1) * side)
+        for hop in range(hops):
+            out[hop, :, columns] = placed[hop * channels : (hop + 1) * channels]
+        columns = pl.ds(other * side, side)
+        copies.append(
+            pltpu.make_async_copy(
+                out.at[:, :, columns], out_ref.at[:, :, columns], sems.at[other]
+            )
+        )
+        copies[-1].start()
+    for copy in copies:
+        copy.wait()
 
 
 def place_kernel(side, index_ref, arrived_ref, out_ref):
@@ -307,6 +390,56 @@
         name="combine_pick",
     )(in_hbm(tile_dst), in_hbm(tile_src), in_hbm(halo_index), in_hbm(tiles), hop0, halo0)
     halo1 = exchange(send, peers)
+    slot = nodes // peers
+    if slot % 128 == 0 and peers & (peers - 1) == 0:
+        near = max(peers // 2, 1)
+        rank = lax.axis_index("dom").astype(jnp.int32).reshape(1, 1)
+        two, one = out((2 * channels, slot)), out((channels, slot))
+        early = pl.pallas_call(
+            early_kernel,
+            out_shape=(two,) * peers,
+            in_specs=[SMEM, HBM, VMEM, VMEM],
+            out_specs=(VMEM,) * peers,
+            scratch_shapes=[
+                vmem((peers, 2 * channels, slot), BF16),
+                vmem(send_order.shape, jnp.int32),
+                dma,
+            ],
+            compiler_params=params(),
+            cost_estimate=cost(4 * channels * nodes * nodes, 8 * channels * nodes),
+            name="early",
+        )(rank, in_hbm(send_order), hop0, hop1)
+        sent = [
+            lax.ppermute(early[step], "dom", pairs(step, peers)) for step in range(near, peers)
+        ]
+        late = pl.pallas_call(
+            lambda *refs: late_kernel(peers, near, *refs),
+            out_shape=(out((3 * channels, slot)),) * near + (one,) * (peers - near),
+            in_specs=[SMEM] + [HBM] * 4 + [VMEM] * (2 + near),
+            out_specs=(VMEM,) * peers,
+            scratch_shapes=[vmem((peers, channels, slot), BF16)] + work(send_order),
+            compiler_params=params(),
+            name="late",
+        )(
+            rank, in_hbm(tile_dst), in_hbm(tile_src), in_hbm(send_order), in_hbm(tiles),
+            hop1, halo1, *early[:near],
+        )
+        order = list(range(near, peers)) + list(range(1, near))
+        moved = {0: late[0]}
+        for step in order:
+            moved[step] = lax.ppermute(late[step], "dom", pairs(step, peers))
+        return pl.pallas_call(
+            lambda *refs: place_steps_kernel(peers, near, side, *refs),
+            out_shape=out((3, channels, nodes)),
+            in_specs=[SMEM, VMEM] + [VMEM] * (2 * peers - near),
+            out_specs=HBM,
+            scratch_shapes=[vmem((3, channels, nodes), BF16), dma((blocks,))],
+            compiler_params=params(),
+            name="place",
+        )(
+            rank, arrival_place, *[moved[step] for step in range(near)], *sent,
+            *[moved[step] for step in range(near, peers)],
+        )
     send = pl.pallas_call(
         lambda *refs: combine_last_kernel(group, *refs),
         out_shape=out(last_shape),

time: 66.5 us -> 66.9 us (level)
  blocking collectives: 44.2 us -> 13 us
  starting transfers between devices: 3.15 us -> 27.2 us
  waiting for transfers between devices: 4.02 us -> 9.85 us
  Pallas kernels: 14.7 us -> 16.4 us
    all_to_all x3 -> x1, blocking collectives: 44.2 us -> 13 us  [exchange(): arrived = lax.all_to_all(send, 'dom', 0, 0, tiled=True)]
    ppermute x0 -> x11, starting transfers between devices: none -> 20.7 us  [the longest x7 12.9 us: on_device(): moved[step] = lax.ppermute(late[step], 'dom', pairs(step, peers))]
    ppermute x0 -> x11, waiting for transfers between devices: none -> 5.82 us  [the longest x7 5.74 us: on_device(): moved[step] = lax.ppermute(late[step], 'dom', pairs(step, peers))]
    all_to_all x0 -> x1, starting transfers between devices: none -> 3.38 us  [exchange(): arrived = lax.all_to_all(send, 'dom', 0, 0, tiled=True)]
    pallas_call x2 -> x3, Pallas kernels: 8.13 us -> 9.11 us  [the longest x1 3.66 us: on_device(): pl.pallas_call(lambda *refs: place_steps_kernel(peers, near, side, *refs)...]
  transfers between devices with their start and end apart: 3 -> 15, of which waited for: 2 -> 6; matrix products, arithmetic and copies ran while one was open for 0% -> 0% of each run, Pallas kernels for 0% -> 8%
where the time goes in v4:
time: 66.9 us; the launch traced here: 66.5 us
  starting transfers between devices  27.2 us (41%)
  Pallas kernels  16.4 us (25%)
  blocking collectives  13 us (19%)
  waiting for transfers between devices  9.85 us (15%)
    all_to_all x1, blocking collectives, exchange(): arrived = lax.all_to_all(send, 'dom', 0, 0, tiled=True)  13 us
    ppermute x7, starting transfers between devices, on_device(): moved[step] = lax.ppermute(late[step], 'dom', pairs(step, peers))  12.9 us
    ppermute x4, starting transfers between devices, on_device(): lax.ppermute(early[step], 'dom', pairs(step, peers))  7.71 us
    ppermute x7, waiting for transfers between devices, on_device(): moved[step] = lax.ppermute(late[step], 'dom', pairs(step, peers))  5.74 us
    ppermute x3, waiting for transfers between devices, on_device(): arrived.append(lax.ppermute(own[step], 'rep', pairs(step, reps)))  4.02 us
    pallas_call x1, Pallas kernels, on_device(): pl.pallas_call(lambda *refs: combine_pick_kernel(group, *refs), out_shape...  3.7 us
    pallas_call x1, Pallas kernels, on_device(): pl.pallas_call(lambda *refs: place_steps_kernel(peers, near, side, *refs)...  3.66 us
    pallas_call x1, Pallas kernels, on_device(): pl.pallas_call(lambda *refs: late_kernel(peers, near, *refs), out_shape=(...  3.41 us
  transfers between devices with their start and end apart: 15, of which 6 were waited for; matrix products, arithmetic and copies ran while one was open for 0% of the time, Pallas kernels for 8%

profile of v4, /device:TPU:0, one launch (start us, length us, event | category | flops | bytes accessed | tf_op | source)
XLA Modules:
  0.0 66.5 jit_solution(394873297416617799)
XLA Ops:
  0.0 2.4 %sketch.1 = (bf16[64,512]{1,0:T(8,128)(2,1)S(1)}, bf16[64,512]{1,0:T(8,128)(2,1)S(1)}, bf16[64,512]{1,0:T(8,128)(2,1)S(1)}, bf16[64,512]{1,0:T(8,128)(2,1)S(1)}) custom-call(s32[1,1]{1,0:T(1,128)} %bitcast.2.refs_0_, bf16[512,768]{1,0:T(8,128)(2,1)} %refs_1_.5, bf16[768,256]{1,0:T(8,128)(2,1)} %refs_2_.3), custom_call_target="tpu_custom_call" | custom-call | tf_op jit(solution)/shard_map/sketch/pallas_call | solution.py:344
  2.4 0.6 collective-permute-start
  3.0 2.6 %collective-permute-start.1 = (bf16[64,512]{1,0:T(8,128)(2,1)S(1)}, bf16[64,512]{1,0:T(8,128)(2,1)S(1)}, u32[]{:S(2)}, u32[]{:S(2)}) collective-permute-start(bf16[64,512]{1,0:T(8,128)(2,1)S(1)} %get-tuple-element.31), channel_id=1, source_target_pairs={{0,2},{1,3},{2,0},{3,1},{4,6},{5,7},{6,4},{7,5},{8,10},{9,11},{10,... | collective-permute-start | bytes 196616 | tf_op jit(solution)/shard_map/ppermute | solution.py:360
  5.5 0.0 collective-permute-start.2
  5.6 0.0 collective-permute-done.refs_3_
  5.6 2.6 %collective-permute-done.1.refs_4_ = bf16[64,512]{1,0:T(8,128)(2,1)S(1)} collective-permute-done((bf16[64,512]{1,0:T(8,128)(2,1)S(1)}, bf16[64,512]{1,0:T(8,128)(2,1)S(1)}, u32[]{:S(2)}, u32[]{:S(2)}) %collective-permute-start.1) | collective-permute-done | bytes 65568 | tf_op jit(solution)/shard_map/ppermute | solution.py:360
  8.2 1.4 %collective-permute-done.2.refs_5_ = bf16[64,512]{1,0:T(8,128)(2,1)S(1)} collective-permute-done((bf16[64,512]{1,0:T(8,128)(2,1)S(1)}, bf16[64,512]{1,0:T(8,128)(2,1)S(1)}, u32[]{:S(2)}, u32[]{:S(2)}) %collective-permute-start.2) | collective-permute-done | bytes 65568 | tf_op jit(solution)/shard_map/ppermute | solution.py:360
  9.6 1.2 %pick.1 = (bf16[8,64,256]{2,1,0:T(8,128)(2,1)S(1)}, bf16[8,64,128]{2,1,0:T(8,128)(2,1)S(1)}) custom-call(s32[1,1]{1,0:T(1,128)} %bitcast.2.refs_0_, s32[1,1024]{1,0:T(1,128)} %refs_2_.4, bf16[64,512]{1,0:T(8,128)(2,1)S(1)} %get-tuple-element.29.refs_2_, bf16[64,512]{1,0:T(8,128)(2,1)S(1)} %collective-permute-done.refs_3_, ...), custom_call_target="tpu_custom_call" | custom-call | tf_op jit(solution)/shard_map/pick/pallas_call | solution.py:361
  10.7 13.0 %all_to_all.10.refs_5_ = bf16[8,64,128]{2,1,0:T(8,128)(2,1)S(1)} all-to-all(bf16[8,64,128]{2,1,0:T(8,128)(2,1)S(1)} %get-tuple-element.34), channel_id=1, replica_groups=mesh['dom'=8,'rep'=4] {'dom'}, dimensions={0} | all-to-all | bytes 262144 | tf_op jit(solution)/shard_map/all_to_all | solution.py:79
  23.7 3.7 %combine_pick.1 = (bf16[8,64,256]{2,1,0:T(8,128)(2,1)S(1)}, bf16[8,64,128]{2,1,0:T(8,128)(2,1)}) custom-call(s32[1,20]{1,0:T(1,128)} %refs_1_.8, s32[1,20]{1,0:T(1,128)} %refs_2_.5, s32[1,1024]{1,0:T(1,128)} %refs_2_.4, bf16[20,256,256]{2,1,0:T(8,128)(2,1)} %bitcast.3, bf16[8,64,256]{2,1,0:T(8,128)(2,1)S(1)} %get-tuple-element.33.refs_4_.hop0, ...), custom_call_target="tpu_custom_call" | custom-call | tf_op jit(solution)/shard_map/combine_pick/pallas_call | solution.py:383
  27.4 3.4 %all-to-all-start.1 = ((bf16[8,64,128]{2,1,0:T(8,128)(2,1)}), bf16[8,64,128]{2,1,0:T(8,128)(2,1)S(1)}, u32[]{:S(2)}, u32[]{:S(2)}) async-start(bf16[8,64,128]{2,1,0:T(8,128)(2,1)} %get-tuple-element.36), calls=%async_computation.1 | async-start | bytes 262144 | tf_op jit(solution)/shard_map/all_to_all | solution.py:79
  30.8 2.0 %early.1 = (bf16[128,256]{1,0:T(8,128)(2,1)S(1)}, bf16[128,256]{1,0:T(8,128)(2,1)S(1)}, bf16[128,256]{1,0:T(8,128)(2,1)S(1)}, bf16[128,256]{1,0:T(8,128)(2,1)S(1...) custom-call(s32[1,1]{1,0:T(1,128)} %bitcast.me_ref.refs_0_, ...), custom_call_target="tpu_custom_call" | custom-call | flops 1073741824 | bytes 1048576 | tf_op jit(solution)/shard_map/early/pallas_call | solution.py:398
  32.9 0.0 copy-start
  32.9 2.9 %collective-permute-start.6 = (bf16[128,256]{1,0:T(8,128)(2,1)S(1)}, bf16[128,256]{1,0:T(8,128)(2,1)S(1)}, u32[]{:S(2)}, u32[]{:S(2)}) collective-permute-start(bf16[128,256]{1,0:T(8,128)(2,1)S(1)} %get-tuple-element.45), channel_id=1, source_target_pairs={{0,16},{4,20},{8,24},{12,28},{16,0},{20,4},{24,8},{28,12},{1,17},{... | collective-permute-start | bytes 196616 | tf_op jit(solution)/shard_map/ppermute | solution.py:413
  35.8 1.4 %collective-permute-start.7 = (bf16[128,256]{1,0:T(8,128)(2,1)S(1)}, bf16[128,256]{1,0:T(8,128)(2,1)S(1)}, u32[]{:S(2)}, u32[]{:S(2)}) collective-permute-start(bf16[128,256]{1,0:T(8,128)(2,1)S(1)} %get-tuple-element.46), channel_id=1, source_target_pairs={{0,20},{4,16},{8,28},{12,24},{16,4},{20,0},{24,12},{28,8},{1,21},{... | collective-permute-start | bytes 196616 | tf_op jit(solution)/shard_map/ppermute | solution.py:413
  37.2 3.3 %collective-permute-start.8 = (bf16[128,256]{1,0:T(8,128)(2,1)S(1)}, bf16[128,256]{1,0:T(8,128)(2,1)S(1)}, u32[]{:S(2)}, u32[]{:S(2)}) collective-permute-start(bf16[128,256]{1,0:T(8,128)(2,1)S(1)} %get-tuple-element.47), channel_id=1, source_target_pairs={{0,24},{4,28},{8,16},{12,20},{16,8},{20,12},{24,0},{28,4},{1,25},{... | collective-permute-start | bytes 196616 | tf_op jit(solution)/shard_map/ppermute | solution.py:413
  40.5 0.1 collective-permute-start.9
  40.6 0.0 all-to-all-done.1.refs_6_
  40.6 3.4 %late.1 = (bf16[192,256]{1,0:T(8,128)(2,1)S(1)}, bf16[192,256]{1,0:T(8,128)(2,1)S(1)}, bf16[192,256]{1,0:T(8,128)(2,1)S(1)}, bf16[192,256]{1,0:T(8,128)(2,1)S(1)...) custom-call(s32[1,1]{1,0:T(1,128)} %bitcast.me_ref.refs_0_, ...), custom_call_target="tpu_custom_call" | custom-call | tf_op jit(solution)/shard_map/late/pallas_call | solution.py:415
  44.0 2.0 %collective-permute-start.3 = (bf16[192,256]{1,0:T(8,128)(2,1)S(1)}, bf16[192,256]{1,0:T(8,128)(2,1)S(1)}, u32[]{:S(2)}, u32[]{:S(2)}) collective-permute-start(bf16[192,256]{1,0:T(8,128)(2,1)S(1)} %get-tuple-element.42), channel_id=1, source_target_pairs={{0,4},{4,0},{8,12},{12,8},{16,20},{20,16},{24,28},{28,24},{1,5},{5... | collective-permute-start | bytes 294920 | tf_op jit(solution)/shard_map/ppermute | solution.py:430
  46.0 0.0 collective-permute-done.6.refs_6_
  46.0 0.0 collective-permute-start.4
  46.0 0.1 collective-permute-done.7.refs_7_
  46.1 1.5 %collective-permute-start.5 = (bf16[192,256]{1,0:T(8,128)(2,1)S(1)}, bf16[192,256]{1,0:T(8,128)(2,1)S(1)}, u32[]{:S(2)}, u32[]{:S(2)}) collective-permute-start(bf16[192,256]{1,0:T(8,128)(2,1)S(1)} %get-tuple-element.44), channel_id=1, source_target_pairs={{0,12},{4,8},{8,4},{12,0},{16,28},{20,24},{24,20},{28,16},{1,13},{... | collective-permute-start | bytes 294920 | tf_op jit(solution)/shard_map/ppermute | solution.py:430
  47.6 0.0 collective-permute-done.8.refs_8_
  47.6 2.4 %collective-permute-start.10 = (bf16[64,256]{1,0:T(8,128)(2,1)S(1)}, bf16[64,256]{1,0:T(8,128)(2,1)S(1)}, u32[]{:S(2)}, u32[]{:S(2)}) collective-permute-start(bf16[64,256]{1,0:T(8,128)(2,1)S(1)} %get-tuple-element.49), channel_id=1, source_target_pairs={{0,16},{4,20},{8,24},{12,28},{16,0},{20,4},{24,8},{28,12},{1,17},{... | collective-permute-start | bytes 98312 | tf_op jit(solution)/shard_map/ppermute | solution.py:430
  50.0 0.0 collective-permute-done.9.refs_9_
  50.0 1.9 %collective-permute-start.11 = (bf16[64,256]{1,0:T(8,128)(2,1)S(1)}, bf16[64,256]{1,0:T(8,128)(2,1)S(1)}, u32[]{:S(2)}, u32[]{:S(2)}) collective-permute-start(bf16[64,256]{1,0:T(8,128)(2,1)S(1)} %get-tuple-element.50), channel_id=1, source_target_pairs={{0,20},{4,16},{8,28},{12,24},{16,4},{20,0},{24,12},{28,8},{1,21},{... | collective-permute-start | bytes 98312 | tf_op jit(solution)/shard_map/ppermute | solution.py:430
  51.9 1.0 %collective-permute-done.10.refs_10_ = bf16[64,256]{1,0:T(8,128)(2,1)S(1)} collective-permute-done((bf16[64,256]{1,0:T(8,128)(2,1)S(1)}, bf16[64,256]{1,0:T(8,128)(2,1)S(1)}, u32[]{:S(2)}, u32[]{:S(2)}) %collective-permute-start.10) | collective-permute-done | bytes 32800 | tf_op jit(solution)/shard_map/ppermute | solution.py:430
  52.9 3.3 %collective-permute-start.12 = (bf16[64,256]{1,0:T(8,128)(2,1)S(1)}, bf16[64,256]{1,0:T(8,128)(2,1)S(1)}, u32[]{:S(2)}, u32[]{:S(2)}) collective-permute-start(bf16[64,256]{1,0:T(8,128)(2,1)S(1)} %get-tuple-element.51), channel_id=1, source_target_pairs={{0,24},{4,28},{8,16},{12,20},{16,8},{20,12},{24,0},{28,4},{1,25},{... | collective-permute-start | bytes 98312 | tf_op jit(solution)/shard_map/ppermute | solution.py:430
  56.2 0.0 collective-permute-done.11.refs_11_
  56.2 1.9 %collective-permute-start.13 = (bf16[64,256]{1,0:T(8,128)(2,1)S(1)}, bf16[64,256]{1,0:T(8,128)(2,1)S(1)}, u32[]{:S(2)}, u32[]{:S(2)}) collective-permute-start(bf16[64,256]{1,0:T(8,128)(2,1)S(1)} %get-tuple-element.52), channel_id=1, source_target_pairs={{0,28},{4,24},{8,20},{12,16},{16,12},{20,8},{24,4},{28,0},{1,29},{... | collective-permute-start | bytes 98312 | tf_op jit(solution)/shard_map/ppermute | solution.py:430
  58.0 0.6 collective-permute-done.12.refs_12_
  58.7 4.1 %collective-permute-done.13.refs_13_ = bf16[64,256]{1,0:T(8,128)(2,1)S(1)} collective-permute-done((bf16[64,256]{1,0:T(8,128)(2,1)S(1)}, bf16[64,256]{1,0:T(8,128)(2,1)S(1)}, u32[]{:S(2)}, u32[]{:S(2)}) %collective-permute-start.13) | collective-permute-done | bytes 32800 | tf_op jit(solution)/shard_map/ppermute | solution.py:430
  62.8 0.0 collective-permute-done.3.refs_3_
  62.8 0.0 collective-permute-done.4.refs_4_
  62.8 0.0 collective-permute-done.5.refs_5_
  62.8 0.0 copy-done
  62.8 3.7 %place.1 = bf16[3,64,2048]{2,1,0:T(8,128)(2,1)} custom-call(s32[1,1]{1,0:T(1,128)} %bitcast.me_ref.refs_0_, s32[1,2048]{1,0:T(1,128)S(1)} %copy-done, bf16[192,256]{1,0:T(8,128)(2,1)S(1)} %get-tuple-element.41.refs_2_, bf16[192,256]{1,0:T(8,128)(2,1)S(1)} %collective-permute-done.3.refs_3_, bf16[192,256]{1,0:T(8,128)(2,1)S(1)} %collective-permute-done.4.refs_4_, ...), custom_call_target="tpu_custom_call" | custom-call | tf_op jit(solution)/shard_map/place/pallas_call | solution.py:431
Async XLA Ops:
  2.4 3.2 %collective-permute-start = (bf16[64,512]{1,0:T(8,128)(2,1)S(1)}, bf16[64,512]{1,0:T(8,128)(2,1)S(1)}, u32[]{:S(2)}, u32[]{:S(2)}) collective-permute-start(bf16[64,512]{1,0:T(8,128)(2,1)S(1)} %get-tuple-element.30), channel_id=1, source_target_pairs={{0,1},{1,0},{2,3},{3,2},{4,5},{5,4},{6,7},{7,6},{8,9},{9,8},{10,11... | collective-permute-start | bytes 196616 | tf_op jit(solution)/shard_map/ppermute | solution.py:360
  3.0 5.2 %collective-permute-start.1 = (bf16[64,512]{1,0:T(8,128)(2,1)S(1)}, bf16[64,512]{1,0:T(8,128)(2,1)S(1)}, u32[]{:S(2)}, u32[]{:S(2)}) collective-permute-start(bf16[64,512]{1,0:T(8,128)(2,1)S(1)} %get-tuple-element.31), channel_id=1, source_target_pairs={{0,2},{1,3},{2,0},{3,1},{4,6},{5,7},{6,4},{7,5},{8,10},{9,11},{10,... | collective-permute-start | bytes 196616 | tf_op jit(solution)/shard_map/ppermute | solution.py:360
  5.5 4.1 %collective-permute-start.2 = (bf16[64,512]{1,0:T(8,128)(2,1)S(1)}, bf16[64,512]{1,0:T(8,128)(2,1)S(1)}, u32[]{:S(2)}, u32[]{:S(2)}) collective-permute-start(bf16[64,512]{1,0:T(8,128)(2,1)S(1)} %get-tuple-element.32), channel_id=1, source_target_pairs={{0,3},{1,2},{2,1},{3,0},{4,7},{5,6},{6,5},{7,4},{8,11},{9,10},{10,... | collective-permute-start | bytes 196616 | tf_op jit(solution)/shard_map/ppermute | solution.py:360
  27.4 13.2 %all-to-all-start.1 = ((bf16[8,64,128]{2,1,0:T(8,128)(2,1)}), bf16[8,64,128]{2,1,0:T(8,128)(2,1)S(1)}, u32[]{:S(2)}, u32[]{:S(2)}) async-start(bf16[8,64,128]{2,1,0:T(8,128)(2,1)} %get-tuple-element.36), calls=%async_computation.1 | async-start | bytes 262144 | tf_op jit(solution)/shard_map/all_to_all | solution.py:79
  32.9 29.9 %copy-start = (s32[1,2048]{1,0:T(1,128)S(1)}, s32[1,2048]{1,0:T(1,128)}, u32[]{:S(2)}) copy-start(s32[1,2048]{1,0:T(1,128)} %refs_1_.9) | copy-start | bytes 24580
  32.9 13.1 %collective-permute-start.6 = (bf16[128,256]{1,0:T(8,128)(2,1)S(1)}, bf16[128,256]{1,0:T(8,128)(2,1)S(1)}, u32[]{:S(2)}, u32[]{:S(2)}) collective-permute-start(bf16[128,256]{1,0:T(8,128)(2,1)S(1)} %get-tuple-element.45), channel_id=1, source_target_pairs={{0,16},{4,20},{8,24},{12,28},{16,0},{20,4},{24,8},{28,12},{1,17},{... | collective-permute-start | bytes 196616 | tf_op jit(solution)/shard_map/ppermute | solution.py:413
  35.8 10.3 %collective-permute-start.7 = (bf16[128,256]{1,0:T(8,128)(2,1)S(1)}, bf16[128,256]{1,0:T(8,128)(2,1)S(1)}, u32[]{:S(2)}, u32[]{:S(2)}) collective-permute-start(bf16[128,256]{1,0:T(8,128)(2,1)S(1)} %get-tuple-element.46), channel_id=1, source_target_pairs={{0,20},{4,16},{8,28},{12,24},{16,4},{20,0},{24,12},{28,8},{1,21},{... | collective-permute-start | bytes 196616 | tf_op jit(solution)/shard_map/ppermute | solution.py:413
  37.2 10.4 %collective-permute-start.8 = (bf16[128,256]{1,0:T(8,128)(2,1)S(1)}, bf16[128,256]{1,0:T(8,128)(2,1)S(1)}, u32[]{:S(2)}, u32[]{:S(2)}) collective-permute-start(bf16[128,256]{1,0:T(8,128)(2,1)S(1)} %get-tuple-element.47), channel_id=1, source_target_pairs={{0,24},{4,28},{8,16},{12,20},{16,8},{20,12},{24,0},{28,4},{1,25},{... | collective-permute-start | bytes 196616 | tf_op jit(solution)/shard_map/ppermute | solution.py:413
  40.5 9.4 %collective-permute-start.9 = (bf16[128,256]{1,0:T(8,128)(2,1)S(1)}, bf16[128,256]{1,0:T(8,128)(2,1)S(1)}, u32[]{:S(2)}, u32[]{:S(2)}) collective-permute-start(bf16[128,256]{1,0:T(8,128)(2,1)S(1)} %get-tuple-element.48), channel_id=1, source_target_pairs={{0,28},{4,24},{8,20},{12,16},{16,12},{20,8},{24,4},{28,0},{1,29},{... | collective-permute-start | bytes 196616 | tf_op jit(solution)/shard_map/ppermute | solution.py:413
  44.0 18.8 %collective-permute-start.3 = (bf16[192,256]{1,0:T(8,128)(2,1)S(1)}, bf16[192,256]{1,0:T(8,128)(2,1)S(1)}, u32[]{:S(2)}, u32[]{:S(2)}) collective-permute-start(bf16[192,256]{1,0:T(8,128)(2,1)S(1)} %get-tuple-element.42), channel_id=1, source_target_pairs={{0,4},{4,0},{8,12},{12,8},{16,20},{20,16},{24,28},{28,24},{1,5},{5... | collective-permute-start | bytes 294920 | tf_op jit(solution)/shard_map/ppermute | solution.py:430
  46.0 16.8 %collective-permute-start.4 = (bf16[192,256]{1,0:T(8,128)(2,1)S(1)}, bf16[192,256]{1,0:T(8,128)(2,1)S(1)}, u32[]{:S(2)}, u32[]{:S(2)}) collective-permute-start(bf16[192,256]{1,0:T(8,128)(2,1)S(1)} %get-tuple-element.43), channel_id=1, source_target_pairs={{0,8},{4,12},{8,0},{12,4},{16,24},{20,28},{24,16},{28,20},{1,9},{5... | collective-permute-start | bytes 294920 | tf_op jit(solution)/shard_map/ppermute | solution.py:430
  46.1 16.7 %collective-permute-start.5 = (bf16[192,256]{1,0:T(8,128)(2,1)S(1)}, bf16[192,256]{1,0:T(8,128)(2,1)S(1)}, u32[]{:S(2)}, u32[]{:S(2)}) collective-permute-start(bf16[192,256]{1,0:T(8,128)(2,1)S(1)} %get-tuple-element.44), channel_id=1, source_target_pairs={{0,12},{4,8},{8,4},{12,0},{16,28},{20,24},{24,20},{28,16},{1,13},{... | collective-permute-start | bytes 294920 | tf_op jit(solution)/shard_map/ppermute | solution.py:430
  47.6 5.3 %collective-permute-start.10 = (bf16[64,256]{1,0:T(8,128)(2,1)S(1)}, bf16[64,256]{1,0:T(8,128)(2,1)S(1)}, u32[]{:S(2)}, u32[]{:S(2)}) collective-permute-start(bf16[64,256]{1,0:T(8,128)(2,1)S(1)} %get-tuple-element.49), channel_id=1, source_target_pairs={{0,16},{4,20},{8,24},{12,28},{16,0},{20,4},{24,8},{28,12},{1,17},{... | collective-permute-start | bytes 98312 | tf_op jit(solution)/shard_map/ppermute | solution.py:430
  50.0 6.2 %collective-permute-start.11 = (bf16[64,256]{1,0:T(8,128)(2,1)S(1)}, bf16[64,256]{1,0:T(8,128)(2,1)S(1)}, u32[]{:S(2)}, u32[]{:S(2)}) collective-permute-start(bf16[64,256]{1,0:T(8,128)(2,1)S(1)} %get-tuple-element.50), channel_id=1, source_target_pairs={{0,20},{4,16},{8,28},{12,24},{16,4},{20,0},{24,12},{28,8},{1,21},{... | collective-permute-start | bytes 98312 | tf_op jit(solution)/shard_map/ppermute | solution.py:430
  52.9 5.8 %collective-permute-start.12 = (bf16[64,256]{1,0:T(8,128)(2,1)S(1)}, bf16[64,256]{1,0:T(8,128)(2,1)S(1)}, u32[]{:S(2)}, u32[]{:S(2)}) collective-permute-start(bf16[64,256]{1,0:T(8,128)(2,1)S(1)} %get-tuple-element.51), channel_id=1, source_target_pairs={{0,24},{4,28},{8,16},{12,20},{16,8},{20,12},{24,0},{28,4},{1,25},{... | collective-permute-start | bytes 98312 | tf_op jit(solution)/shard_map/ppermute | solution.py:430
  56.2 6.6 %collective-permute-start.13 = (bf16[64,256]{1,0:T(8,128)(2,1)S(1)}, bf16[64,256]{1,0:T(8,128)(2,1)S(1)}, u32[]{:S(2)}, u32[]{:S(2)}) collective-permute-start(bf16[64,256]{1,0:T(8,128)(2,1)S(1)} %get-tuple-element.52), channel_id=1, source_target_pairs={{0,28},{4,24},{8,20},{12,16},{16,12},{20,8},{24,4},{28,0},{1,29},{... | collective-permute-start | bytes 98312 | tf_op jit(solution)/shard_map/ppermute | solution.py:430

commit v5 on v3

--- a/solution.py
+++ b/solution.py
@@ -4,6 +4,7 @@
 from jax.experimental import pallas as pl
 from jax.experimental.pallas import tpu as pltpu
 from jax.sharding import PartitionSpec as P
+
 
 BF16 = jnp.bfloat16
 F32 = jnp.float32
@@ -17,6 +18,10 @@
 
 def params():
     return pltpu.CompilerParams(vmem_limit_bytes=40 * 1024 * 1024)
+
+
+def cost(flops, size):
+    return pl.CostEstimate(flops=flops, bytes_accessed=size, transcendentals=0)
 
 
 def in_hbm(array):
@@ -203,6 +208,42 @@
     store_slots(send, pick(stack, blocks, index[...], side, group), group)
 
 
+def early_kernel(me_ref, index_in, hop, near, far, full, index, sem):
+    fetch = pltpu.make_async_copy(index_in, index, sem)
+    fetch.start()
+    blocks, _, side = hop.shape
+    peers, _, slot = full.shape
+    stack = jnp.concatenate([hop[block] for block in range(blocks)], 0)
+    fetch.wait()
+    for peer, part in enumerate(pick(stack, blocks, index[...], side, slot)):
+        full[peer] = part
+    me = me_ref[0, 0]
+    half = peers // 2
+    for step in range(half):
+        near[step] = full[me ^ step]
+        far[step] = full[me ^ half ^ step]
+
+
+def relay_kernel(*refs):
+    half = refs[0].shape[0]
+    ins, outs = refs[: len(refs) - half], refs[len(refs) - half :]
+    channels = ins[0].shape[1]
+    for step in range(half):
+        for place, blocks in enumerate(ins):
+            outs[step][place * channels : (place + 1) * channels] = blocks[step]
+
+
+def combine_alone_kernel(
+    group, dst_in, src_in, index_in, tiles_in, hop, arrived_ref, send, *scratch
+):
+    results = combine(
+        dst_in, src_in, index_in, tiles_in, hop, arrived_ref, scratch, lambda *_: None
+    )
+    blocks, _, side = hop.shape
+    stack = jnp.concatenate(results, 0)
+    store_slots(send, pick(stack, blocks, scratch[2][...], side, group), group)
+
+
 def combine_last_kernel(
     group, dst_in, src_in, index_in, tiles_in, hop, arrived_ref, hop0, send, *scratch
 ):
@@ -218,11 +259,55 @@
     store_slots(send, pick(stack, blocks, index[...], side, group), group)
 
 
+def place_steps_kernel(peers, side, me_ref, index_ref, *rest):
+    half = peers // 2
+    moved, last, (out_ref, out, sems) = rest[:half], rest[half], rest[half + 1 :]
+    hops, channels, nodes = out.shape
+    blocks = nodes // side
+    slot = nodes // peers
+    me = me_ref[0, 0]
+    parts, indexes = [], []
+    for step in range(peers):
+        origin = me ^ step
+        start = pl.multiple_of(origin * slot, slot)
+        indexes.append(index_ref[:, pl.ds(start, slot)])
+        first = (step // half) * channels
+        from_step = moved[step % half]
+        parts.append(
+            jnp.concatenate(
+                [
+                    from_step[first + 2 * channels * hop : first + (2 * hop + 1) * channels]
+                    for hop in range(hops - 1)
+                ]
+                + [last[origin]],
+                0,
+            )
+        )
+    block, inner = split(jnp.concatenate(indexes, 1), side, blocks)
+    table = one_hot(inner, side)
+    stacked = jnp.concatenate(parts, 1)
+    copies = []
+    for other in range(blocks):
+        mask = jnp.where(block == other, 1.0, 0.0).astype(BF16)
+        placed = dot(stacked * mask, table, NT).astype(BF16)
+        columns = slice(other * side, (other + 1) * side)
+        for hop in range(hops):
+            out[hop, :, columns] = placed[hop * channels : (hop + 1) * channels]
+        columns = pl.ds(other * side, side)
+        copies.append(
+            pltpu.make_async_copy(
+                out.at[:, :, columns], out_ref.at[:, :, columns], sems.at[other]
+            )
+        )
+        copies[-1].start()
+    for copy in copies:
+        copy.wait()
+
+
 def place_kernel(side, index_ref, arrived_ref, out_ref):
     hops, channels, nodes = out_ref.shape
     blocks = nodes // side
     stacked = load_wide(arrived_ref)
-    rows = hops * channels
     block, inner = split(index_ref[...], side, blocks)
     table = one_hot(inner, side)
     for other in range(blocks):
@@ -257,6 +342,27 @@
 
     def out(shape):
         return jax.ShapeDtypeStruct(shape, BF16)
+
+    def early(hop):
+        shape = (peers // 2, channels, slot)
+        near, far = early_call(hop, shape)
+        return near, lax.ppermute(far, "dom", pairs(peers // 2, peers))
+
+    def early_call(hop, shape):
+        return pl.pallas_call(
+            early_kernel,
+            out_shape=(out(shape), out(shape)),
+            in_specs=[SMEM, HBM, VMEM],
+            out_specs=(VMEM, VMEM),
+            scratch_shapes=[
+                vmem((peers, channels, slot), BF16),
+                vmem(send_order.shape, jnp.int32),
+                dma,
+            ],
+            compiler_params=params(),
+            cost_estimate=cost(2 * channels * nodes * nodes, 8 * channels * nodes),
+            name="early",
+        )(rank, in_hbm(send_order), hop)
 
     own = pl.pallas_call(
         lambda *refs: sketch_kernel(reps, chunks, *refs),
@@ -284,6 +390,11 @@
         compiler_params=params(),
         name="pick",
     )(me, in_hbm(halo_index), *arrived)
+    slot = nodes // peers
+    stepped = slot % 128 == 0 and peers > 1 and peers & (peers - 1) == 0
+    if stepped:
+        rank = lax.axis_index("dom").astype(jnp.int32).reshape(1, 1)
+        early0 = early(hop0)
     halo0 = exchange(send, peers)
 
     def work(index):
@@ -307,6 +418,39 @@
         name="combine_pick",
     )(in_hbm(tile_dst), in_hbm(tile_src), in_hbm(halo_index), in_hbm(tiles), hop0, halo0)
     halo1 = exchange(send, peers)
+    if stepped:
+        half = peers // 2
+        moved = pl.pallas_call(
+            relay_kernel,
+            out_shape=(out((4 * channels, slot)),) * half,
+            in_specs=[VMEM] * 4,
+            out_specs=(VMEM,) * half,
+            compiler_params=params(),
+            cost_estimate=cost(0, 16 * channels * nodes),
+            name="relay",
+        )(*early0, *early(hop1))
+        moved = [moved[0]] + [
+            lax.ppermute(moved[step], "dom", pairs(step, peers)) for step in range(1, half)
+        ]
+        send = pl.pallas_call(
+            lambda *refs: combine_alone_kernel(group, *refs),
+            out_shape=out((peers, channels, slot)),
+            in_specs=[HBM] * 4 + [VMEM] * 2,
+            out_specs=VMEM,
+            scratch_shapes=work(send_order),
+            compiler_params=params(),
+            name="combine_last",
+        )(in_hbm(tile_dst), in_hbm(tile_src), in_hbm(send_order), in_hbm(tiles), hop1, halo1)
+        last = exchange(send, peers)
+        return pl.pallas_call(
+            lambda *refs: place_steps_kernel(peers, side, *refs),
+            out_shape=out((3, channels, nodes)),
+            in_specs=[SMEM, VMEM] + [VMEM] * (half + 1),
+            out_specs=HBM,
+            scratch_shapes=[vmem((3, channels, nodes), BF16), dma((blocks,))],
+            compiler_params=params(),
+            name="place",
+        )(rank, arrival_place, *moved, last)
     send = pl.pallas_call(
         lambda *refs: combine_last_kernel(group, *refs),
         out_shape=out(last_shape),
@@ -339,6 +483,7 @@
         P("dom", None),
     )
     out_specs = P(None, "rep", "dom")
+
     return jax.shard_map(
         on_device, mesh=mesh, in_specs=in_specs, out_specs=out_specs, check_vma=False
     )

time: 66.5 us -> 75.2 us (1.13)
  blocking collectives: 44.2 us -> 22.8 us
  waiting for transfers between devices: 4.02 us -> 21.2 us
  starting transfers between devices: 3.15 us -> 13.2 us
  Pallas kernels: 14.7 us -> 17.4 us
    all_to_all x3 -> x2, blocking collectives: 44.2 us -> 22.8 us  [exchange(): arrived = lax.all_to_all(send, 'dom', 0, 0, tiled=True)]
    ppermute x0 -> x5, waiting for transfers between devices: none -> 17.2 us  [the longest x2 12.8 us: early(): return (near, lax.ppermute(far, 'dom', pairs(peers // 2, peers)))]
    ppermute x0 -> x5, starting transfers between devices: none -> 6.61 us  [the longest x3 3.55 us: on_device(): lax.ppermute(moved[step], 'dom', pairs(step, peers))]
    all_to_all x0 -> x1, starting transfers between devices: none -> 3.42 us  [exchange(): arrived = lax.all_to_all(send, 'dom', 0, 0, tiled=True)]
    pallas_call x2 -> x5, Pallas kernels: 8.13 us -> 10.8 us  [the longest x1 4.08 us: on_device(): pl.pallas_call(lambda *refs: combine_alone_kernel(group, *refs), out_shap...]
  transfers between devices with their start and end apart: 3 -> 9, of which waited for: 2 -> 7; matrix products, arithmetic and copies ran while one was open for 0% -> 0% of each run, Pallas kernels for 0% -> 4%
where the time goes in v5:
time: 75.2 us; the launch traced here: 74.7 us
  blocking collectives  22.8 us (30%)
  waiting for transfers between devices  21.2 us (28%)
  Pallas kernels  17.4 us (23%)
  starting transfers between devices  13.2 us (18%)
    all_to_all x2, blocking collectives, exchange(): arrived = lax.all_to_all(send, 'dom', 0, 0, tiled=True)  22.8 us
    ppermute x2, waiting for transfers between devices, early(): return (near, lax.ppermute(far, 'dom', pairs(peers // 2, peers)))  12.8 us
    ppermute x3, waiting for transfers between devices, on_device(): lax.ppermute(moved[step], 'dom', pairs(step, peers))  4.44 us
    pallas_call x1, Pallas kernels, on_device(): pl.pallas_call(lambda *refs: combine_alone_kernel(group, *refs), out_shap...  4.08 us
    ppermute x3, waiting for transfers between devices, on_device(): arrived.append(lax.ppermute(own[step], 'rep', pairs(step, reps)))  4.02 us
    pallas_call x1, Pallas kernels, on_device(): pl.pallas_call(lambda *refs: place_steps_kernel(peers, side, *refs), out_...  3.65 us
    ppermute x3, starting transfers between devices, on_device(): lax.ppermute(moved[step], 'dom', pairs(step, peers))  3.55 us
    all_to_all x1, starting transfers between devices, exchange(): arrived = lax.all_to_all(send, 'dom', 0, 0, tiled=True)  3.42 us
  transfers between devices with their start and end apart: 9, of which 7 were waited for; matrix products, arithmetic and copies ran while one was open for 0% of the time, Pallas kernels for 4%

profile of v5, /device:TPU:0, one launch (start us, length us, event | category | flops | bytes accessed | tf_op | source)
XLA Modules:
  0.0 74.7 jit_solution(124698666945134520)
XLA Ops:
  0.0 2.4 %sketch.1 = (bf16[64,512]{1,0:T(8,128)(2,1)S(1)}, bf16[64,512]{1,0:T(8,128)(2,1)S(1)}, bf16[64,512]{1,0:T(8,128)(2,1)S(1)}, bf16[64,512]{1,0:T(8,128)(2,1)S(1)}) custom-call(s32[1,1]{1,0:T(1,128)} %bitcast.1.refs_0_, bf16[512,768]{1,0:T(8,128)(2,1)} %refs_1_.5, bf16[768,256]{1,0:T(8,128)(2,1)} %refs_2_.3), custom_call_target="tpu_custom_call" | custom-call | tf_op jit(solution)/shard_map/sketch/pallas_call | solution.py:367
  2.4 0.6 collective-permute-start
  3.0 2.6 %collective-permute-start.1 = (bf16[64,512]{1,0:T(8,128)(2,1)S(1)}, bf16[64,512]{1,0:T(8,128)(2,1)S(1)}, u32[]{:S(2)}, u32[]{:S(2)}) collective-permute-start(bf16[64,512]{1,0:T(8,128)(2,1)S(1)} %get-tuple-element.23), channel_id=1, source_target_pairs={{0,2},{1,3},{2,0},{3,1},{4,6},{5,7},{6,4},{7,5},{8,10},{9,11},{10,... | collective-permute-start | bytes 196616 | tf_op jit(solution)/shard_map/ppermute | solution.py:383
  5.5 0.0 collective-permute-start.2
  5.6 0.0 collective-permute-done.refs_3_
  5.6 2.6 %collective-permute-done.1.refs_4_ = bf16[64,512]{1,0:T(8,128)(2,1)S(1)} collective-permute-done((bf16[64,512]{1,0:T(8,128)(2,1)S(1)}, bf16[64,512]{1,0:T(8,128)(2,1)S(1)}, u32[]{:S(2)}, u32[]{:S(2)}) %collective-permute-start.1) | collective-permute-done | bytes 65568 | tf_op jit(solution)/shard_map/ppermute | solution.py:383
  8.2 1.4 %collective-permute-done.2.refs_5_ = bf16[64,512]{1,0:T(8,128)(2,1)S(1)} collective-permute-done((bf16[64,512]{1,0:T(8,128)(2,1)S(1)}, bf16[64,512]{1,0:T(8,128)(2,1)S(1)}, u32[]{:S(2)}, u32[]{:S(2)}) %collective-permute-start.2) | collective-permute-done | bytes 65568 | tf_op jit(solution)/shard_map/ppermute | solution.py:383
  9.6 1.2 %pick.1 = (bf16[8,64,256]{2,1,0:T(8,128)(2,1)S(1)}, bf16[8,64,128]{2,1,0:T(8,128)(2,1)S(1)}) custom-call(s32[1,1]{1,0:T(1,128)} %bitcast.1.refs_0_, s32[1,1024]{1,0:T(1,128)} %refs_2_.4, bf16[64,512]{1,0:T(8,128)(2,1)S(1)} %get-tuple-element.21.refs_2_, bf16[64,512]{1,0:T(8,128)(2,1)S(1)} %collective-permute-done.refs_3_, ...), custom_call_target="tpu_custom_call" | custom-call | tf_op jit(solution)/shard_map/pick/pallas_call | solution.py:384
  10.7 13.0 %all_to_all.15.refs_5_ = bf16[8,64,128]{2,1,0:T(8,128)(2,1)S(1)} all-to-all(bf16[8,64,128]{2,1,0:T(8,128)(2,1)S(1)} %get-tuple-element.28), channel_id=1, replica_groups=mesh['dom'=8,'rep'=4] {'dom'}, dimensions={0} | all-to-all | bytes 262144 | tf_op jit(solution)/shard_map/all_to_all | solution.py:80
  23.7 3.1 %combine_pick.1 = (bf16[8,64,256]{2,1,0:T(8,128)(2,1)S(1)}, bf16[8,64,128]{2,1,0:T(8,128)(2,1)S(1)}) custom-call(s32[1,20]{1,0:T(1,128)} %refs_0_.3, s32[1,20]{1,0:T(1,128)} %refs_1_.8, s32[1,1024]{1,0:T(1,128)} %refs_2_.4, bf16[20,256,256]{2,1,0:T(8,128)(2,1)} %bitcast.3, bf16[8,64,256]{2,1,0:T(8,128)(2,1)S(1)} %get-tuple-element.25.hop.refs_4_, ...), custom_call_target="tpu_custom_call" | custom-call | tf_op jit(solution)/shard_map/combine_pick/pallas_call | solution.py:411
  26.8 9.8 %all_to_all.16.refs_5_ = bf16[8,64,128]{2,1,0:T(8,128)(2,1)S(1)} all-to-all(bf16[8,64,128]{2,1,0:T(8,128)(2,1)S(1)} %get-tuple-element.36), channel_id=1, replica_groups=mesh['dom'=8,'rep'=4] {'dom'}, dimensions={0} | all-to-all | bytes 262144 | tf_op jit(solution)/shard_map/all_to_all | solution.py:80
  36.6 4.1 %combine_last.1 = bf16[8,64,256]{2,1,0:T(8,128)(2,1)} custom-call(s32[1,20]{1,0:T(1,128)} %refs_0_.3, s32[1,20]{1,0:T(1,128)} %refs_1_.8, s32[1,2048]{1,0:T(1,128)} %refs_2_.5, bf16[20,256,256]{2,1,0:T(8,128)(2,1)} %bitcast.4, bf16[8,64,256]{2,1,0:T(8,128)(2,1)S(1)} %get-tuple-element.29.hop.refs_4_, bf16[8,64,128]{2,1,0:T(8,128)(2,1)S(1)} %all_to_all.16.refs_5_), custom_call_target="tpu_custom_call" | custom-call | tf_op jit(solution)/shard_map/combine_last/pallas_call | solution.py:435
  40.7 0.0 copy-start
  40.7 3.4 %all-to-all-start.2 = ((bf16[8,64,256]{2,1,0:T(8,128)(2,1)}), bf16[8,64,256]{2,1,0:T(8,128)(2,1)S(1)}, u32[]{:S(2)}, u32[]{:S(2)}) async-start(bf16[8,64,256]{2,1,0:T(8,128)(2,1)} %combine_last.1), calls=%async_computation.2 | async-start | bytes 524288 | tf_op jit(solution)/shard_map/all_to_all | solution.py:80
  44.1 1.5 %early.2 = (bf16[4,64,256]{2,1,0:T(8,128)(2,1)S(1)}, bf16[4,64,256]{2,1,0:T(8,128)(2,1)S(1)}) custom-call(s32[1,1]{1,0:T(1,128)} %bitcast.me_ref.refs_0_, s32[1,2048]{1,0:T(1,128)} %refs_2_.5, bf16[8,64,256]{2,1,0:T(8,128)(2,1)S(1)} %get-tuple-element.25.hop.refs_4_), custom_call_target="tpu_custom_call" | custom-call | flops 536870912 | bytes 1048576 | tf_op jit(solution)/shard_map/early/pallas_call | solution.py:352
  45.7 2.9 %collective-permute-start.3 = (bf16[4,64,256]{2,1,0:T(8,128)(2,1)S(1)}, bf16[4,64,256]{2,1,0:T(8,128)(2,1)S(1)}, u32[]{:S(2)}, u32[]{:S(2)}) collective-permute-start(bf16[4,64,256]{2,1,0:T(8,128)(2,1)S(1)} %get-tuple-element.27), channel_id=1, source_target_pairs={{0,16},{4,20},{8,24},{12,28},{16,0},{20,4},{24,8},{28,12},{1,17},{... | collective-permute-start | bytes 393224 | tf_op jit(solution)/shard_map/ppermute | solution.py:349
  48.6 1.5 %early.3 = (bf16[4,64,256]{2,1,0:T(8,128)(2,1)S(1)}, bf16[4,64,256]{2,1,0:T(8,128)(2,1)S(1)}) custom-call(s32[1,1]{1,0:T(1,128)} %bitcast.me_ref.refs_0_, s32[1,2048]{1,0:T(1,128)} %refs_2_.5, bf16[8,64,256]{2,1,0:T(8,128)(2,1)S(1)} %get-tuple-element.29.hop.refs_4_), custom_call_target="tpu_custom_call" | custom-call | flops 536870912 | bytes 1048576 | tf_op jit(solution)/shard_map/early/pallas_call | solution.py:352
  50.1 0.2 collective-permute-start.4
  50.2 11.4 %collective-permute-done.3.refs_1_ = bf16[4,64,256]{2,1,0:T(8,128)(2,1)S(1)} collective-permute-done((bf16[4,64,256]{2,1,0:T(8,128)(2,1)S(1)}, bf16[4,64,256]{2,1,0:T(8,128)(2,1)S(1)}, u32[]{:S(2)}, u32[]{:S(2)}) %collective-permute-start.3) | collective-permute-done | bytes 131104 | tf_op jit(solution)/shard_map/ppermute | solution.py:349
  61.6 1.4 %collective-permute-done.4.refs_3_ = bf16[4,64,256]{2,1,0:T(8,128)(2,1)S(1)} collective-permute-done((bf16[4,64,256]{2,1,0:T(8,128)(2,1)S(1)}, bf16[4,64,256]{2,1,0:T(8,128)(2,1)S(1)}, u32[]{:S(2)}, u32[]{:S(2)}) %collective-permute-start.4) | collective-permute-done | bytes 131104 | tf_op jit(solution)/shard_map/ppermute | solution.py:349
  63.0 1.5 %collective-permute-start.5 = (bf16[256,256]{1,0:T(8,128)(2,1)S(1)}, bf16[256,256]{1,0:T(8,128)(2,1)S(1)}, u32[]{:S(2)}, u32[]{:S(2)}) collective-permute-start(bf16[256,256]{1,0:T(8,128)(2,1)S(1)} %get-tuple-element.33), channel_id=1, source_target_pairs={{0,4},{4,0},{8,12},{12,8},{16,20},{20,16},{24,28},{28,24},{1,5},{5... | collective-permute-start | bytes 393224 | tf_op jit(solution)/shard_map/ppermute | solution.py:433
  64.6 0.0 collective-permute-start.6
  64.6 2.0 %collective-permute-start.7 = (bf16[256,256]{1,0:T(8,128)(2,1)S(1)}, bf16[256,256]{1,0:T(8,128)(2,1)S(1)}, u32[]{:S(2)}, u32[]{:S(2)}) collective-permute-start(bf16[256,256]{1,0:T(8,128)(2,1)S(1)} %get-tuple-element.35), channel_id=1, source_target_pairs={{0,12},{4,8},{8,4},{12,0},{16,28},{20,24},{24,20},{28,16},{1,13},{... | collective-permute-start | bytes 393224 | tf_op jit(solution)/shard_map/ppermute | solution.py:433
  66.6 2.9 %collective-permute-done.5.refs_3_ = bf16[256,256]{1,0:T(8,128)(2,1)S(1)} collective-permute-done((bf16[256,256]{1,0:T(8,128)(2,1)S(1)}, bf16[256,256]{1,0:T(8,128)(2,1)S(1)}, u32[]{:S(2)}, u32[]{:S(2)}) %collective-permute-start.5) | collective-permute-done | bytes 131104 | tf_op jit(solution)/shard_map/ppermute | solution.py:433
  69.5 0.2 collective-permute-done.6.refs_4_
  69.6 1.4 %collective-permute-done.7.refs_5_ = bf16[256,256]{1,0:T(8,128)(2,1)S(1)} collective-permute-done((bf16[256,256]{1,0:T(8,128)(2,1)S(1)}, bf16[256,256]{1,0:T(8,128)(2,1)S(1)}, u32[]{:S(2)}, u32[]{:S(2)}) %collective-permute-start.7) | collective-permute-done | bytes 131104 | tf_op jit(solution)/shard_map/ppermute | solution.py:433
  71.0 0.0 all-to-all-done.2.refs_6_
  71.0 0.0 copy-done
  71.0 3.7 %place.1 = bf16[3,64,2048]{2,1,0:T(8,128)(2,1)} custom-call(s32[1,1]{1,0:T(1,128)} %bitcast.me_ref.refs_0_, s32[1,2048]{1,0:T(1,128)S(1)} %copy-done, bf16[256,256]{1,0:T(8,128)(2,1)S(1)} %get-tuple-element.32.refs_2_, bf16[256,256]{1,0:T(8,128)(2,1)S(1)} %collective-permute-done.5.refs_3_, bf16[256,256]{1,0:T(8,128)(2,1)S(1)} %collective-permute-done.6.refs_4_, ...), custom_call_target="tpu_custom_call" | custom-call | tf_op jit(solution)/shard_map/place/pallas_call | solution.py:445
  (1 shorter events, 0.0 us)
Async XLA Ops:
  2.4 3.2 %collective-permute-start = (bf16[64,512]{1,0:T(8,128)(2,1)S(1)}, bf16[64,512]{1,0:T(8,128)(2,1)S(1)}, u32[]{:S(2)}, u32[]{:S(2)}) collective-permute-start(bf16[64,512]{1,0:T(8,128)(2,1)S(1)} %get-tuple-element.22), channel_id=1, source_target_pairs={{0,1},{1,0},{2,3},{3,2},{4,5},{5,4},{6,7},{7,6},{8,9},{9,8},{10,11... | collective-permute-start | bytes 196616 | tf_op jit(solution)/shard_map/ppermute | solution.py:383
  3.0 5.2 %collective-permute-start.1 = (bf16[64,512]{1,0:T(8,128)(2,1)S(1)}, bf16[64,512]{1,0:T(8,128)(2,1)S(1)}, u32[]{:S(2)}, u32[]{:S(2)}) collective-permute-start(bf16[64,512]{1,0:T(8,128)(2,1)S(1)} %get-tuple-element.23), channel_id=1, source_target_pairs={{0,2},{1,3},{2,0},{3,1},{4,6},{5,7},{6,4},{7,5},{8,10},{9,11},{10,... | collective-permute-start | bytes 196616 | tf_op jit(solution)/shard_map/ppermute | solution.py:383
  5.5 4.1 %collective-permute-start.2 = (bf16[64,512]{1,0:T(8,128)(2,1)S(1)}, bf16[64,512]{1,0:T(8,128)(2,1)S(1)}, u32[]{:S(2)}, u32[]{:S(2)}) collective-permute-start(bf16[64,512]{1,0:T(8,128)(2,1)S(1)} %get-tuple-element.24), channel_id=1, source_target_pairs={{0,3},{1,2},{2,1},{3,0},{4,7},{5,6},{6,5},{7,4},{8,11},{9,10},{10,... | collective-permute-start | bytes 196616 | tf_op jit(solution)/shard_map/ppermute | solution.py:383
  40.7 30.4 %copy-start = (s32[1,2048]{1,0:T(1,128)S(1)}, s32[1,2048]{1,0:T(1,128)}, u32[]{:S(2)}) copy-start(s32[1,2048]{1,0:T(1,128)} %refs_1_.9) | copy-start | bytes 24580
  40.7 30.3 %all-to-all-start.2 = ((bf16[8,64,256]{2,1,0:T(8,128)(2,1)}), bf16[8,64,256]{2,1,0:T(8,128)(2,1)S(1)}, u32[]{:S(2)}, u32[]{:S(2)}) async-start(bf16[8,64,256]{2,1,0:T(8,128)(2,1)} %combine_last.1), calls=%async_computation.2 | async-start | bytes 524288 | tf_op jit(solution)/shard_map/all_to_all | solution.py:80
  45.7 15.9 %collective-permute-start.3 = (bf16[4,64,256]{2,1,0:T(8,128)(2,1)S(1)}, bf16[4,64,256]{2,1,0:T(8,128)(2,1)S(1)}, u32[]{:S(2)}, u32[]{:S(2)}) collective-permute-start(bf16[4,64,256]{2,1,0:T(8,128)(2,1)S(1)} %get-tuple-element.27), channel_id=1, source_target_pairs={{0,16},{4,20},{8,24},{12,28},{16,0},{20,4},{24,8},{28,12},{1,17},{... | collective-permute-start | bytes 393224 | tf_op jit(solution)/shard_map/ppermute | solution.py:349
  50.1 12.9 %collective-permute-start.4 = (bf16[4,64,256]{2,1,0:T(8,128)(2,1)S(1)}, bf16[4,64,256]{2,1,0:T(8,128)(2,1)S(1)}, u32[]{:S(2)}, u32[]{:S(2)}) collective-permute-start(bf16[4,64,256]{2,1,0:T(8,128)(2,1)S(1)} %get-tuple-element.31), channel_id=1, source_target_pairs={{0,16},{4,20},{8,24},{12,28},{16,0},{20,4},{24,8},{28,12},{1,17},{... | collective-permute-start | bytes 393224 | tf_op jit(solution)/shard_map/ppermute | solution.py:349
  63.0 6.4 %collective-permute-start.5 = (bf16[256,256]{1,0:T(8,128)(2,1)S(1)}, bf16[256,256]{1,0:T(8,128)(2,1)S(1)}, u32[]{:S(2)}, u32[]{:S(2)}) collective-permute-start(bf16[256,256]{1,0:T(8,128)(2,1)S(1)} %get-tuple-element.33), channel_id=1, source_target_pairs={{0,4},{4,0},{8,12},{12,8},{16,20},{20,16},{24,28},{28,24},{1,5},{5... | collective-permute-start | bytes 393224 | tf_op jit(solution)/shard_map/ppermute | solution.py:433
  64.6 5.1 %collective-permute-start.6 = (bf16[256,256]{1,0:T(8,128)(2,1)S(1)}, bf16[256,256]{1,0:T(8,128)(2,1)S(1)}, u32[]{:S(2)}, u32[]{:S(2)}) collective-permute-start(bf16[256,256]{1,0:T(8,128)(2,1)S(1)} %get-tuple-element.34), channel_id=1, source_target_pairs={{0,8},{4,12},{8,0},{12,4},{16,24},{20,28},{24,16},{28,20},{1,9},{5... | collective-permute-start | bytes 393224 | tf_op jit(solution)/shard_map/ppermute | solution.py:433
  64.6 6.5 %collective-permute-start.7 = (bf16[256,256]{1,0:T(8,128)(2,1)S(1)}, bf16[256,256]{1,0:T(8,128)(2,1)S(1)}, u32[]{:S(2)}, u32[]{:S(2)}) collective-permute-start(bf16[256,256]{1,0:T(8,128)(2,1)S(1)} %get-tuple-element.35), channel_id=1, source_target_pairs={{0,12},{4,8},{8,4},{12,0},{16,28},{20,24},{24,20},{28,16},{1,13},{... | collective-permute-start | bytes 393224 | tf_op jit(solution)/shard_map/ppermute | solution.py:433

commit v6 on v5

--- a/solution.py
+++ b/solution.py
@@ -208,13 +208,23 @@
     store_slots(send, pick(stack, blocks, index[...], side, group), group)
 
 
-def early_kernel(me_ref, index_in, hop, near, far, full, index, sem):
-    fetch = pltpu.make_async_copy(index_in, index, sem)
-    fetch.start()
+def early_kernel(staged, me_ref, index_in, tiles_in, hop, near, far, total, *rest):
+    full, index, tiles, sems = rest[-4:]
     blocks, _, side = hop.shape
+    copies = [
+        pltpu.make_async_copy(index_in, index, sems.at[0]),
+        pltpu.make_async_copy(tiles_in.at[pl.ds(0, blocks)], tiles, sems.at[1]),
+    ]
+    if staged:
+        others = tiles_in.shape[0] - blocks
+        copies.append(
+            pltpu.make_async_copy(tiles_in.at[pl.ds(blocks, others)], rest[0], sems.at[2])
+        )
+    for copy in copies:
+        copy.start()
     peers, _, slot = full.shape
     stack = jnp.concatenate([hop[block] for block in range(blocks)], 0)
-    fetch.wait()
+    copies[0].wait()
     for peer, part in enumerate(pick(stack, blocks, index[...], side, slot)):
         full[peer] = part
     me = me_ref[0, 0]
@@ -222,6 +232,51 @@
     for step in range(half):
         near[step] = full[me ^ step]
         far[step] = full[me ^ half ^ step]
+    ones = jnp.ones((EXTRA, side), BF16)
+    copies[1].wait()
+    for block in range(blocks):
+        columns = jnp.concatenate([hop[block], ones], 0)
+        total[block] = dot(columns, tiles[block], NT)
+    if staged:
+        copies[2].wait()
+
+
+def finish(dst, src, tiles, total, hop, arrived, columns, sums):
+    blocks, channels, side = hop.shape
+    fixed = columns.shape[0]
+    columns[:, channels:, :] = jnp.ones((fixed, EXTRA, side), BF16)
+    for block in range(blocks):
+        columns[block, :channels, :] = hop[block]
+        sums[block] = total[block]
+    wide = load_wide(arrived)
+    for block in range(blocks, fixed):
+        start = (block - blocks) * side
+        columns[block, :channels, :] = wide[:, start : start + side]
+    for other in range(tiles.shape[0]):
+        slot = blocks + other
+        target = dst[0, slot]
+        target = jnp.where(target < 0, blocks, target)
+        start = slot if slot < fixed else src[0, slot]
+        sums[target] = sums[target] + dot(columns[start], tiles[other], NT)
+    results = []
+    for block in range(blocks):
+        whole = sums[block]
+        results.append((whole[:channels] / whole[channels : channels + 1]).astype(BF16))
+    return results
+
+
+def finish_kernel(
+    group, keep, dst, src, index, tiles, total, hop, arrived, *rest
+):
+    columns, sums = rest[-2:]
+    send = rest[-3]
+    results = finish(dst, src, tiles, total, hop, arrived, columns, sums)
+    blocks, _, side = hop.shape
+    if keep:
+        for block, result in enumerate(results):
+            rest[0][block] = result
+    stack = jnp.concatenate(results, 0)
+    store_slots(send, pick(stack, blocks, index[...], side, group), group)
 
 
 def relay_kernel(*refs):
@@ -231,17 +286,6 @@
     for step in range(half):
         for place, blocks in enumerate(ins):
             outs[step][place * channels : (place + 1) * channels] = blocks[step]
-
-
-def combine_alone_kernel(
-    group, dst_in, src_in, index_in, tiles_in, hop, arrived_ref, send, *scratch
-):
-    results = combine(
-        dst_in, src_in, index_in, tiles_in, hop, arrived_ref, scratch, lambda *_: None
-    )
-    blocks, _, side = hop.shape
-    stack = jnp.concatenate(results, 0)
-    store_slots(send, pick(stack, blocks, scratch[2][...], side, group), group)
 
 
 def combine_last_kernel(
@@ -343,26 +387,45 @@
     def out(shape):
         return jax.ShapeDtypeStruct(shape, BF16)
 
-    def early(hop):
+    def early(hop, staged):
         shape = (peers // 2, channels, slot)
-        near, far = early_call(hop, shape)
-        return near, lax.ppermute(far, "dom", pairs(peers // 2, peers))
-
-    def early_call(hop, shape):
-        return pl.pallas_call(
-            early_kernel,
-            out_shape=(out(shape), out(shape)),
-            in_specs=[SMEM, HBM, VMEM],
-            out_specs=(VMEM, VMEM),
+        others = (slots - blocks, side, side)
+        near, far, total, *rest = pl.pallas_call(
+            lambda *refs: early_kernel(staged, *refs),
+            out_shape=(
+                out(shape),
+                out(shape),
+                jax.ShapeDtypeStruct((blocks, channels + EXTRA, side), F32),
+            )
+            + (out(others),) * staged,
+            in_specs=[SMEM, HBM, HBM, VMEM],
+            out_specs=(VMEM,) * (3 + staged),
             scratch_shapes=[
                 vmem((peers, channels, slot), BF16),
                 vmem(send_order.shape, jnp.int32),
-                dma,
+                vmem((blocks, side, side), BF16),
+                dma((3,)),
             ],
             compiler_params=params(),
             cost_estimate=cost(2 * channels * nodes * nodes, 8 * channels * nodes),
             name="early",
-        )(rank, in_hbm(send_order), hop)
+        )(rank, in_hbm(send_order), in_hbm(tiles), hop)
+        sent = lax.ppermute(far, "dom", pairs(peers // 2, peers))
+        return (near, sent), total, rest
+
+    def late(keep, index, others, total, hop, arrived):
+        shape = (peers, channels, index.shape[1] // peers)
+        return pl.pallas_call(
+            lambda *refs: finish_kernel(group, keep, *refs),
+            out_shape=(out(hop_shape),) * keep + (out(shape),),
+            in_specs=[SMEM, SMEM] + [VMEM] * 5,
+            out_specs=(VMEM,) * (keep + 1),
+            scratch_shapes=[
+                vmem((fixed, channels + EXTRA, side), BF16),
+                vmem((blocks + 1, channels + EXTRA, side), F32),
+            ],
+            compiler_params=params(),
+        )(tile_dst, tile_src, index, others, total, hop, arrived)
 
     own = pl.pallas_call(
         lambda *refs: sketch_kernel(reps, chunks, *refs),
@@ -391,10 +454,39 @@
         name="pick",
     )(me, in_hbm(halo_index), *arrived)
     slot = nodes // peers
-    stepped = slot % 128 == 0 and peers > 1 and peers & (peers - 1) == 0
-    if stepped:
+    whole_lanes = slot % 128 == 0 and (halo // peers) % 128 == 0
+    if whole_lanes and peers > 1 and peers & (peers - 1) == 0:
+        half = peers // 2
         rank = lax.axis_index("dom").astype(jnp.int32).reshape(1, 1)
-        early0 = early(hop0)
+        halo0 = exchange(send, peers)
+        early0, total, others = early(hop0, 1)
+        others = others[0]
+        hop1, send = late(1, halo_index, others, total, hop0, halo0)
+        halo1 = exchange(send, peers)
+        early1, total, _ = early(hop1, 0)
+        (send,) = late(0, send_order, others, total, hop1, halo1)
+        last = exchange(send, peers)
+        moved = pl.pallas_call(
+            relay_kernel,
+            out_shape=(out((4 * channels, slot)),) * half,
+            in_specs=[VMEM] * 4,
+            out_specs=(VMEM,) * half,
+            compiler_params=params(),
+            cost_estimate=cost(0, 16 * channels * nodes),
+            name="relay",
+        )(*early0, *early1)
+        moved = [moved[0]] + [
+            lax.ppermute(moved[step], "dom", pairs(step, peers)) for step in range(1, half)
+        ]
+        return pl.pallas_call(
+            lambda *refs: place_steps_kernel(peers, side, *refs),
+            out_shape=out((3, channels, nodes)),
+            in_specs=[SMEM, VMEM] + [VMEM] * (half + 1),
+            out_specs=HBM,
+            scratch_shapes=[vmem((3, channels, nodes), BF16), dma((blocks,))],
+            compiler_params=params(),
+            name="place",
+        )(rank, arrival_place, *moved, last)
     halo0 = exchange(send, peers)
 
     def work(index):
@@ -418,39 +510,6 @@
         name="combine_pick",
     )(in_hbm(tile_dst), in_hbm(tile_src), in_hbm(halo_index), in_hbm(tiles), hop0, halo0)
     halo1 = exchange(send, peers)
-    if stepped:
-        half = peers // 2
-        moved = pl.pallas_call(
-            relay_kernel,
-            out_shape=(out((4 * channels, slot)),) * half,
-            in_specs=[VMEM] * 4,
-            out_specs=(VMEM,) * half,
-            compiler_params=params(),
-            cost_estimate=cost(0, 16 * channels * nodes),
-            name="relay",
-        )(*early0, *early(hop1))
-        moved = [moved[0]] + [
-            lax.ppermute(moved[step], "dom", pairs(step, peers)) for step in range(1, half)
-        ]
-        send = pl.pallas_call(
-            lambda *refs: combine_alone_kernel(group, *refs),
-            out_shape=out((peers, channels, slot)),
-            in_specs=[HBM] * 4 + [VMEM] * 2,
-            out_specs=VMEM,
-            scratch_shapes=work(send_order),
-            compiler_params=params(),
-            name="combine_last",
-        )(in_hbm(tile_dst), in_hbm(tile_src), in_hbm(send_order), in_hbm(tiles), hop1, halo1)
-        last = exchange(send, peers)
-        return pl.pallas_call(
-            lambda *refs: place_steps_kernel(peers, side, *refs),
-            out_shape=out((3, channels, nodes)),
-            in_specs=[SMEM, VMEM] + [VMEM] * (half + 1),
-            out_specs=HBM,
-            scratch_shapes=[vmem((3, channels, nodes), BF16), dma((blocks,))],
-            compiler_params=params(),
-            name="place",
-        )(rank, arrival_place, *moved, last)
     send = pl.pallas_call(
         lambda *refs: combine_last_kernel(group, *refs),
         out_shape=out(last_shape),

time: 75.2 us -> 74 us (0.984)
  blocking collectives: 22.8 us -> 0 us
  waiting for transfers between devices: 21.2 us -> 34.2 us
  starting transfers between devices: 13.2 us -> 22.3 us
    all_to_all x2 -> x0, blocking collectives: 22.8 us -> none  [exchange(): arrived = lax.all_to_all(send, 'dom', 0, 0, tiled=True)]
    all_to_all x1 -> x3, waiting for transfers between devices: 0.01 us -> 10.6 us  [exchange(): arrived = lax.all_to_all(send, 'dom', 0, 0, tiled=True)]
    all_to_all x1 -> x3, starting transfers between devices: 3.42 us -> 12.6 us  [exchange(): arrived = lax.all_to_all(send, 'dom', 0, 0, tiled=True)]
    ppermute x2, waiting for transfers between devices: 12.8 us -> 15.1 us  [early(): sent = lax.ppermute(far, 'dom', pairs(peers // 2, peers))]
    pallas_call x4, Pallas kernels: 10.2 us -> 8.86 us  [the longest x2 4.9 us: late(): pl.pallas_call(lambda *refs: finish_kernel(group, keep, *refs), out_shape...]
  transfers between devices with their start and end apart: 9 -> 11, of which waited for: 7 -> 9; matrix products, arithmetic and copies ran while one was open for 0% -> 0% of each run, Pallas kernels for 4% -> 5%
where the time goes in v6:
time: 74 us; the launch traced here: 73.5 us
  waiting for transfers between devices  34.2 us (46%)
  starting transfers between devices  22.3 us (30%)
  Pallas kernels  16.8 us (23%)
    ppermute x2, waiting for transfers between devices, early(): sent = lax.ppermute(far, 'dom', pairs(peers // 2, peers))  15.1 us
    all_to_all x3, starting transfers between devices, exchange(): arrived = lax.all_to_all(send, 'dom', 0, 0, tiled=True)  12.6 us
    all_to_all x3, waiting for transfers between devices, exchange(): arrived = lax.all_to_all(send, 'dom', 0, 0, tiled=True)  10.6 us
    pallas_call x2, Pallas kernels, late(): pl.pallas_call(lambda *refs: finish_kernel(group, keep, *refs), out_shape...  4.9 us
    ppermute x3, waiting for transfers between devices, on_device(): lax.ppermute(moved[step], 'dom', pairs(step, peers))  4.44 us
    ppermute x3, waiting for transfers between devices, on_device(): arrived.append(lax.ppermute(own[step], 'rep', pairs(step, reps)))  4.02 us
    pallas_call x2, Pallas kernels, early(): pl.pallas_call(lambda *refs: early_kernel(staged, *refs), out_shape=(out(...  3.96 us
    pallas_call x1, Pallas kernels, on_device(): pl.pallas_call(lambda *refs: place_steps_kernel(peers, side, *refs), out_...  3.65 us
  transfers between devices with their start and end apart: 11, of which 9 were waited for; matrix products, arithmetic and copies ran while one was open for 0% of the time, Pallas kernels for 5%

profile of v6, /device:TPU:0, one launch (start us, length us, event | category | flops | bytes accessed | tf_op | source)
XLA Modules:
  0.0 73.5 jit_solution(9180354470853615386)
XLA Ops:
  0.0 0.0 copy-start.1
  0.0 0.0 copy-start.4
  0.0 0.0 copy-start.3
  0.0 2.4 %sketch.1 = (bf16[64,512]{1,0:T(8,128)(2,1)S(1)}, bf16[64,512]{1,0:T(8,128)(2,1)S(1)}, bf16[64,512]{1,0:T(8,128)(2,1)S(1)}, bf16[64,512]{1,0:T(8,128)(2,1)S(1)}) custom-call(s32[1,1]{1,0:T(1,128)} %bitcast.2.refs_0_, bf16[512,768]{1,0:T(8,128)(2,1)} %refs_1_.7, bf16[768,256]{1,0:T(8,128)(2,1)} %refs_2_.3), custom_call_target="tpu_custom_call" | custom-call | tf_op jit(solution)/shard_map/sketch/pallas_call | solution.py:430
  2.5 0.6 collective-permute-start
  3.0 2.6 %collective-permute-start.1 = (bf16[64,512]{1,0:T(8,128)(2,1)S(1)}, bf16[64,512]{1,0:T(8,128)(2,1)S(1)}, u32[]{:S(2)}, u32[]{:S(2)}) collective-permute-start(bf16[64,512]{1,0:T(8,128)(2,1)S(1)} %get-tuple-element.26), channel_id=1, source_target_pairs={{0,2},{1,3},{2,0},{3,1},{4,6},{5,7},{6,4},{7,5},{8,10},{9,11},{10,... | collective-permute-start | bytes 196616 | tf_op jit(solution)/shard_map/ppermute | solution.py:446
  5.6 0.0 collective-permute-start.2
  5.6 0.0 collective-permute-done.refs_3_
  5.6 2.6 %collective-permute-done.1.refs_4_ = bf16[64,512]{1,0:T(8,128)(2,1)S(1)} collective-permute-done((bf16[64,512]{1,0:T(8,128)(2,1)S(1)}, bf16[64,512]{1,0:T(8,128)(2,1)S(1)}, u32[]{:S(2)}, u32[]{:S(2)}) %collective-permute-start.1) | collective-permute-done | bytes 65568 | tf_op jit(solution)/shard_map/ppermute | solution.py:446
  8.2 1.4 %collective-permute-done.2.refs_5_ = bf16[64,512]{1,0:T(8,128)(2,1)S(1)} collective-permute-done((bf16[64,512]{1,0:T(8,128)(2,1)S(1)}, bf16[64,512]{1,0:T(8,128)(2,1)S(1)}, u32[]{:S(2)}, u32[]{:S(2)}) %collective-permute-start.2) | collective-permute-done | bytes 65568 | tf_op jit(solution)/shard_map/ppermute | solution.py:446
  9.6 1.8 %pick.1 = (bf16[8,64,256]{2,1,0:T(8,128)(2,1)S(1)}, bf16[8,64,128]{2,1,0:T(8,128)(2,1)}) custom-call(s32[1,1]{1,0:T(1,128)} %bitcast.2.refs_0_, s32[1,1024]{1,0:T(1,128)} %refs_2_.4, bf16[64,512]{1,0:T(8,128)(2,1)S(1)} %get-tuple-element.24.refs_2_, bf16[64,512]{1,0:T(8,128)(2,1)S(1)} %collective-permute-done.refs_3_, ...), custom_call_target="tpu_custom_call" | custom-call | tf_op jit(solution)/shard_map/pick/pallas_call | solution.py:447
  11.4 5.8 %all-to-all-start = ((bf16[8,64,128]{2,1,0:T(8,128)(2,1)}), bf16[8,64,128]{2,1,0:T(8,128)(2,1)S(1)}, u32[]{:S(2)}, u32[]{:S(2)}) async-start(bf16[8,64,128]{2,1,0:T(8,128)(2,1)} %get-tuple-element.33), calls=%async_computation | async-start | bytes 262144 | tf_op jit(solution)/shard_map/all_to_all | solution.py:80
  17.3 2.0 %early.2 = (bf16[4,64,256]{2,1,0:T(8,128)(2,1)S(1)}, bf16[4,64,256]{2,1,0:T(8,128)(2,1)S(1)}, f32[8,80,256]{2,1,0:T(8,128)S(1)}, bf16[12,256,256]{2,1,0:T(8,128)(2,1)S(1)}) custom-call(s32[1,1]{1,0:T(1,128)} %bitcast.refs_0_, s32[1,2048]{1,0:T(1,128)} %refs_2_.5, bf16[20,256,256]{2,1,0:T(8,128)(2,1)} %bitcast.3, ...), custom_call_target="tpu_custom_call" | custom-call | flops 536870912 | bytes 1048576 | tf_op jit(solution)/shard_map/early/pallas_call | solution.py:393
  19.3 5.4 %all-to-all-done.refs_6_ = bf16[8,64,128]{2,1,0:T(8,128)(2,1)S(1)} async-done(((bf16[8,64,128]{2,1,0:T(8,128)(2,1)}), bf16[8,64,128]{2,1,0:T(8,128)(2,1)S(1)}, u32[]{:S(2)}, u32[]{:S(2)}) %all-to-all-start) | async-done | bytes 131104 | tf_op jit(solution)/shard_map/all_to_all | solution.py:80
  24.6 0.0 copy-done.1
  24.6 0.0 copy-done.4
  24.6 0.0 copy-done.3
  24.6 0.0 copy-start
  24.7 2.3 %shard_map.82 = (bf16[8,64,256]{2,1,0:T(8,128)(2,1)S(1)}, bf16[8,64,128]{2,1,0:T(8,128)(2,1)}) custom-call(s32[1,20]{1,0:T(1,128)S(1)} %copy-done.3, s32[1,20]{1,0:T(1,128)S(1)} %copy-done.4, s32[1,1024]{1,0:T(1,128)S(1)} %copy-done.1, bf16[12,256,256]{2,1,0:T(8,128)(2,1)S(1)} %get-tuple-element.31.refs_3_, f32[8,80,256]{2,1,0:T(8,128)S(1)} %get-tuple-element.32.refs_4_, ...), custom_call_target="tpu_custom_call" | custom-call | tf_op jit(solution)/shard_map/pallas_call | solution.py:418
  26.9 3.4 %all-to-all-start.1 = ((bf16[8,64,128]{2,1,0:T(8,128)(2,1)}), bf16[8,64,128]{2,1,0:T(8,128)(2,1)S(1)}, u32[]{:S(2)}, u32[]{:S(2)}) async-start(bf16[8,64,128]{2,1,0:T(8,128)(2,1)} %get-tuple-element.42), calls=%async_computation.1 | async-start | bytes 262144 | tf_op jit(solution)/shard_map/all_to_all | solution.py:80
  30.3 2.0 %early.3 = (bf16[4,64,256]{2,1,0:T(8,128)(2,1)S(1)}, bf16[4,64,256]{2,1,0:T(8,128)(2,1)S(1)}, f32[8,80,256]{2,1,0:T(8,128)S(1)}) custom-call(s32[1,1]{1,0:T(1,128)} %bitcast.refs_0_, s32[1,2048]{1,0:T(1,128)} %refs_2_.5, bf16[20,256,256]{2,1,0:T(8,128)(2,1)} %bitcast.4, bf16[8,64,256]{2,1,0:T(8,128)(2,1)S(1)} %get-tuple-element.34.refs_3_.refs_5_), custom_call_target="tpu_custom_call" | custom-call | flops 536870912 | bytes 1048576 | tf_op jit(solution)/shard_map/early/pallas_call | solution.py:393
  32.3 0.0 copy-start.2
  32.3 5.3 %all-to-all-done.1.refs_6_ = bf16[8,64,128]{2,1,0:T(8,128)(2,1)S(1)} async-done(((bf16[8,64,128]{2,1,0:T(8,128)(2,1)}), bf16[8,64,128]{2,1,0:T(8,128)(2,1)S(1)}, u32[]{:S(2)}, u32[]{:S(2)}) %all-to-all-start.1) | async-done | bytes 131104 | tf_op jit(solution)/shard_map/all_to_all | solution.py:80
  37.6 0.0 copy-done
  37.6 2.6 %shard_map.83 = bf16[8,64,256]{2,1,0:T(8,128)(2,1)} custom-call(s32[1,20]{1,0:T(1,128)S(1)} %copy-done.3, s32[1,20]{1,0:T(1,128)S(1)} %copy-done.4, s32[1,2048]{1,0:T(1,128)S(1)} %copy-done, bf16[12,256,256]{2,1,0:T(8,128)(2,1)S(1)} %get-tuple-element.31.refs_3_, f32[8,80,256]{2,1,0:T(8,128)S(1)} %get-tuple-element.41.refs_4_, ...), custom_call_target="tpu_custom_call" | custom-call | tf_op jit(solution)/shard_map/pallas_call | solution.py:418
  40.2 3.4 %all-to-all-start.2 = ((bf16[8,64,256]{2,1,0:T(8,128)(2,1)}), bf16[8,64,256]{2,1,0:T(8,128)(2,1)S(1)}, u32[]{:S(2)}, u32[]{:S(2)}) async-start(bf16[8,64,256]{2,1,0:T(8,128)(2,1)} %shard_map.83), calls=%async_computation.2 | async-start | bytes 524288 | tf_op jit(solution)/shard_map/all_to_all | solution.py:80
  43.6 2.8 %collective-permute-start.3 = (bf16[4,64,256]{2,1,0:T(8,128)(2,1)S(1)}, bf16[4,64,256]{2,1,0:T(8,128)(2,1)S(1)}, u32[]{:S(2)}, u32[]{:S(2)}) collective-permute-start(bf16[4,64,256]{2,1,0:T(8,128)(2,1)S(1)} %get-tuple-element.30), channel_id=1, source_target_pairs={{0,16},{4,20},{8,24},{12,28},{16,0},{20,4},{24,8},{28,12},{1,17},{... | collective-permute-start | bytes 393224 | tf_op jit(solution)/shard_map/ppermute | solution.py:413
  46.5 0.2 collective-permute-start.4
  46.6 13.7 %collective-permute-done.3.refs_1_ = bf16[4,64,256]{2,1,0:T(8,128)(2,1)S(1)} collective-permute-done((bf16[4,64,256]{2,1,0:T(8,128)(2,1)S(1)}, bf16[4,64,256]{2,1,0:T(8,128)(2,1)S(1)}, u32[]{:S(2)}, u32[]{:S(2)}) %collective-permute-start.3) | collective-permute-done | bytes 131104 | tf_op jit(solution)/shard_map/ppermute | solution.py:413
  60.4 1.4 %collective-permute-done.4.refs_3_ = bf16[4,64,256]{2,1,0:T(8,128)(2,1)S(1)} collective-permute-done((bf16[4,64,256]{2,1,0:T(8,128)(2,1)S(1)}, bf16[4,64,256]{2,1,0:T(8,128)(2,1)S(1)}, u32[]{:S(2)}, u32[]{:S(2)}) %collective-permute-start.4) | collective-permute-done | bytes 131104 | tf_op jit(solution)/shard_map/ppermute | solution.py:413
  61.8 1.5 %collective-permute-start.5 = (bf16[256,256]{1,0:T(8,128)(2,1)S(1)}, bf16[256,256]{1,0:T(8,128)(2,1)S(1)}, u32[]{:S(2)}, u32[]{:S(2)}) collective-permute-start(bf16[256,256]{1,0:T(8,128)(2,1)S(1)} %get-tuple-element.38), channel_id=1, source_target_pairs={{0,4},{4,0},{8,12},{12,8},{16,20},{20,16},{24,28},{28,24},{1,5},{5... | collective-permute-start | bytes 393224 | tf_op jit(solution)/shard_map/ppermute | solution.py:479
  63.3 0.0 collective-permute-start.6
  63.3 2.0 %collective-permute-start.7 = (bf16[256,256]{1,0:T(8,128)(2,1)S(1)}, bf16[256,256]{1,0:T(8,128)(2,1)S(1)}, u32[]{:S(2)}, u32[]{:S(2)}) collective-permute-start(bf16[256,256]{1,0:T(8,128)(2,1)S(1)} %get-tuple-element.40), channel_id=1, source_target_pairs={{0,12},{4,8},{8,4},{12,0},{16,28},{20,24},{24,20},{28,16},{1,13},{... | collective-permute-start | bytes 393224 | tf_op jit(solution)/shard_map/ppermute | solution.py:479
  65.4 2.9 %collective-permute-done.5.refs_3_ = bf16[256,256]{1,0:T(8,128)(2,1)S(1)} collective-permute-done((bf16[256,256]{1,0:T(8,128)(2,1)S(1)}, bf16[256,256]{1,0:T(8,128)(2,1)S(1)}, u32[]{:S(2)}, u32[]{:S(2)}) %collective-permute-start.5) | collective-permute-done | bytes 131104 | tf_op jit(solution)/shard_map/ppermute | solution.py:479
  68.2 0.2 collective-permute-done.6.refs_4_
  68.4 1.4 %collective-permute-done.7.refs_5_ = bf16[256,256]{1,0:T(8,128)(2,1)S(1)} collective-permute-done((bf16[256,256]{1,0:T(8,128)(2,1)S(1)}, bf16[256,256]{1,0:T(8,128)(2,1)S(1)}, u32[]{:S(2)}, u32[]{:S(2)}) %collective-permute-start.7) | collective-permute-done | bytes 131104 | tf_op jit(solution)/shard_map/ppermute | solution.py:479
  69.8 0.0 all-to-all-done.2.refs_6_
  69.8 0.0 copy-done.2
  69.8 3.7 %place.1 = bf16[3,64,2048]{2,1,0:T(8,128)(2,1)} custom-call(s32[1,1]{1,0:T(1,128)} %bitcast.refs_0_, s32[1,2048]{1,0:T(1,128)S(1)} %copy-done.2, bf16[256,256]{1,0:T(8,128)(2,1)S(1)} %get-tuple-element.37.refs_2_, bf16[256,256]{1,0:T(8,128)(2,1)S(1)} %collective-permute-done.5.refs_3_, bf16[256,256]{1,0:T(8,128)(2,1)S(1)} %collective-permute-done.6.refs_4_, ...), custom_call_target="tpu_custom_call" | custom-call | tf_op jit(solution)/shard_map/place/pallas_call | solution.py:481
  (1 shorter events, 0.0 us)
Async XLA Ops:
  0.0 24.6 %copy-start.1 = (s32[1,1024]{1,0:T(1,128)S(1)}, s32[1,1024]{1,0:T(1,128)}, u32[]{:S(2)}) copy-start(s32[1,1024]{1,0:T(1,128)} %refs_2_.4) | copy-start | bytes 12292
  0.0 24.6 %copy-start.4 = (s32[1,20]{1,0:T(1,128)S(1)}, s32[1,20]{1,0:T(1,128)}, u32[]{:S(2)}) copy-start(s32[1,20]{1,0:T(1,128)} %refs_1_.12) | copy-start | bytes 244
  0.0 24.6 %copy-start.3 = (s32[1,20]{1,0:T(1,128)S(1)}, s32[1,20]{1,0:T(1,128)}, u32[]{:S(2)}) copy-start(s32[1,20]{1,0:T(1,128)} %refs_0_.3) | copy-start | bytes 244
  2.5 3.2 %collective-permute-start = (bf16[64,512]{1,0:T(8,128)(2,1)S(1)}, bf16[64,512]{1,0:T(8,128)(2,1)S(1)}, u32[]{:S(2)}, u32[]{:S(2)}) collective-permute-start(bf16[64,512]{1,0:T(8,128)(2,1)S(1)} %get-tuple-element.25), channel_id=1, source_target_pairs={{0,1},{1,0},{2,3},{3,2},{4,5},{5,4},{6,7},{7,6},{8,9},{9,8},{10,11... | collective-permute-start | bytes 196616 | tf_op jit(solution)/shard_map/ppermute | solution.py:446
  3.0 5.2 %collective-permute-start.1 = (bf16[64,512]{1,0:T(8,128)(2,1)S(1)}, bf16[64,512]{1,0:T(8,128)(2,1)S(1)}, u32[]{:S(2)}, u32[]{:S(2)}) collective-permute-start(bf16[64,512]{1,0:T(8,128)(2,1)S(1)} %get-tuple-element.26), channel_id=1, source_target_pairs={{0,2},{1,3},{2,0},{3,1},{4,6},{5,7},{6,4},{7,5},{8,10},{9,11},{10,... | collective-permute-start | bytes 196616 | tf_op jit(solution)/shard_map/ppermute | solution.py:446
  5.6 4.1 %collective-permute-start.2 = (bf16[64,512]{1,0:T(8,128)(2,1)S(1)}, bf16[64,512]{1,0:T(8,128)(2,1)S(1)}, u32[]{:S(2)}, u32[]{:S(2)}) collective-permute-start(bf16[64,512]{1,0:T(8,128)(2,1)S(1)} %get-tuple-element.27), channel_id=1, source_target_pairs={{0,3},{1,2},{2,1},{3,0},{4,7},{5,6},{6,5},{7,4},{8,11},{9,10},{10,... | collective-permute-start | bytes 196616 | tf_op jit(solution)/shard_map/ppermute | solution.py:446
  11.4 13.2 %all-to-all-start = ((bf16[8,64,128]{2,1,0:T(8,128)(2,1)}), bf16[8,64,128]{2,1,0:T(8,128)(2,1)S(1)}, u32[]{:S(2)}, u32[]{:S(2)}) async-start(bf16[8,64,128]{2,1,0:T(8,128)(2,1)} %get-tuple-element.33), calls=%async_computation | async-start | bytes 262144 | tf_op jit(solution)/shard_map/all_to_all | solution.py:80
  24.6 12.9 %copy-start = (s32[1,2048]{1,0:T(1,128)S(1)}, s32[1,2048]{1,0:T(1,128)}, u32[]{:S(2)}) copy-start(s32[1,2048]{1,0:T(1,128)} %refs_2_.5) | copy-start | bytes 24580
  26.9 10.7 %all-to-all-start.1 = ((bf16[8,64,128]{2,1,0:T(8,128)(2,1)}), bf16[8,64,128]{2,1,0:T(8,128)(2,1)S(1)}, u32[]{:S(2)}, u32[]{:S(2)}) async-start(bf16[8,64,128]{2,1,0:T(8,128)(2,1)} %get-tuple-element.42), calls=%async_computation.1 | async-start | bytes 262144 | tf_op jit(solution)/shard_map/all_to_all | solution.py:80
  32.3 37.5 %copy-start.2 = (s32[1,2048]{1,0:T(1,128)S(1)}, s32[1,2048]{1,0:T(1,128)}, u32[]{:S(2)}) copy-start(s32[1,2048]{1,0:T(1,128)} %refs_1_.13) | copy-start | bytes 24580
  40.2 29.6 %all-to-all-start.2 = ((bf16[8,64,256]{2,1,0:T(8,128)(2,1)}), bf16[8,64,256]{2,1,0:T(8,128)(2,1)S(1)}, u32[]{:S(2)}, u32[]{:S(2)}) async-start(bf16[8,64,256]{2,1,0:T(8,128)(2,1)} %shard_map.83), calls=%async_computation.2 | async-start | bytes 524288 | tf_op jit(solution)/shard_map/all_to_all | solution.py:80
  43.6 16.7 %collective-permute-start.3 = (bf16[4,64,256]{2,1,0:T(8,128)(2,1)S(1)}, bf16[4,64,256]{2,1,0:T(8,128)(2,1)S(1)}, u32[]{:S(2)}, u32[]{:S(2)}) collective-permute-start(bf16[4,64,256]{2,1,0:T(8,128)(2,1)S(1)} %get-tuple-element.30), channel_id=1, source_target_pairs={{0,16},{4,20},{8,24},{12,28},{16,0},{20,4},{24,8},{28,12},{1,17},{... | collective-permute-start | bytes 393224 | tf_op jit(solution)/shard_map/ppermute | solution.py:413
  46.5 15.3 %collective-permute-start.4 = (bf16[4,64,256]{2,1,0:T(8,128)(2,1)S(1)}, bf16[4,64,256]{2,1,0:T(8,128)(2,1)S(1)}, u32[]{:S(2)}, u32[]{:S(2)}) collective-permute-start(bf16[4,64,256]{2,1,0:T(8,128)(2,1)S(1)} %get-tuple-element.36), channel_id=1, source_target_pairs={{0,16},{4,20},{8,24},{12,28},{16,0},{20,4},{24,8},{28,12},{1,17},{... | collective-permute-start | bytes 393224 | tf_op jit(solution)/shard_map/ppermute | solution.py:413
  61.8 6.4 %collective-permute-start.5 = (bf16[256,256]{1,0:T(8,128)(2,1)S(1)}, bf16[256,256]{1,0:T(8,128)(2,1)S(1)}, u32[]{:S(2)}, u32[]{:S(2)}) collective-permute-start(bf16[256,256]{1,0:T(8,128)(2,1)S(1)} %get-tuple-element.38), channel_id=1, source_target_pairs={{0,4},{4,0},{8,12},{12,8},{16,20},{20,16},{24,28},{28,24},{1,5},{5... | collective-permute-start | bytes 393224 | tf_op jit(solution)/shard_map/ppermute | solution.py:479
  63.3 5.1 %collective-permute-start.6 = (bf16[256,256]{1,0:T(8,128)(2,1)S(1)}, bf16[256,256]{1,0:T(8,128)(2,1)S(1)}, u32[]{:S(2)}, u32[]{:S(2)}) collective-permute-start(bf16[256,256]{1,0:T(8,128)(2,1)S(1)} %get-tuple-element.39), channel_id=1, source_target_pairs={{0,8},{4,12},{8,0},{12,4},{16,24},{20,28},{24,16},{28,20},{1,9},{5... | collective-permute-start | bytes 393224 | tf_op jit(solution)/shard_map/ppermute | solution.py:479
  63.3 6.5 %collective-permute-start.7 = (bf16[256,256]{1,0:T(8,128)(2,1)S(1)}, bf16[256,256]{1,0:T(8,128)(2,1)S(1)}, u32[]{:S(2)}, u32[]{:S(2)}) collective-permute-start(bf16[256,256]{1,0:T(8,128)(2,1)S(1)} %get-tuple-element.40), channel_id=1, source_target_pairs={{0,12},{4,8},{8,4},{12,0},{16,28},{20,24},{24,20},{28,16},{1,13},{... | collective-permute-start | bytes 393224 | tf_op jit(solution)/shard_map/ppermute | solution.py:479

commit v7 on v6

--- a/solution.py
+++ b/solution.py
@@ -12,8 +12,8 @@
 NN = (((1,), (0,)), ((), ()))
 NT = (((1,), (1,)), ((), ()))
 VMEM = pl.BlockSpec(memory_space=pltpu.VMEM)
-SMEM = pl.BlockSpec(memory_space=pltpu.SMEM)
 HBM = pl.BlockSpec(memory_space=pltpu.HBM)
+ANY = pl.BlockSpec(memory_space=pl.ANY)
 
 
 def params():
@@ -107,8 +107,8 @@
     return [(rank, (rank + step) % count) for rank in range(count)]
 
 
-def sketch_kernel(count, chunks, me_ref, features_in, sketch_in, *rest):
-    outs, (full, features, sketch, sems) = rest[:count], rest[count:]
+def sketch_kernel(count, chunks, features_in, sketch_in, index_in, *rest):
+    outs, (index_out, full, features, sketch, sems) = rest[:count], rest[count:]
     channels, width = outs[0].shape
     step = width // chunks
     copies = [pltpu.make_async_copy(sketch_in, sketch, sems.at[chunks])]
@@ -117,6 +117,7 @@
         copies.append(
             pltpu.make_async_copy(features_in.at[rows, :], features.at[rows, :], sems.at[chunk])
         )
+    copies.append(pltpu.make_async_copy(index_in, index_out, sems.at[chunks + 1]))
     for copy in copies:
         copy.start()
     copies[0].wait()
@@ -126,24 +127,22 @@
         product = dot(features[rows, :], sketch[...]).T.astype(BF16)
         for part in range(count):
             full[part, :, rows] = product[part * channels : (part + 1) * channels]
-    me = me_ref[0, 0]
+    me = lax.axis_index("rep")
     for part in range(count):
         outs[part][...] = full[partner(me, part, count)]
-
-
-def pick_kernel(count, group, me_ref, index_in, *rest):
-    arrived, (hop, send, index, sem) = rest[:count], rest[count:]
-    fetch = pltpu.make_async_copy(index_in, index, sem)
-    fetch.start()
+    copies[-1].wait()
+
+
+def pick_kernel(count, group, index, *rest):
+    arrived, (hop, send) = rest[:count], rest[count:]
     blocks, _, side = hop.shape
     per = blocks // count
-    me = me_ref[0, 0]
+    me = lax.axis_index("rep")
     for step in range(count):
         first = source(me, step, count) * per
         for part in range(per):
             hop[first + part] = arrived[step][:, part * side : (part + 1) * side]
     stack = jnp.concatenate([hop[block] for block in range(blocks)], 0)
-    fetch.wait()
     store_slots(send, pick(stack, blocks, index[...], side, group), group)
 
 
@@ -208,7 +207,7 @@
     store_slots(send, pick(stack, blocks, index[...], side, group), group)
 
 
-def early_kernel(staged, me_ref, index_in, tiles_in, hop, near, far, total, *rest):
+def early_kernel(staged, index_in, tiles_in, hop, near, far, total, *rest):
     full, index, tiles, sems = rest[-4:]
     blocks, _, side = hop.shape
     copies = [
@@ -227,7 +226,7 @@
     copies[0].wait()
     for peer, part in enumerate(pick(stack, blocks, index[...], side, slot)):
         full[peer] = part
-    me = me_ref[0, 0]
+    me = lax.axis_index("dom")
     half = peers // 2
     for step in range(half):
         near[step] = full[me ^ step]
@@ -241,9 +240,15 @@
         copies[2].wait()
 
 
-def finish(dst, src, tiles, total, hop, arrived, columns, sums):
+def finish(dst_in, src_in, tiles, total, hop, arrived, columns, sums, products, dst, src, sems):
     blocks, channels, side = hop.shape
     fixed = columns.shape[0]
+    copies = [
+        pltpu.make_async_copy(dst_in, dst, sems.at[0]),
+        pltpu.make_async_copy(src_in, src, sems.at[1]),
+    ]
+    for copy in copies:
+        copy.start()
     columns[:, channels:, :] = jnp.ones((fixed, EXTRA, side), BF16)
     for block in range(blocks):
         columns[block, :channels, :] = hop[block]
@@ -252,12 +257,19 @@
     for block in range(blocks, fixed):
         start = (block - blocks) * side
         columns[block, :channels, :] = wide[:, start : start + side]
+    for other in range(fixed - blocks):
+        products[other] = dot(columns[blocks + other], tiles[other], NT)
+    for copy in copies:
+        copy.wait()
     for other in range(tiles.shape[0]):
         slot = blocks + other
         target = dst[0, slot]
         target = jnp.where(target < 0, blocks, target)
-        start = slot if slot < fixed else src[0, slot]
-        sums[target] = sums[target] + dot(columns[start], tiles[other], NT)
+        if slot < fixed:
+            product = products[other]
+        else:
+            product = dot(columns[src[0, slot]], tiles[other], NT)
+        sums[target] = sums[target] + product
     results = []
     for block in range(blocks):
         whole = sums[block]
@@ -268,9 +280,8 @@
 def finish_kernel(
     group, keep, dst, src, index, tiles, total, hop, arrived, *rest
 ):
-    columns, sums = rest[-2:]
-    send = rest[-3]
-    results = finish(dst, src, tiles, total, hop, arrived, columns, sums)
+    send, scratch = rest[keep], rest[keep + 1 :]
+    results = finish(dst, src, tiles, total, hop, arrived, *scratch)
     blocks, _, side = hop.shape
     if keep:
         for block, result in enumerate(results):
@@ -303,13 +314,13 @@
     store_slots(send, pick(stack, blocks, index[...], side, group), group)
 
 
-def place_steps_kernel(peers, side, me_ref, index_ref, *rest):
+def place_steps_kernel(peers, side, index_ref, *rest):
     half = peers // 2
     moved, last, (out_ref, out, sems) = rest[:half], rest[half], rest[half + 1 :]
     hops, channels, nodes = out.shape
     blocks = nodes // side
     slot = nodes // peers
-    me = me_ref[0, 0]
+    me = lax.axis_index("dom")
     parts, indexes = [], []
     for step in range(peers):
         origin = me ^ step
@@ -328,12 +339,14 @@
             )
         )
     block, inner = split(jnp.concatenate(indexes, 1), side, blocks)
-    table = one_hot(inner, side)
+    table = jnp.concatenate(
+        [one_hot(inner[:, start : start + side], side).T for start in range(0, nodes, side)], 0
+    )
     stacked = jnp.concatenate(parts, 1)
     copies = []
     for other in range(blocks):
         mask = jnp.where(block == other, 1.0, 0.0).astype(BF16)
-        placed = dot(stacked * mask, table, NT).astype(BF16)
+        placed = dot(stacked * mask, table).astype(BF16)
         columns = slice(other * side, (other + 1) * side)
         for hop in range(hops):
             out[hop, :, columns] = placed[hop * channels : (hop + 1) * channels]
@@ -376,7 +389,6 @@
     slots, side, _ = tiles.shape
     blocks = nodes // side
     fixed = (nodes + halo) // side
-    me = lax.axis_index("rep").astype(jnp.int32).reshape(1, 1)
     vmem, smem, dma = pltpu.VMEM, pltpu.SMEM, pltpu.SemaphoreType.DMA
     hop_shape = (blocks, channels, side)
     halo_shape = send_shape(channels, peers, halo // peers)
@@ -398,7 +410,7 @@
                 jax.ShapeDtypeStruct((blocks, channels + EXTRA, side), F32),
             )
             + (out(others),) * staged,
-            in_specs=[SMEM, HBM, HBM, VMEM],
+            in_specs=[HBM, HBM, VMEM],
             out_specs=(VMEM,) * (3 + staged),
             scratch_shapes=[
                 vmem((peers, channels, slot), BF16),
@@ -409,7 +421,7 @@
             compiler_params=params(),
             cost_estimate=cost(2 * channels * nodes * nodes, 8 * channels * nodes),
             name="early",
-        )(rank, in_hbm(send_order), in_hbm(tiles), hop)
+        )(in_hbm(send_order), in_hbm(tiles), hop)
         sent = lax.ppermute(far, "dom", pairs(peers // 2, peers))
         return (near, sent), total, rest
 
@@ -418,50 +430,53 @@
         return pl.pallas_call(
             lambda *refs: finish_kernel(group, keep, *refs),
             out_shape=(out(hop_shape),) * keep + (out(shape),),
-            in_specs=[SMEM, SMEM] + [VMEM] * 5,
+            in_specs=[ANY] * 2 + [VMEM] * 5,
             out_specs=(VMEM,) * (keep + 1),
             scratch_shapes=[
                 vmem((fixed, channels + EXTRA, side), BF16),
                 vmem((blocks + 1, channels + EXTRA, side), F32),
+                vmem((fixed - blocks, channels + EXTRA, side), F32),
+                smem(tile_dst.shape, jnp.int32),
+                smem(tile_src.shape, jnp.int32),
+                dma((2,)),
             ],
             compiler_params=params(),
         )(tile_dst, tile_src, index, others, total, hop, arrived)
 
-    own = pl.pallas_call(
+    *own, halo_rows = pl.pallas_call(
         lambda *refs: sketch_kernel(reps, chunks, *refs),
-        out_shape=(out((channels, width)),) * reps,
-        in_specs=[SMEM, HBM, HBM],
-        out_specs=(VMEM,) * reps,
+        out_shape=(out((channels, width)),) * reps
+        + (jax.ShapeDtypeStruct(halo_index.shape, jnp.int32),),
+        in_specs=[HBM] * 3,
+        out_specs=(VMEM,) * (reps + 1),
         scratch_shapes=[
             vmem((reps, channels, width), BF16),
             vmem(features.shape, BF16),
             vmem(sketch_matrix.shape, BF16),
-            dma((chunks + 1,)),
+            dma((chunks + 2,)),
         ],
         compiler_params=params(),
         name="sketch",
-    )(me, in_hbm(features), in_hbm(sketch_matrix))
+    )(in_hbm(features), in_hbm(sketch_matrix), in_hbm(halo_index))
     arrived = [own[0]]
     for step in range(1, reps):
         arrived.append(lax.ppermute(own[step], "rep", pairs(step, reps)))
     hop0, send = pl.pallas_call(
         lambda *refs: pick_kernel(reps, group, *refs),
         out_shape=(out(hop_shape), out(halo_shape)),
-        in_specs=[SMEM, HBM] + [VMEM] * reps,
+        in_specs=[VMEM] * (reps + 1),
         out_specs=(VMEM, VMEM),
-        scratch_shapes=[vmem(halo_index.shape, jnp.int32), dma],
         compiler_params=params(),
         name="pick",
-    )(me, in_hbm(halo_index), *arrived)
+    )(halo_rows, *arrived)
     slot = nodes // peers
     whole_lanes = slot % 128 == 0 and (halo // peers) % 128 == 0
     if whole_lanes and peers > 1 and peers & (peers - 1) == 0:
         half = peers // 2
-        rank = lax.axis_index("dom").astype(jnp.int32).reshape(1, 1)
         halo0 = exchange(send, peers)
         early0, total, others = early(hop0, 1)
         others = others[0]
-        hop1, send = late(1, halo_index, others, total, hop0, halo0)
+        hop1, send = late(1, halo_rows, others, total, hop0, halo0)
         halo1 = exchange(send, peers)
         early1, total, _ = early(hop1, 0)
         (send,) = late(0, send_order, others, total, hop1, halo1)
@@ -481,12 +496,12 @@
         return pl.pallas_call(
             lambda *refs: place_steps_kernel(peers, side, *refs),
             out_shape=out((3, channels, nodes)),
-            in_specs=[SMEM, VMEM] + [VMEM] * (half + 1),
+            in_specs=[VMEM] * (half + 2),
             out_specs=HBM,
             scratch_shapes=[vmem((3, channels, nodes), BF16), dma((blocks,))],
             compiler_params=params(),
             name="place",
-        )(rank, arrival_place, *moved, last)
+        )(arrival_place, *moved, last)
     halo0 = exchange(send, peers)
 
     def work(index):

time: 74 us -> 72.3 us (0.977)
  Pallas kernels: 16.8 us -> 15 us
    pallas_call x1, Pallas kernels: 3.65 us -> 2.64 us  [on_device(): pl.pallas_call(lambda *refs: place_steps_kernel(peers, side, *refs), out_...]
  transfers between devices with their start and end apart: 11 -> 11, of which waited for: 9 -> 9; matrix products, arithmetic and copies ran while one was open for 0% -> 0% of each run, Pallas kernels for 5% -> 6%
where the time goes in v7:
time: 72.3 us; the launch traced here: 71.7 us
  waiting for transfers between devices  34.2 us (47%)
  starting transfers between devices  22.3 us (31%)
  Pallas kernels  15 us (21%)
    ppermute x2, waiting for transfers between devices, early(): sent = lax.ppermute(far, 'dom', pairs(peers // 2, peers))  15.1 us
    all_to_all x3, starting transfers between devices, exchange(): arrived = lax.all_to_all(send, 'dom', 0, 0, tiled=True)  12.6 us
    all_to_all x3, waiting for transfers between devices, exchange(): arrived = lax.all_to_all(send, 'dom', 0, 0, tiled=True)  10.6 us
    pallas_call x2, Pallas kernels, late(): pl.pallas_call(lambda *refs: finish_kernel(group, keep, *refs), out_shape...  4.84 us
    ppermute x3, waiting for transfers between devices, on_device(): lax.ppermute(moved[step], 'dom', pairs(step, peers))  4.44 us
    ppermute x3, waiting for transfers between devices, on_device(): arrived.append(lax.ppermute(own[step], 'rep', pairs(step, reps)))  4.02 us
    pallas_call x2, Pallas kernels, early(): pl.pallas_call(lambda *refs: early_kernel(staged, *refs), out_shape=(out(...  3.96 us
    ppermute x3, starting transfers between devices, on_device(): lax.ppermute(moved[step], 'dom', pairs(step, peers))  3.55 us
  transfers between devices with their start and end apart: 11, of which 9 were waited for; matrix products, arithmetic and copies ran while one was open for 0% of the time, Pallas kernels for 6%

profile of v7, /device:TPU:0, one launch (start us, length us, event | category | flops | bytes accessed | tf_op | source)
XLA Modules:
  0.0 71.7 jit_solution(10353916268640976173)
XLA Ops:
  0.0 0.0 copy-start.3
  0.0 0.0 copy-start.2
  0.0 2.4 %sketch.1 = (bf16[64,512]{1,0:T(8,128)(2,1)S(1)}, bf16[64,512]{1,0:T(8,128)(2,1)S(1)}, bf16[64,512]{1,0:T(8,128)(2,1)S(1)}, bf16[64,512]{1,0:T(8,128)(2,1)S(1)}, s32[1,1024]{1,0:T(1,128)S(1)}) custom-call(bf16[512,768]{1,0:T(8,128)(2,1)} %refs_0_.6, bf16[768,256]{1,0:T(8,128)(2,1)} %refs_1_.3, s32[1,1024]{1,0:T(1,128)} %refs_2_.2), custom_call_target="tpu_custom_call" | custom-call | tf_op jit(solution)/shard_map/sketch/pallas_call | solution.py:446
  2.5 0.6 collective-permute-start
  3.0 2.5 %collective-permute-start.1 = (bf16[64,512]{1,0:T(8,128)(2,1)S(1)}, bf16[64,512]{1,0:T(8,128)(2,1)S(1)}, u32[]{:S(2)}, u32[]{:S(2)}) collective-permute-start(bf16[64,512]{1,0:T(8,128)(2,1)S(1)} %get-tuple-element.28), channel_id=1, source_target_pairs={{0,2},{1,3},{2,0},{3,1},{4,6},{5,7},{6,4},{7,5},{8,10},{9,11},{10,... | collective-permute-start | bytes 196616 | tf_op jit(solution)/shard_map/ppermute | solution.py:463
  5.6 0.0 collective-permute-start.2
  5.6 0.0 collective-permute-done.refs_2_
  5.6 2.6 %collective-permute-done.1.refs_3_ = bf16[64,512]{1,0:T(8,128)(2,1)S(1)} collective-permute-done((bf16[64,512]{1,0:T(8,128)(2,1)S(1)}, bf16[64,512]{1,0:T(8,128)(2,1)S(1)}, u32[]{:S(2)}, u32[]{:S(2)}) %collective-permute-start.1) | collective-permute-done | bytes 65568 | tf_op jit(solution)/shard_map/ppermute | solution.py:463
  8.2 1.4 %collective-permute-done.2.refs_4_ = bf16[64,512]{1,0:T(8,128)(2,1)S(1)} collective-permute-done((bf16[64,512]{1,0:T(8,128)(2,1)S(1)}, bf16[64,512]{1,0:T(8,128)(2,1)S(1)}, u32[]{:S(2)}, u32[]{:S(2)}) %collective-permute-start.2) | collective-permute-done | bytes 65568 | tf_op jit(solution)/shard_map/ppermute | solution.py:463
  9.6 1.1 %pick.1 = (bf16[8,64,256]{2,1,0:T(8,128)(2,1)S(1)}, bf16[8,64,128]{2,1,0:T(8,128)(2,1)}) custom-call(s32[1,1024]{1,0:T(1,128)S(1)} %get-tuple-element.25.refs_0_.refs_2_, bf16[64,512]{1,0:T(8,128)(2,1)S(1)} %get-tuple-element.26.refs_1_, bf16[64,512]{1,0:T(8,128)(2,1)S(1)} %collective-permute-done.refs_2_, ...), custom_call_target="tpu_custom_call" | custom-call | tf_op jit(solution)/shard_map/pick/pallas_call | solution.py:464
  10.7 5.8 %all-to-all-start = ((bf16[8,64,128]{2,1,0:T(8,128)(2,1)}), bf16[8,64,128]{2,1,0:T(8,128)(2,1)S(1)}, u32[]{:S(2)}, u32[]{:S(2)}) async-start(bf16[8,64,128]{2,1,0:T(8,128)(2,1)} %get-tuple-element.35), calls=%async_computation | async-start | bytes 262144 | tf_op jit(solution)/shard_map/all_to_all | solution.py:80
  16.6 2.0 %early.2 = (bf16[4,64,256]{2,1,0:T(8,128)(2,1)S(1)}, bf16[4,64,256]{2,1,0:T(8,128)(2,1)S(1)}, f32[8,80,256]{2,1,0:T(8,128)S(1)}, bf16[12,256,256]{2,1,0:T(8,128)(2,1)S(1)}) custom-call(s32[1,2048]{1,0:T(1,128)} %refs_2_.3, bf16[20,256,256]{2,1,0:T(8,128)(2,1)} %bitcast.1, bf16[8,64,256]{2,1,0:T(8,128)(2,1)S(1)} %get-tuple-element.30.refs_2_.refs_5_), custom_call_target="tpu_custom_call" | custom-call | flops 536870912 | bytes 1048576 | tf_op jit(solution)/shard_map/early/pallas_call | solution.py:405
  18.6 5.4 %all-to-all-done.refs_6_ = bf16[8,64,128]{2,1,0:T(8,128)(2,1)S(1)} async-done(((bf16[8,64,128]{2,1,0:T(8,128)(2,1)}), bf16[8,64,128]{2,1,0:T(8,128)(2,1)S(1)}, u32[]{:S(2)}, u32[]{:S(2)}) %all-to-all-start) | async-done | bytes 131104 | tf_op jit(solution)/shard_map/all_to_all | solution.py:80
  23.9 0.0 copy-done.3
  23.9 0.0 copy-done.2
  23.9 0.0 copy-start
  23.9 2.2 %shard_map.82 = (bf16[8,64,256]{2,1,0:T(8,128)(2,1)S(1)}, bf16[8,64,128]{2,1,0:T(8,128)(2,1)}) custom-call(s32[1,20]{1,0:T(1,128)S(1)} %copy-done.2, s32[1,20]{1,0:T(1,128)S(1)} %copy-done.3, s32[1,1024]{1,0:T(1,128)S(1)} %get-tuple-element.25.refs_0_.refs_2_, bf16[12,256,256]{2,1,0:T(8,128)(2,1)S(1)} %get-tuple-element.33.refs_3_, ...), custom_call_target="tpu_custom_call" | custom-call | tf_op jit(solution)/shard_map/pallas_call | solution.py:430
  26.2 3.4 %all-to-all-start.1 = ((bf16[8,64,128]{2,1,0:T(8,128)(2,1)}), bf16[8,64,128]{2,1,0:T(8,128)(2,1)S(1)}, u32[]{:S(2)}, u32[]{:S(2)}) async-start(bf16[8,64,128]{2,1,0:T(8,128)(2,1)} %get-tuple-element.44), calls=%async_computation.1 | async-start | bytes 262144 | tf_op jit(solution)/shard_map/all_to_all | solution.py:80
  29.6 2.0 %early.3 = (bf16[4,64,256]{2,1,0:T(8,128)(2,1)S(1)}, bf16[4,64,256]{2,1,0:T(8,128)(2,1)S(1)}, f32[8,80,256]{2,1,0:T(8,128)S(1)}) custom-call(s32[1,2048]{1,0:T(1,128)} %refs_2_.3, bf16[20,256,256]{2,1,0:T(8,128)(2,1)} %bitcast.2, bf16[8,64,256]{2,1,0:T(8,128)(2,1)S(1)} %get-tuple-element.36.refs_2_.refs_5_), custom_call_target="tpu_custom_call" | custom-call | flops 536870912 | bytes 1048576 | tf_op jit(solution)/shard_map/early/pallas_call | solution.py:405
  31.6 0.0 copy-start.1
  31.6 5.3 %all-to-all-done.1.refs_6_ = bf16[8,64,128]{2,1,0:T(8,128)(2,1)S(1)} async-done(((bf16[8,64,128]{2,1,0:T(8,128)(2,1)}), bf16[8,64,128]{2,1,0:T(8,128)(2,1)S(1)}, u32[]{:S(2)}, u32[]{:S(2)}) %all-to-all-start.1) | async-done | bytes 131104 | tf_op jit(solution)/shard_map/all_to_all | solution.py:80
  36.8 0.0 copy-done
  36.9 2.6 %shard_map.83 = bf16[8,64,256]{2,1,0:T(8,128)(2,1)} custom-call(s32[1,20]{1,0:T(1,128)S(1)} %copy-done.2, s32[1,20]{1,0:T(1,128)S(1)} %copy-done.3, s32[1,2048]{1,0:T(1,128)S(1)} %copy-done, bf16[12,256,256]{2,1,0:T(8,128)(2,1)S(1)} %get-tuple-element.33.refs_3_, f32[8,80,256]{2,1,0:T(8,128)S(1)} %get-tuple-element.43.refs_4_, ...), custom_call_target="tpu_custom_call" | custom-call | tf_op jit(solution)/shard_map/pallas_call | solution.py:430
  39.5 3.4 %all-to-all-start.2 = ((bf16[8,64,256]{2,1,0:T(8,128)(2,1)}), bf16[8,64,256]{2,1,0:T(8,128)(2,1)S(1)}, u32[]{:S(2)}, u32[]{:S(2)}) async-start(bf16[8,64,256]{2,1,0:T(8,128)(2,1)} %shard_map.83), calls=%async_computation.2 | async-start | bytes 524288 | tf_op jit(solution)/shard_map/all_to_all | solution.py:80
  42.9 2.8 %collective-permute-start.3 = (bf16[4,64,256]{2,1,0:T(8,128)(2,1)S(1)}, bf16[4,64,256]{2,1,0:T(8,128)(2,1)S(1)}, u32[]{:S(2)}, u32[]{:S(2)}) collective-permute-start(bf16[4,64,256]{2,1,0:T(8,128)(2,1)S(1)} %get-tuple-element.32), channel_id=1, source_target_pairs={{0,16},{4,20},{8,24},{12,28},{16,0},{20,4},{24,8},{28,12},{1,17},{... | collective-permute-start | bytes 393224 | tf_op jit(solution)/shard_map/ppermute | solution.py:425
  45.7 0.2 collective-permute-start.4
  45.9 13.7 %collective-permute-done.3.refs_1_ = bf16[4,64,256]{2,1,0:T(8,128)(2,1)S(1)} collective-permute-done((bf16[4,64,256]{2,1,0:T(8,128)(2,1)S(1)}, bf16[4,64,256]{2,1,0:T(8,128)(2,1)S(1)}, u32[]{:S(2)}, u32[]{:S(2)}) %collective-permute-start.3) | collective-permute-done | bytes 131104 | tf_op jit(solution)/shard_map/ppermute | solution.py:425
  59.6 1.4 %collective-permute-done.4.refs_3_ = bf16[4,64,256]{2,1,0:T(8,128)(2,1)S(1)} collective-permute-done((bf16[4,64,256]{2,1,0:T(8,128)(2,1)S(1)}, bf16[4,64,256]{2,1,0:T(8,128)(2,1)S(1)}, u32[]{:S(2)}, u32[]{:S(2)}) %collective-permute-start.4) | collective-permute-done | bytes 131104 | tf_op jit(solution)/shard_map/ppermute | solution.py:425
  61.1 1.5 %collective-permute-start.5 = (bf16[256,256]{1,0:T(8,128)(2,1)S(1)}, bf16[256,256]{1,0:T(8,128)(2,1)S(1)}, u32[]{:S(2)}, u32[]{:S(2)}) collective-permute-start(bf16[256,256]{1,0:T(8,128)(2,1)S(1)} %get-tuple-element.40), channel_id=1, source_target_pairs={{0,4},{4,0},{8,12},{12,8},{16,20},{20,16},{24,28},{28,24},{1,5},{5... | collective-permute-start | bytes 393224 | tf_op jit(solution)/shard_map/ppermute | solution.py:494
  62.6 0.0 collective-permute-start.6
  62.6 2.0 %collective-permute-start.7 = (bf16[256,256]{1,0:T(8,128)(2,1)S(1)}, bf16[256,256]{1,0:T(8,128)(2,1)S(1)}, u32[]{:S(2)}, u32[]{:S(2)}) collective-permute-start(bf16[256,256]{1,0:T(8,128)(2,1)S(1)} %get-tuple-element.42), channel_id=1, source_target_pairs={{0,12},{4,8},{8,4},{12,0},{16,28},{20,24},{24,20},{28,16},{1,13},{... | collective-permute-start | bytes 393224 | tf_op jit(solution)/shard_map/ppermute | solution.py:494
  64.6 2.9 %collective-permute-done.5.refs_2_ = bf16[256,256]{1,0:T(8,128)(2,1)S(1)} collective-permute-done((bf16[256,256]{1,0:T(8,128)(2,1)S(1)}, bf16[256,256]{1,0:T(8,128)(2,1)S(1)}, u32[]{:S(2)}, u32[]{:S(2)}) %collective-permute-start.5) | collective-permute-done | bytes 131104 | tf_op jit(solution)/shard_map/ppermute | solution.py:494
  67.5 0.2 collective-permute-done.6.refs_3_
  67.7 1.4 %collective-permute-done.7.refs_4_ = bf16[256,256]{1,0:T(8,128)(2,1)S(1)} collective-permute-done((bf16[256,256]{1,0:T(8,128)(2,1)S(1)}, bf16[256,256]{1,0:T(8,128)(2,1)S(1)}, u32[]{:S(2)}, u32[]{:S(2)}) %collective-permute-start.7) | collective-permute-done | bytes 131104 | tf_op jit(solution)/shard_map/ppermute | solution.py:494
  69.1 0.0 all-to-all-done.2.refs_5_
  69.1 0.0 copy-done.1
  69.1 2.6 %place.1 = bf16[3,64,2048]{2,1,0:T(8,128)(2,1)} custom-call(s32[1,2048]{1,0:T(1,128)S(1)} %copy-done.1, bf16[256,256]{1,0:T(8,128)(2,1)S(1)} %get-tuple-element.39.refs_1_, bf16[256,256]{1,0:T(8,128)(2,1)S(1)} %collective-permute-done.5.refs_2_, bf16[256,256]{1,0:T(8,128)(2,1)S(1)} %collective-permute-done.6.refs_3_, ...), custom_call_target="tpu_custom_call" | custom-call | tf_op jit(solution)/shard_map/place/pallas_call | solution.py:496
  (1 shorter events, 0.0 us)
Async XLA Ops:
  0.0 23.9 %copy-start.3 = (s32[1,20]{1,0:T(1,128)S(1)}, s32[1,20]{1,0:T(1,128)}, u32[]{:S(2)}) copy-start(s32[1,20]{1,0:T(1,128)} %refs_1_.5) | copy-start | bytes 244
  0.0 23.9 %copy-start.2 = (s32[1,20]{1,0:T(1,128)S(1)}, s32[1,20]{1,0:T(1,128)}, u32[]{:S(2)}) copy-start(s32[1,20]{1,0:T(1,128)} %refs_0_.10) | copy-start | bytes 244
  2.5 3.2 %collective-permute-start = (bf16[64,512]{1,0:T(8,128)(2,1)S(1)}, bf16[64,512]{1,0:T(8,128)(2,1)S(1)}, u32[]{:S(2)}, u32[]{:S(2)}) collective-permute-start(bf16[64,512]{1,0:T(8,128)(2,1)S(1)} %get-tuple-element.27), channel_id=1, source_target_pairs={{0,1},{1,0},{2,3},{3,2},{4,5},{5,4},{6,7},{7,6},{8,9},{9,8},{10,11... | collective-permute-start | bytes 196616 | tf_op jit(solution)/shard_map/ppermute | solution.py:463
  3.0 5.2 %collective-permute-start.1 = (bf16[64,512]{1,0:T(8,128)(2,1)S(1)}, bf16[64,512]{1,0:T(8,128)(2,1)S(1)}, u32[]{:S(2)}, u32[]{:S(2)}) collective-permute-start(bf16[64,512]{1,0:T(8,128)(2,1)S(1)} %get-tuple-element.28), channel_id=1, source_target_pairs={{0,2},{1,3},{2,0},{3,1},{4,6},{5,7},{6,4},{7,5},{8,10},{9,11},{10,... | collective-permute-start | bytes 196616 | tf_op jit(solution)/shard_map/ppermute | solution.py:463
  5.6 4.1 %collective-permute-start.2 = (bf16[64,512]{1,0:T(8,128)(2,1)S(1)}, bf16[64,512]{1,0:T(8,128)(2,1)S(1)}, u32[]{:S(2)}, u32[]{:S(2)}) collective-permute-start(bf16[64,512]{1,0:T(8,128)(2,1)S(1)} %get-tuple-element.29), channel_id=1, source_target_pairs={{0,3},{1,2},{2,1},{3,0},{4,7},{5,6},{6,5},{7,4},{8,11},{9,10},{10,... | collective-permute-start | bytes 196616 | tf_op jit(solution)/shard_map/ppermute | solution.py:463
  10.7 13.2 %all-to-all-start = ((bf16[8,64,128]{2,1,0:T(8,128)(2,1)}), bf16[8,64,128]{2,1,0:T(8,128)(2,1)S(1)}, u32[]{:S(2)}, u32[]{:S(2)}) async-start(bf16[8,64,128]{2,1,0:T(8,128)(2,1)} %get-tuple-element.35), calls=%async_computation | async-start | bytes 262144 | tf_op jit(solution)/shard_map/all_to_all | solution.py:80
  23.9 12.9 %copy-start = (s32[1,2048]{1,0:T(1,128)S(1)}, s32[1,2048]{1,0:T(1,128)}, u32[]{:S(2)}) copy-start(s32[1,2048]{1,0:T(1,128)} %refs_2_.3) | copy-start | bytes 24580
  26.2 10.7 %all-to-all-start.1 = ((bf16[8,64,128]{2,1,0:T(8,128)(2,1)}), bf16[8,64,128]{2,1,0:T(8,128)(2,1)S(1)}, u32[]{:S(2)}, u32[]{:S(2)}) async-start(bf16[8,64,128]{2,1,0:T(8,128)(2,1)} %get-tuple-element.44), calls=%async_computation.1 | async-start | bytes 262144 | tf_op jit(solution)/shard_map/all_to_all | solution.py:80
  31.6 37.5 %copy-start.1 = (s32[1,2048]{1,0:T(1,128)S(1)}, s32[1,2048]{1,0:T(1,128)}, u32[]{:S(2)}) copy-start(s32[1,2048]{1,0:T(1,128)} %refs_0_.11) | copy-start | bytes 24580
  39.5 29.6 %all-to-all-start.2 = ((bf16[8,64,256]{2,1,0:T(8,128)(2,1)}), bf16[8,64,256]{2,1,0:T(8,128)(2,1)S(1)}, u32[]{:S(2)}, u32[]{:S(2)}) async-start(bf16[8,64,256]{2,1,0:T(8,128)(2,1)} %shard_map.83), calls=%async_computation.2 | async-start | bytes 524288 | tf_op jit(solution)/shard_map/all_to_all | solution.py:80
  42.9 16.7 %collective-permute-start.3 = (bf16[4,64,256]{2,1,0:T(8,128)(2,1)S(1)}, bf16[4,64,256]{2,1,0:T(8,128)(2,1)S(1)}, u32[]{:S(2)}, u32[]{:S(2)}) collective-permute-start(bf16[4,64,256]{2,1,0:T(8,128)(2,1)S(1)} %get-tuple-element.32), channel_id=1, source_target_pairs={{0,16},{4,20},{8,24},{12,28},{16,0},{20,4},{24,8},{28,12},{1,17},{... | collective-permute-start | bytes 393224 | tf_op jit(solution)/shard_map/ppermute | solution.py:425
  45.7 15.3 %collective-permute-start.4 = (bf16[4,64,256]{2,1,0:T(8,128)(2,1)S(1)}, bf16[4,64,256]{2,1,0:T(8,128)(2,1)S(1)}, u32[]{:S(2)}, u32[]{:S(2)}) collective-permute-start(bf16[4,64,256]{2,1,0:T(8,128)(2,1)S(1)} %get-tuple-element.38), channel_id=1, source_target_pairs={{0,16},{4,20},{8,24},{12,28},{16,0},{20,4},{24,8},{28,12},{1,17},{... | collective-permute-start | bytes 393224 | tf_op jit(solution)/shard_map/ppermute | solution.py:425
  61.1 6.4 %collective-permute-start.5 = (bf16[256,256]{1,0:T(8,128)(2,1)S(1)}, bf16[256,256]{1,0:T(8,128)(2,1)S(1)}, u32[]{:S(2)}, u32[]{:S(2)}) collective-permute-start(bf16[256,256]{1,0:T(8,128)(2,1)S(1)} %get-tuple-element.40), channel_id=1, source_target_pairs={{0,4},{4,0},{8,12},{12,8},{16,20},{20,16},{24,28},{28,24},{1,5},{5... | collective-permute-start | bytes 393224 | tf_op jit(solution)/shard_map/ppermute | solution.py:494
  62.6 5.1 %collective-permute-start.6 = (bf16[256,256]{1,0:T(8,128)(2,1)S(1)}, bf16[256,256]{1,0:T(8,128)(2,1)S(1)}, u32[]{:S(2)}, u32[]{:S(2)}) collective-permute-start(bf16[256,256]{1,0:T(8,128)(2,1)S(1)} %get-tuple-element.41), channel_id=1, source_target_pairs={{0,8},{4,12},{8,0},{12,4},{16,24},{20,28},{24,16},{28,20},{1,9},{5... | collective-permute-start | bytes 393224 | tf_op jit(solution)/shard_map/ppermute | solution.py:494
  62.6 6.5 %collective-permute-start.7 = (bf16[256,256]{1,0:T(8,128)(2,1)S(1)}, bf16[256,256]{1,0:T(8,128)(2,1)S(1)}, u32[]{:S(2)}, u32[]{:S(2)}) collective-permute-start(bf16[256,256]{1,0:T(8,128)(2,1)S(1)} %get-tuple-element.42), channel_id=1, source_target_pairs={{0,12},{4,8},{8,4},{12,0},{16,28},{20,24},{24,20},{28,16},{1,13},{... | collective-permute-start | bytes 393224 | tf_op jit(solution)/shard_map/ppermute | solution.py:494

commit v8 on v7

--- a/solution.py
+++ b/solution.py
@@ -13,7 +13,6 @@
 NT = (((1,), (1,)), ((), ()))
 VMEM = pl.BlockSpec(memory_space=pltpu.VMEM)
 HBM = pl.BlockSpec(memory_space=pltpu.HBM)
-ANY = pl.BlockSpec(memory_space=pl.ANY)
 
 
 def params():
@@ -240,15 +239,17 @@
         copies[2].wait()
 
 
-def finish(dst_in, src_in, tiles, total, hop, arrived, columns, sums, products, dst, src, sems):
+def finish(dst, src, tiles, total, hop, arrived, columns, sums):
     blocks, channels, side = hop.shape
     fixed = columns.shape[0]
-    copies = [
-        pltpu.make_async_copy(dst_in, dst, sems.at[0]),
-        pltpu.make_async_copy(src_in, src, sems.at[1]),
-    ]
-    for copy in copies:
-        copy.start()
+    slots = blocks + tiles.shape[0]
+    lane = lax.broadcasted_iota(jnp.int32, dst.shape, 1)
+    targets, starts = {}, {slot: slot for slot in range(fixed)}
+    for slot in range(blocks, slots):
+        target = jnp.sum(jnp.where(lane == slot, dst[...], 0))
+        targets[slot] = jnp.where(target < 0, blocks, target)
+    for slot in range(fixed, slots):
+        starts[slot] = jnp.sum(jnp.where(lane == slot, src[...], 0))
     columns[:, channels:, :] = jnp.ones((fixed, EXTRA, side), BF16)
     for block in range(blocks):
         columns[block, :channels, :] = hop[block]
@@ -257,18 +258,15 @@
     for block in range(blocks, fixed):
         start = (block - blocks) * side
         columns[block, :channels, :] = wide[:, start : start + side]
-    for other in range(fixed - blocks):
-        products[other] = dot(columns[blocks + other], tiles[other], NT)
-    for copy in copies:
-        copy.wait()
-    for other in range(tiles.shape[0]):
-        slot = blocks + other
-        target = dst[0, slot]
-        target = jnp.where(target < 0, blocks, target)
+    products = [
+        dot(columns[starts[slot]], tiles[slot - blocks], NT) for slot in range(blocks, fixed)
+    ]
+    for slot in range(blocks, slots):
+        target = targets[slot]
         if slot < fixed:
-            product = products[other]
+            product = products[slot - blocks]
         else:
-            product = dot(columns[src[0, slot]], tiles[other], NT)
+            product = dot(columns[starts[slot]], tiles[slot - blocks], NT)
         sums[target] = sums[target] + product
     results = []
     for block in range(blocks):
@@ -394,7 +392,7 @@
     halo_shape = send_shape(channels, peers, halo // peers)
     last_shape = send_shape(3 * channels, peers, nodes // peers)
     group = 256
-    chunks = 4
+    chunks = 1
 
     def out(shape):
         return jax.ShapeDtypeStruct(shape, BF16)
@@ -430,15 +428,11 @@
         return pl.pallas_call(
             lambda *refs: finish_kernel(group, keep, *refs),
             out_shape=(out(hop_shape),) * keep + (out(shape),),
-            in_specs=[ANY] * 2 + [VMEM] * 5,
+            in_specs=[VMEM] * 7,
             out_specs=(VMEM,) * (keep + 1),
             scratch_shapes=[
                 vmem((fixed, channels + EXTRA, side), BF16),
                 vmem((blocks + 1, channels + EXTRA, side), F32),
-                vmem((fixed - blocks, channels + EXTRA, side), F32),
-                smem(tile_dst.shape, jnp.int32),
-                smem(tile_src.shape, jnp.int32),
-                dma((2,)),
             ],
             compiler_params=params(),
         )(tile_dst, tile_src, index, others, total, hop, arrived)

time: 72.3 us -> 70.6 us (0.976)
  Pallas kernels: 15 us -> 13.4 us
    pallas_call x2, Pallas kernels: 4.84 us -> 3.89 us  [late(): pl.pallas_call(lambda *refs: finish_kernel(group, keep, *refs), out_shape...]
where the time goes in v8:
time: 70.6 us; the launch traced here: 70 us
  waiting for transfers between devices  34.2 us (48%)
  starting transfers between devices  22.3 us (32%)
  Pallas kernels  13.4 us (19%)
    ppermute x2, waiting for transfers between devices, early(): sent = lax.ppermute(far, 'dom', pairs(peers // 2, peers))  15.1 us
    all_to_all x3, starting transfers between devices, exchange(): arrived = lax.all_to_all(send, 'dom', 0, 0, tiled=True)  12.6 us
    all_to_all x3, waiting for transfers between devices, exchange(): arrived = lax.all_to_all(send, 'dom', 0, 0, tiled=True)  10.6 us
    ppermute x3, waiting for transfers between devices, on_device(): lax.ppermute(moved[step], 'dom', pairs(step, peers))  4.44 us
    ppermute x3, waiting for transfers between devices, on_device(): arrived.append(lax.ppermute(own[step], 'rep', pairs(step, reps)))  4.02 us
    pallas_call x2, Pallas kernels, early(): pl.pallas_call(lambda *refs: early_kernel(staged, *refs), out_shape=(out(...  3.96 us
    pallas_call x2, Pallas kernels, late(): pl.pallas_call(lambda *refs: finish_kernel(group, keep, *refs), out_shape...  3.89 us
    ppermute x3, starting transfers between devices, on_device(): lax.ppermute(moved[step], 'dom', pairs(step, peers))  3.55 us
  transfers between devices with their start and end apart: 11, of which 9 were waited for; matrix products, arithmetic and copies ran while one was open for 0% of the time, Pallas kernels for 6%

profile of v8, /device:TPU:0, one launch (start us, length us, event | category | flops | bytes accessed | tf_op | source)
XLA Modules:
  0.0 70.0 jit_solution(6711539933086754940)
XLA Ops:
  0.0 0.0 copy-start.3
  0.0 0.0 copy-start.2
  0.0 1.8 %sketch.1 = (bf16[64,512]{1,0:T(8,128)(2,1)S(1)}, bf16[64,512]{1,0:T(8,128)(2,1)S(1)}, bf16[64,512]{1,0:T(8,128)(2,1)S(1)}, bf16[64,512]{1,0:T(8,128)(2,1)S(1)}, s32[1,1024]{1,0:T(1,128)S(1)}) custom-call(bf16[512,768]{1,0:T(8,128)(2,1)} %refs_0_.6, bf16[768,256]{1,0:T(8,128)(2,1)} %refs_1_.3, s32[1,1024]{1,0:T(1,128)} %refs_2_.2), custom_call_target="tpu_custom_call" | custom-call | tf_op jit(solution)/shard_map/sketch/pallas_call | solution.py:440
  1.8 0.6 collective-permute-start
  2.4 2.5 %collective-permute-start.1 = (bf16[64,512]{1,0:T(8,128)(2,1)S(1)}, bf16[64,512]{1,0:T(8,128)(2,1)S(1)}, u32[]{:S(2)}, u32[]{:S(2)}) collective-permute-start(bf16[64,512]{1,0:T(8,128)(2,1)S(1)} %get-tuple-element.28), channel_id=1, source_target_pairs={{0,2},{1,3},{2,0},{3,1},{4,6},{5,7},{6,4},{7,5},{8,10},{9,11},{10,... | collective-permute-start | bytes 196616 | tf_op jit(solution)/shard_map/ppermute | solution.py:457
  4.9 0.0 collective-permute-start.2
  4.9 0.0 collective-permute-done.refs_2_
  4.9 2.6 %collective-permute-done.1.refs_3_ = bf16[64,512]{1,0:T(8,128)(2,1)S(1)} collective-permute-done((bf16[64,512]{1,0:T(8,128)(2,1)S(1)}, bf16[64,512]{1,0:T(8,128)(2,1)S(1)}, u32[]{:S(2)}, u32[]{:S(2)}) %collective-permute-start.1) | collective-permute-done | bytes 65568 | tf_op jit(solution)/shard_map/ppermute | solution.py:457
  7.6 1.4 %collective-permute-done.2.refs_4_ = bf16[64,512]{1,0:T(8,128)(2,1)S(1)} collective-permute-done((bf16[64,512]{1,0:T(8,128)(2,1)S(1)}, bf16[64,512]{1,0:T(8,128)(2,1)S(1)}, u32[]{:S(2)}, u32[]{:S(2)}) %collective-permute-start.2) | collective-permute-done | bytes 65568 | tf_op jit(solution)/shard_map/ppermute | solution.py:457
  9.0 1.1 %pick.1 = (bf16[8,64,256]{2,1,0:T(8,128)(2,1)S(1)}, bf16[8,64,128]{2,1,0:T(8,128)(2,1)}) custom-call(s32[1,1024]{1,0:T(1,128)S(1)} %get-tuple-element.25.refs_0_.refs_2_, bf16[64,512]{1,0:T(8,128)(2,1)S(1)} %get-tuple-element.26.refs_1_, bf16[64,512]{1,0:T(8,128)(2,1)S(1)} %collective-permute-done.refs_2_, ...), custom_call_target="tpu_custom_call" | custom-call | tf_op jit(solution)/shard_map/pick/pallas_call | solution.py:458
  10.1 5.8 %all-to-all-start = ((bf16[8,64,128]{2,1,0:T(8,128)(2,1)}), bf16[8,64,128]{2,1,0:T(8,128)(2,1)S(1)}, u32[]{:S(2)}, u32[]{:S(2)}) async-start(bf16[8,64,128]{2,1,0:T(8,128)(2,1)} %get-tuple-element.35), calls=%async_computation | async-start | bytes 262144 | tf_op jit(solution)/shard_map/all_to_all | solution.py:79
  15.9 2.0 %early.2 = (bf16[4,64,256]{2,1,0:T(8,128)(2,1)S(1)}, bf16[4,64,256]{2,1,0:T(8,128)(2,1)S(1)}, f32[8,80,256]{2,1,0:T(8,128)S(1)}, bf16[12,256,256]{2,1,0:T(8,128)(2,1)S(1)}) custom-call(s32[1,2048]{1,0:T(1,128)} %refs_2_.3, bf16[20,256,256]{2,1,0:T(8,128)(2,1)} %bitcast.1, bf16[8,64,256]{2,1,0:T(8,128)(2,1)S(1)} %get-tuple-element.30.refs_2_.refs_5_), custom_call_target="tpu_custom_call" | custom-call | flops 536870912 | bytes 1048576 | tf_op jit(solution)/shard_map/early/pallas_call | solution.py:403
  17.9 5.4 %all-to-all-done.refs_6_ = bf16[8,64,128]{2,1,0:T(8,128)(2,1)S(1)} async-done(((bf16[8,64,128]{2,1,0:T(8,128)(2,1)}), bf16[8,64,128]{2,1,0:T(8,128)(2,1)S(1)}, u32[]{:S(2)}, u32[]{:S(2)}) %all-to-all-start) | async-done | bytes 131104 | tf_op jit(solution)/shard_map/all_to_all | solution.py:79
  23.3 0.0 copy-done.3
  23.3 0.0 copy-done.2
  23.3 0.0 copy-start
  23.3 1.8 %shard_map.82 = (bf16[8,64,256]{2,1,0:T(8,128)(2,1)S(1)}, bf16[8,64,128]{2,1,0:T(8,128)(2,1)}) custom-call(s32[1,20]{1,0:T(1,128)S(1)} %copy-done.2, s32[1,20]{1,0:T(1,128)S(1)} %copy-done.3, s32[1,1024]{1,0:T(1,128)S(1)} %get-tuple-element.25.refs_0_.refs_2_, bf16[12,256,256]{2,1,0:T(8,128)(2,1)S(1)} %get-tuple-element.33.refs_3_, ...), custom_call_target="tpu_custom_call" | custom-call | tf_op jit(solution)/shard_map/pallas_call | solution.py:428
  25.0 3.4 %all-to-all-start.1 = ((bf16[8,64,128]{2,1,0:T(8,128)(2,1)}), bf16[8,64,128]{2,1,0:T(8,128)(2,1)S(1)}, u32[]{:S(2)}, u32[]{:S(2)}) async-start(bf16[8,64,128]{2,1,0:T(8,128)(2,1)} %get-tuple-element.44), calls=%async_computation.1 | async-start | bytes 262144 | tf_op jit(solution)/shard_map/all_to_all | solution.py:79
  28.4 2.0 %early.3 = (bf16[4,64,256]{2,1,0:T(8,128)(2,1)S(1)}, bf16[4,64,256]{2,1,0:T(8,128)(2,1)S(1)}, f32[8,80,256]{2,1,0:T(8,128)S(1)}) custom-call(s32[1,2048]{1,0:T(1,128)} %refs_2_.3, bf16[20,256,256]{2,1,0:T(8,128)(2,1)} %bitcast.2, bf16[8,64,256]{2,1,0:T(8,128)(2,1)S(1)} %get-tuple-element.36.refs_2_.refs_5_), custom_call_target="tpu_custom_call" | custom-call | flops 536870912 | bytes 1048576 | tf_op jit(solution)/shard_map/early/pallas_call | solution.py:403
  30.4 0.0 copy-start.1
  30.4 5.3 %all-to-all-done.1.refs_6_ = bf16[8,64,128]{2,1,0:T(8,128)(2,1)S(1)} async-done(((bf16[8,64,128]{2,1,0:T(8,128)(2,1)}), bf16[8,64,128]{2,1,0:T(8,128)(2,1)S(1)}, u32[]{:S(2)}, u32[]{:S(2)}) %all-to-all-start.1) | async-done | bytes 131104 | tf_op jit(solution)/shard_map/all_to_all | solution.py:79
  35.7 0.0 copy-done
  35.7 2.1 %shard_map.83 = bf16[8,64,256]{2,1,0:T(8,128)(2,1)} custom-call(s32[1,20]{1,0:T(1,128)S(1)} %copy-done.2, s32[1,20]{1,0:T(1,128)S(1)} %copy-done.3, s32[1,2048]{1,0:T(1,128)S(1)} %copy-done, bf16[12,256,256]{2,1,0:T(8,128)(2,1)S(1)} %get-tuple-element.33.refs_3_, f32[8,80,256]{2,1,0:T(8,128)S(1)} %get-tuple-element.43.refs_4_, ...), custom_call_target="tpu_custom_call" | custom-call | tf_op jit(solution)/shard_map/pallas_call | solution.py:428
  37.8 3.4 %all-to-all-start.2 = ((bf16[8,64,256]{2,1,0:T(8,128)(2,1)}), bf16[8,64,256]{2,1,0:T(8,128)(2,1)S(1)}, u32[]{:S(2)}, u32[]{:S(2)}) async-start(bf16[8,64,256]{2,1,0:T(8,128)(2,1)} %shard_map.83), calls=%async_computation.2 | async-start | bytes 524288 | tf_op jit(solution)/shard_map/all_to_all | solution.py:79
  41.2 2.8 %collective-permute-start.3 = (bf16[4,64,256]{2,1,0:T(8,128)(2,1)S(1)}, bf16[4,64,256]{2,1,0:T(8,128)(2,1)S(1)}, u32[]{:S(2)}, u32[]{:S(2)}) collective-permute-start(bf16[4,64,256]{2,1,0:T(8,128)(2,1)S(1)} %get-tuple-element.32), channel_id=1, source_target_pairs={{0,16},{4,20},{8,24},{12,28},{16,0},{20,4},{24,8},{28,12},{1,17},{... | collective-permute-start | bytes 393224 | tf_op jit(solution)/shard_map/ppermute | solution.py:423
  44.1 0.2 collective-permute-start.4
  44.2 13.7 %collective-permute-done.3.refs_1_ = bf16[4,64,256]{2,1,0:T(8,128)(2,1)S(1)} collective-permute-done((bf16[4,64,256]{2,1,0:T(8,128)(2,1)S(1)}, bf16[4,64,256]{2,1,0:T(8,128)(2,1)S(1)}, u32[]{:S(2)}, u32[]{:S(2)}) %collective-permute-start.3) | collective-permute-done | bytes 131104 | tf_op jit(solution)/shard_map/ppermute | solution.py:423
  58.0 1.4 %collective-permute-done.4.refs_3_ = bf16[4,64,256]{2,1,0:T(8,128)(2,1)S(1)} collective-permute-done((bf16[4,64,256]{2,1,0:T(8,128)(2,1)S(1)}, bf16[4,64,256]{2,1,0:T(8,128)(2,1)S(1)}, u32[]{:S(2)}, u32[]{:S(2)}) %collective-permute-start.4) | collective-permute-done | bytes 131104 | tf_op jit(solution)/shard_map/ppermute | solution.py:423
  59.4 1.5 %collective-permute-start.5 = (bf16[256,256]{1,0:T(8,128)(2,1)S(1)}, bf16[256,256]{1,0:T(8,128)(2,1)S(1)}, u32[]{:S(2)}, u32[]{:S(2)}) collective-permute-start(bf16[256,256]{1,0:T(8,128)(2,1)S(1)} %get-tuple-element.40), channel_id=1, source_target_pairs={{0,4},{4,0},{8,12},{12,8},{16,20},{20,16},{24,28},{28,24},{1,5},{5... | collective-permute-start | bytes 393224 | tf_op jit(solution)/shard_map/ppermute | solution.py:488
  60.9 0.0 collective-permute-start.6
  60.9 2.0 %collective-permute-start.7 = (bf16[256,256]{1,0:T(8,128)(2,1)S(1)}, bf16[256,256]{1,0:T(8,128)(2,1)S(1)}, u32[]{:S(2)}, u32[]{:S(2)}) collective-permute-start(bf16[256,256]{1,0:T(8,128)(2,1)S(1)} %get-tuple-element.42), channel_id=1, source_target_pairs={{0,12},{4,8},{8,4},{12,0},{16,28},{20,24},{24,20},{28,16},{1,13},{... | collective-permute-start | bytes 393224 | tf_op jit(solution)/shard_map/ppermute | solution.py:488
  63.0 2.9 %collective-permute-done.5.refs_2_ = bf16[256,256]{1,0:T(8,128)(2,1)S(1)} collective-permute-done((bf16[256,256]{1,0:T(8,128)(2,1)S(1)}, bf16[256,256]{1,0:T(8,128)(2,1)S(1)}, u32[]{:S(2)}, u32[]{:S(2)}) %collective-permute-start.5) | collective-permute-done | bytes 131104 | tf_op jit(solution)/shard_map/ppermute | solution.py:488
  65.8 0.2 collective-permute-done.6.refs_3_
  66.0 1.4 %collective-permute-done.7.refs_4_ = bf16[256,256]{1,0:T(8,128)(2,1)S(1)} collective-permute-done((bf16[256,256]{1,0:T(8,128)(2,1)S(1)}, bf16[256,256]{1,0:T(8,128)(2,1)S(1)}, u32[]{:S(2)}, u32[]{:S(2)}) %collective-permute-start.7) | collective-permute-done | bytes 131104 | tf_op jit(solution)/shard_map/ppermute | solution.py:488
  67.4 0.0 all-to-all-done.2.refs_5_
  67.4 0.0 copy-done.1
  67.4 2.6 %place.1 = bf16[3,64,2048]{2,1,0:T(8,128)(2,1)} custom-call(s32[1,2048]{1,0:T(1,128)S(1)} %copy-done.1, bf16[256,256]{1,0:T(8,128)(2,1)S(1)} %get-tuple-element.39.refs_1_, bf16[256,256]{1,0:T(8,128)(2,1)S(1)} %collective-permute-done.5.refs_2_, bf16[256,256]{1,0:T(8,128)(2,1)S(1)} %collective-permute-done.6.refs_3_, ...), custom_call_target="tpu_custom_call" | custom-call | tf_op jit(solution)/shard_map/place/pallas_call | solution.py:490
  (1 shorter events, 0.0 us)
Async XLA Ops:
  0.0 23.3 %copy-start.3 = (s32[1,20]{1,0:T(1,128)S(1)}, s32[1,20]{1,0:T(1,128)}, u32[]{:S(2)}) copy-start(s32[1,20]{1,0:T(1,128)} %refs_1_.5) | copy-start | bytes 244
  0.0 23.3 %copy-start.2 = (s32[1,20]{1,0:T(1,128)S(1)}, s32[1,20]{1,0:T(1,128)}, u32[]{:S(2)}) copy-start(s32[1,20]{1,0:T(1,128)} %refs_0_.10) | copy-start | bytes 244
  1.8 3.2 %collective-permute-start = (bf16[64,512]{1,0:T(8,128)(2,1)S(1)}, bf16[64,512]{1,0:T(8,128)(2,1)S(1)}, u32[]{:S(2)}, u32[]{:S(2)}) collective-permute-start(bf16[64,512]{1,0:T(8,128)(2,1)S(1)} %get-tuple-element.27), channel_id=1, source_target_pairs={{0,1},{1,0},{2,3},{3,2},{4,5},{5,4},{6,7},{7,6},{8,9},{9,8},{10,11... | collective-permute-start | bytes 196616 | tf_op jit(solution)/shard_map/ppermute | solution.py:457
  2.4 5.2 %collective-permute-start.1 = (bf16[64,512]{1,0:T(8,128)(2,1)S(1)}, bf16[64,512]{1,0:T(8,128)(2,1)S(1)}, u32[]{:S(2)}, u32[]{:S(2)}) collective-permute-start(bf16[64,512]{1,0:T(8,128)(2,1)S(1)} %get-tuple-element.28), channel_id=1, source_target_pairs={{0,2},{1,3},{2,0},{3,1},{4,6},{5,7},{6,4},{7,5},{8,10},{9,11},{10,... | collective-permute-start | bytes 196616 | tf_op jit(solution)/shard_map/ppermute | solution.py:457
  4.9 4.1 %collective-permute-start.2 = (bf16[64,512]{1,0:T(8,128)(2,1)S(1)}, bf16[64,512]{1,0:T(8,128)(2,1)S(1)}, u32[]{:S(2)}, u32[]{:S(2)}) collective-permute-start(bf16[64,512]{1,0:T(8,128)(2,1)S(1)} %get-tuple-element.29), channel_id=1, source_target_pairs={{0,3},{1,2},{2,1},{3,0},{4,7},{5,6},{6,5},{7,4},{8,11},{9,10},{10,... | collective-permute-start | bytes 196616 | tf_op jit(solution)/shard_map/ppermute | solution.py:457
  10.1 13.2 %all-to-all-start = ((bf16[8,64,128]{2,1,0:T(8,128)(2,1)}), bf16[8,64,128]{2,1,0:T(8,128)(2,1)S(1)}, u32[]{:S(2)}, u32[]{:S(2)}) async-start(bf16[8,64,128]{2,1,0:T(8,128)(2,1)} %get-tuple-element.35), calls=%async_computation | async-start | bytes 262144 | tf_op jit(solution)/shard_map/all_to_all | solution.py:79
  23.3 12.4 %copy-start = (s32[1,2048]{1,0:T(1,128)S(1)}, s32[1,2048]{1,0:T(1,128)}, u32[]{:S(2)}) copy-start(s32[1,2048]{1,0:T(1,128)} %refs_2_.3) | copy-start | bytes 24580
  25.0 10.7 %all-to-all-start.1 = ((bf16[8,64,128]{2,1,0:T(8,128)(2,1)}), bf16[8,64,128]{2,1,0:T(8,128)(2,1)S(1)}, u32[]{:S(2)}, u32[]{:S(2)}) async-start(bf16[8,64,128]{2,1,0:T(8,128)(2,1)} %get-tuple-element.44), calls=%async_computation.1 | async-start | bytes 262144 | tf_op jit(solution)/shard_map/all_to_all | solution.py:79
  30.4 37.0 %copy-start.1 = (s32[1,2048]{1,0:T(1,128)S(1)}, s32[1,2048]{1,0:T(1,128)}, u32[]{:S(2)}) copy-start(s32[1,2048]{1,0:T(1,128)} %refs_0_.11) | copy-start | bytes 24580
  37.8 29.6 %all-to-all-start.2 = ((bf16[8,64,256]{2,1,0:T(8,128)(2,1)}), bf16[8,64,256]{2,1,0:T(8,128)(2,1)S(1)}, u32[]{:S(2)}, u32[]{:S(2)}) async-start(bf16[8,64,256]{2,1,0:T(8,128)(2,1)} %shard_map.83), calls=%async_computation.2 | async-start | bytes 524288 | tf_op jit(solution)/shard_map/all_to_all | solution.py:79
  41.2 16.7 %collective-permute-start.3 = (bf16[4,64,256]{2,1,0:T(8,128)(2,1)S(1)}, bf16[4,64,256]{2,1,0:T(8,128)(2,1)S(1)}, u32[]{:S(2)}, u32[]{:S(2)}) collective-permute-start(bf16[4,64,256]{2,1,0:T(8,128)(2,1)S(1)} %get-tuple-element.32), channel_id=1, source_target_pairs={{0,16},{4,20},{8,24},{12,28},{16,0},{20,4},{24,8},{28,12},{1,17},{... | collective-permute-start | bytes 393224 | tf_op jit(solution)/shard_map/ppermute | solution.py:423
  44.1 15.3 %collective-permute-start.4 = (bf16[4,64,256]{2,1,0:T(8,128)(2,1)S(1)}, bf16[4,64,256]{2,1,0:T(8,128)(2,1)S(1)}, u32[]{:S(2)}, u32[]{:S(2)}) collective-permute-start(bf16[4,64,256]{2,1,0:T(8,128)(2,1)S(1)} %get-tuple-element.38), channel_id=1, source_target_pairs={{0,16},{4,20},{8,24},{12,28},{16,0},{20,4},{24,8},{28,12},{1,17},{... | collective-permute-start | bytes 393224 | tf_op jit(solution)/shard_map/ppermute | solution.py:423
  59.4 6.4 %collective-permute-start.5 = (bf16[256,256]{1,0:T(8,128)(2,1)S(1)}, bf16[256,256]{1,0:T(8,128)(2,1)S(1)}, u32[]{:S(2)}, u32[]{:S(2)}) collective-permute-start(bf16[256,256]{1,0:T(8,128)(2,1)S(1)} %get-tuple-element.40), channel_id=1, source_target_pairs={{0,4},{4,0},{8,12},{12,8},{16,20},{20,16},{24,28},{28,24},{1,5},{5... | collective-permute-start | bytes 393224 | tf_op jit(solution)/shard_map/ppermute | solution.py:488
  60.9 5.1 %collective-permute-start.6 = (bf16[256,256]{1,0:T(8,128)(2,1)S(1)}, bf16[256,256]{1,0:T(8,128)(2,1)S(1)}, u32[]{:S(2)}, u32[]{:S(2)}) collective-permute-start(bf16[256,256]{1,0:T(8,128)(2,1)S(1)} %get-tuple-element.41), channel_id=1, source_target_pairs={{0,8},{4,12},{8,0},{12,4},{16,24},{20,28},{24,16},{28,20},{1,9},{5... | collective-permute-start | bytes 393224 | tf_op jit(solution)/shard_map/ppermute | solution.py:488
  60.9 6.5 %collective-permute-start.7 = (bf16[256,256]{1,0:T(8,128)(2,1)S(1)}, bf16[256,256]{1,0:T(8,128)(2,1)S(1)}, u32[]{:S(2)}, u32[]{:S(2)}) collective-permute-start(bf16[256,256]{1,0:T(8,128)(2,1)S(1)} %get-tuple-element.42), channel_id=1, source_target_pairs={{0,12},{4,8},{8,4},{12,0},{16,28},{20,24},{24,20},{28,16},{1,13},{... | collective-permute-start | bytes 393224 | tf_op jit(solution)/shard_map/ppermute | solution.py:488

commit v9 on v8

--- a/solution.py
+++ b/solution.py
@@ -288,13 +288,11 @@
     store_slots(send, pick(stack, blocks, index[...], side, group), group)
 
 
-def relay_kernel(*refs):
-    half = refs[0].shape[0]
-    ins, outs = refs[: len(refs) - half], refs[len(refs) - half :]
-    channels = ins[0].shape[1]
-    for step in range(half):
-        for place, blocks in enumerate(ins):
-            outs[step][place * channels : (place + 1) * channels] = blocks[step]
+def relay_kernel(near, sent, *outs):
+    channels = near.shape[1]
+    for step, out in enumerate(outs):
+        out[:channels] = near[step]
+        out[channels:] = sent[step]
 
 
 def combine_last_kernel(
@@ -314,7 +312,7 @@
 
 def place_steps_kernel(peers, side, index_ref, *rest):
     half = peers // 2
-    moved, last, (out_ref, out, sems) = rest[:half], rest[half], rest[half + 1 :]
+    moved, last, (out_ref, out, sems) = rest[:-4], rest[-4], rest[-3:]
     hops, channels, nodes = out.shape
     blocks = nodes // side
     slot = nodes // peers
@@ -325,17 +323,10 @@
         start = pl.multiple_of(origin * slot, slot)
         indexes.append(index_ref[:, pl.ds(start, slot)])
         first = (step // half) * channels
-        from_step = moved[step % half]
-        parts.append(
-            jnp.concatenate(
-                [
-                    from_step[first + 2 * channels * hop : first + (2 * hop + 1) * channels]
-                    for hop in range(hops - 1)
-                ]
-                + [last[origin]],
-                0,
-            )
-        )
+        arrived = [
+            moved[hop * half + step % half][first : first + channels] for hop in range(hops - 1)
+        ]
+        parts.append(jnp.concatenate(arrived + [last[origin]], 0))
     block, inner = split(jnp.concatenate(indexes, 1), side, blocks)
     table = jnp.concatenate(
         [one_hot(inner[:, start : start + side], side).T for start in range(0, nodes, side)], 0
@@ -422,6 +413,21 @@
         )(in_hbm(send_order), in_hbm(tiles), hop)
         sent = lax.ppermute(far, "dom", pairs(peers // 2, peers))
         return (near, sent), total, rest
+
+    def relay(blocks_of):
+        steps = peers // 2
+        moved = pl.pallas_call(
+            relay_kernel,
+            out_shape=(out((2 * channels, slot)),) * steps,
+            in_specs=[VMEM] * 2,
+            out_specs=(VMEM,) * steps,
+            compiler_params=params(),
+            cost_estimate=cost(0, 8 * channels * nodes),
+            name="relay",
+        )(*blocks_of)
+        return [moved[0]] + [
+            lax.ppermute(moved[step], "dom", pairs(step, peers)) for step in range(1, steps)
+        ]
 
     def late(keep, index, others, total, hop, arrived):
         shape = (peers, channels, index.shape[1] // peers)
@@ -475,27 +481,15 @@
         early1, total, _ = early(hop1, 0)
         (send,) = late(0, send_order, others, total, hop1, halo1)
         last = exchange(send, peers)
-        moved = pl.pallas_call(
-            relay_kernel,
-            out_shape=(out((4 * channels, slot)),) * half,
-            in_specs=[VMEM] * 4,
-            out_specs=(VMEM,) * half,
-            compiler_params=params(),
-            cost_estimate=cost(0, 16 * channels * nodes),
-            name="relay",
-        )(*early0, *early1)
-        moved = [moved[0]] + [
-            lax.ppermute(moved[step], "dom", pairs(step, peers)) for step in range(1, half)
-        ]
         return pl.pallas_call(
             lambda *refs: place_steps_kernel(peers, side, *refs),
             out_shape=out((3, channels, nodes)),
-            in_specs=[VMEM] * (half + 2),
+            in_specs=[VMEM] * (2 * half + 2),
             out_specs=HBM,
             scratch_shapes=[vmem((3, channels, nodes), BF16), dma((blocks,))],
             compiler_params=params(),
             name="place",
-        )(arrival_place, *moved, last)
+        )(arrival_place, *relay(early0), *relay(early1), last)
     halo0 = exchange(send, peers)
 
     def work(index):

time: 70.6 us -> 71.4 us (1.011)
  starting transfers between devices: 22.3 us -> 25.9 us
  waiting for transfers between devices: 34.2 us -> 31.5 us
    ppermute x3 -> x6, starting transfers between devices: 3.55 us -> 7.11 us  [relay(): lax.ppermute(moved[step], 'dom', pairs(step, peers))]
    ppermute x2, waiting for transfers between devices: 15.1 us -> 13.7 us  [early(): sent = lax.ppermute(far, 'dom', pairs(peers // 2, peers))]
    ppermute x3 -> x6, waiting for transfers between devices: 4.44 us -> 3.15 us  [relay(): lax.ppermute(moved[step], 'dom', pairs(step, peers))]
  transfers between devices with their start and end apart: 11 -> 14, of which waited for: 9 -> 8; matrix products, arithmetic and copies ran while one was open for 0% -> 0% of each run, Pallas kernels for 6% -> 6%
where the time goes in v9:
time: 71.4 us; the launch traced here: 70.9 us
  waiting for transfers between devices  31.5 us (44%)
  starting transfers between devices  25.9 us (36%)
  Pallas kernels  13.4 us (19%)
    ppermute x2, waiting for transfers between devices, early(): sent = lax.ppermute(far, 'dom', pairs(peers // 2, peers))  13.7 us
    all_to_all x3, starting transfers between devices, exchange(): arrived = lax.all_to_all(send, 'dom', 0, 0, tiled=True)  12.6 us
    all_to_all x3, waiting for transfers between devices, exchange(): arrived = lax.all_to_all(send, 'dom', 0, 0, tiled=True)  10.6 us
    ppermute x6, starting transfers between devices, relay(): lax.ppermute(moved[step], 'dom', pairs(step, peers))  7.11 us
    ppermute x3, waiting for transfers between devices, on_device(): arrived.append(lax.ppermute(own[step], 'rep', pairs(step, reps)))  4.02 us
    pallas_call x2, Pallas kernels, early(): pl.pallas_call(lambda *refs: early_kernel(staged, *refs), out_shape=(out(...  3.96 us
    pallas_call x2, Pallas kernels, late(): pl.pallas_call(lambda *refs: finish_kernel(group, keep, *refs), out_shape...  3.89 us
    ppermute x6, waiting for transfers between devices, relay(): lax.ppermute(moved[step], 'dom', pairs(step, peers))  3.15 us
  transfers between devices with their start and end apart: 14, of which 8 were waited for; matrix products, arithmetic and copies ran while one was open for 0% of the time, Pallas kernels for 6%

profile of v9, /device:TPU:0, one launch (start us, length us, event | category | flops | bytes accessed | tf_op | source)
XLA Modules:
  0.0 70.9 jit_solution(17530694568133761895)
XLA Ops:
  0.0 0.0 copy-start.3
  0.0 0.0 copy-start.2
  0.0 1.8 %sketch.1 = (bf16[64,512]{1,0:T(8,128)(2,1)S(1)}, bf16[64,512]{1,0:T(8,128)(2,1)S(1)}, bf16[64,512]{1,0:T(8,128)(2,1)S(1)}, bf16[64,512]{1,0:T(8,128)(2,1)S(1)}, s32[1,1024]{1,0:T(1,128)S(1)}) custom-call(bf16[512,768]{1,0:T(8,128)(2,1)} %refs_0_.6, bf16[768,256]{1,0:T(8,128)(2,1)} %refs_1_.3, s32[1,1024]{1,0:T(1,128)} %refs_2_.2), custom_call_target="tpu_custom_call" | custom-call | tf_op jit(solution)/shard_map/sketch/pallas_call | solution.py:446
  1.8 0.6 collective-permute-start
  2.4 2.5 %collective-permute-start.1 = (bf16[64,512]{1,0:T(8,128)(2,1)S(1)}, bf16[64,512]{1,0:T(8,128)(2,1)S(1)}, u32[]{:S(2)}, u32[]{:S(2)}) collective-permute-start(bf16[64,512]{1,0:T(8,128)(2,1)S(1)} %get-tuple-element.32), channel_id=1, source_target_pairs={{0,2},{1,3},{2,0},{3,1},{4,6},{5,7},{6,4},{7,5},{8,10},{9,11},{10,... | collective-permute-start | bytes 196616 | tf_op jit(solution)/shard_map/ppermute | solution.py:463
  4.9 0.0 collective-permute-start.2
  4.9 0.0 collective-permute-done.refs_2_
  4.9 2.6 %collective-permute-done.1.refs_3_ = bf16[64,512]{1,0:T(8,128)(2,1)S(1)} collective-permute-done((bf16[64,512]{1,0:T(8,128)(2,1)S(1)}, bf16[64,512]{1,0:T(8,128)(2,1)S(1)}, u32[]{:S(2)}, u32[]{:S(2)}) %collective-permute-start.1) | collective-permute-done | bytes 65568 | tf_op jit(solution)/shard_map/ppermute | solution.py:463
  7.6 1.4 %collective-permute-done.2.refs_4_ = bf16[64,512]{1,0:T(8,128)(2,1)S(1)} collective-permute-done((bf16[64,512]{1,0:T(8,128)(2,1)S(1)}, bf16[64,512]{1,0:T(8,128)(2,1)S(1)}, u32[]{:S(2)}, u32[]{:S(2)}) %collective-permute-start.2) | collective-permute-done | bytes 65568 | tf_op jit(solution)/shard_map/ppermute | solution.py:463
  9.0 1.1 %pick.1 = (bf16[8,64,256]{2,1,0:T(8,128)(2,1)S(1)}, bf16[8,64,128]{2,1,0:T(8,128)(2,1)}) custom-call(s32[1,1024]{1,0:T(1,128)S(1)} %get-tuple-element.29.refs_0_.refs_2_, bf16[64,512]{1,0:T(8,128)(2,1)S(1)} %get-tuple-element.30.refs_1_, bf16[64,512]{1,0:T(8,128)(2,1)S(1)} %collective-permute-done.refs_2_, ...), custom_call_target="tpu_custom_call" | custom-call | tf_op jit(solution)/shard_map/pick/pallas_call | solution.py:464
  10.1 5.8 %all-to-all-start = ((bf16[8,64,128]{2,1,0:T(8,128)(2,1)}), bf16[8,64,128]{2,1,0:T(8,128)(2,1)S(1)}, u32[]{:S(2)}, u32[]{:S(2)}) async-start(bf16[8,64,128]{2,1,0:T(8,128)(2,1)} %get-tuple-element.43), calls=%async_computation | async-start | bytes 262144 | tf_op jit(solution)/shard_map/all_to_all | solution.py:79
  15.9 2.0 %early.2 = (bf16[4,64,256]{2,1,0:T(8,128)(2,1)S(1)}, bf16[4,64,256]{2,1,0:T(8,128)(2,1)S(1)}, f32[8,80,256]{2,1,0:T(8,128)S(1)}, bf16[12,256,256]{2,1,0:T(8,128)(2,1)S(1)}) custom-call(s32[1,2048]{1,0:T(1,128)} %refs_2_.3, bf16[20,256,256]{2,1,0:T(8,128)(2,1)} %bitcast.1, bf16[8,64,256]{2,1,0:T(8,128)(2,1)S(1)} %get-tuple-element.34.refs_2_.refs_5_), custom_call_target="tpu_custom_call" | custom-call | flops 536870912 | bytes 1048576 | tf_op jit(solution)/shard_map/early/pallas_call | solution.py:394
  17.9 5.4 %all-to-all-done.refs_6_ = bf16[8,64,128]{2,1,0:T(8,128)(2,1)S(1)} async-done(((bf16[8,64,128]{2,1,0:T(8,128)(2,1)}), bf16[8,64,128]{2,1,0:T(8,128)(2,1)S(1)}, u32[]{:S(2)}, u32[]{:S(2)}) %all-to-all-start) | async-done | bytes 131104 | tf_op jit(solution)/shard_map/all_to_all | solution.py:79
  23.3 0.0 copy-done.3
  23.3 0.0 copy-done.2
  23.3 0.0 copy-start
  23.3 1.8 %shard_map.82 = (bf16[8,64,256]{2,1,0:T(8,128)(2,1)S(1)}, bf16[8,64,128]{2,1,0:T(8,128)(2,1)}) custom-call(s32[1,20]{1,0:T(1,128)S(1)} %copy-done.2, s32[1,20]{1,0:T(1,128)S(1)} %copy-done.3, s32[1,1024]{1,0:T(1,128)S(1)} %get-tuple-element.29.refs_0_.refs_2_, bf16[12,256,256]{2,1,0:T(8,128)(2,1)S(1)} %get-tuple-element.41.refs_3_, ...), custom_call_target="tpu_custom_call" | custom-call | tf_op jit(solution)/shard_map/pallas_call | solution.py:434
  25.0 3.4 %all-to-all-start.1 = ((bf16[8,64,128]{2,1,0:T(8,128)(2,1)}), bf16[8,64,128]{2,1,0:T(8,128)(2,1)S(1)}, u32[]{:S(2)}, u32[]{:S(2)}) async-start(bf16[8,64,128]{2,1,0:T(8,128)(2,1)} %get-tuple-element.52), calls=%async_computation.1 | async-start | bytes 262144 | tf_op jit(solution)/shard_map/all_to_all | solution.py:79
  28.4 2.0 %early.3 = (bf16[4,64,256]{2,1,0:T(8,128)(2,1)S(1)}, bf16[4,64,256]{2,1,0:T(8,128)(2,1)S(1)}, f32[8,80,256]{2,1,0:T(8,128)S(1)}) custom-call(s32[1,2048]{1,0:T(1,128)} %refs_2_.3, bf16[20,256,256]{2,1,0:T(8,128)(2,1)} %bitcast.2, bf16[8,64,256]{2,1,0:T(8,128)(2,1)S(1)} %get-tuple-element.44.refs_2_.refs_5_), custom_call_target="tpu_custom_call" | custom-call | flops 536870912 | bytes 1048576 | tf_op jit(solution)/shard_map/early/pallas_call | solution.py:394
  30.4 0.0 copy-start.1
  30.4 5.3 %all-to-all-done.1.refs_6_ = bf16[8,64,128]{2,1,0:T(8,128)(2,1)S(1)} async-done(((bf16[8,64,128]{2,1,0:T(8,128)(2,1)}), bf16[8,64,128]{2,1,0:T(8,128)(2,1)S(1)}, u32[]{:S(2)}, u32[]{:S(2)}) %all-to-all-start.1) | async-done | bytes 131104 | tf_op jit(solution)/shard_map/all_to_all | solution.py:79
  35.7 0.0 copy-done
  35.7 2.1 %shard_map.83 = bf16[8,64,256]{2,1,0:T(8,128)(2,1)} custom-call(s32[1,20]{1,0:T(1,128)S(1)} %copy-done.2, s32[1,20]{1,0:T(1,128)S(1)} %copy-done.3, s32[1,2048]{1,0:T(1,128)S(1)} %copy-done, bf16[12,256,256]{2,1,0:T(8,128)(2,1)S(1)} %get-tuple-element.41.refs_3_, f32[8,80,256]{2,1,0:T(8,128)S(1)} %get-tuple-element.51.refs_4_, ...), custom_call_target="tpu_custom_call" | custom-call | tf_op jit(solution)/shard_map/pallas_call | solution.py:434
  37.8 3.4 %all-to-all-start.2 = ((bf16[8,64,256]{2,1,0:T(8,128)(2,1)}), bf16[8,64,256]{2,1,0:T(8,128)(2,1)S(1)}, u32[]{:S(2)}, u32[]{:S(2)}) async-start(bf16[8,64,256]{2,1,0:T(8,128)(2,1)} %shard_map.83), calls=%async_computation.2 | async-start | bytes 524288 | tf_op jit(solution)/shard_map/all_to_all | solution.py:79
  41.2 2.8 %collective-permute-start.3 = (bf16[4,64,256]{2,1,0:T(8,128)(2,1)S(1)}, bf16[4,64,256]{2,1,0:T(8,128)(2,1)S(1)}, u32[]{:S(2)}, u32[]{:S(2)}) collective-permute-start(bf16[4,64,256]{2,1,0:T(8,128)(2,1)S(1)} %get-tuple-element.36), channel_id=1, source_target_pairs={{0,16},{4,20},{8,24},{12,28},{16,0},{20,4},{24,8},{28,12},{1,17},{... | collective-permute-start | bytes 393224 | tf_op jit(solution)/shard_map/ppermute | solution.py:414
  44.1 0.2 collective-permute-start.7
  44.2 13.7 %collective-permute-done.3.sent = bf16[4,64,256]{2,1,0:T(8,128)(2,1)S(1)} collective-permute-done((bf16[4,64,256]{2,1,0:T(8,128)(2,1)S(1)}, bf16[4,64,256]{2,1,0:T(8,128)(2,1)S(1)}, u32[]{:S(2)}, u32[]{:S(2)}) %collective-permute-start.3) | collective-permute-done | bytes 131104 | tf_op jit(solution)/shard_map/ppermute | solution.py:414
  58.0 1.5 %collective-permute-start.4 = (bf16[128,256]{1,0:T(8,128)(2,1)S(1)}, bf16[128,256]{1,0:T(8,128)(2,1)S(1)}, u32[]{:S(2)}, u32[]{:S(2)}) collective-permute-start(bf16[128,256]{1,0:T(8,128)(2,1)S(1)} %get-tuple-element.38), channel_id=1, source_target_pairs={{0,4},{4,0},{8,12},{12,8},{16,20},{20,16},{24,28},{28,24},{1,5},{5... | collective-permute-start | bytes 196616 | tf_op jit(solution)/shard_map/ppermute | solution.py:429
  59.5 0.0 collective-permute-start.5
  59.5 2.0 %collective-permute-start.6 = (bf16[128,256]{1,0:T(8,128)(2,1)S(1)}, bf16[128,256]{1,0:T(8,128)(2,1)S(1)}, u32[]{:S(2)}, u32[]{:S(2)}) collective-permute-start(bf16[128,256]{1,0:T(8,128)(2,1)S(1)} %get-tuple-element.40), channel_id=1, source_target_pairs={{0,12},{4,8},{8,4},{12,0},{16,28},{20,24},{24,20},{28,16},{1,13},{... | collective-permute-start | bytes 196616 | tf_op jit(solution)/shard_map/ppermute | solution.py:429
  61.5 0.0 collective-permute-done.7.sent
  61.6 1.5 %collective-permute-start.8 = (bf16[128,256]{1,0:T(8,128)(2,1)S(1)}, bf16[128,256]{1,0:T(8,128)(2,1)S(1)}, u32[]{:S(2)}, u32[]{:S(2)}) collective-permute-start(bf16[128,256]{1,0:T(8,128)(2,1)S(1)} %get-tuple-element.48), channel_id=1, source_target_pairs={{0,4},{4,0},{8,12},{12,8},{16,20},{20,16},{24,28},{28,24},{1,5},{5... | collective-permute-start | bytes 196616 | tf_op jit(solution)/shard_map/ppermute | solution.py:429
  63.1 0.0 collective-permute-start.9
  63.1 0.0 collective-permute-done.4.refs_2_
  63.1 2.0 %collective-permute-start.10 = (bf16[128,256]{1,0:T(8,128)(2,1)S(1)}, bf16[128,256]{1,0:T(8,128)(2,1)S(1)}, u32[]{:S(2)}, u32[]{:S(2)}) collective-permute-start(bf16[128,256]{1,0:T(8,128)(2,1)S(1)} %get-tuple-element.50), channel_id=1, source_target_pairs={{0,12},{4,8},{8,4},{12,0},{16,28},{20,24},{24,20},{28,16},{1,13},{... | collective-permute-start | bytes 196616 | tf_op jit(solution)/shard_map/ppermute | solution.py:429
  65.1 0.0 collective-permute-done.5.refs_3_
  65.1 0.0 collective-permute-done.6.refs_4_
  65.1 0.8 %collective-permute-done.8.refs_6_ = bf16[128,256]{1,0:T(8,128)(2,1)S(1)} collective-permute-done((bf16[128,256]{1,0:T(8,128)(2,1)S(1)}, bf16[128,256]{1,0:T(8,128)(2,1)S(1)}, u32[]{:S(2)}, u32[]{:S(2)}) %collective-permute-start.8) | collective-permute-done | bytes 65568 | tf_op jit(solution)/shard_map/ppermute | solution.py:429
  65.9 1.5 %collective-permute-done.9.refs_7_ = bf16[128,256]{1,0:T(8,128)(2,1)S(1)} collective-permute-done((bf16[128,256]{1,0:T(8,128)(2,1)S(1)}, bf16[128,256]{1,0:T(8,128)(2,1)S(1)}, u32[]{:S(2)}, u32[]{:S(2)}) %collective-permute-start.9) | collective-permute-done | bytes 65568 | tf_op jit(solution)/shard_map/ppermute | solution.py:429
  67.4 0.9 %collective-permute-done.10.refs_8_ = bf16[128,256]{1,0:T(8,128)(2,1)S(1)} collective-permute-done((bf16[128,256]{1,0:T(8,128)(2,1)S(1)}, bf16[128,256]{1,0:T(8,128)(2,1)S(1)}, u32[]{:S(2)}, u32[]{:S(2)}) %collective-permute-start.10) | collective-permute-done | bytes 65568 | tf_op jit(solution)/shard_map/ppermute | solution.py:429
  68.3 0.0 all-to-all-done.2.refs_9_
  68.3 0.0 copy-done.1
  68.3 2.6 %place.1 = bf16[3,64,2048]{2,1,0:T(8,128)(2,1)} custom-call(s32[1,2048]{1,0:T(1,128)S(1)} %copy-done.1, bf16[128,256]{1,0:T(8,128)(2,1)S(1)} %get-tuple-element.37.refs_1_, bf16[128,256]{1,0:T(8,128)(2,1)S(1)} %collective-permute-done.4.refs_2_, bf16[128,256]{1,0:T(8,128)(2,1)S(1)} %collective-permute-done.5.refs_3_, ...), custom_call_target="tpu_custom_call" | custom-call | tf_op jit(solution)/shard_map/place/pallas_call | solution.py:484
  (2 shorter events, 0.0 us)
Async XLA Ops:
  0.0 23.3 %copy-start.3 = (s32[1,20]{1,0:T(1,128)S(1)}, s32[1,20]{1,0:T(1,128)}, u32[]{:S(2)}) copy-start(s32[1,20]{1,0:T(1,128)} %refs_1_.5) | copy-start | bytes 244
  0.0 23.3 %copy-start.2 = (s32[1,20]{1,0:T(1,128)S(1)}, s32[1,20]{1,0:T(1,128)}, u32[]{:S(2)}) copy-start(s32[1,20]{1,0:T(1,128)} %refs_0_.10) | copy-start | bytes 244
  1.8 3.2 %collective-permute-start = (bf16[64,512]{1,0:T(8,128)(2,1)S(1)}, bf16[64,512]{1,0:T(8,128)(2,1)S(1)}, u32[]{:S(2)}, u32[]{:S(2)}) collective-permute-start(bf16[64,512]{1,0:T(8,128)(2,1)S(1)} %get-tuple-element.31), channel_id=1, source_target_pairs={{0,1},{1,0},{2,3},{3,2},{4,5},{5,4},{6,7},{7,6},{8,9},{9,8},{10,11... | collective-permute-start | bytes 196616 | tf_op jit(solution)/shard_map/ppermute | solution.py:463
  2.4 5.2 %collective-permute-start.1 = (bf16[64,512]{1,0:T(8,128)(2,1)S(1)}, bf16[64,512]{1,0:T(8,128)(2,1)S(1)}, u32[]{:S(2)}, u32[]{:S(2)}) collective-permute-start(bf16[64,512]{1,0:T(8,128)(2,1)S(1)} %get-tuple-element.32), channel_id=1, source_target_pairs={{0,2},{1,3},{2,0},{3,1},{4,6},{5,7},{6,4},{7,5},{8,10},{9,11},{10,... | collective-permute-start | bytes 196616 | tf_op jit(solution)/shard_map/ppermute | solution.py:463
  4.9 4.1 %collective-permute-start.2 = (bf16[64,512]{1,0:T(8,128)(2,1)S(1)}, bf16[64,512]{1,0:T(8,128)(2,1)S(1)}, u32[]{:S(2)}, u32[]{:S(2)}) collective-permute-start(bf16[64,512]{1,0:T(8,128)(2,1)S(1)} %get-tuple-element.33), channel_id=1, source_target_pairs={{0,3},{1,2},{2,1},{3,0},{4,7},{5,6},{6,5},{7,4},{8,11},{9,10},{10,... | collective-permute-start | bytes 196616 | tf_op jit(solution)/shard_map/ppermute | solution.py:463
  10.1 13.2 %all-to-all-start = ((bf16[8,64,128]{2,1,0:T(8,128)(2,1)}), bf16[8,64,128]{2,1,0:T(8,128)(2,1)S(1)}, u32[]{:S(2)}, u32[]{:S(2)}) async-start(bf16[8,64,128]{2,1,0:T(8,128)(2,1)} %get-tuple-element.43), calls=%async_computation | async-start | bytes 262144 | tf_op jit(solution)/shard_map/all_to_all | solution.py:79
  23.3 12.4 %copy-start = (s32[1,2048]{1,0:T(1,128)S(1)}, s32[1,2048]{1,0:T(1,128)}, u32[]{:S(2)}) copy-start(s32[1,2048]{1,0:T(1,128)} %refs_2_.3) | copy-start | bytes 24580
  25.0 10.7 %all-to-all-start.1 = ((bf16[8,64,128]{2,1,0:T(8,128)(2,1)}), bf16[8,64,128]{2,1,0:T(8,128)(2,1)S(1)}, u32[]{:S(2)}, u32[]{:S(2)}) async-start(bf16[8,64,128]{2,1,0:T(8,128)(2,1)} %get-tuple-element.52), calls=%async_computation.1 | async-start | bytes 262144 | tf_op jit(solution)/shard_map/all_to_all | solution.py:79
  30.4 37.9 %copy-start.1 = (s32[1,2048]{1,0:T(1,128)S(1)}, s32[1,2048]{1,0:T(1,128)}, u32[]{:S(2)}) copy-start(s32[1,2048]{1,0:T(1,128)} %refs_0_.11) | copy-start | bytes 24580
  37.8 30.5 %all-to-all-start.2 = ((bf16[8,64,256]{2,1,0:T(8,128)(2,1)}), bf16[8,64,256]{2,1,0:T(8,128)(2,1)S(1)}, u32[]{:S(2)}, u32[]{:S(2)}) async-start(bf16[8,64,256]{2,1,0:T(8,128)(2,1)} %shard_map.83), calls=%async_computation.2 | async-start | bytes 524288 | tf_op jit(solution)/shard_map/all_to_all | solution.py:79
  41.2 16.7 %collective-permute-start.3 = (bf16[4,64,256]{2,1,0:T(8,128)(2,1)S(1)}, bf16[4,64,256]{2,1,0:T(8,128)(2,1)S(1)}, u32[]{:S(2)}, u32[]{:S(2)}) collective-permute-start(bf16[4,64,256]{2,1,0:T(8,128)(2,1)S(1)} %get-tuple-element.36), channel_id=1, source_target_pairs={{0,16},{4,20},{8,24},{12,28},{16,0},{20,4},{24,8},{28,12},{1,17},{... | collective-permute-start | bytes 393224 | tf_op jit(solution)/shard_map/ppermute | solution.py:414
  44.1 17.5 %collective-permute-start.7 = (bf16[4,64,256]{2,1,0:T(8,128)(2,1)S(1)}, bf16[4,64,256]{2,1,0:T(8,128)(2,1)S(1)}, u32[]{:S(2)}, u32[]{:S(2)}) collective-permute-start(bf16[4,64,256]{2,1,0:T(8,128)(2,1)S(1)} %get-tuple-element.46), channel_id=1, source_target_pairs={{0,16},{4,20},{8,24},{12,28},{16,0},{20,4},{24,8},{28,12},{1,17},{... | collective-permute-start | bytes 393224 | tf_op jit(solution)/shard_map/ppermute | solution.py:414
  58.0 5.1 %collective-permute-start.4 = (bf16[128,256]{1,0:T(8,128)(2,1)S(1)}, bf16[128,256]{1,0:T(8,128)(2,1)S(1)}, u32[]{:S(2)}, u32[]{:S(2)}) collective-permute-start(bf16[128,256]{1,0:T(8,128)(2,1)S(1)} %get-tuple-element.38), channel_id=1, source_target_pairs={{0,4},{4,0},{8,12},{12,8},{16,20},{20,16},{24,28},{28,24},{1,5},{5... | collective-permute-start | bytes 196616 | tf_op jit(solution)/shard_map/ppermute | solution.py:429
  59.5 5.6 %collective-permute-start.5 = (bf16[128,256]{1,0:T(8,128)(2,1)S(1)}, bf16[128,256]{1,0:T(8,128)(2,1)S(1)}, u32[]{:S(2)}, u32[]{:S(2)}) collective-permute-start(bf16[128,256]{1,0:T(8,128)(2,1)S(1)} %get-tuple-element.39), channel_id=1, source_target_pairs={{0,8},{4,12},{8,0},{12,4},{16,24},{20,28},{24,16},{28,20},{1,9},{5... | collective-permute-start | bytes 196616 | tf_op jit(solution)/shard_map/ppermute | solution.py:429
  59.5 5.6 %collective-permute-start.6 = (bf16[128,256]{1,0:T(8,128)(2,1)S(1)}, bf16[128,256]{1,0:T(8,128)(2,1)S(1)}, u32[]{:S(2)}, u32[]{:S(2)}) collective-permute-start(bf16[128,256]{1,0:T(8,128)(2,1)S(1)} %get-tuple-element.40), channel_id=1, source_target_pairs={{0,12},{4,8},{8,4},{12,0},{16,28},{20,24},{24,20},{28,16},{1,13},{... | collective-permute-start | bytes 196616 | tf_op jit(solution)/shard_map/ppermute | solution.py:429
  61.6 4.3 %collective-permute-start.8 = (bf16[128,256]{1,0:T(8,128)(2,1)S(1)}, bf16[128,256]{1,0:T(8,128)(2,1)S(1)}, u32[]{:S(2)}, u32[]{:S(2)}) collective-permute-start(bf16[128,256]{1,0:T(8,128)(2,1)S(1)} %get-tuple-element.48), channel_id=1, source_target_pairs={{0,4},{4,0},{8,12},{12,8},{16,20},{20,16},{24,28},{28,24},{1,5},{5... | collective-permute-start | bytes 196616 | tf_op jit(solution)/shard_map/ppermute | solution.py:429
  63.1 4.3 %collective-permute-start.9 = (bf16[128,256]{1,0:T(8,128)(2,1)S(1)}, bf16[128,256]{1,0:T(8,128)(2,1)S(1)}, u32[]{:S(2)}, u32[]{:S(2)}) collective-permute-start(bf16[128,256]{1,0:T(8,128)(2,1)S(1)} %get-tuple-element.49), channel_id=1, source_target_pairs={{0,8},{4,12},{8,0},{12,4},{16,24},{20,28},{24,16},{28,20},{1,9},{5... | collective-permute-start | bytes 196616 | tf_op jit(solution)/shard_map/ppermute | solution.py:429
  63.1 5.2 %collective-permute-start.10 = (bf16[128,256]{1,0:T(8,128)(2,1)S(1)}, bf16[128,256]{1,0:T(8,128)(2,1)S(1)}, u32[]{:S(2)}, u32[]{:S(2)}) collective-permute-start(bf16[128,256]{1,0:T(8,128)(2,1)S(1)} %get-tuple-element.50), channel_id=1, source_target_pairs={{0,12},{4,8},{8,4},{12,0},{16,28},{20,24},{24,20},{28,16},{1,13},{... | collective-permute-start | bytes 196616 | tf_op jit(solution)/shard_map/ppermute | solution.py:429

commit v10 on v9

--- a/solution.py
+++ b/solution.py
@@ -310,44 +310,71 @@
     store_slots(send, pick(stack, blocks, index[...], side, group), group)
 
 
-def place_steps_kernel(peers, side, index_ref, *rest):
-    half = peers // 2
-    moved, last, (out_ref, out, sems) = rest[:-4], rest[-4], rest[-3:]
+def scatter(parts, table, block, out, out_ref, first, sems):
     hops, channels, nodes = out.shape
-    blocks = nodes // side
-    slot = nodes // peers
-    me = lax.axis_index("dom")
-    parts, indexes = [], []
-    for step in range(peers):
-        origin = me ^ step
-        start = pl.multiple_of(origin * slot, slot)
-        indexes.append(index_ref[:, pl.ds(start, slot)])
-        first = (step // half) * channels
-        arrived = [
-            moved[hop * half + step % half][first : first + channels] for hop in range(hops - 1)
+    side = table.shape[1]
+    stacked = jnp.concatenate(parts, 1)
+    rows = stacked.shape[0]
+    group = max(128 // rows, 1)
+    copies = []
+    for start in range(0, nodes // side, group):
+        masks = [
+            jnp.where(block == other, 1.0, 0.0).astype(BF16)
+            for other in range(start, start + group)
         ]
-        parts.append(jnp.concatenate(arrived + [last[origin]], 0))
-    block, inner = split(jnp.concatenate(indexes, 1), side, blocks)
-    table = jnp.concatenate(
-        [one_hot(inner[:, start : start + side], side).T for start in range(0, nodes, side)], 0
-    )
-    stacked = jnp.concatenate(parts, 1)
-    copies = []
-    for other in range(blocks):
-        mask = jnp.where(block == other, 1.0, 0.0).astype(BF16)
-        placed = dot(stacked * mask, table).astype(BF16)
-        columns = slice(other * side, (other + 1) * side)
-        for hop in range(hops):
-            out[hop, :, columns] = placed[hop * channels : (hop + 1) * channels]
-        columns = pl.ds(other * side, side)
+        placed = dot(jnp.concatenate([stacked * mask for mask in masks], 0), table).astype(BF16)
+        for other in range(group):
+            columns = slice((start + other) * side, (start + other + 1) * side)
+            for hop in range(hops):
+                row = other * rows + hop * channels
+                out[hop, :, columns] = placed[row : row + channels]
+        columns = pl.ds(start * side, group * side)
         copies.append(
             pltpu.make_async_copy(
-                out.at[:, :, columns], out_ref.at[:, :, columns], sems.at[other]
+                out.at[:, :, columns],
+                out_ref.at[pl.ds(first, hops), :, columns],
+                sems.at[start],
             )
         )
         copies[-1].start()
     for copy in copies:
         copy.wait()
+
+
+def place_first_kernel(peers, index_ref, *rest):
+    moved, (out_ref, table_ref, block_ref, out, sems) = rest[:-5], rest[-5:]
+    _, channels, nodes = out.shape
+    side = table_ref.shape[1]
+    blocks = nodes // side
+    half = peers // 2
+    slot = nodes // peers
+    me = lax.axis_index("dom")
+    parts, indexes = [], []
+    for step in range(peers):
+        start = pl.multiple_of((me ^ step) * slot, slot)
+        indexes.append(index_ref[:, pl.ds(start, slot)])
+        first = (step // half) * channels
+        parts.append(moved[step % half][first : first + channels])
+    block, inner = split(jnp.concatenate(indexes, 1), side, blocks)
+    block_ref[...] = block
+    table = jnp.concatenate(
+        [one_hot(inner[:, start : start + side], side).T for start in range(0, nodes, side)], 0
+    )
+    table_ref[...] = table
+    scatter(parts, table, block, out, out_ref, 0, sems)
+
+
+def place_rest_kernel(peers, _, table_ref, block_ref, *rest):
+    moved, last, (out_ref, out, sems) = rest[:-4], rest[-4], rest[-3:]
+    channels = out.shape[1]
+    half = peers // 2
+    me = lax.axis_index("dom")
+    parts = []
+    for step in range(peers):
+        first = (step // half) * channels
+        arrived = moved[step % half][first : first + channels]
+        parts.append(jnp.concatenate([arrived, last[me ^ step]], 0))
+    scatter(parts, table_ref[...], block_ref[...], out, out_ref, 1, sems)
 
 
 def place_kernel(side, index_ref, arrived_ref, out_ref):
@@ -481,15 +508,32 @@
         early1, total, _ = early(hop1, 0)
         (send,) = late(0, send_order, others, total, hop1, halo1)
         last = exchange(send, peers)
+        moved0, moved1 = relay(early0), relay(early1)
+        whole = out((3, channels, nodes))
+        placed, table, block = pl.pallas_call(
+            lambda *refs: place_first_kernel(peers, *refs),
+            out_shape=(
+                whole,
+                out((nodes, side)),
+                jax.ShapeDtypeStruct((1, nodes), jnp.int32),
+            ),
+            in_specs=[VMEM] * (half + 1),
+            out_specs=(HBM, VMEM, VMEM),
+            scratch_shapes=[vmem((1, channels, nodes), BF16), dma((blocks,))],
+            compiler_params=params(),
+            cost_estimate=cost(2 * channels * nodes * nodes, 4 * channels * nodes),
+            name="place0",
+        )(arrival_place, *moved0)
         return pl.pallas_call(
-            lambda *refs: place_steps_kernel(peers, side, *refs),
-            out_shape=out((3, channels, nodes)),
-            in_specs=[VMEM] * (2 * half + 2),
+            lambda *refs: place_rest_kernel(peers, *refs),
+            out_shape=whole,
+            in_specs=[HBM] + [VMEM] * (half + 3),
             out_specs=HBM,
-            scratch_shapes=[vmem((3, channels, nodes), BF16), dma((blocks,))],
+            scratch_shapes=[vmem((2, channels, nodes), BF16), dma((blocks,))],
+            input_output_aliases={0: 0},
             compiler_params=params(),
             name="place",
-        )(arrival_place, *relay(early0), *relay(early1), last)
+        )(placed, table, block, *moved1, last)
     halo0 = exchange(send, peers)
 
     def work(index):

time: 71.4 us -> 70.8 us (level)
  waiting for transfers between devices: 31.5 us -> 29.9 us
  Pallas kernels: 13.4 us -> 14.4 us
    ppermute x6, waiting for transfers between devices: 3.15 us -> 1.53 us  [relay(): lax.ppermute(moved[step], 'dom', pairs(step, peers))]
    pallas_call x1 -> x2, Pallas kernels: 2.64 us -> 3.59 us  [the longest x1 1.99 us: on_device(): pl.pallas_call(lambda *refs: place_rest_kernel(peers, *refs), out_shape=w...]
  transfers between devices with their start and end apart: 14 -> 14, of which waited for: 8 -> 7; matrix products, arithmetic and copies ran while one was open for 0% -> 0% of each run, Pallas kernels for 6% -> 8%
where the time goes in v10:
time: 70.8 us; the launch traced here: 70.3 us
  waiting for transfers between devices  29.9 us (42%)
  starting transfers between devices  25.9 us (37%)
  Pallas kernels  14.4 us (20%)
    ppermute x2, waiting for transfers between devices, early(): sent = lax.ppermute(far, 'dom', pairs(peers // 2, peers))  13.7 us
    all_to_all x3, starting transfers between devices, exchange(): arrived = lax.all_to_all(send, 'dom', 0, 0, tiled=True)  12.6 us
    all_to_all x3, waiting for transfers between devices, exchange(): arrived = lax.all_to_all(send, 'dom', 0, 0, tiled=True)  10.6 us
    ppermute x6, starting transfers between devices, relay(): lax.ppermute(moved[step], 'dom', pairs(step, peers))  7.11 us
    ppermute x3, waiting for transfers between devices, on_device(): arrived.append(lax.ppermute(own[step], 'rep', pairs(step, reps)))  4.02 us
    pallas_call x2, Pallas kernels, early(): pl.pallas_call(lambda *refs: early_kernel(staged, *refs), out_shape=(out(...  3.96 us
    pallas_call x2, Pallas kernels, late(): pl.pallas_call(lambda *refs: finish_kernel(group, keep, *refs), out_shape...  3.9 us
    ppermute x3, starting transfers between devices, on_device(): arrived.append(lax.ppermute(own[step], 'rep', pairs(step, reps)))  3.15 us
  transfers between devices with their start and end apart: 14, of which 7 were waited for; matrix products, arithmetic and copies ran while one was open for 0% of the time, Pallas kernels for 8%

profile of v10, /device:TPU:0, one launch (start us, length us, event | category | flops | bytes accessed | tf_op | source)
XLA Modules:
  0.0 70.3 jit_solution(720003582184729897)
XLA Ops:
  0.0 0.0 copy-start.2
  0.0 0.0 copy-start.1
  0.0 1.8 %sketch.1 = (bf16[64,512]{1,0:T(8,128)(2,1)S(1)}, bf16[64,512]{1,0:T(8,128)(2,1)S(1)}, bf16[64,512]{1,0:T(8,128)(2,1)S(1)}, bf16[64,512]{1,0:T(8,128)(2,1)S(1)}, s32[1,1024]{1,0:T(1,128)S(1)}) custom-call(bf16[512,768]{1,0:T(8,128)(2,1)} %refs_0_.6, bf16[768,256]{1,0:T(8,128)(2,1)} %refs_1_.3, s32[1,1024]{1,0:T(1,128)} %refs_2_.2), custom_call_target="tpu_custom_call" | custom-call | tf_op jit(solution)/shard_map/sketch/pallas_call | solution.py:473
  1.8 0.6 collective-permute-start
  2.4 2.5 %collective-permute-start.1 = (bf16[64,512]{1,0:T(8,128)(2,1)S(1)}, bf16[64,512]{1,0:T(8,128)(2,1)S(1)}, u32[]{:S(2)}, u32[]{:S(2)}) collective-permute-start(bf16[64,512]{1,0:T(8,128)(2,1)S(1)} %get-tuple-element.35), channel_id=1, source_target_pairs={{0,2},{1,3},{2,0},{3,1},{4,6},{5,7},{6,4},{7,5},{8,10},{9,11},{10,... | collective-permute-start | bytes 196616 | tf_op jit(solution)/shard_map/ppermute | solution.py:490
  4.9 0.0 collective-permute-start.2
  4.9 0.0 collective-permute-done.refs_2_
  4.9 2.6 %collective-permute-done.1.refs_3_ = bf16[64,512]{1,0:T(8,128)(2,1)S(1)} collective-permute-done((bf16[64,512]{1,0:T(8,128)(2,1)S(1)}, bf16[64,512]{1,0:T(8,128)(2,1)S(1)}, u32[]{:S(2)}, u32[]{:S(2)}) %collective-permute-start.1) | collective-permute-done | bytes 65568 | tf_op jit(solution)/shard_map/ppermute | solution.py:490
  7.6 1.4 %collective-permute-done.2.refs_4_ = bf16[64,512]{1,0:T(8,128)(2,1)S(1)} collective-permute-done((bf16[64,512]{1,0:T(8,128)(2,1)S(1)}, bf16[64,512]{1,0:T(8,128)(2,1)S(1)}, u32[]{:S(2)}, u32[]{:S(2)}) %collective-permute-start.2) | collective-permute-done | bytes 65568 | tf_op jit(solution)/shard_map/ppermute | solution.py:490
  9.0 1.1 %pick.1 = (bf16[8,64,256]{2,1,0:T(8,128)(2,1)S(1)}, bf16[8,64,128]{2,1,0:T(8,128)(2,1)}) custom-call(s32[1,1024]{1,0:T(1,128)S(1)} %get-tuple-element.32.refs_0_.refs_2_, bf16[64,512]{1,0:T(8,128)(2,1)S(1)} %get-tuple-element.33.refs_1_, bf16[64,512]{1,0:T(8,128)(2,1)S(1)} %collective-permute-done.refs_2_, ...), custom_call_target="tpu_custom_call" | custom-call | tf_op jit(solution)/shard_map/pick/pallas_call | solution.py:491
  10.1 5.8 %all-to-all-start = ((bf16[8,64,128]{2,1,0:T(8,128)(2,1)}), bf16[8,64,128]{2,1,0:T(8,128)(2,1)S(1)}, u32[]{:S(2)}, u32[]{:S(2)}) async-start(bf16[8,64,128]{2,1,0:T(8,128)(2,1)} %get-tuple-element.49), calls=%async_computation | async-start | bytes 262144 | tf_op jit(solution)/shard_map/all_to_all | solution.py:79
  15.9 2.0 %early.2 = (bf16[4,64,256]{2,1,0:T(8,128)(2,1)S(1)}, bf16[4,64,256]{2,1,0:T(8,128)(2,1)S(1)}, f32[8,80,256]{2,1,0:T(8,128)S(1)}, bf16[12,256,256]{2,1,0:T(8,128)(2,1)S(1)}) custom-call(s32[1,2048]{1,0:T(1,128)} %refs_2_.3, bf16[20,256,256]{2,1,0:T(8,128)(2,1)} %bitcast.1, bf16[8,64,256]{2,1,0:T(8,128)(2,1)S(1)} %get-tuple-element.37.refs_2_.refs_5_), custom_call_target="tpu_custom_call" | custom-call | flops 536870912 | bytes 1048576 | tf_op jit(solution)/shard_map/early/pallas_call | solution.py:421
  17.9 5.4 %all-to-all-done.refs_6_ = bf16[8,64,128]{2,1,0:T(8,128)(2,1)S(1)} async-done(((bf16[8,64,128]{2,1,0:T(8,128)(2,1)}), bf16[8,64,128]{2,1,0:T(8,128)(2,1)S(1)}, u32[]{:S(2)}, u32[]{:S(2)}) %all-to-all-start) | async-done | bytes 131104 | tf_op jit(solution)/shard_map/all_to_all | solution.py:79
  23.3 0.0 copy-done.2
  23.3 0.0 copy-done.1
  23.3 0.0 copy-start
  23.3 1.8 %shard_map.82 = (bf16[8,64,256]{2,1,0:T(8,128)(2,1)S(1)}, bf16[8,64,128]{2,1,0:T(8,128)(2,1)}) custom-call(s32[1,20]{1,0:T(1,128)S(1)} %copy-done.1, s32[1,20]{1,0:T(1,128)S(1)} %copy-done.2, s32[1,1024]{1,0:T(1,128)S(1)} %get-tuple-element.32.refs_0_.refs_2_, bf16[12,256,256]{2,1,0:T(8,128)(2,1)S(1)} %get-tuple-element.47.refs_3_, ...), custom_call_target="tpu_custom_call" | custom-call | tf_op jit(solution)/shard_map/pallas_call | solution.py:461
  25.0 3.4 %all-to-all-start.1 = ((bf16[8,64,128]{2,1,0:T(8,128)(2,1)}), bf16[8,64,128]{2,1,0:T(8,128)(2,1)S(1)}, u32[]{:S(2)}, u32[]{:S(2)}) async-start(bf16[8,64,128]{2,1,0:T(8,128)(2,1)} %get-tuple-element.58), calls=%async_computation.1 | async-start | bytes 262144 | tf_op jit(solution)/shard_map/all_to_all | solution.py:79
  28.4 2.0 %early.3 = (bf16[4,64,256]{2,1,0:T(8,128)(2,1)S(1)}, bf16[4,64,256]{2,1,0:T(8,128)(2,1)S(1)}, f32[8,80,256]{2,1,0:T(8,128)S(1)}) custom-call(s32[1,2048]{1,0:T(1,128)} %refs_2_.3, bf16[20,256,256]{2,1,0:T(8,128)(2,1)} %bitcast.2, bf16[8,64,256]{2,1,0:T(8,128)(2,1)S(1)} %get-tuple-element.50.refs_2_.refs_5_), custom_call_target="tpu_custom_call" | custom-call | flops 536870912 | bytes 1048576 | tf_op jit(solution)/shard_map/early/pallas_call | solution.py:421
  30.4 0.0 copy-start.3
  30.4 5.3 %all-to-all-done.1.refs_6_ = bf16[8,64,128]{2,1,0:T(8,128)(2,1)S(1)} async-done(((bf16[8,64,128]{2,1,0:T(8,128)(2,1)}), bf16[8,64,128]{2,1,0:T(8,128)(2,1)S(1)}, u32[]{:S(2)}, u32[]{:S(2)}) %all-to-all-start.1) | async-done | bytes 131104 | tf_op jit(solution)/shard_map/all_to_all | solution.py:79
  35.7 0.0 copy-done
  35.7 2.1 %shard_map.83 = bf16[8,64,256]{2,1,0:T(8,128)(2,1)} custom-call(s32[1,20]{1,0:T(1,128)S(1)} %copy-done.1, s32[1,20]{1,0:T(1,128)S(1)} %copy-done.2, s32[1,2048]{1,0:T(1,128)S(1)} %copy-done, bf16[12,256,256]{2,1,0:T(8,128)(2,1)S(1)} %get-tuple-element.47.refs_3_, f32[8,80,256]{2,1,0:T(8,128)S(1)} %get-tuple-element.57.refs_4_, ...), custom_call_target="tpu_custom_call" | custom-call | tf_op jit(solution)/shard_map/pallas_call | solution.py:461
  37.8 3.4 %all-to-all-start.2 = ((bf16[8,64,256]{2,1,0:T(8,128)(2,1)}), bf16[8,64,256]{2,1,0:T(8,128)(2,1)S(1)}, u32[]{:S(2)}, u32[]{:S(2)}) async-start(bf16[8,64,256]{2,1,0:T(8,128)(2,1)} %shard_map.83), calls=%async_computation.2 | async-start | bytes 524288 | tf_op jit(solution)/shard_map/all_to_all | solution.py:79
  41.2 2.8 %collective-permute-start.3 = (bf16[4,64,256]{2,1,0:T(8,128)(2,1)S(1)}, bf16[4,64,256]{2,1,0:T(8,128)(2,1)S(1)}, u32[]{:S(2)}, u32[]{:S(2)}) collective-permute-start(bf16[4,64,256]{2,1,0:T(8,128)(2,1)S(1)} %get-tuple-element.39), channel_id=1, source_target_pairs={{0,16},{4,20},{8,24},{12,28},{16,0},{20,4},{24,8},{28,12},{1,17},{... | collective-permute-start | bytes 393224 | tf_op jit(solution)/shard_map/ppermute | solution.py:441
  44.1 0.2 collective-permute-start.7
  44.2 13.7 %collective-permute-done.3.sent = bf16[4,64,256]{2,1,0:T(8,128)(2,1)S(1)} collective-permute-done((bf16[4,64,256]{2,1,0:T(8,128)(2,1)S(1)}, bf16[4,64,256]{2,1,0:T(8,128)(2,1)S(1)}, u32[]{:S(2)}, u32[]{:S(2)}) %collective-permute-start.3) | collective-permute-done | bytes 131104 | tf_op jit(solution)/shard_map/ppermute | solution.py:441
  58.0 1.5 %collective-permute-start.4 = (bf16[128,256]{1,0:T(8,128)(2,1)S(1)}, bf16[128,256]{1,0:T(8,128)(2,1)S(1)}, u32[]{:S(2)}, u32[]{:S(2)}) collective-permute-start(bf16[128,256]{1,0:T(8,128)(2,1)S(1)} %get-tuple-element.41), channel_id=1, source_target_pairs={{0,4},{4,0},{8,12},{12,8},{16,20},{20,16},{24,28},{28,24},{1,5},{5... | collective-permute-start | bytes 196616 | tf_op jit(solution)/shard_map/ppermute | solution.py:456
  59.5 0.0 collective-permute-start.5
  59.5 2.0 %collective-permute-start.6 = (bf16[128,256]{1,0:T(8,128)(2,1)S(1)}, bf16[128,256]{1,0:T(8,128)(2,1)S(1)}, u32[]{:S(2)}, u32[]{:S(2)}) collective-permute-start(bf16[128,256]{1,0:T(8,128)(2,1)S(1)} %get-tuple-element.43), channel_id=1, source_target_pairs={{0,12},{4,8},{8,4},{12,0},{16,28},{20,24},{24,20},{28,16},{1,13},{... | collective-permute-start | bytes 196616 | tf_op jit(solution)/shard_map/ppermute | solution.py:456
  61.5 0.0 collective-permute-done.7.sent
  61.6 1.5 %collective-permute-start.8 = (bf16[128,256]{1,0:T(8,128)(2,1)S(1)}, bf16[128,256]{1,0:T(8,128)(2,1)S(1)}, u32[]{:S(2)}, u32[]{:S(2)}) collective-permute-start(bf16[128,256]{1,0:T(8,128)(2,1)S(1)} %get-tuple-element.54), channel_id=1, source_target_pairs={{0,4},{4,0},{8,12},{12,8},{16,20},{20,16},{24,28},{28,24},{1,5},{5... | collective-permute-start | bytes 196616 | tf_op jit(solution)/shard_map/ppermute | solution.py:456
  63.1 0.0 collective-permute-start.9
  63.1 0.0 collective-permute-done.4.refs_2_
  63.1 2.0 %collective-permute-start.10 = (bf16[128,256]{1,0:T(8,128)(2,1)S(1)}, bf16[128,256]{1,0:T(8,128)(2,1)S(1)}, u32[]{:S(2)}, u32[]{:S(2)}) collective-permute-start(bf16[128,256]{1,0:T(8,128)(2,1)S(1)} %get-tuple-element.56), channel_id=1, source_target_pairs={{0,12},{4,8},{8,4},{12,0},{16,28},{20,24},{24,20},{28,16},{1,13},{... | collective-permute-start | bytes 196616 | tf_op jit(solution)/shard_map/ppermute | solution.py:456
  65.1 0.0 collective-permute-done.5.refs_3_
  65.1 0.0 collective-permute-done.6.refs_4_
  65.1 0.0 copy-done.3
  65.1 1.6 %place0.1 = (bf16[3,64,2048]{2,1,0:T(8,128)(2,1)}, bf16[2048,256]{1,0:T(8,128)(2,1)S(1)}, s32[1,2048]{1,0:T(1,128)S(1)}) custom-call(s32[1,2048]{1,0:T(1,128)S(1)} %copy-done.3, bf16[128,256]{1,0:T(8,128)(2,1)S(1)} %get-tuple-element.40.refs_1_, bf16[128,256]{1,0:T(8,128)(2,1)S(1)} %collective-permute-done.4.refs_2_, ...), custom_call_target="tpu_custom_call" | custom-call | flops 536870912 | bytes 524288 | tf_op jit(solution)/shard_map/place0/pallas_call | solution.py:513
  66.7 0.0 collective-permute-done.8.refs_4_
  66.8 0.6 collective-permute-done.9.refs_5_
  67.4 0.9 %collective-permute-done.10.refs_6_ = bf16[128,256]{1,0:T(8,128)(2,1)S(1)} collective-permute-done((bf16[128,256]{1,0:T(8,128)(2,1)S(1)}, bf16[128,256]{1,0:T(8,128)(2,1)S(1)}, u32[]{:S(2)}, u32[]{:S(2)}) %collective-permute-start.10) | collective-permute-done | bytes 65568 | tf_op jit(solution)/shard_map/ppermute | solution.py:456
  68.3 0.0 all-to-all-done.2.refs_7_
  68.3 2.0 %place.1 = bf16[3,64,2048]{2,1,0:T(8,128)(2,1)} custom-call(bf16[3,64,2048]{2,1,0:T(8,128)(2,1)} %get-tuple-element.44.refs_0_, bf16[2048,256]{1,0:T(8,128)(2,1)S(1)} %get-tuple-element.45.refs_1_, s32[1,2048]{1,0:T(1,128)S(1)} %get-tuple-element.46.refs_2_, bf16[128,256]{1,0:T(8,128)(2,1)S(1)} %get-tuple-element.53.refs_3_, ...), custom_call_target="tpu_custom_call", output_to_operand_aliasing={{}: (0, {})} | custom-call | tf_op jit(solution)/shard_map/place/pallas_call | solution.py:527
  (2 shorter events, 0.0 us)
Async XLA Ops:
  0.0 23.3 %copy-start.2 = (s32[1,20]{1,0:T(1,128)S(1)}, s32[1,20]{1,0:T(1,128)}, u32[]{:S(2)}) copy-start(s32[1,20]{1,0:T(1,128)} %refs_1_.5) | copy-start | bytes 244
  0.0 23.3 %copy-start.1 = (s32[1,20]{1,0:T(1,128)S(1)}, s32[1,20]{1,0:T(1,128)}, u32[]{:S(2)}) copy-start(s32[1,20]{1,0:T(1,128)} %refs_0_.11) | copy-start | bytes 244
  1.8 3.2 %collective-permute-start = (bf16[64,512]{1,0:T(8,128)(2,1)S(1)}, bf16[64,512]{1,0:T(8,128)(2,1)S(1)}, u32[]{:S(2)}, u32[]{:S(2)}) collective-permute-start(bf16[64,512]{1,0:T(8,128)(2,1)S(1)} %get-tuple-element.34), channel_id=1, source_target_pairs={{0,1},{1,0},{2,3},{3,2},{4,5},{5,4},{6,7},{7,6},{8,9},{9,8},{10,11... | collective-permute-start | bytes 196616 | tf_op jit(solution)/shard_map/ppermute | solution.py:490
  2.4 5.2 %collective-permute-start.1 = (bf16[64,512]{1,0:T(8,128)(2,1)S(1)}, bf16[64,512]{1,0:T(8,128)(2,1)S(1)}, u32[]{:S(2)}, u32[]{:S(2)}) collective-permute-start(bf16[64,512]{1,0:T(8,128)(2,1)S(1)} %get-tuple-element.35), channel_id=1, source_target_pairs={{0,2},{1,3},{2,0},{3,1},{4,6},{5,7},{6,4},{7,5},{8,10},{9,11},{10,... | collective-permute-start | bytes 196616 | tf_op jit(solution)/shard_map/ppermute | solution.py:490
  4.9 4.1 %collective-permute-start.2 = (bf16[64,512]{1,0:T(8,128)(2,1)S(1)}, bf16[64,512]{1,0:T(8,128)(2,1)S(1)}, u32[]{:S(2)}, u32[]{:S(2)}) collective-permute-start(bf16[64,512]{1,0:T(8,128)(2,1)S(1)} %get-tuple-element.36), channel_id=1, source_target_pairs={{0,3},{1,2},{2,1},{3,0},{4,7},{5,6},{6,5},{7,4},{8,11},{9,10},{10,... | collective-permute-start | bytes 196616 | tf_op jit(solution)/shard_map/ppermute | solution.py:490
  10.1 13.2 %all-to-all-start = ((bf16[8,64,128]{2,1,0:T(8,128)(2,1)}), bf16[8,64,128]{2,1,0:T(8,128)(2,1)S(1)}, u32[]{:S(2)}, u32[]{:S(2)}) async-start(bf16[8,64,128]{2,1,0:T(8,128)(2,1)} %get-tuple-element.49), calls=%async_computation | async-start | bytes 262144 | tf_op jit(solution)/shard_map/all_to_all | solution.py:79
  23.3 12.4 %copy-start = (s32[1,2048]{1,0:T(1,128)S(1)}, s32[1,2048]{1,0:T(1,128)}, u32[]{:S(2)}) copy-start(s32[1,2048]{1,0:T(1,128)} %refs_2_.3) | copy-start | bytes 24580
  25.0 10.7 %all-to-all-start.1 = ((bf16[8,64,128]{2,1,0:T(8,128)(2,1)}), bf16[8,64,128]{2,1,0:T(8,128)(2,1)S(1)}, u32[]{:S(2)}, u32[]{:S(2)}) async-start(bf16[8,64,128]{2,1,0:T(8,128)(2,1)} %get-tuple-element.58), calls=%async_computation.1 | async-start | bytes 262144 | tf_op jit(solution)/shard_map/all_to_all | solution.py:79
  30.4 34.7 %copy-start.3 = (s32[1,2048]{1,0:T(1,128)S(1)}, s32[1,2048]{1,0:T(1,128)}, u32[]{:S(2)}) copy-start(s32[1,2048]{1,0:T(1,128)} %refs_0_.8) | copy-start | bytes 24580
  37.8 30.4 %all-to-all-start.2 = ((bf16[8,64,256]{2,1,0:T(8,128)(2,1)}), bf16[8,64,256]{2,1,0:T(8,128)(2,1)S(1)}, u32[]{:S(2)}, u32[]{:S(2)}) async-start(bf16[8,64,256]{2,1,0:T(8,128)(2,1)} %shard_map.83), calls=%async_computation.2 | async-start | bytes 524288 | tf_op jit(solution)/shard_map/all_to_all | solution.py:79
  41.2 16.7 %collective-permute-start.3 = (bf16[4,64,256]{2,1,0:T(8,128)(2,1)S(1)}, bf16[4,64,256]{2,1,0:T(8,128)(2,1)S(1)}, u32[]{:S(2)}, u32[]{:S(2)}) collective-permute-start(bf16[4,64,256]{2,1,0:T(8,128)(2,1)S(1)} %get-tuple-element.39), channel_id=1, source_target_pairs={{0,16},{4,20},{8,24},{12,28},{16,0},{20,4},{24,8},{28,12},{1,17},{... | collective-permute-start | bytes 393224 | tf_op jit(solution)/shard_map/ppermute | solution.py:441
  44.1 17.5 %collective-permute-start.7 = (bf16[4,64,256]{2,1,0:T(8,128)(2,1)S(1)}, bf16[4,64,256]{2,1,0:T(8,128)(2,1)S(1)}, u32[]{:S(2)}, u32[]{:S(2)}) collective-permute-start(bf16[4,64,256]{2,1,0:T(8,128)(2,1)S(1)} %get-tuple-element.52), channel_id=1, source_target_pairs={{0,16},{4,20},{8,24},{12,28},{16,0},{20,4},{24,8},{28,12},{1,17},{... | collective-permute-start | bytes 393224 | tf_op jit(solution)/shard_map/ppermute | solution.py:441
  58.0 5.1 %collective-permute-start.4 = (bf16[128,256]{1,0:T(8,128)(2,1)S(1)}, bf16[128,256]{1,0:T(8,128)(2,1)S(1)}, u32[]{:S(2)}, u32[]{:S(2)}) collective-permute-start(bf16[128,256]{1,0:T(8,128)(2,1)S(1)} %get-tuple-element.41), channel_id=1, source_target_pairs={{0,4},{4,0},{8,12},{12,8},{16,20},{20,16},{24,28},{28,24},{1,5},{5... | collective-permute-start | bytes 196616 | tf_op jit(solution)/shard_map/ppermute | solution.py:456
  59.5 5.6 %collective-permute-start.5 = (bf16[128,256]{1,0:T(8,128)(2,1)S(1)}, bf16[128,256]{1,0:T(8,128)(2,1)S(1)}, u32[]{:S(2)}, u32[]{:S(2)}) collective-permute-start(bf16[128,256]{1,0:T(8,128)(2,1)S(1)} %get-tuple-element.42), channel_id=1, source_target_pairs={{0,8},{4,12},{8,0},{12,4},{16,24},{20,28},{24,16},{28,20},{1,9},{5... | collective-permute-start | bytes 196616 | tf_op jit(solution)/shard_map/ppermute | solution.py:456
  59.5 5.6 %collective-permute-start.6 = (bf16[128,256]{1,0:T(8,128)(2,1)S(1)}, bf16[128,256]{1,0:T(8,128)(2,1)S(1)}, u32[]{:S(2)}, u32[]{:S(2)}) collective-permute-start(bf16[128,256]{1,0:T(8,128)(2,1)S(1)} %get-tuple-element.43), channel_id=1, source_target_pairs={{0,12},{4,8},{8,4},{12,0},{16,28},{20,24},{24,20},{28,16},{1,13},{... | collective-permute-start | bytes 196616 | tf_op jit(solution)/shard_map/ppermute | solution.py:456
  61.6 5.2 %collective-permute-start.8 = (bf16[128,256]{1,0:T(8,128)(2,1)S(1)}, bf16[128,256]{1,0:T(8,128)(2,1)S(1)}, u32[]{:S(2)}, u32[]{:S(2)}) collective-permute-start(bf16[128,256]{1,0:T(8,128)(2,1)S(1)} %get-tuple-element.54), channel_id=1, source_target_pairs={{0,4},{4,0},{8,12},{12,8},{16,20},{20,16},{24,28},{28,24},{1,5},{5... | collective-permute-start | bytes 196616 | tf_op jit(solution)/shard_map/ppermute | solution.py:456
  63.1 4.3 %collective-permute-start.9 = (bf16[128,256]{1,0:T(8,128)(2,1)S(1)}, bf16[128,256]{1,0:T(8,128)(2,1)S(1)}, u32[]{:S(2)}, u32[]{:S(2)}) collective-permute-start(bf16[128,256]{1,0:T(8,128)(2,1)S(1)} %get-tuple-element.55), channel_id=1, source_target_pairs={{0,8},{4,12},{8,0},{12,4},{16,24},{20,28},{24,16},{28,20},{1,9},{5... | collective-permute-start | bytes 196616 | tf_op jit(solution)/shard_map/ppermute | solution.py:456
  63.1 5.2 %collective-permute-start.10 = (bf16[128,256]{1,0:T(8,128)(2,1)S(1)}, bf16[128,256]{1,0:T(8,128)(2,1)S(1)}, u32[]{:S(2)}, u32[]{:S(2)}) collective-permute-start(bf16[128,256]{1,0:T(8,128)(2,1)S(1)} %get-tuple-element.56), channel_id=1, source_target_pairs={{0,12},{4,8},{8,4},{12,0},{16,28},{20,24},{24,20},{28,16},{1,13},{... | collective-permute-start | bytes 196616 | tf_op jit(solution)/shard_map/ppermute | solution.py:456

commit v11 on v10

--- a/solution.py
+++ b/solution.py
@@ -9,6 +9,7 @@
 BF16 = jnp.bfloat16
 F32 = jnp.float32
 EXTRA = 16
+KEPT = 8
 NN = (((1,), (0,)), ((), ()))
 NT = (((1,), (1,)), ((), ()))
 VMEM = pl.BlockSpec(memory_space=pltpu.VMEM)
@@ -208,7 +209,7 @@
 
 def early_kernel(staged, index_in, tiles_in, hop, near, far, total, *rest):
     full, index, tiles, sems = rest[-4:]
-    blocks, _, side = hop.shape
+    blocks, channels, side = hop.shape
     copies = [
         pltpu.make_async_copy(index_in, index, sems.at[0]),
         pltpu.make_async_copy(tiles_in.at[pl.ds(0, blocks)], tiles, sems.at[1]),
@@ -234,7 +235,7 @@
     copies[1].wait()
     for block in range(blocks):
         columns = jnp.concatenate([hop[block], ones], 0)
-        total[block] = dot(columns, tiles[block], NT)
+        total[block] = dot(columns, tiles[block], NT)[: channels + KEPT]
     if staged:
         copies[2].wait()
 
@@ -267,7 +268,7 @@
             product = products[slot - blocks]
         else:
             product = dot(columns[starts[slot]], tiles[slot - blocks], NT)
-        sums[target] = sums[target] + product
+        sums[target] = sums[target] + product[: channels + KEPT]
     results = []
     for block in range(blocks):
         whole = sums[block]
@@ -423,7 +424,7 @@
             out_shape=(
                 out(shape),
                 out(shape),
-                jax.ShapeDtypeStruct((blocks, channels + EXTRA, side), F32),
+                jax.ShapeDtypeStruct((blocks, channels + KEPT, side), F32),
             )
             + (out(others),) * staged,
             in_specs=[HBM, HBM, VMEM],
@@ -452,9 +453,10 @@
             cost_estimate=cost(0, 8 * channels * nodes),
             name="relay",
         )(*blocks_of)
-        return [moved[0]] + [
-            lax.ppermute(moved[step], "dom", pairs(step, peers)) for step in range(1, steps)
-        ]
+        sent = [moved[0]]
+        for step in range(1, steps):
+            sent.append(lax.ppermute(moved[step], "dom", pairs(step, peers)))
+        return sent
 
     def late(keep, index, others, total, hop, arrived):
         shape = (peers, channels, index.shape[1] // peers)
@@ -465,7 +467,7 @@
             out_specs=(VMEM,) * (keep + 1),
             scratch_shapes=[
                 vmem((fixed, channels + EXTRA, side), BF16),
-                vmem((blocks + 1, channels + EXTRA, side), F32),
+                vmem((blocks + 1, channels + KEPT, side), F32),
             ],
             compiler_params=params(),
         )(tile_dst, tile_src, index, others, total, hop, arrived)

time: 70.8 us -> 70.8 us (level)
  no operation moved by 1% of the time
where the time goes in v11:
time: 70.8 us; the launch traced here: 70.3 us
  waiting for transfers between devices  29.9 us (42%)
  starting transfers between devices  25.9 us (37%)
  Pallas kernels  14.4 us (20%)
    ppermute x2, waiting for transfers between devices, early(): sent = lax.ppermute(far, 'dom', pairs(peers // 2, peers))  13.7 us
    all_to_all x3, starting transfers between devices, exchange(): arrived = lax.all_to_all(send, 'dom', 0, 0, tiled=True)  12.6 us
    all_to_all x3, waiting for transfers between devices, exchange(): arrived = lax.all_to_all(send, 'dom', 0, 0, tiled=True)  10.6 us
    ppermute x6, starting transfers between devices, relay(): sent.append(lax.ppermute(moved[step], 'dom', pairs(step, peers)))  7.11 us
    ppermute x3, waiting for transfers between devices, on_device(): arrived.append(lax.ppermute(own[step], 'rep', pairs(step, reps)))  4.02 us
    pallas_call x2, Pallas kernels, early(): pl.pallas_call(lambda *refs: early_kernel(staged, *refs), out_shape=(out(...  3.96 us
    pallas_call x2, Pallas kernels, late(): pl.pallas_call(lambda *refs: finish_kernel(group, keep, *refs), out_shape...  3.91 us
    ppermute x3, starting transfers between devices, on_device(): arrived.append(lax.ppermute(own[step], 'rep', pairs(step, reps)))  3.15 us
  transfers between devices with their start and end apart: 14, of which 7 were waited for; matrix products, arithmetic and copies ran while one was open for 0% of the time, Pallas kernels for 8%

profile of v11, /device:TPU:0, one launch (start us, length us, event | category | flops | bytes accessed | tf_op | source)
XLA Modules:
  0.0 70.3 jit_solution(12373771188382059874)
XLA Ops:
  0.0 0.0 copy-start.2
  0.0 0.0 copy-start.1
  0.0 1.8 %sketch.1 = (bf16[64,512]{1,0:T(8,128)(2,1)S(1)}, bf16[64,512]{1,0:T(8,128)(2,1)S(1)}, bf16[64,512]{1,0:T(8,128)(2,1)S(1)}, bf16[64,512]{1,0:T(8,128)(2,1)S(1)}, s32[1,1024]{1,0:T(1,128)S(1)}) custom-call(bf16[512,768]{1,0:T(8,128)(2,1)} %refs_0_.6, bf16[768,256]{1,0:T(8,128)(2,1)} %refs_1_.3, s32[1,1024]{1,0:T(1,128)} %refs_2_.2), custom_call_target="tpu_custom_call" | custom-call | tf_op jit(solution)/shard_map/sketch/pallas_call | solution.py:475
  1.8 0.6 collective-permute-start
  2.4 2.5 %collective-permute-start.1 = (bf16[64,512]{1,0:T(8,128)(2,1)S(1)}, bf16[64,512]{1,0:T(8,128)(2,1)S(1)}, u32[]{:S(2)}, u32[]{:S(2)}) collective-permute-start(bf16[64,512]{1,0:T(8,128)(2,1)S(1)} %get-tuple-element.35), channel_id=1, source_target_pairs={{0,2},{1,3},{2,0},{3,1},{4,6},{5,7},{6,4},{7,5},{8,10},{9,11},{10,... | collective-permute-start | bytes 196616 | tf_op jit(solution)/shard_map/ppermute | solution.py:492
  4.9 0.0 collective-permute-start.2
  4.9 0.0 collective-permute-done.refs_2_
  4.9 2.6 %collective-permute-done.1.refs_3_ = bf16[64,512]{1,0:T(8,128)(2,1)S(1)} collective-permute-done((bf16[64,512]{1,0:T(8,128)(2,1)S(1)}, bf16[64,512]{1,0:T(8,128)(2,1)S(1)}, u32[]{:S(2)}, u32[]{:S(2)}) %collective-permute-start.1) | collective-permute-done | bytes 65568 | tf_op jit(solution)/shard_map/ppermute | solution.py:492
  7.6 1.4 %collective-permute-done.2.refs_4_ = bf16[64,512]{1,0:T(8,128)(2,1)S(1)} collective-permute-done((bf16[64,512]{1,0:T(8,128)(2,1)S(1)}, bf16[64,512]{1,0:T(8,128)(2,1)S(1)}, u32[]{:S(2)}, u32[]{:S(2)}) %collective-permute-start.2) | collective-permute-done | bytes 65568 | tf_op jit(solution)/shard_map/ppermute | solution.py:492
  9.0 1.1 %pick.1 = (bf16[8,64,256]{2,1,0:T(8,128)(2,1)S(1)}, bf16[8,64,128]{2,1,0:T(8,128)(2,1)}) custom-call(s32[1,1024]{1,0:T(1,128)S(1)} %get-tuple-element.32.refs_0_.refs_2_, bf16[64,512]{1,0:T(8,128)(2,1)S(1)} %get-tuple-element.33.refs_1_, bf16[64,512]{1,0:T(8,128)(2,1)S(1)} %collective-permute-done.refs_2_, ...), custom_call_target="tpu_custom_call" | custom-call | tf_op jit(solution)/shard_map/pick/pallas_call | solution.py:493
  10.1 5.8 %all-to-all-start = ((bf16[8,64,128]{2,1,0:T(8,128)(2,1)}), bf16[8,64,128]{2,1,0:T(8,128)(2,1)S(1)}, u32[]{:S(2)}, u32[]{:S(2)}) async-start(bf16[8,64,128]{2,1,0:T(8,128)(2,1)} %get-tuple-element.49), calls=%async_computation | async-start | bytes 262144 | tf_op jit(solution)/shard_map/all_to_all | solution.py:80
  15.9 2.0 %early.2 = (bf16[4,64,256]{2,1,0:T(8,128)(2,1)S(1)}, bf16[4,64,256]{2,1,0:T(8,128)(2,1)S(1)}, f32[8,72,256]{2,1,0:T(8,128)S(1)}, bf16[12,256,256]{2,1,0:T(8,128)(2,1)S(1)}) custom-call(s32[1,2048]{1,0:T(1,128)} %refs_2_.3, bf16[20,256,256]{2,1,0:T(8,128)(2,1)} %bitcast.1, bf16[8,64,256]{2,1,0:T(8,128)(2,1)S(1)} %get-tuple-element.37.refs_2_.refs_5_), custom_call_target="tpu_custom_call" | custom-call | flops 536870912 | bytes 1048576 | tf_op jit(solution)/shard_map/early/pallas_call | solution.py:422
  17.9 5.4 %all-to-all-done.refs_6_ = bf16[8,64,128]{2,1,0:T(8,128)(2,1)S(1)} async-done(((bf16[8,64,128]{2,1,0:T(8,128)(2,1)}), bf16[8,64,128]{2,1,0:T(8,128)(2,1)S(1)}, u32[]{:S(2)}, u32[]{:S(2)}) %all-to-all-start) | async-done | bytes 131104 | tf_op jit(solution)/shard_map/all_to_all | solution.py:80
  23.3 0.0 copy-done.2
  23.3 0.0 copy-done.1
  23.3 0.0 copy-start
  23.3 1.8 %shard_map.82 = (bf16[8,64,256]{2,1,0:T(8,128)(2,1)S(1)}, bf16[8,64,128]{2,1,0:T(8,128)(2,1)}) custom-call(s32[1,20]{1,0:T(1,128)S(1)} %copy-done.1, s32[1,20]{1,0:T(1,128)S(1)} %copy-done.2, s32[1,1024]{1,0:T(1,128)S(1)} %get-tuple-element.32.refs_0_.refs_2_, bf16[12,256,256]{2,1,0:T(8,128)(2,1)S(1)} %get-tuple-element.47.refs_3_, ...), custom_call_target="tpu_custom_call" | custom-call | tf_op jit(solution)/shard_map/pallas_call | solution.py:463
  25.0 3.4 %all-to-all-start.1 = ((bf16[8,64,128]{2,1,0:T(8,128)(2,1)}), bf16[8,64,128]{2,1,0:T(8,128)(2,1)S(1)}, u32[]{:S(2)}, u32[]{:S(2)}) async-start(bf16[8,64,128]{2,1,0:T(8,128)(2,1)} %get-tuple-element.58), calls=%async_computation.1 | async-start | bytes 262144 | tf_op jit(solution)/shard_map/all_to_all | solution.py:80
  28.4 2.0 %early.3 = (bf16[4,64,256]{2,1,0:T(8,128)(2,1)S(1)}, bf16[4,64,256]{2,1,0:T(8,128)(2,1)S(1)}, f32[8,72,256]{2,1,0:T(8,128)S(1)}) custom-call(s32[1,2048]{1,0:T(1,128)} %refs_2_.3, bf16[20,256,256]{2,1,0:T(8,128)(2,1)} %bitcast.2, bf16[8,64,256]{2,1,0:T(8,128)(2,1)S(1)} %get-tuple-element.50.refs_2_.refs_5_), custom_call_target="tpu_custom_call" | custom-call | flops 536870912 | bytes 1048576 | tf_op jit(solution)/shard_map/early/pallas_call | solution.py:422
  30.4 0.0 copy-start.3
  30.4 5.3 %all-to-all-done.1.refs_6_ = bf16[8,64,128]{2,1,0:T(8,128)(2,1)S(1)} async-done(((bf16[8,64,128]{2,1,0:T(8,128)(2,1)}), bf16[8,64,128]{2,1,0:T(8,128)(2,1)S(1)}, u32[]{:S(2)}, u32[]{:S(2)}) %all-to-all-start.1) | async-done | bytes 131104 | tf_op jit(solution)/shard_map/all_to_all | solution.py:80
  35.7 0.0 copy-done
  35.7 2.1 %shard_map.83 = bf16[8,64,256]{2,1,0:T(8,128)(2,1)} custom-call(s32[1,20]{1,0:T(1,128)S(1)} %copy-done.1, s32[1,20]{1,0:T(1,128)S(1)} %copy-done.2, s32[1,2048]{1,0:T(1,128)S(1)} %copy-done, bf16[12,256,256]{2,1,0:T(8,128)(2,1)S(1)} %get-tuple-element.47.refs_3_, f32[8,72,256]{2,1,0:T(8,128)S(1)} %get-tuple-element.57.refs_4_, ...), custom_call_target="tpu_custom_call" | custom-call | tf_op jit(solution)/shard_map/pallas_call | solution.py:463
  37.8 3.4 %all-to-all-start.2 = ((bf16[8,64,256]{2,1,0:T(8,128)(2,1)}), bf16[8,64,256]{2,1,0:T(8,128)(2,1)S(1)}, u32[]{:S(2)}, u32[]{:S(2)}) async-start(bf16[8,64,256]{2,1,0:T(8,128)(2,1)} %shard_map.83), calls=%async_computation.2 | async-start | bytes 524288 | tf_op jit(solution)/shard_map/all_to_all | solution.py:80
  41.3 2.8 %collective-permute-start.3 = (bf16[4,64,256]{2,1,0:T(8,128)(2,1)S(1)}, bf16[4,64,256]{2,1,0:T(8,128)(2,1)S(1)}, u32[]{:S(2)}, u32[]{:S(2)}) collective-permute-start(bf16[4,64,256]{2,1,0:T(8,128)(2,1)S(1)} %get-tuple-element.39), channel_id=1, source_target_pairs={{0,16},{4,20},{8,24},{12,28},{16,0},{20,4},{24,8},{28,12},{1,17},{... | collective-permute-start | bytes 393224 | tf_op jit(solution)/shard_map/ppermute | solution.py:442
  44.1 0.2 collective-permute-start.7
  44.2 13.7 %collective-permute-done.3.sent = bf16[4,64,256]{2,1,0:T(8,128)(2,1)S(1)} collective-permute-done((bf16[4,64,256]{2,1,0:T(8,128)(2,1)S(1)}, bf16[4,64,256]{2,1,0:T(8,128)(2,1)S(1)}, u32[]{:S(2)}, u32[]{:S(2)}) %collective-permute-start.3) | collective-permute-done | bytes 131104 | tf_op jit(solution)/shard_map/ppermute | solution.py:442
  58.0 1.5 %collective-permute-start.4 = (bf16[128,256]{1,0:T(8,128)(2,1)S(1)}, bf16[128,256]{1,0:T(8,128)(2,1)S(1)}, u32[]{:S(2)}, u32[]{:S(2)}) collective-permute-start(bf16[128,256]{1,0:T(8,128)(2,1)S(1)} %get-tuple-element.41), channel_id=1, source_target_pairs={{0,4},{4,0},{8,12},{12,8},{16,20},{20,16},{24,28},{28,24},{1,5},{5... | collective-permute-start | bytes 196616 | tf_op jit(solution)/shard_map/ppermute | solution.py:458
  59.5 0.0 collective-permute-start.5
  59.5 2.0 %collective-permute-start.6 = (bf16[128,256]{1,0:T(8,128)(2,1)S(1)}, bf16[128,256]{1,0:T(8,128)(2,1)S(1)}, u32[]{:S(2)}, u32[]{:S(2)}) collective-permute-start(bf16[128,256]{1,0:T(8,128)(2,1)S(1)} %get-tuple-element.43), channel_id=1, source_target_pairs={{0,12},{4,8},{8,4},{12,0},{16,28},{20,24},{24,20},{28,16},{1,13},{... | collective-permute-start | bytes 196616 | tf_op jit(solution)/shard_map/ppermute | solution.py:458
  61.5 0.0 collective-permute-done.7.sent
  61.6 1.5 %collective-permute-start.8 = (bf16[128,256]{1,0:T(8,128)(2,1)S(1)}, bf16[128,256]{1,0:T(8,128)(2,1)S(1)}, u32[]{:S(2)}, u32[]{:S(2)}) collective-permute-start(bf16[128,256]{1,0:T(8,128)(2,1)S(1)} %get-tuple-element.54), channel_id=1, source_target_pairs={{0,4},{4,0},{8,12},{12,8},{16,20},{20,16},{24,28},{28,24},{1,5},{5... | collective-permute-start | bytes 196616 | tf_op jit(solution)/shard_map/ppermute | solution.py:458
  63.1 0.0 collective-permute-start.9
  63.1 0.0 collective-permute-done.4.refs_2_
  63.1 2.0 %collective-permute-start.10 = (bf16[128,256]{1,0:T(8,128)(2,1)S(1)}, bf16[128,256]{1,0:T(8,128)(2,1)S(1)}, u32[]{:S(2)}, u32[]{:S(2)}) collective-permute-start(bf16[128,256]{1,0:T(8,128)(2,1)S(1)} %get-tuple-element.56), channel_id=1, source_target_pairs={{0,12},{4,8},{8,4},{12,0},{16,28},{20,24},{24,20},{28,16},{1,13},{... | collective-permute-start | bytes 196616 | tf_op jit(solution)/shard_map/ppermute | solution.py:458
  65.1 0.0 collective-permute-done.5.refs_3_
  65.1 0.0 collective-permute-done.6.refs_4_
  65.1 0.0 copy-done.3
  65.1 1.6 %place0.1 = (bf16[3,64,2048]{2,1,0:T(8,128)(2,1)}, bf16[2048,256]{1,0:T(8,128)(2,1)S(1)}, s32[1,2048]{1,0:T(1,128)S(1)}) custom-call(s32[1,2048]{1,0:T(1,128)S(1)} %copy-done.3, bf16[128,256]{1,0:T(8,128)(2,1)S(1)} %get-tuple-element.40.refs_1_, bf16[128,256]{1,0:T(8,128)(2,1)S(1)} %collective-permute-done.4.refs_2_, ...), custom_call_target="tpu_custom_call" | custom-call | flops 536870912 | bytes 524288 | tf_op jit(solution)/shard_map/place0/pallas_call | solution.py:515
  66.8 0.0 collective-permute-done.8.refs_4_
  66.8 0.6 collective-permute-done.9.refs_5_
  67.4 0.9 %collective-permute-done.10.refs_6_ = bf16[128,256]{1,0:T(8,128)(2,1)S(1)} collective-permute-done((bf16[128,256]{1,0:T(8,128)(2,1)S(1)}, bf16[128,256]{1,0:T(8,128)(2,1)S(1)}, u32[]{:S(2)}, u32[]{:S(2)}) %collective-permute-start.10) | collective-permute-done | bytes 65568 | tf_op jit(solution)/shard_map/ppermute | solution.py:458
  68.3 0.0 all-to-all-done.2.refs_7_
  68.3 2.0 %place.1 = bf16[3,64,2048]{2,1,0:T(8,128)(2,1)} custom-call(bf16[3,64,2048]{2,1,0:T(8,128)(2,1)} %get-tuple-element.44.refs_0_, bf16[2048,256]{1,0:T(8,128)(2,1)S(1)} %get-tuple-element.45.refs_1_, s32[1,2048]{1,0:T(1,128)S(1)} %get-tuple-element.46.refs_2_, bf16[128,256]{1,0:T(8,128)(2,1)S(1)} %get-tuple-element.53.refs_3_, ...), custom_call_target="tpu_custom_call", output_to_operand_aliasing={{}: (0, {})} | custom-call | tf_op jit(solution)/shard_map/place/pallas_call | solution.py:529
  (2 shorter events, 0.0 us)
Async XLA Ops:
  0.0 23.3 %copy-start.2 = (s32[1,20]{1,0:T(1,128)S(1)}, s32[1,20]{1,0:T(1,128)}, u32[]{:S(2)}) copy-start(s32[1,20]{1,0:T(1,128)} %refs_1_.5) | copy-start | bytes 244
  0.0 23.3 %copy-start.1 = (s32[1,20]{1,0:T(1,128)S(1)}, s32[1,20]{1,0:T(1,128)}, u32[]{:S(2)}) copy-start(s32[1,20]{1,0:T(1,128)} %refs_0_.11) | copy-start | bytes 244
  1.8 3.2 %collective-permute-start = (bf16[64,512]{1,0:T(8,128)(2,1)S(1)}, bf16[64,512]{1,0:T(8,128)(2,1)S(1)}, u32[]{:S(2)}, u32[]{:S(2)}) collective-permute-start(bf16[64,512]{1,0:T(8,128)(2,1)S(1)} %get-tuple-element.34), channel_id=1, source_target_pairs={{0,1},{1,0},{2,3},{3,2},{4,5},{5,4},{6,7},{7,6},{8,9},{9,8},{10,11... | collective-permute-start | bytes 196616 | tf_op jit(solution)/shard_map/ppermute | solution.py:492
  2.4 5.2 %collective-permute-start.1 = (bf16[64,512]{1,0:T(8,128)(2,1)S(1)}, bf16[64,512]{1,0:T(8,128)(2,1)S(1)}, u32[]{:S(2)}, u32[]{:S(2)}) collective-permute-start(bf16[64,512]{1,0:T(8,128)(2,1)S(1)} %get-tuple-element.35), channel_id=1, source_target_pairs={{0,2},{1,3},{2,0},{3,1},{4,6},{5,7},{6,4},{7,5},{8,10},{9,11},{10,... | collective-permute-start | bytes 196616 | tf_op jit(solution)/shard_map/ppermute | solution.py:492
  4.9 4.1 %collective-permute-start.2 = (bf16[64,512]{1,0:T(8,128)(2,1)S(1)}, bf16[64,512]{1,0:T(8,128)(2,1)S(1)}, u32[]{:S(2)}, u32[]{:S(2)}) collective-permute-start(bf16[64,512]{1,0:T(8,128)(2,1)S(1)} %get-tuple-element.36), channel_id=1, source_target_pairs={{0,3},{1,2},{2,1},{3,0},{4,7},{5,6},{6,5},{7,4},{8,11},{9,10},{10,... | collective-permute-start | bytes 196616 | tf_op jit(solution)/shard_map/ppermute | solution.py:492
  10.1 13.2 %all-to-all-start = ((bf16[8,64,128]{2,1,0:T(8,128)(2,1)}), bf16[8,64,128]{2,1,0:T(8,128)(2,1)S(1)}, u32[]{:S(2)}, u32[]{:S(2)}) async-start(bf16[8,64,128]{2,1,0:T(8,128)(2,1)} %get-tuple-element.49), calls=%async_computation | async-start | bytes 262144 | tf_op jit(solution)/shard_map/all_to_all | solution.py:80
  23.3 12.4 %copy-start = (s32[1,2048]{1,0:T(1,128)S(1)}, s32[1,2048]{1,0:T(1,128)}, u32[]{:S(2)}) copy-start(s32[1,2048]{1,0:T(1,128)} %refs_2_.3) | copy-start | bytes 24580
  25.0 10.7 %all-to-all-start.1 = ((bf16[8,64,128]{2,1,0:T(8,128)(2,1)}), bf16[8,64,128]{2,1,0:T(8,128)(2,1)S(1)}, u32[]{:S(2)}, u32[]{:S(2)}) async-start(bf16[8,64,128]{2,1,0:T(8,128)(2,1)} %get-tuple-element.58), calls=%async_computation.1 | async-start | bytes 262144 | tf_op jit(solution)/shard_map/all_to_all | solution.py:80
  30.4 34.7 %copy-start.3 = (s32[1,2048]{1,0:T(1,128)S(1)}, s32[1,2048]{1,0:T(1,128)}, u32[]{:S(2)}) copy-start(s32[1,2048]{1,0:T(1,128)} %refs_0_.8) | copy-start | bytes 24580
  37.8 30.4 %all-to-all-start.2 = ((bf16[8,64,256]{2,1,0:T(8,128)(2,1)}), bf16[8,64,256]{2,1,0:T(8,128)(2,1)S(1)}, u32[]{:S(2)}, u32[]{:S(2)}) async-start(bf16[8,64,256]{2,1,0:T(8,128)(2,1)} %shard_map.83), calls=%async_computation.2 | async-start | bytes 524288 | tf_op jit(solution)/shard_map/all_to_all | solution.py:80
  41.3 16.7 %collective-permute-start.3 = (bf16[4,64,256]{2,1,0:T(8,128)(2,1)S(1)}, bf16[4,64,256]{2,1,0:T(8,128)(2,1)S(1)}, u32[]{:S(2)}, u32[]{:S(2)}) collective-permute-start(bf16[4,64,256]{2,1,0:T(8,128)(2,1)S(1)} %get-tuple-element.39), channel_id=1, source_target_pairs={{0,16},{4,20},{8,24},{12,28},{16,0},{20,4},{24,8},{28,12},{1,17},{... | collective-permute-start | bytes 393224 | tf_op jit(solution)/shard_map/ppermute | solution.py:442
  44.1 17.5 %collective-permute-start.7 = (bf16[4,64,256]{2,1,0:T(8,128)(2,1)S(1)}, bf16[4,64,256]{2,1,0:T(8,128)(2,1)S(1)}, u32[]{:S(2)}, u32[]{:S(2)}) collective-permute-start(bf16[4,64,256]{2,1,0:T(8,128)(2,1)S(1)} %get-tuple-element.52), channel_id=1, source_target_pairs={{0,16},{4,20},{8,24},{12,28},{16,0},{20,4},{24,8},{28,12},{1,17},{... | collective-permute-start | bytes 393224 | tf_op jit(solution)/shard_map/ppermute | solution.py:442
  58.0 5.1 %collective-permute-start.4 = (bf16[128,256]{1,0:T(8,128)(2,1)S(1)}, bf16[128,256]{1,0:T(8,128)(2,1)S(1)}, u32[]{:S(2)}, u32[]{:S(2)}) collective-permute-start(bf16[128,256]{1,0:T(8,128)(2,1)S(1)} %get-tuple-element.41), channel_id=1, source_target_pairs={{0,4},{4,0},{8,12},{12,8},{16,20},{20,16},{24,28},{28,24},{1,5},{5... | collective-permute-start | bytes 196616 | tf_op jit(solution)/shard_map/ppermute | solution.py:458
  59.5 5.6 %collective-permute-start.5 = (bf16[128,256]{1,0:T(8,128)(2,1)S(1)}, bf16[128,256]{1,0:T(8,128)(2,1)S(1)}, u32[]{:S(2)}, u32[]{:S(2)}) collective-permute-start(bf16[128,256]{1,0:T(8,128)(2,1)S(1)} %get-tuple-element.42), channel_id=1, source_target_pairs={{0,8},{4,12},{8,0},{12,4},{16,24},{20,28},{24,16},{28,20},{1,9},{5... | collective-permute-start | bytes 196616 | tf_op jit(solution)/shard_map/ppermute | solution.py:458
  59.5 5.6 %collective-permute-start.6 = (bf16[128,256]{1,0:T(8,128)(2,1)S(1)}, bf16[128,256]{1,0:T(8,128)(2,1)S(1)}, u32[]{:S(2)}, u32[]{:S(2)}) collective-permute-start(bf16[128,256]{1,0:T(8,128)(2,1)S(1)} %get-tuple-element.43), channel_id=1, source_target_pairs={{0,12},{4,8},{8,4},{12,0},{16,28},{20,24},{24,20},{28,16},{1,13},{... | collective-permute-start | bytes 196616 | tf_op jit(solution)/shard_map/ppermute | solution.py:458
  61.6 5.2 %collective-permute-start.8 = (bf16[128,256]{1,0:T(8,128)(2,1)S(1)}, bf16[128,256]{1,0:T(8,128)(2,1)S(1)}, u32[]{:S(2)}, u32[]{:S(2)}) collective-permute-start(bf16[128,256]{1,0:T(8,128)(2,1)S(1)} %get-tuple-element.54), channel_id=1, source_target_pairs={{0,4},{4,0},{8,12},{12,8},{16,20},{20,16},{24,28},{28,24},{1,5},{5... | collective-permute-start | bytes 196616 | tf_op jit(solution)/shard_map/ppermute | solution.py:458
  63.1 4.3 %collective-permute-start.9 = (bf16[128,256]{1,0:T(8,128)(2,1)S(1)}, bf16[128,256]{1,0:T(8,128)(2,1)S(1)}, u32[]{:S(2)}, u32[]{:S(2)}) collective-permute-start(bf16[128,256]{1,0:T(8,128)(2,1)S(1)} %get-tuple-element.55), channel_id=1, source_target_pairs={{0,8},{4,12},{8,0},{12,4},{16,24},{20,28},{24,16},{28,20},{1,9},{5... | collective-permute-start | bytes 196616 | tf_op jit(solution)/shard_map/ppermute | solution.py:458
  63.1 5.2 %collective-permute-start.10 = (bf16[128,256]{1,0:T(8,128)(2,1)S(1)}, bf16[128,256]{1,0:T(8,128)(2,1)S(1)}, u32[]{:S(2)}, u32[]{:S(2)}) collective-permute-start(bf16[128,256]{1,0:T(8,128)(2,1)S(1)} %get-tuple-element.56), channel_id=1, source_target_pairs={{0,12},{4,8},{8,4},{12,0},{16,28},{20,24},{24,20},{28,16},{1,13},{... | collective-permute-start | bytes 196616 | tf_op jit(solution)/shard_map/ppermute | solution.py:458

commit v12 on v11

--- a/solution.py
+++ b/solution.py
@@ -57,7 +57,7 @@
     return parts
 
 
-def store_slots(buffer, parts, group):
+def store_slots(buffer, parts, group, turn=0):
     if len(buffer.shape) == 2:
         for place, part in enumerate(parts):
             buffer[:, place * group : (place + 1) * group] = part
@@ -65,7 +65,8 @@
     slot = buffer.shape[2]
     for place, part in enumerate(parts):
         for start in range(0, group, slot):
-            buffer[(place * group + start) // slot] = part[:, start : start + slot]
+            peer = (place * group + start) // slot
+            buffer[peer ^ turn] = part[:, start : start + slot]
 
 
 def send_shape(channels, peers, slot):
@@ -74,19 +75,20 @@
     return (peers, channels, slot)
 
 
-def exchange(send, peers):
+def exchange(send, peers, turn=0):
     if send.ndim == 2:
         send = send.reshape(send.shape[0], peers, -1).transpose(1, 0, 2)
-    arrived = lax.all_to_all(send, "dom", 0, 0, tiled=True)
+    ranks = [[rank ^ turn for rank in range(peers)]] if turn else None
+    arrived = lax.all_to_all(send, "dom", 0, 0, tiled=True, axis_index_groups=ranks)
     if arrived.shape[2] % 128 == 0:
         return arrived
     return arrived.transpose(1, 0, 2).reshape(arrived.shape[1], -1)
 
 
-def load_wide(ref):
+def load_wide(ref, turn=0):
     if len(ref.shape) == 2:
         return ref[...]
-    return jnp.concatenate([ref[peer] for peer in range(ref.shape[0])], axis=1)
+    return jnp.concatenate([ref[peer ^ turn] for peer in range(ref.shape[0])], axis=1)
 
 
 def partner(me, step, count):
@@ -133,7 +135,7 @@
     copies[-1].wait()
 
 
-def pick_kernel(count, group, index, *rest):
+def pick_kernel(count, group, turn, index, *rest):
     arrived, (hop, send) = rest[:count], rest[count:]
     blocks, _, side = hop.shape
     per = blocks // count
@@ -143,7 +145,7 @@
         for part in range(per):
             hop[first + part] = arrived[step][:, part * side : (part + 1) * side]
     stack = jnp.concatenate([hop[block] for block in range(blocks)], 0)
-    store_slots(send, pick(stack, blocks, index[...], side, group), group)
+    store_slots(send, pick(stack, blocks, index[...], side, group), group, turn)
 
 
 def combine(dst_in, src_in, index_in, tiles_in, hop, arrived_ref, scratch, store):
@@ -240,7 +242,7 @@
         copies[2].wait()
 
 
-def finish(dst, src, tiles, total, hop, arrived, columns, sums):
+def finish(turn, dst, src, tiles, total, hop, arrived, columns, sums):
     blocks, channels, side = hop.shape
     fixed = columns.shape[0]
     slots = blocks + tiles.shape[0]
@@ -255,7 +257,7 @@
     for block in range(blocks):
         columns[block, :channels, :] = hop[block]
         sums[block] = total[block]
-    wide = load_wide(arrived)
+    wide = load_wide(arrived, turn)
     for block in range(blocks, fixed):
         start = (block - blocks) * side
         columns[block, :channels, :] = wide[:, start : start + side]
@@ -277,16 +279,16 @@
 
 
 def finish_kernel(
-    group, keep, dst, src, index, tiles, total, hop, arrived, *rest
+    group, turn, keep, dst, src, index, tiles, total, hop, arrived, *rest
 ):
     send, scratch = rest[keep], rest[keep + 1 :]
-    results = finish(dst, src, tiles, total, hop, arrived, *scratch)
+    results = finish(turn, dst, src, tiles, total, hop, arrived, *scratch)
     blocks, _, side = hop.shape
     if keep:
         for block, result in enumerate(results):
             rest[0][block] = result
     stack = jnp.concatenate(results, 0)
-    store_slots(send, pick(stack, blocks, index[...], side, group), group)
+    store_slots(send, pick(stack, blocks, index[...], side, group), group, turn)
 
 
 def relay_kernel(near, sent, *outs):
@@ -374,7 +376,7 @@
     for step in range(peers):
         first = (step // half) * channels
         arrived = moved[step % half][first : first + channels]
-        parts.append(jnp.concatenate([arrived, last[me ^ step]], 0))
+        parts.append(jnp.concatenate([arrived, last[me ^ step ^ half]], 0))
     scatter(parts, table_ref[...], block_ref[...], out, out_ref, 1, sems)
 
 
@@ -412,6 +414,10 @@
     last_shape = send_shape(3 * channels, peers, nodes // peers)
     group = 256
     chunks = 1
+    slot = nodes // peers
+    half = peers // 2
+    whole_lanes = slot % 128 == 0 and (halo // peers) % 128 == 0
+    turn = half if whole_lanes and peers & (peers - 1) == 0 else 0
 
     def out(shape):
         return jax.ShapeDtypeStruct(shape, BF16)
@@ -461,7 +467,7 @@
     def late(keep, index, others, total, hop, arrived):
         shape = (peers, channels, index.shape[1] // peers)
         return pl.pallas_call(
-            lambda *refs: finish_kernel(group, keep, *refs),
+            lambda *refs: finish_kernel(group, half, keep, *refs),
             out_shape=(out(hop_shape),) * keep + (out(shape),),
             in_specs=[VMEM] * 7,
             out_specs=(VMEM,) * (keep + 1),
@@ -491,25 +497,22 @@
     for step in range(1, reps):
         arrived.append(lax.ppermute(own[step], "rep", pairs(step, reps)))
     hop0, send = pl.pallas_call(
-        lambda *refs: pick_kernel(reps, group, *refs),
+        lambda *refs: pick_kernel(reps, group, turn, *refs),
         out_shape=(out(hop_shape), out(halo_shape)),
         in_specs=[VMEM] * (reps + 1),
         out_specs=(VMEM, VMEM),
         compiler_params=params(),
         name="pick",
     )(halo_rows, *arrived)
-    slot = nodes // peers
-    whole_lanes = slot % 128 == 0 and (halo // peers) % 128 == 0
-    if whole_lanes and peers > 1 and peers & (peers - 1) == 0:
-        half = peers // 2
-        halo0 = exchange(send, peers)
+    if turn:
+        halo0 = exchange(send, peers, turn)
         early0, total, others = early(hop0, 1)
         others = others[0]
         hop1, send = late(1, halo_rows, others, total, hop0, halo0)
-        halo1 = exchange(send, peers)
+        halo1 = exchange(send, peers, turn)
         early1, total, _ = early(hop1, 0)
         (send,) = late(0, send_order, others, total, hop1, halo1)
-        last = exchange(send, peers)
+        last = exchange(send, peers, turn)
         moved0, moved1 = relay(early0), relay(early1)
         whole = out((3, channels, nodes))
         placed, table, block = pl.pallas_call(

time: 70.8 us -> 65.7 us (0.928)
  waiting for transfers between devices: 29.9 us -> 22.5 us
  starting transfers between devices: 25.9 us -> 28.1 us
    all_to_all x3, waiting for transfers between devices: 10.6 us -> 5.98 us  [exchange(): lax.all_to_all(send, 'dom', 0, 0, tiled=True, axis_index_groups=ranks)]
    ppermute x2, waiting for transfers between devices: 13.7 us -> 11.2 us  [early(): sent = lax.ppermute(far, 'dom', pairs(peers // 2, peers))]
    all_to_all x3, starting transfers between devices: 12.6 us -> 15 us  [exchange(): lax.all_to_all(send, 'dom', 0, 0, tiled=True, axis_index_groups=ranks)]
  transfers between devices with their start and end apart: 14 -> 14, of which waited for: 7 -> 7; matrix products, arithmetic and copies ran while one was open for 0% -> 0% of each run, Pallas kernels for 8% -> 9%
where the time goes in v12:
time: 65.7 us; the launch traced here: 65.2 us
  starting transfers between devices  28.1 us (43%)
  waiting for transfers between devices  22.5 us (34%)
  Pallas kernels  14.4 us (22%)
    all_to_all x3, starting transfers between devices, exchange(): lax.all_to_all(send, 'dom', 0, 0, tiled=True, axis_index_groups=ranks)  15 us
    ppermute x2, waiting for transfers between devices, early(): sent = lax.ppermute(far, 'dom', pairs(peers // 2, peers))  11.2 us
    ppermute x6, starting transfers between devices, relay(): sent.append(lax.ppermute(moved[step], 'dom', pairs(step, peers)))  7.11 us
    all_to_all x3, waiting for transfers between devices, exchange(): lax.all_to_all(send, 'dom', 0, 0, tiled=True, axis_index_groups=ranks)  5.98 us
    ppermute x3, waiting for transfers between devices, on_device(): arrived.append(lax.ppermute(own[step], 'rep', pairs(step, reps)))  4.02 us
    pallas_call x2, Pallas kernels, early(): pl.pallas_call(lambda *refs: early_kernel(staged, *refs), out_shape=(out(...  3.96 us
    pallas_call x2, Pallas kernels, late(): pl.pallas_call(lambda *refs: finish_kernel(group, half, keep, *refs), out...  3.91 us
    ppermute x3, starting transfers between devices, on_device(): arrived.append(lax.ppermute(own[step], 'rep', pairs(step, reps)))  3.15 us
  transfers between devices with their start and end apart: 14, of which 7 were waited for; matrix products, arithmetic and copies ran while one was open for 0% of the time, Pallas kernels for 9%

profile of v12, /device:TPU:0, one launch (start us, length us, event | category | flops | bytes accessed | tf_op | source)
XLA Modules:
  0.0 65.2 jit_solution(404074062052330806)
XLA Ops:
  0.0 0.0 copy-start.2
  0.0 0.0 copy-start.1
  0.0 1.8 %sketch.1 = (bf16[64,512]{1,0:T(8,128)(2,1)S(1)}, bf16[64,512]{1,0:T(8,128)(2,1)S(1)}, bf16[64,512]{1,0:T(8,128)(2,1)S(1)}, bf16[64,512]{1,0:T(8,128)(2,1)S(1)}, s32[1,1024]{1,0:T(1,128)S(1)}) custom-call(bf16[512,768]{1,0:T(8,128)(2,1)} %refs_0_.6, bf16[768,256]{1,0:T(8,128)(2,1)} %refs_1_.3, s32[1,1024]{1,0:T(1,128)} %refs_2_.2), custom_call_target="tpu_custom_call" | custom-call | tf_op jit(solution)/shard_map/sketch/pallas_call | solution.py:481
  1.8 0.6 collective-permute-start
  2.4 2.5 %collective-permute-start.1 = (bf16[64,512]{1,0:T(8,128)(2,1)S(1)}, bf16[64,512]{1,0:T(8,128)(2,1)S(1)}, u32[]{:S(2)}, u32[]{:S(2)}) collective-permute-start(bf16[64,512]{1,0:T(8,128)(2,1)S(1)} %get-tuple-element.35), channel_id=1, source_target_pairs={{0,2},{1,3},{2,0},{3,1},{4,6},{5,7},{6,4},{7,5},{8,10},{9,11},{10,... | collective-permute-start | bytes 196616 | tf_op jit(solution)/shard_map/ppermute | solution.py:498
  4.9 0.0 collective-permute-start.2
  4.9 0.0 collective-permute-done.refs_2_
  4.9 2.6 %collective-permute-done.1.refs_3_ = bf16[64,512]{1,0:T(8,128)(2,1)S(1)} collective-permute-done((bf16[64,512]{1,0:T(8,128)(2,1)S(1)}, bf16[64,512]{1,0:T(8,128)(2,1)S(1)}, u32[]{:S(2)}, u32[]{:S(2)}) %collective-permute-start.1) | collective-permute-done | bytes 65568 | tf_op jit(solution)/shard_map/ppermute | solution.py:498
  7.6 1.4 %collective-permute-done.2.refs_4_ = bf16[64,512]{1,0:T(8,128)(2,1)S(1)} collective-permute-done((bf16[64,512]{1,0:T(8,128)(2,1)S(1)}, bf16[64,512]{1,0:T(8,128)(2,1)S(1)}, u32[]{:S(2)}, u32[]{:S(2)}) %collective-permute-start.2) | collective-permute-done | bytes 65568 | tf_op jit(solution)/shard_map/ppermute | solution.py:498
  9.0 1.1 %pick.1 = (bf16[8,64,256]{2,1,0:T(8,128)(2,1)S(1)}, bf16[8,64,128]{2,1,0:T(8,128)(2,1)}) custom-call(s32[1,1024]{1,0:T(1,128)S(1)} %get-tuple-element.32.refs_0_.refs_2_, bf16[64,512]{1,0:T(8,128)(2,1)S(1)} %get-tuple-element.33.refs_1_, bf16[64,512]{1,0:T(8,128)(2,1)S(1)} %collective-permute-done.refs_2_, ...), custom_call_target="tpu_custom_call" | custom-call | tf_op jit(solution)/shard_map/pick/pallas_call | solution.py:499
  10.1 6.4 %all-to-all-start = ((bf16[8,64,128]{2,1,0:T(8,128)(2,1)}), bf16[8,64,128]{2,1,0:T(8,128)(2,1)S(1)}, u32[]{:S(2)}, u32[]{:S(2)}) async-start(bf16[8,64,128]{2,1,0:T(8,128)(2,1)} %get-tuple-element.49), calls=%async_computation | async-start | bytes 262144 | tf_op jit(solution)/shard_map/all_to_all | solution.py:82
  16.5 2.0 %early.2 = (bf16[4,64,256]{2,1,0:T(8,128)(2,1)S(1)}, bf16[4,64,256]{2,1,0:T(8,128)(2,1)S(1)}, f32[8,72,256]{2,1,0:T(8,128)S(1)}, bf16[12,256,256]{2,1,0:T(8,128)(2,1)S(1)}) custom-call(s32[1,2048]{1,0:T(1,128)} %refs_2_.3, bf16[20,256,256]{2,1,0:T(8,128)(2,1)} %bitcast.1, bf16[8,64,256]{2,1,0:T(8,128)(2,1)S(1)} %get-tuple-element.37.refs_2_.refs_5_), custom_call_target="tpu_custom_call" | custom-call | flops 536870912 | bytes 1048576 | tf_op jit(solution)/shard_map/early/pallas_call | solution.py:428
  18.5 3.0 %all-to-all-done.refs_6_ = bf16[8,64,128]{2,1,0:T(8,128)(2,1)S(1)} async-done(((bf16[8,64,128]{2,1,0:T(8,128)(2,1)}), bf16[8,64,128]{2,1,0:T(8,128)(2,1)S(1)}, u32[]{:S(2)}, u32[]{:S(2)}) %all-to-all-start) | async-done | bytes 131104 | tf_op jit(solution)/shard_map/all_to_all | solution.py:82
  21.5 0.0 copy-done.2
  21.5 0.0 copy-done.1
  21.5 0.0 copy-start
  21.5 1.8 %shard_map.82 = (bf16[8,64,256]{2,1,0:T(8,128)(2,1)S(1)}, bf16[8,64,128]{2,1,0:T(8,128)(2,1)}) custom-call(s32[1,20]{1,0:T(1,128)S(1)} %copy-done.1, s32[1,20]{1,0:T(1,128)S(1)} %copy-done.2, s32[1,1024]{1,0:T(1,128)S(1)} %get-tuple-element.32.refs_0_.refs_2_, bf16[12,256,256]{2,1,0:T(8,128)(2,1)S(1)} %get-tuple-element.47.refs_3_, ...), custom_call_target="tpu_custom_call" | custom-call | tf_op jit(solution)/shard_map/pallas_call | solution.py:469
  23.2 4.4 %all-to-all-start.1 = ((bf16[8,64,128]{2,1,0:T(8,128)(2,1)}), bf16[8,64,128]{2,1,0:T(8,128)(2,1)S(1)}, u32[]{:S(2)}, u32[]{:S(2)}) async-start(bf16[8,64,128]{2,1,0:T(8,128)(2,1)} %get-tuple-element.58), calls=%async_computation.1 | async-start | bytes 262144 | tf_op jit(solution)/shard_map/all_to_all | solution.py:82
  27.6 2.0 %early.3 = (bf16[4,64,256]{2,1,0:T(8,128)(2,1)S(1)}, bf16[4,64,256]{2,1,0:T(8,128)(2,1)S(1)}, f32[8,72,256]{2,1,0:T(8,128)S(1)}) custom-call(s32[1,2048]{1,0:T(1,128)} %refs_2_.3, bf16[20,256,256]{2,1,0:T(8,128)(2,1)} %bitcast.2, bf16[8,64,256]{2,1,0:T(8,128)(2,1)S(1)} %get-tuple-element.50.refs_2_.refs_5_), custom_call_target="tpu_custom_call" | custom-call | flops 536870912 | bytes 1048576 | tf_op jit(solution)/shard_map/early/pallas_call | solution.py:428
  29.6 0.0 copy-start.3
  29.6 3.0 %all-to-all-done.1.refs_6_ = bf16[8,64,128]{2,1,0:T(8,128)(2,1)S(1)} async-done(((bf16[8,64,128]{2,1,0:T(8,128)(2,1)}), bf16[8,64,128]{2,1,0:T(8,128)(2,1)S(1)}, u32[]{:S(2)}, u32[]{:S(2)}) %all-to-all-start.1) | async-done | bytes 131104 | tf_op jit(solution)/shard_map/all_to_all | solution.py:82
  32.6 0.0 copy-done
  32.6 2.1 %shard_map.83 = bf16[8,64,256]{2,1,0:T(8,128)(2,1)} custom-call(s32[1,20]{1,0:T(1,128)S(1)} %copy-done.1, s32[1,20]{1,0:T(1,128)S(1)} %copy-done.2, s32[1,2048]{1,0:T(1,128)S(1)} %copy-done, bf16[12,256,256]{2,1,0:T(8,128)(2,1)S(1)} %get-tuple-element.47.refs_3_, f32[8,72,256]{2,1,0:T(8,128)S(1)} %get-tuple-element.57.refs_4_, ...), custom_call_target="tpu_custom_call" | custom-call | tf_op jit(solution)/shard_map/pallas_call | solution.py:469
  34.7 4.2 %all-to-all-start.2 = ((bf16[8,64,256]{2,1,0:T(8,128)(2,1)}), bf16[8,64,256]{2,1,0:T(8,128)(2,1)S(1)}, u32[]{:S(2)}, u32[]{:S(2)}) async-start(bf16[8,64,256]{2,1,0:T(8,128)(2,1)} %shard_map.83), calls=%async_computation.2 | async-start | bytes 524288 | tf_op jit(solution)/shard_map/all_to_all | solution.py:82
  38.9 0.1 collective-permute-start.3
  39.0 2.9 %collective-permute-start.7 = (bf16[4,64,256]{2,1,0:T(8,128)(2,1)S(1)}, bf16[4,64,256]{2,1,0:T(8,128)(2,1)S(1)}, u32[]{:S(2)}, u32[]{:S(2)}) collective-permute-start(bf16[4,64,256]{2,1,0:T(8,128)(2,1)S(1)} %get-tuple-element.52), channel_id=1, source_target_pairs={{0,16},{4,20},{8,24},{12,28},{16,0},{20,4},{24,8},{28,12},{1,17},{... | collective-permute-start | bytes 393224 | tf_op jit(solution)/shard_map/ppermute | solution.py:448
  41.8 11.2 %collective-permute-done.3.sent = bf16[4,64,256]{2,1,0:T(8,128)(2,1)S(1)} collective-permute-done((bf16[4,64,256]{2,1,0:T(8,128)(2,1)S(1)}, bf16[4,64,256]{2,1,0:T(8,128)(2,1)S(1)}, u32[]{:S(2)}, u32[]{:S(2)}) %collective-permute-start.3) | collective-permute-done | bytes 131104 | tf_op jit(solution)/shard_map/ppermute | solution.py:448
  53.0 1.4 %collective-permute-start.4 = (bf16[128,256]{1,0:T(8,128)(2,1)S(1)}, bf16[128,256]{1,0:T(8,128)(2,1)S(1)}, u32[]{:S(2)}, u32[]{:S(2)}) collective-permute-start(bf16[128,256]{1,0:T(8,128)(2,1)S(1)} %get-tuple-element.41), channel_id=1, source_target_pairs={{0,4},{4,0},{8,12},{12,8},{16,20},{20,16},{24,28},{28,24},{1,5},{5... | collective-permute-start | bytes 196616 | tf_op jit(solution)/shard_map/ppermute | solution.py:464
  54.4 0.0 collective-permute-start.5
  54.4 2.2 %collective-permute-start.6 = (bf16[128,256]{1,0:T(8,128)(2,1)S(1)}, bf16[128,256]{1,0:T(8,128)(2,1)S(1)}, u32[]{:S(2)}, u32[]{:S(2)}) collective-permute-start(bf16[128,256]{1,0:T(8,128)(2,1)S(1)} %get-tuple-element.43), channel_id=1, source_target_pairs={{0,12},{4,8},{8,4},{12,0},{16,28},{20,24},{24,20},{28,16},{1,13},{... | collective-permute-start | bytes 196616 | tf_op jit(solution)/shard_map/ppermute | solution.py:464
  56.6 0.0 collective-permute-done.7.sent
  56.6 1.4 %collective-permute-start.8 = (bf16[128,256]{1,0:T(8,128)(2,1)S(1)}, bf16[128,256]{1,0:T(8,128)(2,1)S(1)}, u32[]{:S(2)}, u32[]{:S(2)}) collective-permute-start(bf16[128,256]{1,0:T(8,128)(2,1)S(1)} %get-tuple-element.54), channel_id=1, source_target_pairs={{0,4},{4,0},{8,12},{12,8},{16,20},{20,16},{24,28},{28,24},{1,5},{5... | collective-permute-start | bytes 196616 | tf_op jit(solution)/shard_map/ppermute | solution.py:464
  58.0 0.0 collective-permute-start.9
  58.0 0.0 collective-permute-done.4.refs_2_
  58.0 2.2 %collective-permute-start.10 = (bf16[128,256]{1,0:T(8,128)(2,1)S(1)}, bf16[128,256]{1,0:T(8,128)(2,1)S(1)}, u32[]{:S(2)}, u32[]{:S(2)}) collective-permute-start(bf16[128,256]{1,0:T(8,128)(2,1)S(1)} %get-tuple-element.56), channel_id=1, source_target_pairs={{0,12},{4,8},{8,4},{12,0},{16,28},{20,24},{24,20},{28,16},{1,13},{... | collective-permute-start | bytes 196616 | tf_op jit(solution)/shard_map/ppermute | solution.py:464
  60.2 0.0 collective-permute-done.5.refs_3_
  60.2 0.0 collective-permute-done.6.refs_4_
  60.2 0.0 copy-done.3
  60.2 1.6 %place0.1 = (bf16[3,64,2048]{2,1,0:T(8,128)(2,1)}, bf16[2048,256]{1,0:T(8,128)(2,1)S(1)}, s32[1,2048]{1,0:T(1,128)S(1)}) custom-call(s32[1,2048]{1,0:T(1,128)S(1)} %copy-done.3, bf16[128,256]{1,0:T(8,128)(2,1)S(1)} %get-tuple-element.40.refs_1_, bf16[128,256]{1,0:T(8,128)(2,1)S(1)} %collective-permute-done.4.refs_2_, ...), custom_call_target="tpu_custom_call" | custom-call | flops 536870912 | bytes 524288 | tf_op jit(solution)/shard_map/place0/pallas_call | solution.py:518
  61.8 0.0 collective-permute-done.8.refs_4_
  61.8 0.5 collective-permute-done.9.refs_5_
  62.3 0.9 %collective-permute-done.10.refs_6_ = bf16[128,256]{1,0:T(8,128)(2,1)S(1)} collective-permute-done((bf16[128,256]{1,0:T(8,128)(2,1)S(1)}, bf16[128,256]{1,0:T(8,128)(2,1)S(1)}, u32[]{:S(2)}, u32[]{:S(2)}) %collective-permute-start.10) | collective-permute-done | bytes 65568 | tf_op jit(solution)/shard_map/ppermute | solution.py:464
  63.2 0.0 all-to-all-done.2.refs_7_
  63.2 2.0 %place.1 = bf16[3,64,2048]{2,1,0:T(8,128)(2,1)} custom-call(bf16[3,64,2048]{2,1,0:T(8,128)(2,1)} %get-tuple-element.44.refs_0_, bf16[2048,256]{1,0:T(8,128)(2,1)S(1)} %get-tuple-element.45.refs_1_, s32[1,2048]{1,0:T(1,128)S(1)} %get-tuple-element.46.refs_2_, bf16[128,256]{1,0:T(8,128)(2,1)S(1)} %get-tuple-element.53.refs_3_, ...), custom_call_target="tpu_custom_call", output_to_operand_aliasing={{}: (0, {})} | custom-call | tf_op jit(solution)/shard_map/place/pallas_call | solution.py:532
  (2 shorter events, 0.0 us)
Async XLA Ops:
  0.0 21.5 %copy-start.2 = (s32[1,20]{1,0:T(1,128)S(1)}, s32[1,20]{1,0:T(1,128)}, u32[]{:S(2)}) copy-start(s32[1,20]{1,0:T(1,128)} %refs_1_.5) | copy-start | bytes 244
  0.0 21.5 %copy-start.1 = (s32[1,20]{1,0:T(1,128)S(1)}, s32[1,20]{1,0:T(1,128)}, u32[]{:S(2)}) copy-start(s32[1,20]{1,0:T(1,128)} %refs_0_.11) | copy-start | bytes 244
  1.8 3.2 %collective-permute-start = (bf16[64,512]{1,0:T(8,128)(2,1)S(1)}, bf16[64,512]{1,0:T(8,128)(2,1)S(1)}, u32[]{:S(2)}, u32[]{:S(2)}) collective-permute-start(bf16[64,512]{1,0:T(8,128)(2,1)S(1)} %get-tuple-element.34), channel_id=1, source_target_pairs={{0,1},{1,0},{2,3},{3,2},{4,5},{5,4},{6,7},{7,6},{8,9},{9,8},{10,11... | collective-permute-start | bytes 196616 | tf_op jit(solution)/shard_map/ppermute | solution.py:498
  2.4 5.2 %collective-permute-start.1 = (bf16[64,512]{1,0:T(8,128)(2,1)S(1)}, bf16[64,512]{1,0:T(8,128)(2,1)S(1)}, u32[]{:S(2)}, u32[]{:S(2)}) collective-permute-start(bf16[64,512]{1,0:T(8,128)(2,1)S(1)} %get-tuple-element.35), channel_id=1, source_target_pairs={{0,2},{1,3},{2,0},{3,1},{4,6},{5,7},{6,4},{7,5},{8,10},{9,11},{10,... | collective-permute-start | bytes 196616 | tf_op jit(solution)/shard_map/ppermute | solution.py:498
  4.9 4.1 %collective-permute-start.2 = (bf16[64,512]{1,0:T(8,128)(2,1)S(1)}, bf16[64,512]{1,0:T(8,128)(2,1)S(1)}, u32[]{:S(2)}, u32[]{:S(2)}) collective-permute-start(bf16[64,512]{1,0:T(8,128)(2,1)S(1)} %get-tuple-element.36), channel_id=1, source_target_pairs={{0,3},{1,2},{2,1},{3,0},{4,7},{5,6},{6,5},{7,4},{8,11},{9,10},{10,... | collective-permute-start | bytes 196616 | tf_op jit(solution)/shard_map/ppermute | solution.py:498
  10.1 11.4 %all-to-all-start = ((bf16[8,64,128]{2,1,0:T(8,128)(2,1)}), bf16[8,64,128]{2,1,0:T(8,128)(2,1)S(1)}, u32[]{:S(2)}, u32[]{:S(2)}) async-start(bf16[8,64,128]{2,1,0:T(8,128)(2,1)} %get-tuple-element.49), calls=%async_computation | async-start | bytes 262144 | tf_op jit(solution)/shard_map/all_to_all | solution.py:82
  21.5 11.1 %copy-start = (s32[1,2048]{1,0:T(1,128)S(1)}, s32[1,2048]{1,0:T(1,128)}, u32[]{:S(2)}) copy-start(s32[1,2048]{1,0:T(1,128)} %refs_2_.3) | copy-start | bytes 24580
  23.2 9.3 %all-to-all-start.1 = ((bf16[8,64,128]{2,1,0:T(8,128)(2,1)}), bf16[8,64,128]{2,1,0:T(8,128)(2,1)S(1)}, u32[]{:S(2)}, u32[]{:S(2)}) async-start(bf16[8,64,128]{2,1,0:T(8,128)(2,1)} %get-tuple-element.58), calls=%async_computation.1 | async-start | bytes 262144 | tf_op jit(solution)/shard_map/all_to_all | solution.py:82
  29.6 30.6 %copy-start.3 = (s32[1,2048]{1,0:T(1,128)S(1)}, s32[1,2048]{1,0:T(1,128)}, u32[]{:S(2)}) copy-start(s32[1,2048]{1,0:T(1,128)} %refs_0_.8) | copy-start | bytes 24580
  34.7 28.5 %all-to-all-start.2 = ((bf16[8,64,256]{2,1,0:T(8,128)(2,1)}), bf16[8,64,256]{2,1,0:T(8,128)(2,1)S(1)}, u32[]{:S(2)}, u32[]{:S(2)}) async-start(bf16[8,64,256]{2,1,0:T(8,128)(2,1)} %shard_map.83), calls=%async_computation.2 | async-start | bytes 524288 | tf_op jit(solution)/shard_map/all_to_all | solution.py:82
  38.9 14.1 %collective-permute-start.3 = (bf16[4,64,256]{2,1,0:T(8,128)(2,1)S(1)}, bf16[4,64,256]{2,1,0:T(8,128)(2,1)S(1)}, u32[]{:S(2)}, u32[]{:S(2)}) collective-permute-start(bf16[4,64,256]{2,1,0:T(8,128)(2,1)S(1)} %get-tuple-element.39), channel_id=1, source_target_pairs={{0,16},{4,20},{8,24},{12,28},{16,0},{20,4},{24,8},{28,12},{1,17},{... | collective-permute-start | bytes 393224 | tf_op jit(solution)/shard_map/ppermute | solution.py:448
  39.0 17.6 %collective-permute-start.7 = (bf16[4,64,256]{2,1,0:T(8,128)(2,1)S(1)}, bf16[4,64,256]{2,1,0:T(8,128)(2,1)S(1)}, u32[]{:S(2)}, u32[]{:S(2)}) collective-permute-start(bf16[4,64,256]{2,1,0:T(8,128)(2,1)S(1)} %get-tuple-element.52), channel_id=1, source_target_pairs={{0,16},{4,20},{8,24},{12,28},{16,0},{20,4},{24,8},{28,12},{1,17},{... | collective-permute-start | bytes 393224 | tf_op jit(solution)/shard_map/ppermute | solution.py:448
  53.0 5.0 %collective-permute-start.4 = (bf16[128,256]{1,0:T(8,128)(2,1)S(1)}, bf16[128,256]{1,0:T(8,128)(2,1)S(1)}, u32[]{:S(2)}, u32[]{:S(2)}) collective-permute-start(bf16[128,256]{1,0:T(8,128)(2,1)S(1)} %get-tuple-element.41), channel_id=1, source_target_pairs={{0,4},{4,0},{8,12},{12,8},{16,20},{20,16},{24,28},{28,24},{1,5},{5... | collective-permute-start | bytes 196616 | tf_op jit(solution)/shard_map/ppermute | solution.py:464
  54.4 5.7 %collective-permute-start.5 = (bf16[128,256]{1,0:T(8,128)(2,1)S(1)}, bf16[128,256]{1,0:T(8,128)(2,1)S(1)}, u32[]{:S(2)}, u32[]{:S(2)}) collective-permute-start(bf16[128,256]{1,0:T(8,128)(2,1)S(1)} %get-tuple-element.42), channel_id=1, source_target_pairs={{0,8},{4,12},{8,0},{12,4},{16,24},{20,28},{24,16},{28,20},{1,9},{5... | collective-permute-start | bytes 196616 | tf_op jit(solution)/shard_map/ppermute | solution.py:464
  54.4 5.7 %collective-permute-start.6 = (bf16[128,256]{1,0:T(8,128)(2,1)S(1)}, bf16[128,256]{1,0:T(8,128)(2,1)S(1)}, u32[]{:S(2)}, u32[]{:S(2)}) collective-permute-start(bf16[128,256]{1,0:T(8,128)(2,1)S(1)} %get-tuple-element.43), channel_id=1, source_target_pairs={{0,12},{4,8},{8,4},{12,0},{16,28},{20,24},{24,20},{28,16},{1,13},{... | collective-permute-start | bytes 196616 | tf_op jit(solution)/shard_map/ppermute | solution.py:464
  56.6 5.2 %collective-permute-start.8 = (bf16[128,256]{1,0:T(8,128)(2,1)S(1)}, bf16[128,256]{1,0:T(8,128)(2,1)S(1)}, u32[]{:S(2)}, u32[]{:S(2)}) collective-permute-start(bf16[128,256]{1,0:T(8,128)(2,1)S(1)} %get-tuple-element.54), channel_id=1, source_target_pairs={{0,4},{4,0},{8,12},{12,8},{16,20},{20,16},{24,28},{28,24},{1,5},{5... | collective-permute-start | bytes 196616 | tf_op jit(solution)/shard_map/ppermute | solution.py:464
  58.0 4.3 %collective-permute-start.9 = (bf16[128,256]{1,0:T(8,128)(2,1)S(1)}, bf16[128,256]{1,0:T(8,128)(2,1)S(1)}, u32[]{:S(2)}, u32[]{:S(2)}) collective-permute-start(bf16[128,256]{1,0:T(8,128)(2,1)S(1)} %get-tuple-element.55), channel_id=1, source_target_pairs={{0,8},{4,12},{8,0},{12,4},{16,24},{20,28},{24,16},{28,20},{1,9},{5... | collective-permute-start | bytes 196616 | tf_op jit(solution)/shard_map/ppermute | solution.py:464
  58.0 5.2 %collective-permute-start.10 = (bf16[128,256]{1,0:T(8,128)(2,1)S(1)}, bf16[128,256]{1,0:T(8,128)(2,1)S(1)}, u32[]{:S(2)}, u32[]{:S(2)}) collective-permute-start(bf16[128,256]{1,0:T(8,128)(2,1)S(1)} %get-tuple-element.56), channel_id=1, source_target_pairs={{0,12},{4,8},{8,4},{12,0},{16,28},{20,24},{24,20},{28,16},{1,13},{... | collective-permute-start | bytes 196616 | tf_op jit(solution)/shard_map/ppermute | solution.py:464

commit v13 on v12

--- a/solution.py
+++ b/solution.py
@@ -17,7 +17,7 @@
 
 
 def params():
-    return pltpu.CompilerParams(vmem_limit_bytes=40 * 1024 * 1024)
+    return pltpu.CompilerParams(vmem_limit_bytes=20 * 1024 * 1024)
 
 
 def cost(flops, size):
@@ -109,8 +109,8 @@
     return [(rank, (rank + step) % count) for rank in range(count)]
 
 
-def sketch_kernel(count, chunks, features_in, sketch_in, index_in, *rest):
-    outs, (index_out, full, features, sketch, sems) = rest[:count], rest[count:]
+def sketch_kernel(count, chunks, features_in, sketch_in, halo_in, order_in, *rest):
+    outs, (halo_out, order_out, full, features, sketch, sems) = rest[:count], rest[count:]
     channels, width = outs[0].shape
     step = width // chunks
     copies = [pltpu.make_async_copy(sketch_in, sketch, sems.at[chunks])]
@@ -119,7 +119,8 @@
         copies.append(
             pltpu.make_async_copy(features_in.at[rows, :], features.at[rows, :], sems.at[chunk])
         )
-    copies.append(pltpu.make_async_copy(index_in, index_out, sems.at[chunks + 1]))
+    copies.append(pltpu.make_async_copy(halo_in, halo_out, sems.at[chunks + 1]))
+    copies.append(pltpu.make_async_copy(order_in, order_out, sems.at[chunks + 2]))
     for copy in copies:
         copy.start()
     copies[0].wait()
@@ -132,6 +133,7 @@
     me = lax.axis_index("rep")
     for part in range(count):
         outs[part][...] = full[partner(me, part, count)]
+    copies[-2].wait()
     copies[-1].wait()
 
 
@@ -209,23 +211,19 @@
     store_slots(send, pick(stack, blocks, index[...], side, group), group)
 
 
-def early_kernel(staged, index_in, tiles_in, hop, near, far, total, *rest):
-    full, index, tiles, sems = rest[-4:]
+def early_kernel(staged, index, tiles_in, hop, near, far, total, *rest):
+    full, tiles, sems = rest[-3:]
     blocks, channels, side = hop.shape
-    copies = [
-        pltpu.make_async_copy(index_in, index, sems.at[0]),
-        pltpu.make_async_copy(tiles_in.at[pl.ds(0, blocks)], tiles, sems.at[1]),
-    ]
+    copies = [pltpu.make_async_copy(tiles_in.at[pl.ds(0, blocks)], tiles, sems.at[0])]
     if staged:
         others = tiles_in.shape[0] - blocks
         copies.append(
-            pltpu.make_async_copy(tiles_in.at[pl.ds(blocks, others)], rest[0], sems.at[2])
+            pltpu.make_async_copy(tiles_in.at[pl.ds(blocks, others)], rest[0], sems.at[1])
         )
     for copy in copies:
         copy.start()
     peers, _, slot = full.shape
     stack = jnp.concatenate([hop[block] for block in range(blocks)], 0)
-    copies[0].wait()
     for peer, part in enumerate(pick(stack, blocks, index[...], side, slot)):
         full[peer] = part
     me = lax.axis_index("dom")
@@ -234,12 +232,12 @@
         near[step] = full[me ^ step]
         far[step] = full[me ^ half ^ step]
     ones = jnp.ones((EXTRA, side), BF16)
-    copies[1].wait()
+    copies[0].wait()
     for block in range(blocks):
         columns = jnp.concatenate([hop[block], ones], 0)
         total[block] = dot(columns, tiles[block], NT)[: channels + KEPT]
     if staged:
-        copies[2].wait()
+        copies[1].wait()
 
 
 def finish(turn, dst, src, tiles, total, hop, arrived, columns, sums):
@@ -367,7 +365,7 @@
     scatter(parts, table, block, out, out_ref, 0, sems)
 
 
-def place_rest_kernel(peers, _, table_ref, block_ref, *rest):
+def place_rest_kernel(peers, turn, _, table_ref, block_ref, *rest):
     moved, last, (out_ref, out, sems) = rest[:-4], rest[-4], rest[-3:]
     channels = out.shape[1]
     half = peers // 2
@@ -376,7 +374,7 @@
     for step in range(peers):
         first = (step // half) * channels
         arrived = moved[step % half][first : first + channels]
-        parts.append(jnp.concatenate([arrived, last[me ^ step ^ half]], 0))
+        parts.append(jnp.concatenate([arrived, last[me ^ step ^ turn]], 0))
     scatter(parts, table_ref[...], block_ref[...], out, out_ref, 1, sems)
 
 
@@ -412,12 +410,12 @@
     hop_shape = (blocks, channels, side)
     halo_shape = send_shape(channels, peers, halo // peers)
     last_shape = send_shape(3 * channels, peers, nodes // peers)
-    group = 256
+    group = 512
     chunks = 1
     slot = nodes // peers
     half = peers // 2
     whole_lanes = slot % 128 == 0 and (halo // peers) % 128 == 0
-    turn = half if whole_lanes and peers & (peers - 1) == 0 else 0
+    turn = half ^ 1 if whole_lanes and peers & (peers - 1) == 0 else 0
 
     def out(shape):
         return jax.ShapeDtypeStruct(shape, BF16)
@@ -433,18 +431,17 @@
                 jax.ShapeDtypeStruct((blocks, channels + KEPT, side), F32),
             )
             + (out(others),) * staged,
-            in_specs=[HBM, HBM, VMEM],
+            in_specs=[VMEM, HBM, VMEM],
             out_specs=(VMEM,) * (3 + staged),
             scratch_shapes=[
                 vmem((peers, channels, slot), BF16),
-                vmem(send_order.shape, jnp.int32),
                 vmem((blocks, side, side), BF16),
-                dma((3,)),
+                dma((2,)),
             ],
             compiler_params=params(),
             cost_estimate=cost(2 * channels * nodes * nodes, 8 * channels * nodes),
             name="early",
-        )(in_hbm(send_order), in_hbm(tiles), hop)
+        )(order_rows, in_hbm(tiles), hop)
         sent = lax.ppermute(far, "dom", pairs(peers // 2, peers))
         return (near, sent), total, rest
 
@@ -467,7 +464,7 @@
     def late(keep, index, others, total, hop, arrived):
         shape = (peers, channels, index.shape[1] // peers)
         return pl.pallas_call(
-            lambda *refs: finish_kernel(group, half, keep, *refs),
+            lambda *refs: finish_kernel(group, turn, keep, *refs),
             out_shape=(out(hop_shape),) * keep + (out(shape),),
             in_specs=[VMEM] * 7,
             out_specs=(VMEM,) * (keep + 1),
@@ -478,21 +475,24 @@
             compiler_params=params(),
         )(tile_dst, tile_src, index, others, total, hop, arrived)
 
-    *own, halo_rows = pl.pallas_call(
+    *own, halo_rows, order_rows = pl.pallas_call(
         lambda *refs: sketch_kernel(reps, chunks, *refs),
         out_shape=(out((channels, width)),) * reps
-        + (jax.ShapeDtypeStruct(halo_index.shape, jnp.int32),),
-        in_specs=[HBM] * 3,
-        out_specs=(VMEM,) * (reps + 1),
+        + (
+            jax.ShapeDtypeStruct(halo_index.shape, jnp.int32),
+            jax.ShapeDtypeStruct(send_order.shape, jnp.int32),
+        ),
+        in_specs=[HBM] * 4,
+        out_specs=(VMEM,) * (reps + 2),
         scratch_shapes=[
             vmem((reps, channels, width), BF16),
             vmem(features.shape, BF16),
             vmem(sketch_matrix.shape, BF16),
-            dma((chunks + 2,)),
+            dma((chunks + 3,)),
         ],
         compiler_params=params(),
         name="sketch",
-    )(in_hbm(features), in_hbm(sketch_matrix), in_hbm(halo_index))
+    )(in_hbm(features), in_hbm(sketch_matrix), in_hbm(halo_index), in_hbm(send_order))
     arrived = [own[0]]
     for step in range(1, reps):
         arrived.append(lax.ppermute(own[step], "rep", pairs(step, reps)))
@@ -511,7 +511,7 @@
         hop1, send = late(1, halo_rows, others, total, hop0, halo0)
         halo1 = exchange(send, peers, turn)
         early1, total, _ = early(hop1, 0)
-        (send,) = late(0, send_order, others, total, hop1, halo1)
+        (send,) = late(0, order_rows, others, total, hop1, halo1)
         last = exchange(send, peers, turn)
         moved0, moved1 = relay(early0), relay(early1)
         whole = out((3, channels, nodes))
@@ -530,7 +530,7 @@
             name="place0",
         )(arrival_place, *moved0)
         return pl.pallas_call(
-            lambda *refs: place_rest_kernel(peers, *refs),
+            lambda *refs: place_rest_kernel(peers, turn, *refs),
             out_shape=whole,
             in_specs=[HBM] + [VMEM] * (half + 3),
             out_specs=HBM,

time: 65.7 us -> 66.4 us (1.011)
  starting transfers between devices: 28.1 us -> 31 us
  waiting for transfers between devices: 22.5 us -> 20.9 us
    all_to_all x3, starting transfers between devices: 15 us -> 17.8 us  [exchange(): lax.all_to_all(send, 'dom', 0, 0, tiled=True, axis_index_groups=ranks)]
    all_to_all x3, waiting for transfers between devices: 5.98 us -> 4.3 us  [exchange(): lax.all_to_all(send, 'dom', 0, 0, tiled=True, axis_index_groups=ranks)]
  transfers between devices with their start and end apart: 14 -> 14, of which waited for: 7 -> 6; matrix products, arithmetic and copies ran while one was open for 0% -> 0% of each run, Pallas kernels for 9% -> 8%
where the time goes in v13:
time: 66.4 us; the launch traced here: 65.9 us
  starting transfers between devices  31 us (47%)
  waiting for transfers between devices  20.9 us (31%)
  Pallas kernels  13.9 us (21%)
    all_to_all x3, starting transfers between devices, exchange(): lax.all_to_all(send, 'dom', 0, 0, tiled=True, axis_index_groups=ranks)  17.8 us
    ppermute x2, waiting for transfers between devices, early(): sent = lax.ppermute(far, 'dom', pairs(peers // 2, peers))  11.3 us
    ppermute x6, starting transfers between devices, relay(): sent.append(lax.ppermute(moved[step], 'dom', pairs(step, peers)))  7.11 us
    all_to_all x3, waiting for transfers between devices, exchange(): lax.all_to_all(send, 'dom', 0, 0, tiled=True, axis_index_groups=ranks)  4.3 us
    ppermute x3, waiting for transfers between devices, on_device(): arrived.append(lax.ppermute(own[step], 'rep', pairs(step, reps)))  4.02 us
    pallas_call x2, Pallas kernels, late(): pl.pallas_call(lambda *refs: finish_kernel(group, turn, keep, *refs), out...  3.89 us
    pallas_call x2, Pallas kernels, early(): pl.pallas_call(lambda *refs: early_kernel(staged, *refs), out_shape=(out(...  3.44 us
    ppermute x3, starting transfers between devices, on_device(): arrived.append(lax.ppermute(own[step], 'rep', pairs(step, reps)))  3.15 us
  transfers between devices with their start and end apart: 14, of which 6 were waited for; matrix products, arithmetic and copies ran while one was open for 0% of the time, Pallas kernels for 8%

profile of v13, /device:TPU:0, one launch (start us, length us, event | category | flops | bytes accessed | tf_op | source)
XLA Modules:
  0.0 65.9 jit_solution(12795074287138840402)
XLA Ops:
  0.0 0.0 copy-start.1
  0.0 0.0 copy-start
  0.0 1.8 %sketch.1 = (bf16[64,512]{1,0:T(8,128)(2,1)S(1)}, bf16[64,512]{1,0:T(8,128)(2,1)S(1)}, bf16[64,512]{1,0:T(8,128)(2,1)S(1)}, bf16[64,512]{1,0:T(8,128)(2,1)S(1)},...) custom-call(bf16[512,768]{1,0:T(8,128)(2,1)} %refs_0_.4, bf16[768,256]{1,0:T(8,128)(2,1)} %refs_1_.3, s32[1,1024]{1,0:T(1,128)} %refs_2_.1, ...), custom_call_target="tpu_custom_call" | custom-call | tf_op jit(solution)/shard_map/sketch/pallas_call | solution.py:478
  1.8 0.6 collective-permute-start
  2.4 2.5 %collective-permute-start.1 = (bf16[64,512]{1,0:T(8,128)(2,1)S(1)}, bf16[64,512]{1,0:T(8,128)(2,1)S(1)}, u32[]{:S(2)}, u32[]{:S(2)}) collective-permute-start(bf16[64,512]{1,0:T(8,128)(2,1)S(1)} %get-tuple-element.37), channel_id=1, source_target_pairs={{0,2},{1,3},{2,0},{3,1},{4,6},{5,7},{6,4},{7,5},{8,10},{9,11},{10,... | collective-permute-start | bytes 196616 | tf_op jit(solution)/shard_map/ppermute | solution.py:498
  4.9 0.0 collective-permute-start.2
  4.9 0.0 collective-permute-done.refs_2_
  4.9 2.6 %collective-permute-done.1.refs_3_ = bf16[64,512]{1,0:T(8,128)(2,1)S(1)} collective-permute-done((bf16[64,512]{1,0:T(8,128)(2,1)S(1)}, bf16[64,512]{1,0:T(8,128)(2,1)S(1)}, u32[]{:S(2)}, u32[]{:S(2)}) %collective-permute-start.1) | collective-permute-done | bytes 65568 | tf_op jit(solution)/shard_map/ppermute | solution.py:498
  7.6 1.4 %collective-permute-done.2.refs_4_ = bf16[64,512]{1,0:T(8,128)(2,1)S(1)} collective-permute-done((bf16[64,512]{1,0:T(8,128)(2,1)S(1)}, bf16[64,512]{1,0:T(8,128)(2,1)S(1)}, u32[]{:S(2)}, u32[]{:S(2)}) %collective-permute-start.2) | collective-permute-done | bytes 65568 | tf_op jit(solution)/shard_map/ppermute | solution.py:498
  9.0 1.1 %pick.1 = (bf16[8,64,256]{2,1,0:T(8,128)(2,1)S(1)}, bf16[8,64,128]{2,1,0:T(8,128)(2,1)}) custom-call(s32[1,1024]{1,0:T(1,128)S(1)} %get-tuple-element.34.refs_0_.refs_2_, bf16[64,512]{1,0:T(8,128)(2,1)S(1)} %get-tuple-element.35.refs_1_, bf16[64,512]{1,0:T(8,128)(2,1)S(1)} %collective-permute-done.refs_2_, ...), custom_call_target="tpu_custom_call" | custom-call | tf_op jit(solution)/shard_map/pick/pallas_call | solution.py:499
  10.1 6.8 %all-to-all-start = ((bf16[8,64,128]{2,1,0:T(8,128)(2,1)}), bf16[8,64,128]{2,1,0:T(8,128)(2,1)S(1)}, u32[]{:S(2)}, u32[]{:S(2)}) async-start(bf16[8,64,128]{2,1,0:T(8,128)(2,1)} %get-tuple-element.51), calls=%async_computation | async-start | bytes 262144 | tf_op jit(solution)/shard_map/all_to_all | solution.py:82
  16.9 1.7 %early.2 = (bf16[4,64,256]{2,1,0:T(8,128)(2,1)S(1)}, bf16[4,64,256]{2,1,0:T(8,128)(2,1)S(1)}, f32[8,72,256]{2,1,0:T(8,128)S(1)}, bf16[12,256,256]{2,1,0:T(8,128)(2,1)S(1)}) custom-call(s32[1,2048]{1,0:T(1,128)S(1)} %get-tuple-element.33.refs_0_.refs_2_, bf16[20,256,256]{2,1,0:T(8,128)(2,1)} %bitcast.1, bf16[8,64,256]{2,1,0:T(8,128)(2,1)S(1)} %get-tuple-element.39.refs_2_.refs_5_), custom_call_target="tpu_custom_call" | custom-call | flops 536870912 | bytes 1048576 | tf_op jit(solution)/shard_map/early/pallas_call | solution.py:426
  18.7 2.3 %all-to-all-done.refs_6_ = bf16[8,64,128]{2,1,0:T(8,128)(2,1)S(1)} async-done(((bf16[8,64,128]{2,1,0:T(8,128)(2,1)}), bf16[8,64,128]{2,1,0:T(8,128)(2,1)S(1)}, u32[]{:S(2)}, u32[]{:S(2)}) %all-to-all-start) | async-done | bytes 131104 | tf_op jit(solution)/shard_map/all_to_all | solution.py:82
  21.0 0.0 copy-done.1
  21.0 0.0 copy-done
  21.0 1.8 %shard_map.82 = (bf16[8,64,256]{2,1,0:T(8,128)(2,1)S(1)}, bf16[8,64,128]{2,1,0:T(8,128)(2,1)}) custom-call(s32[1,20]{1,0:T(1,128)S(1)} %copy-done, s32[1,20]{1,0:T(1,128)S(1)} %copy-done.1, s32[1,1024]{1,0:T(1,128)S(1)} %get-tuple-element.34.refs_0_.refs_2_, bf16[12,256,256]{2,1,0:T(8,128)(2,1)S(1)} %get-tuple-element.49.refs_3_, ...), custom_call_target="tpu_custom_call" | custom-call | tf_op jit(solution)/shard_map/pallas_call | solution.py:466
  22.7 5.5 %all-to-all-start.1 = ((bf16[8,64,128]{2,1,0:T(8,128)(2,1)}), bf16[8,64,128]{2,1,0:T(8,128)(2,1)S(1)}, u32[]{:S(2)}, u32[]{:S(2)}) async-start(bf16[8,64,128]{2,1,0:T(8,128)(2,1)} %get-tuple-element.60), calls=%async_computation.1 | async-start | bytes 262144 | tf_op jit(solution)/shard_map/all_to_all | solution.py:82
  28.3 1.7 %early.3 = (bf16[4,64,256]{2,1,0:T(8,128)(2,1)S(1)}, bf16[4,64,256]{2,1,0:T(8,128)(2,1)S(1)}, f32[8,72,256]{2,1,0:T(8,128)S(1)}) custom-call(s32[1,2048]{1,0:T(1,128)S(1)} %get-tuple-element.33.refs_0_.refs_2_, bf16[20,256,256]{2,1,0:T(8,128)(2,1)} %bitcast.2, bf16[8,64,256]{2,1,0:T(8,128)(2,1)S(1)} %get-tuple-element.52.refs_2_.refs_5_), custom_call_target="tpu_custom_call" | custom-call | flops 536870912 | bytes 1048576 | tf_op jit(solution)/shard_map/early/pallas_call | solution.py:426
  30.0 0.0 copy-start.2
  30.0 2.0 %all-to-all-done.1.refs_6_ = bf16[8,64,128]{2,1,0:T(8,128)(2,1)S(1)} async-done(((bf16[8,64,128]{2,1,0:T(8,128)(2,1)}), bf16[8,64,128]{2,1,0:T(8,128)(2,1)S(1)}, u32[]{:S(2)}, u32[]{:S(2)}) %all-to-all-start.1) | async-done | bytes 131104 | tf_op jit(solution)/shard_map/all_to_all | solution.py:82
  32.0 2.1 %shard_map.83 = bf16[8,64,256]{2,1,0:T(8,128)(2,1)} custom-call(s32[1,20]{1,0:T(1,128)S(1)} %copy-done, s32[1,20]{1,0:T(1,128)S(1)} %copy-done.1, s32[1,2048]{1,0:T(1,128)S(1)} %get-tuple-element.33.refs_0_.refs_2_, bf16[12,256,256]{2,1,0:T(8,128)(2,1)S(1)} %get-tuple-element.49.refs_3_, f32[8,72,256]{2,1,0:T(8,128)S(1)} %get-tuple-element.59.refs_4_, ...), custom_call_target="tpu_custom_call" | custom-call | tf_op jit(solution)/shard_map/pallas_call | solution.py:466
  34.1 5.4 %all-to-all-start.2 = ((bf16[8,64,256]{2,1,0:T(8,128)(2,1)}), bf16[8,64,256]{2,1,0:T(8,128)(2,1)S(1)}, u32[]{:S(2)}, u32[]{:S(2)}) async-start(bf16[8,64,256]{2,1,0:T(8,128)(2,1)} %shard_map.83), calls=%async_computation.2 | async-start | bytes 524288 | tf_op jit(solution)/shard_map/all_to_all | solution.py:82
  39.6 0.6 collective-permute-start.3
  40.1 2.4 %collective-permute-start.7 = (bf16[4,64,256]{2,1,0:T(8,128)(2,1)S(1)}, bf16[4,64,256]{2,1,0:T(8,128)(2,1)S(1)}, u32[]{:S(2)}, u32[]{:S(2)}) collective-permute-start(bf16[4,64,256]{2,1,0:T(8,128)(2,1)S(1)} %get-tuple-element.54), channel_id=1, source_target_pairs={{0,16},{4,20},{8,24},{12,28},{16,0},{20,4},{24,8},{28,12},{1,17},{... | collective-permute-start | bytes 393224 | tf_op jit(solution)/shard_map/ppermute | solution.py:445
  42.5 11.3 %collective-permute-done.3.sent = bf16[4,64,256]{2,1,0:T(8,128)(2,1)S(1)} collective-permute-done((bf16[4,64,256]{2,1,0:T(8,128)(2,1)S(1)}, bf16[4,64,256]{2,1,0:T(8,128)(2,1)S(1)}, u32[]{:S(2)}, u32[]{:S(2)}) %collective-permute-start.3) | collective-permute-done | bytes 131104 | tf_op jit(solution)/shard_map/ppermute | solution.py:445
  53.8 0.8 %collective-permute-start.4 = (bf16[128,256]{1,0:T(8,128)(2,1)S(1)}, bf16[128,256]{1,0:T(8,128)(2,1)S(1)}, u32[]{:S(2)}, u32[]{:S(2)}) collective-permute-start(bf16[128,256]{1,0:T(8,128)(2,1)S(1)} %get-tuple-element.43), channel_id=1, source_target_pairs={{0,4},{4,0},{8,12},{12,8},{16,20},{20,16},{24,28},{28,24},{1,5},{5... | collective-permute-start | bytes 196616 | tf_op jit(solution)/shard_map/ppermute | solution.py:461
  54.6 0.0 collective-permute-start.5
  54.6 2.7 %collective-permute-start.6 = (bf16[128,256]{1,0:T(8,128)(2,1)S(1)}, bf16[128,256]{1,0:T(8,128)(2,1)S(1)}, u32[]{:S(2)}, u32[]{:S(2)}) collective-permute-start(bf16[128,256]{1,0:T(8,128)(2,1)S(1)} %get-tuple-element.45), channel_id=1, source_target_pairs={{0,12},{4,8},{8,4},{12,0},{16,28},{20,24},{24,20},{28,16},{1,13},{... | collective-permute-start | bytes 196616 | tf_op jit(solution)/shard_map/ppermute | solution.py:461
  57.4 0.0 collective-permute-done.7.sent
  57.4 0.8 %collective-permute-start.8 = (bf16[128,256]{1,0:T(8,128)(2,1)S(1)}, bf16[128,256]{1,0:T(8,128)(2,1)S(1)}, u32[]{:S(2)}, u32[]{:S(2)}) collective-permute-start(bf16[128,256]{1,0:T(8,128)(2,1)S(1)} %get-tuple-element.56), channel_id=1, source_target_pairs={{0,4},{4,0},{8,12},{12,8},{16,20},{20,16},{24,28},{28,24},{1,5},{5... | collective-permute-start | bytes 196616 | tf_op jit(solution)/shard_map/ppermute | solution.py:461
  58.2 0.0 collective-permute-start.9
  58.2 0.0 collective-permute-done.4.refs_2_
  58.2 2.7 %collective-permute-start.10 = (bf16[128,256]{1,0:T(8,128)(2,1)S(1)}, bf16[128,256]{1,0:T(8,128)(2,1)S(1)}, u32[]{:S(2)}, u32[]{:S(2)}) collective-permute-start(bf16[128,256]{1,0:T(8,128)(2,1)S(1)} %get-tuple-element.58), channel_id=1, source_target_pairs={{0,12},{4,8},{8,4},{12,0},{16,28},{20,24},{24,20},{28,16},{1,13},{... | collective-permute-start | bytes 196616 | tf_op jit(solution)/shard_map/ppermute | solution.py:461
  61.0 0.0 collective-permute-done.5.refs_3_
  61.0 0.0 collective-permute-done.6.refs_4_
  61.0 0.0 copy-done.2
  61.0 1.6 %place0.1 = (bf16[3,64,2048]{2,1,0:T(8,128)(2,1)}, bf16[2048,256]{1,0:T(8,128)(2,1)S(1)}, s32[1,2048]{1,0:T(1,128)S(1)}) custom-call(s32[1,2048]{1,0:T(1,128)S(1)} %copy-done.2, bf16[128,256]{1,0:T(8,128)(2,1)S(1)} %get-tuple-element.42.refs_1_, bf16[128,256]{1,0:T(8,128)(2,1)S(1)} %collective-permute-done.4.refs_2_, ...), custom_call_target="tpu_custom_call" | custom-call | flops 536870912 | bytes 524288 | tf_op jit(solution)/shard_map/place0/pallas_call | solution.py:518
  62.6 0.0 collective-permute-done.8.refs_4_
  62.6 0.0 collective-permute-done.9.refs_5_
  62.6 1.3 %collective-permute-done.10.refs_6_ = bf16[128,256]{1,0:T(8,128)(2,1)S(1)} collective-permute-done((bf16[128,256]{1,0:T(8,128)(2,1)S(1)}, bf16[128,256]{1,0:T(8,128)(2,1)S(1)}, u32[]{:S(2)}, u32[]{:S(2)}) %collective-permute-start.10) | collective-permute-done | bytes 65568 | tf_op jit(solution)/shard_map/ppermute | solution.py:461
  63.9 0.0 all-to-all-done.2.refs_7_
  63.9 2.0 %place.1 = bf16[3,64,2048]{2,1,0:T(8,128)(2,1)} custom-call(bf16[3,64,2048]{2,1,0:T(8,128)(2,1)} %get-tuple-element.46.refs_0_, bf16[2048,256]{1,0:T(8,128)(2,1)S(1)} %get-tuple-element.47.refs_1_, s32[1,2048]{1,0:T(1,128)S(1)} %get-tuple-element.48.refs_2_, bf16[128,256]{1,0:T(8,128)(2,1)S(1)} %get-tuple-element.55.refs_3_, ...), custom_call_target="tpu_custom_call", output_to_operand_aliasing={{}: (0, {})} | custom-call | tf_op jit(solution)/shard_map/place/pallas_call | solution.py:532
  (2 shorter events, 0.0 us)
Async XLA Ops:
  0.0 21.0 %copy-start.1 = (s32[1,20]{1,0:T(1,128)S(1)}, s32[1,20]{1,0:T(1,128)}, u32[]{:S(2)}) copy-start(s32[1,20]{1,0:T(1,128)} %refs_1_.5) | copy-start | bytes 244
  0.0 21.0 %copy-start = (s32[1,20]{1,0:T(1,128)S(1)}, s32[1,20]{1,0:T(1,128)}, u32[]{:S(2)}) copy-start(s32[1,20]{1,0:T(1,128)} %refs_0_.7) | copy-start | bytes 244
  1.8 3.2 %collective-permute-start = (bf16[64,512]{1,0:T(8,128)(2,1)S(1)}, bf16[64,512]{1,0:T(8,128)(2,1)S(1)}, u32[]{:S(2)}, u32[]{:S(2)}) collective-permute-start(bf16[64,512]{1,0:T(8,128)(2,1)S(1)} %get-tuple-element.36), channel_id=1, source_target_pairs={{0,1},{1,0},{2,3},{3,2},{4,5},{5,4},{6,7},{7,6},{8,9},{9,8},{10,11... | collective-permute-start | bytes 196616 | tf_op jit(solution)/shard_map/ppermute | solution.py:498
  2.4 5.2 %collective-permute-start.1 = (bf16[64,512]{1,0:T(8,128)(2,1)S(1)}, bf16[64,512]{1,0:T(8,128)(2,1)S(1)}, u32[]{:S(2)}, u32[]{:S(2)}) collective-permute-start(bf16[64,512]{1,0:T(8,128)(2,1)S(1)} %get-tuple-element.37), channel_id=1, source_target_pairs={{0,2},{1,3},{2,0},{3,1},{4,6},{5,7},{6,4},{7,5},{8,10},{9,11},{10,... | collective-permute-start | bytes 196616 | tf_op jit(solution)/shard_map/ppermute | solution.py:498
  4.9 4.1 %collective-permute-start.2 = (bf16[64,512]{1,0:T(8,128)(2,1)S(1)}, bf16[64,512]{1,0:T(8,128)(2,1)S(1)}, u32[]{:S(2)}, u32[]{:S(2)}) collective-permute-start(bf16[64,512]{1,0:T(8,128)(2,1)S(1)} %get-tuple-element.38), channel_id=1, source_target_pairs={{0,3},{1,2},{2,1},{3,0},{4,7},{5,6},{6,5},{7,4},{8,11},{9,10},{10,... | collective-permute-start | bytes 196616 | tf_op jit(solution)/shard_map/ppermute | solution.py:498
  10.1 10.9 %all-to-all-start = ((bf16[8,64,128]{2,1,0:T(8,128)(2,1)}), bf16[8,64,128]{2,1,0:T(8,128)(2,1)S(1)}, u32[]{:S(2)}, u32[]{:S(2)}) async-start(bf16[8,64,128]{2,1,0:T(8,128)(2,1)} %get-tuple-element.51), calls=%async_computation | async-start | bytes 262144 | tf_op jit(solution)/shard_map/all_to_all | solution.py:82
  22.7 9.2 %all-to-all-start.1 = ((bf16[8,64,128]{2,1,0:T(8,128)(2,1)}), bf16[8,64,128]{2,1,0:T(8,128)(2,1)S(1)}, u32[]{:S(2)}, u32[]{:S(2)}) async-start(bf16[8,64,128]{2,1,0:T(8,128)(2,1)} %get-tuple-element.60), calls=%async_computation.1 | async-start | bytes 262144 | tf_op jit(solution)/shard_map/all_to_all | solution.py:82
  30.0 31.0 %copy-start.2 = (s32[1,2048]{1,0:T(1,128)S(1)}, s32[1,2048]{1,0:T(1,128)}, u32[]{:S(2)}) copy-start(s32[1,2048]{1,0:T(1,128)} %refs_0_.5) | copy-start | bytes 24580
  34.1 29.8 %all-to-all-start.2 = ((bf16[8,64,256]{2,1,0:T(8,128)(2,1)}), bf16[8,64,256]{2,1,0:T(8,128)(2,1)S(1)}, u32[]{:S(2)}, u32[]{:S(2)}) async-start(bf16[8,64,256]{2,1,0:T(8,128)(2,1)} %shard_map.83), calls=%async_computation.2 | async-start | bytes 524288 | tf_op jit(solution)/shard_map/all_to_all | solution.py:82
  39.6 14.2 %collective-permute-start.3 = (bf16[4,64,256]{2,1,0:T(8,128)(2,1)S(1)}, bf16[4,64,256]{2,1,0:T(8,128)(2,1)S(1)}, u32[]{:S(2)}, u32[]{:S(2)}) collective-permute-start(bf16[4,64,256]{2,1,0:T(8,128)(2,1)S(1)} %get-tuple-element.41), channel_id=1, source_target_pairs={{0,16},{4,20},{8,24},{12,28},{16,0},{20,4},{24,8},{28,12},{1,17},{... | collective-permute-start | bytes 393224 | tf_op jit(solution)/shard_map/ppermute | solution.py:445
  40.1 17.2 %collective-permute-start.7 = (bf16[4,64,256]{2,1,0:T(8,128)(2,1)S(1)}, bf16[4,64,256]{2,1,0:T(8,128)(2,1)S(1)}, u32[]{:S(2)}, u32[]{:S(2)}) collective-permute-start(bf16[4,64,256]{2,1,0:T(8,128)(2,1)S(1)} %get-tuple-element.54), channel_id=1, source_target_pairs={{0,16},{4,20},{8,24},{12,28},{16,0},{20,4},{24,8},{28,12},{1,17},{... | collective-permute-start | bytes 393224 | tf_op jit(solution)/shard_map/ppermute | solution.py:445
  53.8 4.4 %collective-permute-start.4 = (bf16[128,256]{1,0:T(8,128)(2,1)S(1)}, bf16[128,256]{1,0:T(8,128)(2,1)S(1)}, u32[]{:S(2)}, u32[]{:S(2)}) collective-permute-start(bf16[128,256]{1,0:T(8,128)(2,1)S(1)} %get-tuple-element.43), channel_id=1, source_target_pairs={{0,4},{4,0},{8,12},{12,8},{16,20},{20,16},{24,28},{28,24},{1,5},{5... | collective-permute-start | bytes 196616 | tf_op jit(solution)/shard_map/ppermute | solution.py:461
  54.6 6.3 %collective-permute-start.5 = (bf16[128,256]{1,0:T(8,128)(2,1)S(1)}, bf16[128,256]{1,0:T(8,128)(2,1)S(1)}, u32[]{:S(2)}, u32[]{:S(2)}) collective-permute-start(bf16[128,256]{1,0:T(8,128)(2,1)S(1)} %get-tuple-element.44), channel_id=1, source_target_pairs={{0,8},{4,12},{8,0},{12,4},{16,24},{20,28},{24,16},{28,20},{1,9},{5... | collective-permute-start | bytes 196616 | tf_op jit(solution)/shard_map/ppermute | solution.py:461
  54.6 6.3 %collective-permute-start.6 = (bf16[128,256]{1,0:T(8,128)(2,1)S(1)}, bf16[128,256]{1,0:T(8,128)(2,1)S(1)}, u32[]{:S(2)}, u32[]{:S(2)}) collective-permute-start(bf16[128,256]{1,0:T(8,128)(2,1)S(1)} %get-tuple-element.45), channel_id=1, source_target_pairs={{0,12},{4,8},{8,4},{12,0},{16,28},{20,24},{24,20},{28,16},{1,13},{... | collective-permute-start | bytes 196616 | tf_op jit(solution)/shard_map/ppermute | solution.py:461
  57.4 5.2 %collective-permute-start.8 = (bf16[128,256]{1,0:T(8,128)(2,1)S(1)}, bf16[128,256]{1,0:T(8,128)(2,1)S(1)}, u32[]{:S(2)}, u32[]{:S(2)}) collective-permute-start(bf16[128,256]{1,0:T(8,128)(2,1)S(1)} %get-tuple-element.56), channel_id=1, source_target_pairs={{0,4},{4,0},{8,12},{12,8},{16,20},{20,16},{24,28},{28,24},{1,5},{5... | collective-permute-start | bytes 196616 | tf_op jit(solution)/shard_map/ppermute | solution.py:461
  58.2 4.4 %collective-permute-start.9 = (bf16[128,256]{1,0:T(8,128)(2,1)S(1)}, bf16[128,256]{1,0:T(8,128)(2,1)S(1)}, u32[]{:S(2)}, u32[]{:S(2)}) collective-permute-start(bf16[128,256]{1,0:T(8,128)(2,1)S(1)} %get-tuple-element.57), channel_id=1, source_target_pairs={{0,8},{4,12},{8,0},{12,4},{16,24},{20,28},{24,16},{28,20},{1,9},{5... | collective-permute-start | bytes 196616 | tf_op jit(solution)/shard_map/ppermute | solution.py:461
  58.2 5.7 %collective-permute-start.10 = (bf16[128,256]{1,0:T(8,128)(2,1)S(1)}, bf16[128,256]{1,0:T(8,128)(2,1)S(1)}, u32[]{:S(2)}, u32[]{:S(2)}) collective-permute-start(bf16[128,256]{1,0:T(8,128)(2,1)S(1)} %get-tuple-element.58), channel_id=1, source_target_pairs={{0,12},{4,8},{8,4},{12,0},{16,28},{20,24},{24,20},{28,16},{1,13},{... | collective-permute-start | bytes 196616 | tf_op jit(solution)/shard_map/ppermute | solution.py:461
